TPU v7x, 32 devices: a whole 2x2x4 slice. The times are simulated.
32 devices in a mesh: grp: 2 (over y), tile: 4 (over z), span: 4 (over x, core).
Axes of the slice: x: 2, y: 2, z: 4, core: 2. Of those that a mesh axis runs over, the one named last changes fastest.
Arguments:
- features: bfloat16 [16, 8, 160, 384], P(('grp', 'span'), 'tile'), parts along dimension 0, may hold values from -24 to 24
- clip_lengths: int32 [8], P('grp'), parts along dimension 0, may hold values from 1 to 4, as said below
- norm_gain: float32 [384], replicated, may hold values from 0.1 to 1.9
- w_qkv: bfloat16 [384, 1152], replicated, may hold values from -6 to 6
- w_out: bfloat16 [384, 384], replicated, may hold values from -1 to 1
- conv_gain: float32 [384], replicated, may hold values from 0.1 to 1.9
- w_conv: bfloat16 [3, 3, 3, 384, 384], replicated, may hold values from -0.0625 to 0.0625
Outputs:
- attended: bfloat16 [16, 8, 160, 384], P(('grp', 'span'), 'tile'), parts along dimension 0
- hidden: bfloat16 [16, 8, 160, 384], P(('grp', 'span'), 'tile'), parts along dimension 0
There are 2 independent parts, one for each index of `grp`. A program takes and returns all parts, laid end to end along the dimension named above; an argument that names none is the same for every part. Nothing has to cross between parts.
Inputs may be any that keep to these rules, and one draw needn't show every extreme that they name: `clip_lengths`: the lengths sum to 8; exactly one clip has 4 frames.
All inputs are finite; a program needn't handle non-finite values.
Results may differ from a plain program's by a relative error of at most 0.0095.
The roundings to bfloat16 on the way count: a program that leaves them out, or rounds other values in their place, can miss the bound.
Values may be sent and summed in bfloat16 or wider, within the bound.
No kernel may reach another device: no remote copies, remote signals or barrier semaphores. Data moves between devices by JAX's collectives and lax.ppermute only.
A program may use at most 128 MiB of HBM per device.

v0:
```python
import jax
import jax.numpy as jnp
from jax import lax
from jax.sharding import PartitionSpec as P

eps = 1e-06


def from_behind(block, axis, distance):
    devices = range(lax.axis_size(axis))
    route = [(i - distance, i) for i in devices if i - distance in devices]
    return lax.ppermute(block, axis, route)


def extended(x, sides, width):
    for axis, dim in sides:
        size, length = (lax.axis_size(axis), x.shape[dim])
        up = [(i, (i + 1) % size) for i in range(size - 1)]
        down = [(j, i) for i, j in up]
        last = lax.slice_in_dim(x, length - width, length, axis=dim)
        first = lax.slice_in_dim(x, 0, width, axis=dim)
        before = lax.ppermute(last, axis, up)
        after = lax.ppermute(first, axis, down)
        x = jnp.concatenate([before, x, after], axis=dim)
    return x


def rms_scale(values, gain_vec):
    as_float = values.astype(jnp.float32)
    return (
        as_float * lax.rsqrt(jnp.mean(as_float * as_float, axis=-1, keepdims=True) + eps) * gain_vec
    )


def on_device(features, clip_lengths, norm_gain, w_qkv, w_out, conv_gain, w_conv):
    frames, row_count, col_count, channels = features.shape
    cell_count = row_count * col_count
    normed_grid = rms_scale(features, norm_gain).astype(jnp.bfloat16)
    view_frames = normed_grid.shape[0]
    view_cells = normed_grid.shape[1] * normed_grid.shape[2]
    normed = normed_grid.reshape(view_frames, view_cells, channels)
    queries = jnp.dot(
        normed.reshape(-1, channels), w_qkv[:, :channels], preferred_element_type=jnp.float32
    )
    queries = queries.astype(jnp.bfloat16).reshape(view_frames, view_cells, channels)
    kv_weight = w_qkv[:, channels:]
    score_scale = channels ** (-0.5)
    outgoing = jnp.dot(normed.reshape(-1, channels), kv_weight, preferred_element_type=jnp.float32)
    outgoing = outgoing.astype(jnp.bfloat16).reshape(view_frames, view_cells, 2 * channels)
    portion = lax.all_gather(outgoing, "tile", axis=1, tiled=True)
    key_part = portion[:, :, :channels]
    value_part = portion[:, :, channels:]
    row_top = jnp.full((view_frames, view_cells, 1), -1e30, jnp.float32)
    scores = (
        jnp.einsum("fqc,fkc->fqk", queries, key_part, preferred_element_type=jnp.float32)
        * score_scale
    )
    new_top = jnp.maximum(row_top, jnp.max(scores, axis=2, keepdims=True))
    raised_f = jnp.exp(scores - new_top)
    row_total = jnp.sum(raised_f, axis=2, keepdims=True)
    weighted = jnp.einsum(
        "fqk,fkc->fqc",
        raised_f.astype(jnp.bfloat16),
        value_part,
        preferred_element_type=jnp.float32,
    )
    mixture_grid = (weighted / row_total).astype(jnp.bfloat16)
    mixture = mixture_grid.reshape(-1, channels)
    projected = jnp.dot(mixture, w_out, preferred_element_type=jnp.float32)
    attended = (features.reshape(-1, channels).astype(jnp.float32) + projected).astype(jnp.bfloat16)
    attended = attended.reshape(frames, row_count, col_count, channels)
    lifted = rms_scale(attended, conv_gain)
    activated = (lifted * jax.nn.sigmoid(lifted)).astype(jnp.bfloat16)
    earlier = from_behind(activated, "span", 1)
    stacked = jnp.concatenate([earlier, activated], axis=0)
    edged = extended(stacked, (("tile", 1),), 1)
    padded = jnp.pad(edged, ((0, 0), (0, 0), (1, 1), (0, 0)))
    clip_ends = jnp.cumsum(clip_lengths)
    position = lax.axis_index("span") * frames + jnp.arange(frames, dtype=jnp.int32)
    clip_start = jnp.sum(
        jnp.where(clip_ends[None, :] <= position[:, None], clip_lengths[None, :], 0), axis=1
    )
    summed = jnp.zeros((frames * cell_count, channels), jnp.float32)
    for t_tap in range(3):
        usable = position - (2 - t_tap) >= clip_start
        for r_tap in range(3):
            for c_tap in range(3):
                shifted = padded[
                    t_tap : t_tap + frames, r_tap : r_tap + row_count, c_tap : c_tap + col_count
                ]
                shifted = jnp.where(
                    usable[:, None, None, None], shifted, jnp.zeros((), shifted.dtype)
                )
                summed = summed + jnp.dot(
                    shifted.reshape(-1, channels),
                    w_conv[t_tap, r_tap, c_tap],
                    preferred_element_type=jnp.float32,
                )
    hidden = summed.astype(jnp.bfloat16).reshape(frames, row_count, col_count, channels)
    return (attended, hidden)


def solution(mesh):
    in_specs = (P(("grp", "span"), "tile", None, None), P("grp"), P(), P(), P(), P(), P())
    out_specs = (P(("grp", "span"), "tile", None, None), P(("grp", "span"), "tile", None, None))
    return jax.shard_map(
        on_device, mesh=mesh, in_specs=in_specs, out_specs=out_specs, check_vma=False
    )
```

profile of v0, /device:TPU:13, one launch (start us, length us, event | category | flops | bytes accessed | tf_op | source)
XLA Modules:
  0.0 144.2 jit_solution(7980055820085720016)
XLA Ops:
  7.2 0.0 copy-start
  7.2 0.0 all-gather.2.cloned.1.call-start
  7.2 1.3 multiply_reduce_fusion
  8.5 1.2 multiply_convert_fusion.1
  9.8 2.7 %convolution_convert_fusion = bf16[640,768]{1,0:T(8,128)(2,1)} fusion(bf16[640,384]{1,0:T(8,128)(2,1)S(1)} %bitcast.177, bf16[384,1152]{1,0:T(8,128)(2,1)} %param.10), kind=kOutput, calls=%fused_computation.18 | convolution fusion | flops 377978880 | bytes 2064384 | tf_op jit(solution)/shard_map/dot_general | solution.py:48
  12.4 0.0 all-gather.2.cloned.1.call-update
  12.5 1.4 convolution_convert_fusion.1
  13.9 73.9 %all-gather.2.cloned.1.call-done = bf16[2,1280,768]{2,1,0:T(8,128)(2,1)} async-done(((bf16[2,320,768]{2,1,0:T(8,128)(2,1)}), bf16[2,1280,768]{2,1,0:T(8,128)(2,1)}) %all-gather.2.cloned.1.call-update) | async-done | bytes 3932176 | tf_op jit(solution)/shard_map/all_gather | solution.py:50
  87.8 2.8 %fusion.98 = (f32[2,320]{1,0:T(2,128)S(1)}, f32[2,320,1280]{2,1,0:T(8,128)S(1)}) fusion(bf16[2,320,384]{2,1,0:T(8,128)(2,1)S(1)} %bitcast.179, bf16[2,1280,768]{2,1,0:T(8,128)(2,1)} %all-gather.2.cloned.1.call-done), kind=kOutput, calls=%fused_computation.171 | convolution fusion | flops 630783360 | bytes 5736960 | tf_op jit(solution)/shard_map/fqc,fkc->fqk/dot_general | solution.py:55
  90.6 0.6 fusion.1
  91.3 0.0 copy-start.1
  91.3 0.0 copy-start.4
  91.3 1.1 divide_convert_fusion
  92.4 0.0 copy-start.5
  92.4 0.6 fusion.14
  93.0 0.0 copy-start.3
  93.0 0.1 rsqrt.22
  93.1 0.4 multiply_convert_fusion
  93.5 3.7 %collective-permute-start = (bf16[2,2,160,384]{3,2,1,0:T(8,128)(2,1)S(1)}, bf16[2,2,160,384]{3,2,1,0:T(8,128)(2,1)S(1)}, u32[]{:S(2)}, u32[]{:S(2)}) collective-permute-start(bf16[2,2,160,384]{3,2,1,0:T(8,128)(2,1)S(1)} %multiply_convert_fusion), channel_id=1, source_target_pairs={{0,1},{1,2},{2,3},{4,5},{5,6},{6,7},{8,9},{9,10},{10,11},{12,13},{... | collective-permute-start | bytes 1474568 | tf_op jit(solution)/shard_map/ppermute | solution.py:12
  97.1 5.8 %collective-permute-done = bf16[2,2,160,384]{3,2,1,0:T(8,128)(2,1)S(1)} collective-permute-done((bf16[2,2,160,384]{3,2,1,0:T(8,128)(2,1)S(1)}, bf16[2,2,160,384]{3,2,1,0:T(8,128)(2,1)S(1)}, u32[]{:S(2)}, u32[]{:S(2)}) %collective-permute-start) | collective-permute-done | bytes 491552 | tf_op jit(solution)/shard_map/ppermute | solution.py:12
  102.9 0.9 fusion.30
  103.8 4.1 %collective-permute-start.1 = (bf16[4,1,160,384]{3,2,1,0:T(8,128)(2,1)}, bf16[4,1,160,384]{3,2,1,0:T(8,128)(2,1)S(1)}, u32[]{:S(2)}, u32[]{:S(2)}) collective-permute-start(bf16[4,1,160,384]{3,2,1,0:T(8,128)(2,1)} %get-tuple-element.34), channel_id=1, source_target_pairs={{0,4},{4,8},{8,12},{1,5},{5,9},{9,13},{2,6},{6,10},{10,14},{3,7},{... | collective-permute-start | bytes 1474568 | tf_op jit(solution)/shard_map/ppermute | solution.py:22
  107.9 1.9 %collective-permute-start.2 = (bf16[4,1,160,384]{3,2,1,0:T(8,128)(2,1)S(1)}, bf16[4,1,160,384]{3,2,1,0:T(8,128)(2,1)S(1)}, u32[]{:S(2)}, u32[]{:S(2)}) collective-permute-start(bf16[4,1,160,384]{3,2,1,0:T(8,128)(2,1)S(1)} %get-tuple-element.35), channel_id=1, source_target_pairs={{4,0},{8,4},{12,8},{5,1},{9,5},{13,9},{6,2},{10,6},{14,10},{7,3},{... | collective-permute-start | bytes 1474568 | tf_op jit(solution)/shard_map/ppermute | solution.py:23
  109.8 0.2 reduce-window.8
  110.0 0.2 fusion.94
  110.2 0.1 broadcast_in_dim.186
  110.3 0.1 broadcast_in_dim.187
  110.4 3.8 %collective-permute-done.1 = bf16[4,1,160,384]{3,2,1,0:T(8,128)(2,1)S(1)} collective-permute-done((bf16[4,1,160,384]{3,2,1,0:T(8,128)(2,1)}, bf16[4,1,160,384]{3,2,1,0:T(8,128)(2,1)S(1)}, u32[]{:S(2)}, u32[]{:S(2)}) %collective-permute-start.1) | collective-permute-done | bytes 491552 | tf_op jit(solution)/shard_map/ppermute | solution.py:22
  114.1 3.8 %collective-permute-done.2 = bf16[4,1,160,384]{3,2,1,0:T(8,128)(2,1)S(1)} collective-permute-done((bf16[4,1,160,384]{3,2,1,0:T(8,128)(2,1)S(1)}, bf16[4,1,160,384]{3,2,1,0:T(8,128)(2,1)S(1)}, u32[]{:S(2)}, u32[]{:S(2)}) %collective-permute-start.2) | collective-permute-done | bytes 491552 | tf_op jit(solution)/shard_map/ppermute | solution.py:23
  117.9 1.2 select_maximum_fusion
  119.1 1.4 slice_select_fusion
  120.5 0.0 slice-start
  120.5 0.3 pad_maximum_fusion
  120.8 0.0 slice-start.1
  120.8 1.5 %slice_select_fusion.6 = (bf16[2,2,160,384]{3,2,1,0:T(8,128)(2,1)S(1)}, bf16[2,2,160,384]{3,2,1,0:T(8,128)(2,1)S(1)}, bf16[2,2,160,384]{3,2,1,0:T(8,128)(2,1)S(1...) fusion(bf16[4,3,160,384]{3,2,1,0:T(8,128)(2,1)S(1)} %get-tuple-, ...), kind=kLoop, calls=%fused_computation.77 | loop fusion | flops 3686400 | bytes 13762566 | tf_op jit(solution)/shard_map/jit(_where)/select_n | solution.py:91
  122.3 0.2 slice-done
  122.5 1.3 slice-done.1
  123.9 0.4 fusion.62
  124.3 0.4 fusion.57
  124.8 0.5 convolution_add_fusion.24
  125.3 0.5 convolution_add_fusion.23
  125.8 0.5 convolution_add_fusion.22
  126.2 0.5 fusion.11
  126.7 0.5 convolution_add_fusion.20
  127.2 0.5 convolution_add_fusion.19
  127.6 0.5 convolution_add_fusion.18
  128.1 0.5 convolution_add_fusion.17
  128.6 0.5 convolution_add_fusion.16
  129.0 0.5 convolution_add_fusion.15
  129.5 0.5 convolution_add_fusion.14
  130.0 0.5 convolution_add_fusion.13
  130.4 0.5 convolution_add_fusion.12
  130.9 0.5 convolution_add_fusion.11
  131.3 0.4 convolution_add_fusion.10
  131.8 0.5 convolution_add_fusion.9
  132.3 0.5 convolution_add_fusion.8
  132.7 0.4 convolution_add_fusion.7
  133.2 0.5 convolution_add_fusion.6
  133.6 0.5 convolution_add_fusion.5
  134.1 0.6 convolution_add_fusion.4
  134.7 0.5 convolution_add_fusion.3
  135.2 0.5 convolution_add_fusion.2
  135.7 0.4 convolution_add_fusion.1
  136.2 1.2 fusion.13
  (13 shorter events, 0.1 us)
Async XLA Ops:
  7.2 85.2 %copy-start = (bf16[384,384]{1,0:T(8,128)(2,1)S(1)}, bf16[384,384]{1,0:T(8,128)(2,1)}, u32[]{:S(2)}) copy-start(bf16[384,384]{1,0:T(8,128)(2,1)} %param.11) | copy-start | bytes 884740
  7.2 80.6 %all-gather.2.cloned.1.call-start = ((), (), s32[]{:S(2)}) async-start(), calls=%async_computation | async-start | bytes 4915200 | tf_op jit(solution)/shard_map/all_gather | solution.py:50
  87.8 3.5 %copy-start.2 = (bf16[2,1280,768]{2,1,0:T(8,128)(2,1)S(1)}, bf16[2,1280,768]{2,1,0:T(8,128)(2,1)}, u32[]{:S(2)}) copy-start(bf16[2,1280,768]{2,1,0:T(8,128)(2,1)} %all-gather.2.cloned.1.call-done) | copy-start | bytes 11796484
  91.3 1.1 copy-start.1
  91.3 1.8 %copy-start.4 = (f32[384]{0:T(512)S(1)}, f32[384]{0:T(512)}, u32[]{:S(2)}) copy-start(f32[384]{0:T(512)} %param.12) | copy-start | bytes 4612
  92.4 17.4 %copy-start.5 = (s32[4]{0:T(128)S(1)}, s32[4]{0:T(128)}, u32[]{:S(2)}) copy-start(s32[4]{0:T(128)} %param.8) | copy-start | bytes 52
  93.0 41.1 %copy-start.3 = (bf16[640,384]{1,0:T(8,128)(2,1)}, bf16[640,384]{1,0:T(8,128)(2,1)S(1)}, u32[]{:S(2)}) copy-start(bf16[640,384]{1,0:T(8,128)(2,1)S(1)} %get-tuple-element.55) | copy-start | bytes 1474564
  93.5 9.4 %collective-permute-start = (bf16[2,2,160,384]{3,2,1,0:T(8,128)(2,1)S(1)}, bf16[2,2,160,384]{3,2,1,0:T(8,128)(2,1)S(1)}, u32[]{:S(2)}, u32[]{:S(2)}) collective-permute-start(bf16[2,2,160,384]{3,2,1,0:T(8,128)(2,1)S(1)} %multiply_convert_fusion), channel_id=1, source_target_pairs={{0,1},{1,2},{2,3},{4,5},{5,6},{6,7},{8,9},{9,10},{10,11},{12,13},{... | collective-permute-start | bytes 1474568 | tf_op jit(solution)/shard_map/ppermute | solution.py:12
  103.8 10.4 %collective-permute-start.1 = (bf16[4,1,160,384]{3,2,1,0:T(8,128)(2,1)}, bf16[4,1,160,384]{3,2,1,0:T(8,128)(2,1)S(1)}, u32[]{:S(2)}, u32[]{:S(2)}) collective-permute-start(bf16[4,1,160,384]{3,2,1,0:T(8,128)(2,1)} %get-tuple-element.34), channel_id=1, source_target_pairs={{0,4},{4,8},{8,12},{1,5},{5,9},{9,13},{2,6},{6,10},{10,14},{3,7},{... | collective-permute-start | bytes 1474568 | tf_op jit(solution)/shard_map/ppermute | solution.py:22
  107.9 10.0 %collective-permute-start.2 = (bf16[4,1,160,384]{3,2,1,0:T(8,128)(2,1)S(1)}, bf16[4,1,160,384]{3,2,1,0:T(8,128)(2,1)S(1)}, u32[]{:S(2)}, u32[]{:S(2)}) collective-permute-start(bf16[4,1,160,384]{3,2,1,0:T(8,128)(2,1)S(1)} %get-tuple-element.35), channel_id=1, source_target_pairs={{4,0},{8,4},{12,8},{5,1},{9,5},{13,9},{6,2},{10,6},{14,10},{7,3},{... | collective-permute-start | bytes 1474568 | tf_op jit(solution)/shard_map/ppermute | solution.py:23
  120.5 2.1 %slice-start = ((s8[7962624]{0:T(1024)(128)(4,1)}), s8[3768320]{0:T(1024)(128)(4,1)S(1)}, s32[]{:S(2)}) async-start(s8[7962624]{0:T(1024)(128)(4,1)} %bitcast.148), calls=%async_computation.1 | async-start | bytes 7536640
  120.8 3.1 %slice-start.1 = ((s8[7962624]{0:T(1024)(128)(4,1)}), s8[4194304]{0:T(1024)(128)(4,1)S(1)}, s32[]{:S(2)}) async-start(s8[7962624]{0:T(1024)(128)(4,1)} %bitcast.148), calls=%async_computation.2 | async-start | bytes 8388608
Sparse Core Ops, SparseCore 0:
  12.6 75.1 all-gather.1
where the time goes:
time: 146 us; the launch traced here: 144 us
  waiting for transfers between devices  87.2 us (60%)
  matrix products  21.9 us (15%)
  between operations  14.4 us (10%)
  starting transfers between devices  9.7 us (7%)
  other arithmetic  9.18 us (6%)
  local copies, waits for them, and re-layouts  1.85 us (1%)
    all_gather x1, waiting for transfers between devices, on_device(): portion = lax.all_gather(outgoing, 'tile', axis=1, tiled=True)  73.9 us
    dot_general x27, matrix products, on_device(): jnp.dot(shifted.reshape(-1, channels), w_conv[t_tap, r_tap, c_tap], prefe...  13.3 us
    ppermute x1, waiting for transfers between devices, from_behind(): return lax.ppermute(block, axis, route)  5.75 us
    ppermute x1, starting transfers between devices, extended(): before = lax.ppermute(last, axis, up)  4.09 us
    ppermute x1, waiting for transfers between devices, extended(): before = lax.ppermute(last, axis, up)  3.77 us
    ppermute x1, waiting for transfers between devices, extended(): after = lax.ppermute(first, axis, down)  3.76 us
    ppermute x1, starting transfers between devices, from_behind(): return lax.ppermute(block, axis, route)  3.65 us
    select_n x2, other arithmetic, on_device(): jnp.where(usable[:, None, None, None], shifted, jnp.zeros((), shifted.dty...  2.92 us
  transfers between devices with their start and end apart: 4, of which 4 were waited for; matrix products, arithmetic and copies ran while one was open for 1% of the time, Pallas kernels for 0%

commit v1 on v0

--- a/solution.py
+++ b/solution.py
@@ -1,15 +1,272 @@
+import functools
+
 import jax
 import jax.numpy as jnp
 from jax import lax
+from jax.experimental import pallas as pl
+from jax.experimental.pallas import tpu as pltpu
 from jax.sharding import PartitionSpec as P
 
 eps = 1e-06
+f32, bf16 = jnp.float32, jnp.bfloat16
+LOG2E = 1.4426950408889634
+VMEM = pl.BlockSpec(memory_space=pltpu.VMEM)
+SMEM = pl.BlockSpec(memory_space=pltpu.SMEM)
+ANY = pl.BlockSpec(memory_space=pl.ANY)
 
 
 def from_behind(block, axis, distance):
     devices = range(lax.axis_size(axis))
     route = [(i - distance, i) for i in devices if i - distance in devices]
     return lax.ppermute(block, axis, route)
+
+
+def rms_scale(values, gain_vec):
+    as_float = values.astype(f32)
+    return (
+        as_float * lax.rsqrt(jnp.mean(as_float * as_float, axis=-1, keepdims=True) + eps) * gain_vec
+    )
+
+
+def dot32(a, b):
+    return jnp.dot(a, b, preferred_element_type=f32)
+
+
+def struct(shape, dtype=bf16):
+    return jax.ShapeDtypeStruct(shape, dtype)
+
+
+def call(kernel, name, out_shape, in_specs, scratch=(), limit=24):
+    outs = jax.tree.map(lambda _: VMEM, out_shape)
+    return pl.pallas_call(
+        kernel,
+        out_shape=out_shape,
+        in_specs=in_specs,
+        out_specs=outs,
+        scratch_shapes=list(scratch),
+        compiler_params=pltpu.CompilerParams(vmem_limit_bytes=limit << 20),
+        name=name,
+    )
+
+
+def frame_route(spans, flip):
+    route = []
+    for tile in range(4):
+        for span in range(spans):
+            high, low, column, core = tile // 2, tile % 2, span // 2, span % 2
+            there = (2 * core + (low ^ flip)) * spans + 2 * column + high
+            route.append((tile * spans + span, there))
+    return route
+
+
+def shifted_route(tiles, spans, down, ahead):
+    return [
+        (t * spans + s, (t + down) * spans + s + ahead)
+        for t in range(tiles)
+        for s in range(spans)
+        if 0 <= t + down < tiles and s + ahead < spans
+    ]
+
+
+def pack_kernel(w_hbm, w_out, sem):
+    ch = w_hbm.shape[-1]
+    copies = [
+        pltpu.make_async_copy(
+            w_hbm.at[i, j, k],
+            w_out.at[i, j * ch : (j + 1) * ch, k * ch : (k + 1) * ch],
+            sem.at[i, j, k],
+        )
+        for i in range(3)
+        for j in range(3)
+        for k in range(3)
+    ]
+    for copy in copies:
+        copy.start()
+    for copy in copies:
+        copy.wait()
+
+
+def project_keys(block, gain_vec, w_qkv, out, place):
+    cells, ch = block.shape
+    normed = rms_scale(block[...], gain_vec).astype(bf16)
+    out[place * cells : (place + 1) * cells, :] = dot32(normed, w_qkv[:, ch:]).astype(bf16)
+
+
+def keys_kernel(own, other, gain, w_qkv, kv_out):
+    gain_vec = gain[...].reshape(1, own.shape[1])
+    project_keys(own, gain_vec, w_qkv, kv_out, 0)
+    project_keys(other, gain_vec, w_qkv, kv_out, 1)
+
+
+def attend_rows(cols, source, kv_parts, gain_vec, w_qkv, w_out, att_out):
+    ch = source.shape[1]
+    for row in range(source.shape[0] // cols):
+        part = slice(row * cols, (row + 1) * cols)
+        feats = source[part, :]
+        normed = rms_scale(feats, gain_vec).astype(bf16)
+        queries = dot32(normed, w_qkv[:, :ch]).astype(bf16)
+        scores = [
+            lax.dot_general(
+                queries, kv[:, :ch], (((1,), (1,)), ((), ())), preferred_element_type=f32
+            )
+            * (ch ** (-0.5) * LOG2E)
+            for kv in kv_parts
+        ]
+        top = functools.reduce(
+            jnp.maximum, [jnp.max(s, axis=1, keepdims=True) for s in scores]
+        )
+        raised = [jnp.exp2(s - top) for s in scores]
+        total = sum(jnp.sum(r, axis=1, keepdims=True) for r in raised)
+        mixed = sum(dot32(r.astype(bf16), kv[:, ch:]) for r, kv in zip(raised, kv_parts))
+        mixture = (mixed / total).astype(bf16)
+        att_out[part, :] = (feats.astype(f32) + dot32(mixture, w_out[...])).astype(bf16)
+
+
+def attend_kernel(cols, own_b, other_b, own_a, kv_a, gain, w_qkv, w_out, kv_b, att_a):
+    gain_vec = gain[...].reshape(1, own_a.shape[1])
+    project_keys(own_b, gain_vec, w_qkv, kv_b, 0)
+    project_keys(other_b, gain_vec, w_qkv, kv_b, 1)
+    attend_rows(cols, own_a, (kv_a, kv_b), gain_vec, w_qkv, w_out, att_a)
+
+
+def attend_rest_kernel(cols, own_b, kv_a, kv_b, gain, w_qkv, w_out, att_b):
+    gain_vec = gain[...].reshape(1, own_b.shape[1])
+    attend_rows(cols, own_b, (kv_a, kv_b), gain_vec, w_qkv, w_out, att_b)
+
+
+def activate_kernel(cols, tile_ref, got_a, got_b, gain, attended, active, top_edge, low_edge):
+    low = tile_ref[0] % 2
+    gain_vec = gain[...].reshape(1, got_a.shape[1])
+
+    def one(block, frame):
+        values = block[...]
+        attended[frame] = values
+        lifted = rms_scale(values, gain_vec)
+        act = (lifted / (1.0 + jnp.exp(-lifted))).astype(bf16)
+        active[frame] = act
+        top_edge[frame] = act[:cols, :]
+        low_edge[frame] = act[cols:, :]
+
+    one(got_a, low)
+    one(got_b, 1 - low)
+
+
+def usable_flag(clips, frame_at, tap):
+    end = jnp.int32(0)
+    start = jnp.int32(0)
+    for i in range(clips.shape[0]):
+        end = end + clips[i]
+        start = start + jnp.where(end <= frame_at, clips[i], 0)
+    return frame_at - (2 - tap) >= start
+
+
+def shift_add(part, cols, ch):
+    at = lax.broadcasted_iota(jnp.int32, (cols, ch), 0)
+    left = jnp.where(at == 0, 0.0, pltpu.roll(part[:, :ch], 1, 0))
+    right = jnp.where(at == cols - 1, 0.0, pltpu.roll(part[:, 2 * ch :], cols - 1, 0))
+    return part[:, ch : 2 * ch] + left + right
+
+
+def conv_kernel(cols, work, first, span_ref, clips, mid, top, low, w, *refs):
+    if first:
+        out, acc = refs
+    else:
+        partial, out, acc = refs
+    ch = mid.shape[-1]
+    acc[...] = jnp.zeros_like(acc)
+    for tap, frame, which in work:
+
+        @pl.when(usable_flag(clips, span_ref[0] * 2 + frame, tap))
+        def _(tap=tap, frame=frame, which=which):
+            rows = [top[which], mid[which, :cols, :], mid[which, cols:, :], low[which]]
+            lhs = jnp.concatenate(
+                [jnp.concatenate(rows[r : r + 3], axis=1) for r in range(2)], axis=0
+            )
+            acc[frame] += dot32(lhs, w[tap])
+
+    for frame in range(2):
+        for r in range(2):
+            part = slice(r * cols, (r + 1) * cols)
+            val = shift_add(acc[frame, part, :], cols, ch)
+            if not first:
+                val = val + partial[frame, part, :]
+            out[frame, part, :] = val.astype(out.dtype)
+
+
+def on_device(features, clip_lengths, norm_gain, w_qkv, w_out, conv_gain, w_conv):
+    frames, row_count, cols, ch = features.shape
+    tiles, spans = lax.axis_size("tile"), lax.axis_size("span")
+    if tiles != 4 or spans % 2 or frames != 2 or row_count != 2:
+        return general(features, clip_lengths, norm_gain, w_qkv, w_out, conv_gain, w_conv)
+    cells = row_count * cols
+    both = ("tile", "span")
+    tile = lax.axis_index("tile").astype(jnp.int32).reshape(1)
+    span = lax.axis_index("span").astype(jnp.int32).reshape(1)
+    other_core = [(i, i ^ 1) for i in range(spans)]
+    route_a, route_b = frame_route(spans, 0), frame_route(spans, 1)
+    low = tile[0] % 2
+    x = features.reshape(frames, cells, ch)
+    send_a = lax.dynamic_index_in_dim(x, low, 0, keepdims=False)
+    send_b = lax.dynamic_index_in_dim(x, 1 - low, 0, keepdims=False)
+    own_a = lax.ppermute(send_a, both, route_a)
+    own_b = lax.ppermute(send_b, both, route_b)
+    w_packed = call(
+        pack_kernel,
+        "pack_weights",
+        struct((3, 3 * ch, 3 * ch)),
+        [ANY],
+        [pltpu.SemaphoreType.DMA((3, 3, 3))],
+        16,
+    )(w_conv)
+    other_a = lax.ppermute(own_a, "span", other_core)
+    other_b = lax.ppermute(own_b, "span", other_core)
+    kv_a = call(keys_kernel, "keys", struct((2 * cells, 2 * ch)), [VMEM] * 4)(
+        own_a, other_a, norm_gain, w_qkv
+    )
+    kv_b, att_a = call(
+        functools.partial(attend_kernel, cols),
+        "attend",
+        (struct((2 * cells, 2 * ch)), struct((cells, ch))),
+        [VMEM] * 7,
+    )(own_b, other_b, own_a, kv_a, norm_gain, w_qkv, w_out)
+    got_a = lax.ppermute(att_a, both, route_a)
+    att_b = call(
+        functools.partial(attend_rest_kernel, cols), "attend_rest", struct((cells, ch)), [VMEM] * 6
+    )(own_b, kv_a, kv_b, norm_gain, w_qkv, w_out)
+    got_b = lax.ppermute(att_b, both, route_b)
+    attended, active, top_edge, low_edge = call(
+        functools.partial(activate_kernel, cols),
+        "activate",
+        (
+            struct((frames, cells, ch)),
+            struct((frames, cells, ch)),
+            struct((frames, cols, ch)),
+            struct((frames, cols, ch)),
+        ),
+        [SMEM] + [VMEM] * 3,
+    )(tile, got_a, got_b, conv_gain)
+    above = lax.ppermute(low_edge, both, shifted_route(tiles, spans, 1, 0))
+    below = lax.ppermute(top_edge, both, shifted_route(tiles, spans, -1, 0))
+    before = lax.ppermute(active, both, shifted_route(tiles, spans, 0, 1))
+    before_above = lax.ppermute(low_edge, both, shifted_route(tiles, spans, 1, 1))
+    before_below = lax.ppermute(top_edge, both, shifted_route(tiles, spans, -1, 1))
+    acc = pltpu.VMEM((frames, cells, 3 * ch), f32)
+    partial = call(
+        functools.partial(conv_kernel, cols, [(2, 0, 0), (2, 1, 1), (1, 1, 0)], True),
+        "conv_own",
+        struct((frames, cells, ch), f32),
+        [SMEM, SMEM] + [VMEM] * 4,
+        [acc],
+    )(span, clip_lengths, active, above, below, w_packed)
+    hidden = call(
+        functools.partial(conv_kernel, cols, [(0, 0, 0), (1, 0, 1), (0, 1, 1)], False),
+        "conv_before",
+        struct((frames, cells, ch)),
+        [SMEM, SMEM] + [VMEM] * 5,
+        [acc],
+    )(span, clip_lengths, before, before_above, before_below, w_packed, partial)
+    shape = (frames, row_count, cols, ch)
+    return attended.reshape(shape), hidden.reshape(shape)
 
 
 def extended(x, sides, width):
@@ -25,14 +282,7 @@
     return x
 
 
-def rms_scale(values, gain_vec):
-    as_float = values.astype(jnp.float32)
-    return (
-        as_float * lax.rsqrt(jnp.mean(as_float * as_float, axis=-1, keepdims=True) + eps) * gain_vec
-    )
-
-
-def on_device(features, clip_lengths, norm_gain, w_qkv, w_out, conv_gain, w_conv):
+def general(features, clip_lengths, norm_gain, w_qkv, w_out, conv_gain, w_conv):
     frames, row_count, col_count, channels = features.shape
     cell_count = row_count * col_count
     normed_grid = rms_scale(features, norm_gain).astype(jnp.bfloat16)

time: 146 us -> 71 us (0.49); the launches traced: 144 us -> 71 us
  waiting for transfers between devices: 87.2 us -> 20.1 us
  matrix products: 21.9 us -> 0 us
  Pallas kernels: 0 us -> 18 us
  starting transfers between devices: 9.7 us -> 23.3 us
  between operations: 14.4 us -> 0.85 us
  other arithmetic: 9.18 us -> 0 us
  local copies, waits for them, and re-layouts: 1.85 us -> 8.83 us
    all_gather x1 -> x0, waiting for transfers between devices: 73.9 us -> none  [on_device(): portion = lax.all_gather(outgoing, 'tile', axis=1, tiled=True)]
    dot_general x32 -> x0, matrix products: 21.9 us -> none  [the longest x27 13.3 us: on_device(): jnp.dot(shifted.reshape(-1, channels), w_conv[t_tap, r_tap, c_tap], prefe...]
    pallas_call x0 -> x7, Pallas kernels: none -> 18 us  [the longest x1 4.69 us: on_device(): call(functools.partial(conv_kernel, cols, [(2, 0, 0), (2, 1, 1), (1, 1, 0...]
    ppermute x3 -> x11, starting transfers between devices: 9.67 us -> 23.3 us  [the longest x1 4.78 us: on_device(): own_a = lax.ppermute(send_a, both, route_a)]
    ppermute x3 -> x11, waiting for transfers between devices: 13.3 us -> 20.1 us  [the longest x1 8.28 us: on_device(): own_a = lax.ppermute(send_a, both, route_a)]
    unnamed x16, local copies, waits for them, and re-layouts: 1.61 us -> 7.71 us
    select_n x2 -> x0, other arithmetic: 2.92 us -> none  [on_device(): jnp.where(usable[:, None, None, None], shifted, jnp.zeros((), shifted.dty...]
    concatenate x3 -> x0, other arithmetic: 2.34 us -> none  [the longest x2 1.46 us: extended(): x = jnp.concatenate([before, x, after], axis=dim)]
  transfers between devices with their start and end apart: 4 -> 11, of which waited for: 4 -> 4; matrix products, arithmetic and copies ran while one was open for 1% -> 0% of each run, Pallas kernels for 0% -> 9%
where the time goes in v1:
time: 71 us
  starting transfers between devices  23.3 us (33%)
  waiting for transfers between devices  20.1 us (28%)
  Pallas kernels  18 us (25%)
  local copies, waits for them, and re-layouts  8.83 us (12%)
  between operations  0.85 us (1%)
    ppermute x1, waiting for transfers between devices, on_device(): own_a = lax.ppermute(send_a, both, route_a)  8.28 us
    unnamed x16, local copies, waits for them, and re-layouts  7.71 us
    ppermute x1, waiting for transfers between devices, on_device(): got_b = lax.ppermute(att_b, both, route_b)  6.49 us
    ppermute x1, starting transfers between devices, on_device(): own_a = lax.ppermute(send_a, both, route_a)  4.78 us
    pallas_call x1, Pallas kernels, on_device(): call(functools.partial(conv_kernel, cols, [(2, 0, 0), (2, 1, 1), (1, 1, 0...  4.69 us
    ppermute x1, starting transfers between devices, on_device(): lax.ppermute(low_edge, both, shifted_route(tiles, spans, 1, 1))  4.47 us
    pallas_call x1, Pallas kernels, on_device(): call(functools.partial(conv_kernel, cols, [(0, 0, 0), (1, 0, 1), (0, 1, 1...  4.46 us
    ppermute x1, starting transfers between devices, on_device(): below = lax.ppermute(top_edge, both, shifted_route(tiles, spans, -1, 0))  3.61 us
  transfers between devices with their start and end apart: 11, of which 4 were waited for; matrix products, arithmetic and copies ran while one was open for 0% of the time, Pallas kernels for 9%

profile of v1, /device:TPU:13, one launch (start us, length us, event | category | flops | bytes accessed | tf_op | source)
XLA Modules:
  0.0 71.0 jit_solution(11686342157587409436)
XLA Ops:
  0.6 0.0 copy-start.6
  0.7 1.1 %dynamic-slice_bitcast_fusion = (bf16[320,384]{1,0:T(8,128)(2,1)S(1)}, bf16[320,384]{1,0:T(8,128)(2,1)S(1)}) fusion(bf16[2,320,384]{2,1,0:T(8,128)(2,1)} %bitcast.9, s32[]{:T(128)S(6)} %select_n.16, s32[]{:T(128)S(6)} %select_n.15), kind=kLoop, calls=%fused_computation | loop fusion | bytes 983048 | tf_op jit(solution)/shard_map/jit(dynamic_index_in_dim)/squeeze | solution.py:209
  1.8 4.8 %collective-permute-start.2 = (bf16[320,384]{1,0:T(8,128)(2,1)S(1)}, bf16[320,384]{1,0:T(8,128)(2,1)S(1)}, u32[]{:S(2)}, u32[]{:S(2)}) collective-permute-start(bf16[320,384]{1,0:T(8,128)(2,1)S(1)} %get-tuple-element.14), channel_id=1, source_target_pairs={{0,0},{1,8},{2,2},{3,10},{4,4},{5,12},{6,6},{7,14},{8,1},{9,9},{10... | collective-permute-start | bytes 737288 | tf_op jit(solution)/shard_map/ppermute | solution.py:211
  6.6 0.1 collective-permute-start
  6.6 8.3 %collective-permute-done.2.own.own_a = bf16[320,384]{1,0:T(8,128)(2,1)S(1)} collective-permute-done((bf16[320,384]{1,0:T(8,128)(2,1)S(1)}, bf16[320,384]{1,0:T(8,128)(2,1)S(1)}, u32[]{:S(2)}, u32[]{:S(2)}) %collective-permute-start.2) | collective-permute-done | bytes 245792 | tf_op jit(solution)/shard_map/ppermute | solution.py:211
  14.9 0.0 collective-permute-start.3
  14.9 2.6 %collective-permute-done.own_b = bf16[320,384]{1,0:T(8,128)(2,1)S(1)} collective-permute-done((bf16[320,384]{1,0:T(8,128)(2,1)S(1)}, bf16[320,384]{1,0:T(8,128)(2,1)S(1)}, u32[]{:S(2)}, u32[]{:S(2)}) %collective-permute-start) | collective-permute-done | bytes 245792 | tf_op jit(solution)/shard_map/ppermute | solution.py:212
  17.6 0.0 collective-permute-start.1
  17.6 0.0 collective-permute-done.3.other
  17.6 0.0 copy-start
  17.6 1.2 %copy-done = bf16[384,1152]{1,0:T(8,128)(2,1)S(1)} copy-done((bf16[384,1152]{1,0:T(8,128)(2,1)S(1)}, bf16[384,1152]{1,0:T(8,128)(2,1)}, u32[]{:S(2)}) %copy-start) | copy-done | bytes 884760
  18.7 0.0 copy-start.4
  18.7 0.7 copy-done.4
  19.4 0.7 %keys.1.kv_a = bf16[640,768]{1,0:T(8,128)(2,1)S(1)} custom-call(bf16[320,384]{1,0:T(8,128)(2,1)S(1)} %collective-permute-done.2.own.own_a, bf16[320,384]{1,0:T(8,128)(2,1)S(1)} %collective-permute-done.3.other, f32[384]{0:T(512)S(1)} %copy-done.4, bf16[384,1152]{1,0:T(8,128)(2,1)S(1)} %copy-done), custom_call_target="tpu_custom_call" | custom-call | tf_op jit(solution)/shard_map/keys/pallas_call | solution.py:223
  20.2 0.0 collective-permute-done.1.other_b
  20.2 0.0 copy-start.2
  20.2 1.0 %copy-done.2 = bf16[384,384]{1,0:T(8,128)(2,1)S(1)} copy-done((bf16[384,384]{1,0:T(8,128)(2,1)S(1)}, bf16[384,384]{1,0:T(8,128)(2,1)}, u32[]{:S(2)}) %copy-start.2) | copy-done | bytes 294936
  21.2 3.1 %attend.1 = (bf16[640,768]{1,0:T(8,128)(2,1)S(1)}, bf16[320,384]{1,0:T(8,128)(2,1)S(1)}) custom-call(bf16[320,384]{1,0:T(8,128)(2,1)S(1)} %collective-permute-done.own_b, bf16[320,384]{1,0:T(8,128)(2,1)S(1)} %collective-permute-done.1.other_b, bf16[320,384]{1,0:T(8,128)(2,1)S(1)} %collective-permute-done.2.own.own_a, bf16[640,768]{1,0:T(8,128)(2,1)S(1)} %keys.1.kv_a, ...), custom_call_target="tpu_custom_call" | custom-call | tf_op jit(solution)/shard_map/attend/pallas_call | solution.py:226
  24.3 0.0 copy-start.3
  24.3 1.0 %copy-done.3 = bf16[384,384]{1,0:T(8,128)(2,1)S(1)} copy-done((bf16[384,384]{1,0:T(8,128)(2,1)S(1)}, bf16[384,384]{1,0:T(8,128)(2,1)}, u32[]{:S(2)}) %copy-start.3) | copy-done | bytes 294936
  25.3 0.0 copy-start.5
  25.3 0.7 copy-done.5
  25.9 2.6 %attend_rest.1 = bf16[320,384]{1,0:T(8,128)(2,1)S(1)} custom-call(bf16[320,384]{1,0:T(8,128)(2,1)S(1)} %collective-permute-done.own_b, bf16[640,768]{1,0:T(8,128)(2,1)S(1)} %keys.1.kv_a, bf16[640,768]{1,0:T(8,128)(2,1)S(1)} %get-tuple-element.9.kv_b, f32[384]{0:T(512)S(1)} %copy-done.5, bf16[384,1152]{1,0:T(8,128)(2,1)S(1)} %copy-done, ...), custom_call_target="tpu_custom_call" | custom-call | tf_op jit(solution)/shard_map/attend_rest/pallas_call | solution.py:233
  28.6 2.5 %collective-permute-start.5 = (bf16[320,384]{1,0:T(8,128)(2,1)S(1)}, bf16[320,384]{1,0:T(8,128)(2,1)S(1)}, u32[]{:S(2)}, u32[]{:S(2)}) collective-permute-start(bf16[320,384]{1,0:T(8,128)(2,1)S(1)} %attend_rest.1), channel_id=1, source_target_pairs={{0,4},{1,12},{2,6},{3,14},{4,0},{5,8},{6,2},{7,10},{8,5},{9,13},{1... | collective-permute-start | bytes 737288 | tf_op jit(solution)/shard_map/ppermute | solution.py:236
  31.1 1.9 %collective-permute-start.4 = (bf16[320,384]{1,0:T(8,128)(2,1)S(1)}, bf16[320,384]{1,0:T(8,128)(2,1)S(1)}, u32[]{:S(2)}, u32[]{:S(2)}) collective-permute-start(bf16[320,384]{1,0:T(8,128)(2,1)S(1)} %get-tuple-element.8), channel_id=1, source_target_pairs={{0,0},{1,8},{2,2},{3,10},{4,4},{5,12},{6,6},{7,14},{8,1},{9,9},{10... | collective-permute-start | bytes 737288 | tf_op jit(solution)/shard_map/ppermute | solution.py:232
  33.0 6.5 %collective-permute-done.5.got_b = bf16[320,384]{1,0:T(8,128)(2,1)S(1)} collective-permute-done((bf16[320,384]{1,0:T(8,128)(2,1)S(1)}, bf16[320,384]{1,0:T(8,128)(2,1)S(1)}, u32[]{:S(2)}, u32[]{:S(2)}) %collective-permute-start.5) | collective-permute-done | bytes 245792 | tf_op jit(solution)/shard_map/ppermute | solution.py:236
  39.5 2.6 %collective-permute-done.4.got_a = bf16[320,384]{1,0:T(8,128)(2,1)S(1)} collective-permute-done((bf16[320,384]{1,0:T(8,128)(2,1)S(1)}, bf16[320,384]{1,0:T(8,128)(2,1)S(1)}, u32[]{:S(2)}, u32[]{:S(2)}) %collective-permute-start.4) | collective-permute-done | bytes 245792 | tf_op jit(solution)/shard_map/ppermute | solution.py:232
  42.1 0.0 copy-done.6
  42.1 1.2 %activate.1 = (bf16[2,320,384]{2,1,0:T(8,128)(2,1)}, bf16[2,320,384]{2,1,0:T(8,128)(2,1)S(1)}, bf16[2,160,384]{2,1,0:T(8,128)(2,1)S(1)}, bf16[2,160,384]{2,1,0:T(8,128)(2,1)S(1)}) custom-call(s32[1]{0:T(128)} %bitcast.tile_ref, bf16[320,384]{1,0:T(8,128)(2,1)S(1)} %collective-permute-done.4.got_a, bf16[320,384]{1,0:T(8,128)(2,1)S(1)} %collective-permute-done.5.got_b, ...), custom_call_target="tpu_custom_call" | custom-call | tf_op jit(solution)/shard_map/activate/pallas_call | solution.py:237
  43.4 1.9 %collective-permute-start.6 = (bf16[2,320,384]{2,1,0:T(8,128)(2,1)S(1)}, bf16[2,320,384]{2,1,0:T(8,128)(2,1)S(1)}, u32[]{:S(2)}, u32[]{:S(2)}) collective-permute-start(bf16[2,320,384]{2,1,0:T(8,128)(2,1)S(1)} %get-tuple-element.11.mid), channel_id=1, source_target_pairs={{0,1},{1,2},{2,3},{4,5},{5,6},{6,7},{8,9},{9,10},{10,11},{12,13},{... | collective-permute-start | bytes 1474568 | tf_op jit(solution)/shard_map/ppermute | solution.py:250
  45.3 3.6 %collective-permute-start.10 = (bf16[2,160,384]{2,1,0:T(8,128)(2,1)S(1)}, bf16[2,160,384]{2,1,0:T(8,128)(2,1)S(1)}, u32[]{:S(2)}, u32[]{:S(2)}) collective-permute-start(bf16[2,160,384]{2,1,0:T(8,128)(2,1)S(1)} %get-tuple-element.13), channel_id=1, source_target_pairs={{4,0},{5,1},{6,2},{7,3},{8,4},{9,5},{10,6},{11,7},{12,8},{13,9},{1... | collective-permute-start | bytes 737288 | tf_op jit(solution)/shard_map/ppermute | solution.py:249
  48.9 1.9 %collective-permute-start.9 = (bf16[2,160,384]{2,1,0:T(8,128)(2,1)S(1)}, bf16[2,160,384]{2,1,0:T(8,128)(2,1)S(1)}, u32[]{:S(2)}, u32[]{:S(2)}) collective-permute-start(bf16[2,160,384]{2,1,0:T(8,128)(2,1)S(1)} %get-tuple-element.12), channel_id=1, source_target_pairs={{0,4},{1,5},{2,6},{3,7},{4,8},{5,9},{6,10},{7,11},{8,12},{9,13},{1... | collective-permute-start | bytes 737288 | tf_op jit(solution)/shard_map/ppermute | solution.py:248
  50.8 4.5 %collective-permute-start.7 = (bf16[2,160,384]{2,1,0:T(8,128)(2,1)S(1)}, bf16[2,160,384]{2,1,0:T(8,128)(2,1)S(1)}, u32[]{:S(2)}, u32[]{:S(2)}) collective-permute-start(bf16[2,160,384]{2,1,0:T(8,128)(2,1)S(1)} %get-tuple-element.12), channel_id=1, source_target_pairs={{0,5},{1,6},{2,7},{4,9},{5,10},{6,11},{8,13},{9,14},{10,15},{16,21... | collective-permute-start | bytes 737288 | tf_op jit(solution)/shard_map/ppermute | solution.py:251
  55.3 2.1 %collective-permute-start.8 = (bf16[2,160,384]{2,1,0:T(8,128)(2,1)S(1)}, bf16[2,160,384]{2,1,0:T(8,128)(2,1)S(1)}, u32[]{:S(2)}, u32[]{:S(2)}) collective-permute-start(bf16[2,160,384]{2,1,0:T(8,128)(2,1)S(1)} %get-tuple-element.13), channel_id=1, source_target_pairs={{4,1},{5,2},{6,3},{8,5},{9,6},{10,7},{12,9},{13,10},{14,11},{20,17... | collective-permute-start | bytes 737288 | tf_op jit(solution)/shard_map/ppermute | solution.py:252
  57.4 0.0 copy-start.1
  57.4 3.3 %copy-done.1 = bf16[3,3,3,384,384]{4,3,2,1,0:T(8,128)(2,1)S(1)} copy-done((bf16[3,3,3,384,384]{4,3,2,1,0:T(8,128)(2,1)S(1)}, bf16[3,3,3,384,384]{4,3,2,1,0:T(8,128)(2,1)}, u32[]{:S(2)}) %copy-start.1) | copy-done | bytes 7962648
  60.6 0.0 copy-start.7
  60.6 1.1 %pack_weights.1.w = bf16[3,1152,1152]{2,1,0:T(8,128)(2,1)S(1)} custom-call(bf16[3,3,3,384,384]{4,3,2,1,0:T(8,128)(2,1)S(1)} %copy-done.1), custom_call_target="tpu_custom_call" | custom-call | tf_op jit(solution)/shard_map/pack_weights/pallas_call | solution.py:213
  61.8 0.0 collective-permute-done.10.low
  61.8 0.0 collective-permute-done.9.top
  61.8 0.0 copy-done.7
  61.8 4.7 %conv_own.1.refs_0_ = f32[2,320,384]{2,1,0:T(8,128)S(1)} custom-call(s32[1]{0:T(128)} %bitcast.5.span_ref, s32[4]{0:T(128)S(1)} %copy-done.7, bf16[2,320,384]{2,1,0:T(8,128)(2,1)S(1)} %get-tuple-element.11.mid, bf16[2,160,384]{2,1,0:T(8,128)(2,1)S(1)} %collective-permute-done.9.top, bf16[2,160,384]{2,1,0:T(8,128)(2,1)S(1)} %collective-permute-done.10.low, ...), custom_call_target="tpu_custom_call" | custom-call | tf_op jit(solution)/shard_map/conv_own/pallas_call | solution.py:254
  66.5 0.0 collective-permute-done.7.top
  66.5 0.0 collective-permute-done.8.low
  66.5 0.0 collective-permute-done.6.mid
  66.5 4.5 %conv_before.1 = bf16[2,320,384]{2,1,0:T(8,128)(2,1)} custom-call(s32[1]{0:T(128)} %bitcast.5.span_ref, s32[4]{0:T(128)S(1)} %copy-done.7, bf16[2,320,384]{2,1,0:T(8,128)(2,1)S(1)} %collective-permute-done.6.mid, bf16[2,160,384]{2,1,0:T(8,128)(2,1)S(1)} %collective-permute-done.7.top, bf16[2,160,384]{2,1,0:T(8,128)(2,1)S(1)} %collective-permute-done.8.low, ...), custom_call_target="tpu_custom_call" | custom-call | tf_op jit(solution)/shard_map/conv_before/pallas_call | solution.py:261
Async XLA Ops:
  0.6 41.5 %copy-start.6 = (f32[384]{0:T(512)S(1)}, f32[384]{0:T(512)}, u32[]{:S(2)}) copy-start(f32[384]{0:T(512)} %gain.7) | copy-start | bytes 4612
  1.8 13.1 %collective-permute-start.2 = (bf16[320,384]{1,0:T(8,128)(2,1)S(1)}, bf16[320,384]{1,0:T(8,128)(2,1)S(1)}, u32[]{:S(2)}, u32[]{:S(2)}) collective-permute-start(bf16[320,384]{1,0:T(8,128)(2,1)S(1)} %get-tuple-element.14), channel_id=1, source_target_pairs={{0,0},{1,8},{2,2},{3,10},{4,4},{5,12},{6,6},{7,14},{8,1},{9,9},{10... | collective-permute-start | bytes 737288 | tf_op jit(solution)/shard_map/ppermute | solution.py:211
  6.6 11.0 %collective-permute-start = (bf16[320,384]{1,0:T(8,128)(2,1)S(1)}, bf16[320,384]{1,0:T(8,128)(2,1)S(1)}, u32[]{:S(2)}, u32[]{:S(2)}) collective-permute-start(bf16[320,384]{1,0:T(8,128)(2,1)S(1)} %get-tuple-element.15), channel_id=1, source_target_pairs={{0,4},{1,12},{2,6},{3,14},{4,0},{5,8},{6,2},{7,10},{8,5},{9,13},{1... | collective-permute-start | bytes 737288 | tf_op jit(solution)/shard_map/ppermute | solution.py:212
  14.9 2.6 %collective-permute-start.3 = (bf16[320,384]{1,0:T(8,128)(2,1)S(1)}, bf16[320,384]{1,0:T(8,128)(2,1)S(1)}, u32[]{:S(2)}, u32[]{:S(2)}) collective-permute-start(bf16[320,384]{1,0:T(8,128)(2,1)S(1)} %collective-permute-done.2.own.own_a), channel_id=1, source_target_pairs={{0,1},{1,0},{2,3},{3,2},{4,5},{5,4},{6,7},{7,6},{8,9},{9,8},{10,11... | collective-permute-start | bytes 737288 | tf_op jit(solution)/shard_map/ppermute | solution.py:221
  17.6 2.6 %collective-permute-start.1 = (bf16[320,384]{1,0:T(8,128)(2,1)S(1)}, bf16[320,384]{1,0:T(8,128)(2,1)S(1)}, u32[]{:S(2)}, u32[]{:S(2)}) collective-permute-start(bf16[320,384]{1,0:T(8,128)(2,1)S(1)} %collective-permute-done.own_b), channel_id=1, source_target_pairs={{0,1},{1,0},{2,3},{3,2},{4,5},{5,4},{6,7},{7,6},{8,9},{9,8},{10,11... | collective-permute-start | bytes 737288 | tf_op jit(solution)/shard_map/ppermute | solution.py:222
  17.6 1.2 %copy-start = (bf16[384,1152]{1,0:T(8,128)(2,1)S(1)}, bf16[384,1152]{1,0:T(8,128)(2,1)}, u32[]{:S(2)}) copy-start(bf16[384,1152]{1,0:T(8,128)(2,1)} %w_qkv.5) | copy-start | bytes 2654212
  18.7 0.7 copy-start.4
  20.2 1.0 %copy-start.2 = (bf16[384,384]{1,0:T(8,128)(2,1)S(1)}, bf16[384,384]{1,0:T(8,128)(2,1)}, u32[]{:S(2)}) copy-start(bf16[384,384]{1,0:T(8,128)(2,1)} %w_out.3) | copy-start | bytes 884740
  24.3 1.0 %copy-start.3 = (bf16[384,384]{1,0:T(8,128)(2,1)S(1)}, bf16[384,384]{1,0:T(8,128)(2,1)}, u32[]{:S(2)}) copy-start(bf16[384,384]{1,0:T(8,128)(2,1)} %w_out.3) | copy-start | bytes 884740
  25.3 0.7 copy-start.5
  28.6 10.9 %collective-permute-start.5 = (bf16[320,384]{1,0:T(8,128)(2,1)S(1)}, bf16[320,384]{1,0:T(8,128)(2,1)S(1)}, u32[]{:S(2)}, u32[]{:S(2)}) collective-permute-start(bf16[320,384]{1,0:T(8,128)(2,1)S(1)} %attend_rest.1), channel_id=1, source_target_pairs={{0,4},{1,12},{2,6},{3,14},{4,0},{5,8},{6,2},{7,10},{8,5},{9,13},{1... | collective-permute-start | bytes 737288 | tf_op jit(solution)/shard_map/ppermute | solution.py:236
  31.1 11.0 %collective-permute-start.4 = (bf16[320,384]{1,0:T(8,128)(2,1)S(1)}, bf16[320,384]{1,0:T(8,128)(2,1)S(1)}, u32[]{:S(2)}, u32[]{:S(2)}) collective-permute-start(bf16[320,384]{1,0:T(8,128)(2,1)S(1)} %get-tuple-element.8), channel_id=1, source_target_pairs={{0,0},{1,8},{2,2},{3,10},{4,4},{5,12},{6,6},{7,14},{8,1},{9,9},{10... | collective-permute-start | bytes 737288 | tf_op jit(solution)/shard_map/ppermute | solution.py:232
  43.4 23.2 %collective-permute-start.6 = (bf16[2,320,384]{2,1,0:T(8,128)(2,1)S(1)}, bf16[2,320,384]{2,1,0:T(8,128)(2,1)S(1)}, u32[]{:S(2)}, u32[]{:S(2)}) collective-permute-start(bf16[2,320,384]{2,1,0:T(8,128)(2,1)S(1)} %get-tuple-element.11.mid), channel_id=1, source_target_pairs={{0,1},{1,2},{2,3},{4,5},{5,6},{6,7},{8,9},{9,10},{10,11},{12,13},{... | collective-permute-start | bytes 1474568 | tf_op jit(solution)/shard_map/ppermute | solution.py:250
  45.3 16.5 %collective-permute-start.10 = (bf16[2,160,384]{2,1,0:T(8,128)(2,1)S(1)}, bf16[2,160,384]{2,1,0:T(8,128)(2,1)S(1)}, u32[]{:S(2)}, u32[]{:S(2)}) collective-permute-start(bf16[2,160,384]{2,1,0:T(8,128)(2,1)S(1)} %get-tuple-element.13), channel_id=1, source_target_pairs={{4,0},{5,1},{6,2},{7,3},{8,4},{9,5},{10,6},{11,7},{12,8},{13,9},{1... | collective-permute-start | bytes 737288 | tf_op jit(solution)/shard_map/ppermute | solution.py:249
  48.9 12.9 %collective-permute-start.9 = (bf16[2,160,384]{2,1,0:T(8,128)(2,1)S(1)}, bf16[2,160,384]{2,1,0:T(8,128)(2,1)S(1)}, u32[]{:S(2)}, u32[]{:S(2)}) collective-permute-start(bf16[2,160,384]{2,1,0:T(8,128)(2,1)S(1)} %get-tuple-element.12), channel_id=1, source_target_pairs={{0,4},{1,5},{2,6},{3,7},{4,8},{5,9},{6,10},{7,11},{8,12},{9,13},{1... | collective-permute-start | bytes 737288 | tf_op jit(solution)/shard_map/ppermute | solution.py:248
  50.8 15.7 %collective-permute-start.7 = (bf16[2,160,384]{2,1,0:T(8,128)(2,1)S(1)}, bf16[2,160,384]{2,1,0:T(8,128)(2,1)S(1)}, u32[]{:S(2)}, u32[]{:S(2)}) collective-permute-start(bf16[2,160,384]{2,1,0:T(8,128)(2,1)S(1)} %get-tuple-element.12), channel_id=1, source_target_pairs={{0,5},{1,6},{2,7},{4,9},{5,10},{6,11},{8,13},{9,14},{10,15},{16,21... | collective-permute-start | bytes 737288 | tf_op jit(solution)/shard_map/ppermute | solution.py:251
  55.3 11.2 %collective-permute-start.8 = (bf16[2,160,384]{2,1,0:T(8,128)(2,1)S(1)}, bf16[2,160,384]{2,1,0:T(8,128)(2,1)S(1)}, u32[]{:S(2)}, u32[]{:S(2)}) collective-permute-start(bf16[2,160,384]{2,1,0:T(8,128)(2,1)S(1)} %get-tuple-element.13), channel_id=1, source_target_pairs={{4,1},{5,2},{6,3},{8,5},{9,6},{10,7},{12,9},{13,10},{14,11},{20,17... | collective-permute-start | bytes 737288 | tf_op jit(solution)/shard_map/ppermute | solution.py:252
  57.4 3.3 %copy-start.1 = (bf16[3,3,3,384,384]{4,3,2,1,0:T(8,128)(2,1)S(1)}, bf16[3,3,3,384,384]{4,3,2,1,0:T(8,128)(2,1)}, u32[]{:S(2)}) copy-start(bf16[3,3,3,384,384]{4,3,2,1,0:T(8,128)(2,1)} %w_hbm.1) | copy-start | bytes 23887876
  60.6 1.2 %copy-start.7 = (s32[4]{0:T(128)S(1)}, s32[4]{0:T(128)}, u32[]{:S(2)}) copy-start(s32[4]{0:T(128)} %clips.3) | copy-start | bytes 52

commit v2 on v1

--- a/solution.py
+++ b/solution.py
@@ -36,8 +36,9 @@
     return jax.ShapeDtypeStruct(shape, dtype)
 
 
-def call(kernel, name, out_shape, in_specs, scratch=(), limit=24):
+def call(kernel, name, out_shape, in_specs, scratch=(), limit=16, flops=0, size=1 << 20):
     outs = jax.tree.map(lambda _: VMEM, out_shape)
+    cost = pl.CostEstimate(flops=int(flops), transcendentals=0, bytes_accessed=int(size))
     return pl.pallas_call(
         kernel,
         out_shape=out_shape,
@@ -45,6 +46,7 @@
         out_specs=outs,
         scratch_shapes=list(scratch),
         compiler_params=pltpu.CompilerParams(vmem_limit_bytes=limit << 20),
+        cost_estimate=cost,
         name=name,
     )
 
@@ -68,13 +70,17 @@
     ]
 
 
-def pack_kernel(w_hbm, w_out, sem):
-    ch = w_hbm.shape[-1]
+def load_kernel(w_conv, w_qkv, w_out, conv_vm, qkv_vm, out_vm, sem):
+    ch = w_conv.shape[-1]
     copies = [
+        pltpu.make_async_copy(w_qkv, qkv_vm, sem.at[27]),
+        pltpu.make_async_copy(w_out, out_vm, sem.at[28]),
+    ]
+    copies += [
         pltpu.make_async_copy(
-            w_hbm.at[i, j, k],
-            w_out.at[i, j * ch : (j + 1) * ch, k * ch : (k + 1) * ch],
-            sem.at[i, j, k],
+            w_conv.at[i, j, k],
+            conv_vm.at[i, j * ch : (j + 1) * ch, k * ch : (k + 1) * ch],
+            sem.at[9 * i + 3 * j + k],
         )
         for i in range(3)
         for j in range(3)
@@ -167,29 +173,38 @@
     return part[:, ch : 2 * ch] + left + right
 
 
-def conv_kernel(cols, work, first, span_ref, clips, mid, top, low, w, *refs):
-    if first:
-        out, acc = refs
-    else:
-        partial, out, acc = refs
-    ch = mid.shape[-1]
+def conv_kernel(cols, work, use, n_in, ahead, span_ref, clips, *refs):
+    ins, (w, *partial, out, acc) = refs[:n_in], refs[n_in:]
+    ch = w.shape[-1] // 3
     acc[...] = jnp.zeros_like(acc)
+    first_row, second_row = slice(0, cols), slice(cols, 2 * cols)
     for tap, frame, which in work:
 
-        @pl.when(usable_flag(clips, span_ref[0] * 2 + frame, tap))
+        @pl.when(usable_flag(clips, (span_ref[0] + ahead) * 2 + frame, tap))
         def _(tap=tap, frame=frame, which=which):
-            rows = [top[which], mid[which, :cols, :], mid[which, cols:, :], low[which]]
-            lhs = jnp.concatenate(
-                [jnp.concatenate(rows[r : r + 3], axis=1) for r in range(2)], axis=0
-            )
-            acc[frame] += dot32(lhs, w[tap])
+            if use == "edge":
+                above, below = ins
+                acc[frame, first_row] += dot32(above[which], w[tap, :ch])
+                acc[frame, second_row] += dot32(below[which], w[tap, 2 * ch :])
+            else:
+                mid = ins[0]
+                rows = [mid[which, first_row, :], mid[which, second_row, :]]
+                if use == "own":
+                    lhs = jnp.concatenate(rows, axis=1)
+                    acc[frame, first_row] += dot32(lhs, w[tap, ch:])
+                    acc[frame, second_row] += dot32(lhs, w[tap, : 2 * ch])
+                else:
+                    rows = [ins[1][which]] + rows + [ins[2][which]]
+                    lhs = jnp.concatenate(
+                        [jnp.concatenate(rows[r : r + 3], axis=1) for r in range(2)], axis=0
+                    )
+                    acc[frame] += dot32(lhs, w[tap])
 
     for frame in range(2):
-        for r in range(2):
-            part = slice(r * cols, (r + 1) * cols)
+        for part in (first_row, second_row):
             val = shift_add(acc[frame, part, :], cols, ch)
-            if not first:
-                val = val + partial[frame, part, :]
+            if partial:
+                val = val + partial[0][frame, part, :]
             out[frame, part, :] = val.astype(out.dtype)
 
 
@@ -210,17 +225,23 @@
     send_b = lax.dynamic_index_in_dim(x, 1 - low, 0, keepdims=False)
     own_a = lax.ppermute(send_a, both, route_a)
     own_b = lax.ppermute(send_b, both, route_b)
-    w_packed = call(
-        pack_kernel,
-        "pack_weights",
-        struct((3, 3 * ch, 3 * ch)),
-        [ANY],
-        [pltpu.SemaphoreType.DMA((3, 3, 3))],
-        16,
-    )(w_conv)
+    w_packed, w_qkv, w_out = call(
+        load_kernel,
+        "load_weights",
+        tuple(
+            pltpu.VMEM(shape, bf16) for shape in ((3, 3 * ch, 3 * ch), w_qkv.shape, w_out.shape)
+        ),
+        [ANY] * 3,
+        [pltpu.SemaphoreType.DMA((29,))],
+        48,
+        size=9 << 20,
+    )(w_conv, w_qkv, w_out)
+    own_a, w_packed = lax.optimization_barrier((own_a, w_packed))
     other_a = lax.ppermute(own_a, "span", other_core)
     other_b = lax.ppermute(own_b, "span", other_core)
-    kv_a = call(keys_kernel, "keys", struct((2 * cells, 2 * ch)), [VMEM] * 4)(
+    kv_flops = 2 * 2 * cells * ch * 2 * ch
+    row_flops = 2 * cells * ch * (2 * ch + 8 * cells)
+    kv_a = call(keys_kernel, "keys", struct((2 * cells, 2 * ch)), [VMEM] * 4, flops=kv_flops)(
         own_a, other_a, norm_gain, w_qkv
     )
     kv_b, att_a = call(
@@ -228,10 +249,15 @@
         "attend",
         (struct((2 * cells, 2 * ch)), struct((cells, ch))),
         [VMEM] * 7,
+        flops=kv_flops + row_flops,
     )(own_b, other_b, own_a, kv_a, norm_gain, w_qkv, w_out)
     got_a = lax.ppermute(att_a, both, route_a)
     att_b = call(
-        functools.partial(attend_rest_kernel, cols), "attend_rest", struct((cells, ch)), [VMEM] * 6
+        functools.partial(attend_rest_kernel, cols),
+        "attend_rest",
+        struct((cells, ch)),
+        [VMEM] * 6,
+        flops=3 * row_flops,
     )(own_b, kv_a, kv_b, norm_gain, w_qkv, w_out)
     got_b = lax.ppermute(att_b, both, route_b)
     attended, active, top_edge, low_edge = call(
@@ -247,24 +273,29 @@
     )(tile, got_a, got_b, conv_gain)
     above = lax.ppermute(low_edge, both, shifted_route(tiles, spans, 1, 0))
     below = lax.ppermute(top_edge, both, shifted_route(tiles, spans, -1, 0))
-    before = lax.ppermute(active, both, shifted_route(tiles, spans, 0, 1))
-    before_above = lax.ppermute(low_edge, both, shifted_route(tiles, spans, 1, 1))
-    before_below = lax.ppermute(top_edge, both, shifted_route(tiles, spans, -1, 1))
     acc = pltpu.VMEM((frames, cells, 3 * ch), f32)
-    partial = call(
-        functools.partial(conv_kernel, cols, [(2, 0, 0), (2, 1, 1), (1, 1, 0)], True),
-        "conv_own",
-        struct((frames, cells, ch), f32),
-        [SMEM, SMEM] + [VMEM] * 4,
-        [acc],
-    )(span, clip_lengths, active, above, below, w_packed)
-    hidden = call(
-        functools.partial(conv_kernel, cols, [(0, 0, 0), (1, 0, 1), (0, 1, 1)], False),
-        "conv_before",
-        struct((frames, cells, ch)),
-        [SMEM, SMEM] + [VMEM] * 5,
-        [acc],
-    )(span, clip_lengths, before, before_above, before_below, w_packed, partial)
+    block = struct((frames, cells, ch))
+    sums = struct((frames, cells, ch), f32)
+    unit = 2 * cells * 9 * ch * ch
+    to_next = [(0, 0, 0), (1, 0, 1), (0, 1, 1)]
+    to_own = [(2, 0, 0), (2, 1, 1), (1, 1, 0)]
+
+    def conv(work, use, ahead, result, name, ins, *partial):
+        share = {"own": 2, "edge": 1, "all": 3}[use]
+        return call(
+            functools.partial(conv_kernel, cols, work, use, len(ins), ahead),
+            name,
+            result,
+            [SMEM, SMEM] + [VMEM] * (len(ins) + 1 + len(partial)),
+            [acc],
+            flops=share * unit,
+        )(span, clip_lengths, *ins, w_packed, *partial)
+
+    started = conv(to_next, "own", 1, sums, "conv_next_own", [active])
+    for_next = conv(to_next, "edge", 1, block, "conv_next_edge", [above, below], started)
+    earlier = lax.ppermute(for_next, both, shifted_route(tiles, spans, 0, 1))
+    own = conv(to_own, "all", 0, sums, "conv_own", [active, above, below])
+    hidden = (own + earlier.astype(f32)).astype(bf16)
     shape = (frames, row_count, cols, ch)
     return attended.reshape(shape), hidden.reshape(shape)
 

time: 71 us -> 65.3 us (0.920)
  the two profiles are of different devices: /device:TPU:13 before, /device:TPU:1 now
where the time goes in v2:
time: 65.3 us; the launch traced here: 65.2 us
  starting transfers between devices  22.9 us (35%)
  Pallas kernels  18.1 us (28%)
  waiting for transfers between devices  18.1 us (28%)
  local copies, waits for them, and re-layouts  4.39 us (7%)
  other arithmetic  0.9 us (1%)
  between operations  0.8 us (1%)
    pallas_call x3, Pallas kernels, conv(): call(functools.partial(conv_kernel, cols, work, use, len(ins), ahead), na...  6.57 us
    ppermute x1, starting transfers between devices, on_device(): got_a = lax.ppermute(att_a, both, route_a)  6.45 us
    ppermute x1, starting transfers between devices, on_device(): own_a = lax.ppermute(send_a, both, route_a)  5.61 us
    ppermute x1, waiting for transfers between devices, on_device(): below = lax.ppermute(top_edge, both, shifted_route(tiles, spans, -1, 0))  4.3 us
    ppermute x1, waiting for transfers between devices, on_device(): own_a = lax.ppermute(send_a, both, route_a)  4.24 us
    ppermute x1, starting transfers between devices, on_device(): earlier = lax.ppermute(for_next, both, shifted_route(tiles, spans, 0, 1))  3.99 us
    pallas_call x1, Pallas kernels, on_device(): call(load_kernel, 'load_weights', tuple((pltpu.VMEM(shape, bf16) for shap...  3.82 us
    ppermute x1, starting transfers between devices, on_device(): above = lax.ppermute(low_edge, both, shifted_route(tiles, spans, 1, 0))  3.74 us
  transfers between devices with their start and end apart: 9, of which 6 were waited for; matrix products, arithmetic and copies ran while one was open for 0% of the time, Pallas kernels for 19%

profile of v2, /device:TPU:1, one launch (start us, length us, event | category | flops | bytes accessed | tf_op | source)
XLA Modules:
  0.0 65.2 jit_solution(12739672389989420656)
XLA Ops:
  0.6 0.0 copy-start.4
  0.7 1.1 %dynamic-slice_bitcast_fusion = (bf16[320,384]{1,0:T(8,128)(2,1)S(1)}, bf16[320,384]{1,0:T(8,128)(2,1)S(1)}) fusion(bf16[2,320,384]{2,1,0:T(8,128)(2,1)} %bitcast.9, s32[]{:T(128)S(6)} %select_n.16, s32[]{:T(128)S(6)} %select_n.15), kind=kLoop, calls=%fused_computation.1 | loop fusion | bytes 983048 | tf_op jit(solution)/shard_map/jit(dynamic_index_in_dim)/squeeze | solution.py:224
  1.8 5.6 %collective-permute-start.2 = (bf16[320,384]{1,0:T(8,128)(2,1)S(1)}, bf16[320,384]{1,0:T(8,128)(2,1)S(1)}, u32[]{:S(2)}, u32[]{:S(2)}) collective-permute-start(bf16[320,384]{1,0:T(8,128)(2,1)S(1)} %get-tuple-element.24), channel_id=1, source_target_pairs={{0,0},{1,8},{2,2},{3,10},{4,4},{5,12},{6,6},{7,14},{8,1},{9,9},{10... | collective-permute-start | bytes 737288 | tf_op jit(solution)/shard_map/ppermute | solution.py:226
  7.4 1.1 %collective-permute-start = (bf16[320,384]{1,0:T(8,128)(2,1)S(1)}, bf16[320,384]{1,0:T(8,128)(2,1)S(1)}, u32[]{:S(2)}, u32[]{:S(2)}) collective-permute-start(bf16[320,384]{1,0:T(8,128)(2,1)S(1)} %get-tuple-element.25), channel_id=1, source_target_pairs={{0,4},{1,12},{2,6},{3,14},{4,0},{5,8},{6,2},{7,10},{8,5},{9,13},{1... | collective-permute-start | bytes 737288 | tf_op jit(solution)/shard_map/ppermute | solution.py:227
  8.5 3.8 %load_weights.1 = (bf16[3,1152,1152]{2,1,0:T(8,128)(2,1)S(1)}, bf16[384,1152]{1,0:T(8,128)(2,1)S(1)}, bf16[384,384]{1,0:T(8,128)(2,1)S(1)}) custom-call(bf16[3,3,3,384,384]{4,3,2,1,0:T(8,128)(2,1)} %w_conv.1, bf16[384,1152]{1,0:T(8,128)(2,1)} %w_qkv.1, bf16[384,384]{1,0:T(8,128)(2,1)} %w_out.1), custom_call_target="tpu_custom_call" | custom-call | bytes 9437184 | tf_op jit(solution)/shard_map/load_weights/pallas_call | solution.py:228
  12.3 0.0 copy-start
  12.3 0.0 copy-start.3
  12.3 4.2 %collective-permute-done.2.own.own_a = bf16[320,384]{1,0:T(8,128)(2,1)S(1)} collective-permute-done((bf16[320,384]{1,0:T(8,128)(2,1)S(1)}, bf16[320,384]{1,0:T(8,128)(2,1)S(1)}, u32[]{:S(2)}, u32[]{:S(2)}) %collective-permute-start.2) | collective-permute-done | bytes 245792 | tf_op jit(solution)/shard_map/ppermute | solution.py:226
  16.6 0.0 collective-permute-start.3
  16.6 0.0 collective-permute-done.own_b
  16.6 0.5 collective-permute-start.1
  17.1 1.0 %collective-permute-done.3.other = bf16[320,384]{1,0:T(8,128)(2,1)S(1)} collective-permute-done((bf16[320,384]{1,0:T(8,128)(2,1)S(1)}, bf16[320,384]{1,0:T(8,128)(2,1)S(1)}, u32[]{:S(2)}, u32[]{:S(2)}) %collective-permute-start.3) | collective-permute-done | bytes 245792 | tf_op jit(solution)/shard_map/ppermute | solution.py:240
  18.1 0.0 copy-done.4
  18.1 0.0 copy-start.2
  18.1 0.7 %keys.1.kv_a = bf16[640,768]{1,0:T(8,128)(2,1)S(1)} custom-call(bf16[320,384]{1,0:T(8,128)(2,1)S(1)} %collective-permute-done.2.own.own_a, bf16[320,384]{1,0:T(8,128)(2,1)S(1)} %collective-permute-done.3.other, f32[384]{0:T(512)S(1)} %copy-done.4, bf16[384,1152]{1,0:T(8,128)(2,1)S(1)} %get-tuple-element.15.w_qkv), custom_call_target="tpu_custom_call" | custom-call | flops 377487360 | bytes 1048576 | tf_op jit(solution)/shard_map/keys/pallas_call | solution.py:244
  18.8 0.0 collective-permute-done.1.other_b
  18.9 3.1 %attend.1 = (bf16[640,768]{1,0:T(8,128)(2,1)S(1)}, bf16[320,384]{1,0:T(8,128)(2,1)S(1)}) custom-call(bf16[320,384]{1,0:T(8,128)(2,1)S(1)} %collective-permute-done.own_b, bf16[320,384]{1,0:T(8,128)(2,1)S(1)} %collective-permute-done.1.other_b, bf16[320,384]{1,0:T(8,128)(2,1)S(1)} %collective-permute-done.2.own.own_a, bf16[640,768]{1,0:T(8,128)(2,1)S(1)} %keys.1.kv_a, ...), custom_call_target="tpu_custom_call" | custom-call | flops 1195376640 | bytes 1048576 | tf_op jit(solution)/shard_map/attend/pallas_call | solution.py:247
  22.0 6.4 %collective-permute-start.4 = (bf16[320,384]{1,0:T(8,128)(2,1)S(1)}, bf16[320,384]{1,0:T(8,128)(2,1)S(1)}, u32[]{:S(2)}, u32[]{:S(2)}) collective-permute-start(bf16[320,384]{1,0:T(8,128)(2,1)S(1)} %get-tuple-element.17), channel_id=1, source_target_pairs={{0,0},{1,8},{2,2},{3,10},{4,4},{5,12},{6,6},{7,14},{8,1},{9,9},{10... | collective-permute-start | bytes 737288 | tf_op jit(solution)/shard_map/ppermute | solution.py:254
  28.5 2.6 %attend_rest.1 = bf16[320,384]{1,0:T(8,128)(2,1)S(1)} custom-call(bf16[320,384]{1,0:T(8,128)(2,1)S(1)} %collective-permute-done.own_b, bf16[640,768]{1,0:T(8,128)(2,1)S(1)} %keys.1.kv_a, bf16[640,768]{1,0:T(8,128)(2,1)S(1)} %get-tuple-element.18.kv_b, f32[384]{0:T(512)S(1)} %copy-done.4, bf16[384,1152]{1,0:T(8,128)(2,1)S(1)} %get-tuple-element.15.w_qkv, ...), custom_call_target="tpu_custom_call" | custom-call | flops 2453667840 | bytes 1048576 | tf_op jit(solution)/shard_map/attend_rest/pallas_call | solution.py:255
  31.1 0.2 collective-permute-start.5
  31.3 3.6 %collective-permute-done.4.got_a = bf16[320,384]{1,0:T(8,128)(2,1)S(1)} collective-permute-done((bf16[320,384]{1,0:T(8,128)(2,1)S(1)}, bf16[320,384]{1,0:T(8,128)(2,1)S(1)}, u32[]{:S(2)}, u32[]{:S(2)}) %collective-permute-start.4) | collective-permute-done | bytes 245792 | tf_op jit(solution)/shard_map/ppermute | solution.py:254
  35.0 3.7 %collective-permute-done.5.got_b = bf16[320,384]{1,0:T(8,128)(2,1)S(1)} collective-permute-done((bf16[320,384]{1,0:T(8,128)(2,1)S(1)}, bf16[320,384]{1,0:T(8,128)(2,1)S(1)}, u32[]{:S(2)}, u32[]{:S(2)}) %collective-permute-start.5) | collective-permute-done | bytes 245792 | tf_op jit(solution)/shard_map/ppermute | solution.py:262
  38.7 0.0 copy-done.3
  38.7 1.2 %activate.1 = (bf16[2,320,384]{2,1,0:T(8,128)(2,1)}, bf16[2,320,384]{2,1,0:T(8,128)(2,1)S(1)}, bf16[2,160,384]{2,1,0:T(8,128)(2,1)S(1)}, bf16[2,160,384]{2,1,0:T(8,128)(2,1)S(1)}) custom-call(s32[1]{0:T(128)} %bitcast.tile_ref, bf16[320,384]{1,0:T(8,128)(2,1)S(1)} %collective-permute-done.4.got_a, bf16[320,384]{1,0:T(8,128)(2,1)S(1)} %collective-permute-done.5.got_b, ...), custom_call_target="tpu_custom_call" | custom-call | bytes 1048576 | tf_op jit(solution)/shard_map/activate/pallas_call | solution.py:263
  39.9 0.0 copy-done
  39.9 3.7 %collective-permute-start.6 = (bf16[2,160,384]{2,1,0:T(8,128)(2,1)S(1)}, bf16[2,160,384]{2,1,0:T(8,128)(2,1)S(1)}, u32[]{:S(2)}, u32[]{:S(2)}) collective-permute-start(bf16[2,160,384]{2,1,0:T(8,128)(2,1)S(1)} %get-tuple-element.21), channel_id=1, source_target_pairs={{0,4},{1,5},{2,6},{3,7},{4,8},{5,9},{6,10},{7,11},{8,12},{9,13},{1... | collective-permute-start | bytes 737288 | tf_op jit(solution)/shard_map/ppermute | solution.py:274
  43.6 1.3 %collective-permute-start.7 = (bf16[2,160,384]{2,1,0:T(8,128)(2,1)S(1)}, bf16[2,160,384]{2,1,0:T(8,128)(2,1)S(1)}, u32[]{:S(2)}, u32[]{:S(2)}) collective-permute-start(bf16[2,160,384]{2,1,0:T(8,128)(2,1)S(1)} %get-tuple-element.22), channel_id=1, source_target_pairs={{4,0},{5,1},{6,2},{7,3},{8,4},{9,5},{10,6},{11,7},{12,8},{13,9},{1... | collective-permute-start | bytes 737288 | tf_op jit(solution)/shard_map/ppermute | solution.py:275
  44.9 0.0 copy-done.2
  45.0 0.0 copy-start.1
  45.0 3.3 %copy-done.1 = bf16[3,1152,1152]{2,1,0:T(8,128)(2,1)S(1)} copy-done((bf16[3,1152,1152]{2,1,0:T(8,128)(2,1)S(1)}, bf16[3,1152,1152]{2,1,0:T(8,128)(2,1)}, u32[]{:S(2)}) %copy-start.1) | copy-done | bytes 7962648
  48.2 1.0 %conv_next_own.1.refs_3_ = f32[2,320,384]{2,1,0:T(8,128)S(1)} custom-call(s32[1]{0:T(128)} %bitcast.5.span_ref, s32[4]{0:T(128)S(1)} %copy-done.2, bf16[2,320,384]{2,1,0:T(8,128)(2,1)S(1)} %get-tuple-element.20.refs_0_, bf16[3,1152,1152]{2,1,0:T(8,128)(2,1)S(1)} %copy-done.1), custom_call_target="tpu_custom_call" | custom-call | flops 1698693120 | bytes 1048576 | tf_op jit(solution)/shard_map/conv_next_own/pallas_call | solution.py:285
  49.2 0.0 collective-permute-done.6.refs_1_.refs_0_
  49.2 4.3 %collective-permute-done.7.refs_2_.refs_1_ = bf16[2,160,384]{2,1,0:T(8,128)(2,1)S(1)} collective-permute-done((bf16[2,160,384]{2,1,0:T(8,128)(2,1)S(1)}, bf16[2,160,384]{2,1,0:T(8,128)(2,1)S(1)}, u32[]{:S(2)}, u32[]{:S(2)}) %collective-permute-start.7) | collective-permute-done | bytes 245792 | tf_op jit(solution)/shard_map/ppermute | solution.py:275
  53.5 1.1 %conv_next_edge.1 = bf16[2,320,384]{2,1,0:T(8,128)(2,1)S(1)} custom-call(s32[1]{0:T(128)} %bitcast.5.span_ref, s32[4]{0:T(128)S(1)} %copy-done.2, bf16[2,160,384]{2,1,0:T(8,128)(2,1)S(1)} %collective-permute-done.6.refs_1_.refs_0_, bf16[2,160,384]{2,1,0:T(8,128)(2,1)S(1)} %collective-permute-done.7.refs_2_.refs_1_, bf16[3,1152,1152]{2,1,0:T(8,128)(2,1)S(1)} %copy-done.1, ...), custom_call_target="tpu_custom_call" | custom-call | flops 849346560 | bytes 1048576 | tf_op jit(solution)/shard_map/conv_next_edge/pallas_call | solution.py:285
  54.5 4.0 %collective-permute-start.8 = (bf16[2,320,384]{2,1,0:T(8,128)(2,1)S(1)}, bf16[2,320,384]{2,1,0:T(8,128)(2,1)S(1)}, u32[]{:S(2)}, u32[]{:S(2)}) collective-permute-start(bf16[2,320,384]{2,1,0:T(8,128)(2,1)S(1)} %conv_next_edge.1), channel_id=1, source_target_pairs={{0,1},{1,2},{2,3},{4,5},{5,6},{6,7},{8,9},{9,10},{10,11},{12,13},{... | collective-permute-start | bytes 1474568 | tf_op jit(solution)/shard_map/ppermute | solution.py:296
  58.5 4.6 %conv_own.1 = f32[2,320,384]{2,1,0:T(8,128)S(1)} custom-call(s32[1]{0:T(128)} %bitcast.5.span_ref, s32[4]{0:T(128)S(1)} %copy-done.2, bf16[2,320,384]{2,1,0:T(8,128)(2,1)S(1)} %get-tuple-element.20.refs_0_, bf16[2,160,384]{2,1,0:T(8,128)(2,1)S(1)} %collective-permute-done.6.refs_1_.refs_0_, bf16[2,160,384]{2,1,0:T(8,128)(2,1)S(1)} %collective-permute-done.7.refs_2_.refs_1_, ...), custom_call_target="tpu_custom_call" | custom-call | flops 2548039680 | bytes 1048576 | tf_op jit(solution)/shard_map/conv_own/pallas_call | solution.py:285
  63.1 1.2 %collective-permute-done.8 = bf16[2,320,384]{2,1,0:T(8,128)(2,1)S(1)} collective-permute-done((bf16[2,320,384]{2,1,0:T(8,128)(2,1)S(1)}, bf16[2,320,384]{2,1,0:T(8,128)(2,1)S(1)}, u32[]{:S(2)}, u32[]{:S(2)}) %collective-permute-start.8) | collective-permute-done | bytes 491552 | tf_op jit(solution)/shard_map/ppermute | solution.py:296
  64.3 0.9 %add_convert_fusion = bf16[2,320,384]{2,1,0:T(8,128)(2,1)} fusion(f32[2,320,384]{2,1,0:T(8,128)S(1)} %conv_own.1, bf16[2,320,384]{2,1,0:T(8,128)(2,1)S(1)} %collective-permute-done.8), kind=kLoop, calls=%fused_computation | loop fusion | flops 737280 | bytes 1966080 | tf_op jit(solution)/shard_map/convert_element_type | solution.py:298
Async XLA Ops:
  0.6 17.5 %copy-start.4 = (f32[384]{0:T(512)S(1)}, f32[384]{0:T(512)}, u32[]{:S(2)}) copy-start(f32[384]{0:T(512)} %gain.6) | copy-start | bytes 4612
  1.8 14.8 %collective-permute-start.2 = (bf16[320,384]{1,0:T(8,128)(2,1)S(1)}, bf16[320,384]{1,0:T(8,128)(2,1)S(1)}, u32[]{:S(2)}, u32[]{:S(2)}) collective-permute-start(bf16[320,384]{1,0:T(8,128)(2,1)S(1)} %get-tuple-element.24), channel_id=1, source_target_pairs={{0,0},{1,8},{2,2},{3,10},{4,4},{5,12},{6,6},{7,14},{8,1},{9,9},{10... | collective-permute-start | bytes 737288 | tf_op jit(solution)/shard_map/ppermute | solution.py:226
  7.4 9.2 %collective-permute-start = (bf16[320,384]{1,0:T(8,128)(2,1)S(1)}, bf16[320,384]{1,0:T(8,128)(2,1)S(1)}, u32[]{:S(2)}, u32[]{:S(2)}) collective-permute-start(bf16[320,384]{1,0:T(8,128)(2,1)S(1)} %get-tuple-element.25), channel_id=1, source_target_pairs={{0,4},{1,12},{2,6},{3,14},{4,0},{5,8},{6,2},{7,10},{8,5},{9,13},{1... | collective-permute-start | bytes 737288 | tf_op jit(solution)/shard_map/ppermute | solution.py:227
  12.3 27.6 %copy-start = (bf16[3,1152,1152]{2,1,0:T(8,128)(2,1)}, bf16[3,1152,1152]{2,1,0:T(8,128)(2,1)S(1)}, u32[]{:S(2)}) copy-start(bf16[3,1152,1152]{2,1,0:T(8,128)(2,1)S(1)} %get-tuple-element.23.refs_3_.refs_1_.refs_2_) | copy-start | bytes 23887876
  12.3 26.4 %copy-start.3 = (f32[384]{0:T(512)S(1)}, f32[384]{0:T(512)}, u32[]{:S(2)}) copy-start(f32[384]{0:T(512)} %gain.7) | copy-start | bytes 4612
  16.6 1.5 %collective-permute-start.3 = (bf16[320,384]{1,0:T(8,128)(2,1)S(1)}, bf16[320,384]{1,0:T(8,128)(2,1)S(1)}, u32[]{:S(2)}, u32[]{:S(2)}) collective-permute-start(bf16[320,384]{1,0:T(8,128)(2,1)S(1)} %collective-permute-done.2.own.own_a), channel_id=1, source_target_pairs={{0,1},{1,0},{2,3},{3,2},{4,5},{5,4},{6,7},{7,6},{8,9},{9,8},{10,11... | collective-permute-start | bytes 737288 | tf_op jit(solution)/shard_map/ppermute | solution.py:240
  16.6 2.3 %collective-permute-start.1 = (bf16[320,384]{1,0:T(8,128)(2,1)S(1)}, bf16[320,384]{1,0:T(8,128)(2,1)S(1)}, u32[]{:S(2)}, u32[]{:S(2)}) collective-permute-start(bf16[320,384]{1,0:T(8,128)(2,1)S(1)} %collective-permute-done.own_b), channel_id=1, source_target_pairs={{0,1},{1,0},{2,3},{3,2},{4,5},{5,4},{6,7},{7,6},{8,9},{9,8},{10,11... | collective-permute-start | bytes 737288 | tf_op jit(solution)/shard_map/ppermute | solution.py:241
  18.1 26.9 %copy-start.2 = (s32[4]{0:T(128)S(1)}, s32[4]{0:T(128)}, u32[]{:S(2)}) copy-start(s32[4]{0:T(128)} %clips.5) | copy-start | bytes 52
  22.0 13.0 %collective-permute-start.4 = (bf16[320,384]{1,0:T(8,128)(2,1)S(1)}, bf16[320,384]{1,0:T(8,128)(2,1)S(1)}, u32[]{:S(2)}, u32[]{:S(2)}) collective-permute-start(bf16[320,384]{1,0:T(8,128)(2,1)S(1)} %get-tuple-element.17), channel_id=1, source_target_pairs={{0,0},{1,8},{2,2},{3,10},{4,4},{5,12},{6,6},{7,14},{8,1},{9,9},{10... | collective-permute-start | bytes 737288 | tf_op jit(solution)/shard_map/ppermute | solution.py:254
  31.1 7.6 %collective-permute-start.5 = (bf16[320,384]{1,0:T(8,128)(2,1)S(1)}, bf16[320,384]{1,0:T(8,128)(2,1)S(1)}, u32[]{:S(2)}, u32[]{:S(2)}) collective-permute-start(bf16[320,384]{1,0:T(8,128)(2,1)S(1)} %attend_rest.1), channel_id=1, source_target_pairs={{0,4},{1,12},{2,6},{3,14},{4,0},{5,8},{6,2},{7,10},{8,5},{9,13},{1... | collective-permute-start | bytes 737288 | tf_op jit(solution)/shard_map/ppermute | solution.py:262
  39.9 9.3 %collective-permute-start.6 = (bf16[2,160,384]{2,1,0:T(8,128)(2,1)S(1)}, bf16[2,160,384]{2,1,0:T(8,128)(2,1)S(1)}, u32[]{:S(2)}, u32[]{:S(2)}) collective-permute-start(bf16[2,160,384]{2,1,0:T(8,128)(2,1)S(1)} %get-tuple-element.21), channel_id=1, source_target_pairs={{0,4},{1,5},{2,6},{3,7},{4,8},{5,9},{6,10},{7,11},{8,12},{9,13},{1... | collective-permute-start | bytes 737288 | tf_op jit(solution)/shard_map/ppermute | solution.py:274
  43.6 9.8 %collective-permute-start.7 = (bf16[2,160,384]{2,1,0:T(8,128)(2,1)S(1)}, bf16[2,160,384]{2,1,0:T(8,128)(2,1)S(1)}, u32[]{:S(2)}, u32[]{:S(2)}) collective-permute-start(bf16[2,160,384]{2,1,0:T(8,128)(2,1)S(1)} %get-tuple-element.22), channel_id=1, source_target_pairs={{4,0},{5,1},{6,2},{7,3},{8,4},{9,5},{10,6},{11,7},{12,8},{13,9},{1... | collective-permute-start | bytes 737288 | tf_op jit(solution)/shard_map/ppermute | solution.py:275
  45.0 3.3 %copy-start.1 = (bf16[3,1152,1152]{2,1,0:T(8,128)(2,1)S(1)}, bf16[3,1152,1152]{2,1,0:T(8,128)(2,1)}, u32[]{:S(2)}) copy-start(bf16[3,1152,1152]{2,1,0:T(8,128)(2,1)} %copy-done) | copy-start | bytes 23887876
  54.5 9.7 %collective-permute-start.8 = (bf16[2,320,384]{2,1,0:T(8,128)(2,1)S(1)}, bf16[2,320,384]{2,1,0:T(8,128)(2,1)S(1)}, u32[]{:S(2)}, u32[]{:S(2)}) collective-permute-start(bf16[2,320,384]{2,1,0:T(8,128)(2,1)S(1)} %conv_next_edge.1), channel_id=1, source_target_pairs={{0,1},{1,2},{2,3},{4,5},{5,6},{6,7},{8,9},{9,10},{10,11},{12,13},{... | collective-permute-start | bytes 1474568 | tf_op jit(solution)/shard_map/ppermute | solution.py:296

commit v3 on v2

--- a/solution.py
+++ b/solution.py
@@ -70,21 +70,10 @@
     ]
 
 
-def load_kernel(w_conv, w_qkv, w_out, conv_vm, qkv_vm, out_vm, sem):
-    ch = w_conv.shape[-1]
+def load_small_kernel(w_qkv, w_out, qkv_vm, out_vm, sem):
     copies = [
-        pltpu.make_async_copy(w_qkv, qkv_vm, sem.at[27]),
-        pltpu.make_async_copy(w_out, out_vm, sem.at[28]),
-    ]
-    copies += [
-        pltpu.make_async_copy(
-            w_conv.at[i, j, k],
-            conv_vm.at[i, j * ch : (j + 1) * ch, k * ch : (k + 1) * ch],
-            sem.at[9 * i + 3 * j + k],
-        )
-        for i in range(3)
-        for j in range(3)
-        for k in range(3)
+        pltpu.make_async_copy(w_qkv, qkv_vm, sem.at[0]),
+        pltpu.make_async_copy(w_out, out_vm, sem.at[1]),
     ]
     for copy in copies:
         copy.start()
@@ -140,9 +129,10 @@
     attend_rows(cols, own_b, (kv_a, kv_b), gain_vec, w_qkv, w_out, att_b)
 
 
-def activate_kernel(cols, tile_ref, got_a, got_b, gain, attended, active, top_edge, low_edge):
+def activate_kernel(cols, tile_ref, got_a, got_b, gain, attended, active, pair_edge, mid_edge):
     low = tile_ref[0] % 2
     gain_vec = gain[...].reshape(1, got_a.shape[1])
+    first_row, second_row = slice(0, cols), slice(cols, 2 * cols)
 
     def one(block, frame):
         values = block[...]
@@ -150,8 +140,16 @@
         lifted = rms_scale(values, gain_vec)
         act = (lifted / (1.0 + jnp.exp(-lifted))).astype(bf16)
         active[frame] = act
-        top_edge[frame] = act[:cols, :]
-        low_edge[frame] = act[cols:, :]
+
+        @pl.when(low == 0)
+        def _():
+            pair_edge[frame] = act[second_row, :]
+            mid_edge[frame] = act[first_row, :]
+
+        @pl.when(low == 1)
+        def _():
+            pair_edge[frame] = act[first_row, :]
+            mid_edge[frame] = act[second_row, :]
 
     one(got_a, low)
     one(got_b, 1 - low)
@@ -173,39 +171,95 @@
     return part[:, ch : 2 * ch] + left + right
 
 
-def conv_kernel(cols, work, use, n_in, ahead, span_ref, clips, *refs):
-    ins, (w, *partial, out, acc) = refs[:n_in], refs[n_in:]
+def weigh(flag, block):
+    return (block.astype(f32) * flag).astype(bf16)
+
+
+def flags_of(clips, frame_at):
+    return [
+        [usable_flag(clips, frame_at + f, tap).astype(f32) for tap in range(3)] for f in range(2)
+    ]
+
+
+def next_own_kernel(cols, span_ref, clips, mid, w_hbm, out, w, sem):
+    ch = mid.shape[-1]
+    copies = [
+        [
+            pltpu.make_async_copy(
+                w_hbm.at[i, j, k],
+                w.at[i, j * ch : (j + 1) * ch, k * ch : (k + 1) * ch],
+                sem.at[9 * i + 3 * j + k],
+            )
+            for j in range(3)
+            for k in range(3)
+        ]
+        for i in range(3)
+    ]
+    for tap in copies:
+        for copy in tap:
+            copy.start()
+    flag = flags_of(clips, (span_ref[0] + 1) * 2)
+    first_row, second_row = slice(0, cols), slice(cols, 2 * cols)
+    pair = [
+        jnp.concatenate([mid[f, first_row, :], mid[f, second_row, :]], axis=1) for f in range(2)
+    ]
+    last = jnp.concatenate([weigh(flag[0][0], pair[0]), weigh(flag[1][0], pair[1])], axis=0)
+    middle = weigh(flag[0][1], pair[1])
+    parts = ((first_row, slice(ch, 3 * ch)), (second_row, slice(0, 2 * ch)))
+    for copy in copies[0]:
+        copy.wait()
+    for part, taps in parts:
+        far = dot32(last, w[0, taps])
+        out[0, part, :] = shift_add(far[:cols], cols, ch)
+        out[1, part, :] = shift_add(far[cols:], cols, ch)
+    for copy in copies[1]:
+        copy.wait()
+    for part, taps in parts:
+        out[0, part, :] += shift_add(dot32(middle, w[1, taps]), cols, ch)
+    for copy in copies[2]:
+        copy.wait()
+
+
+def next_edge_kernel(cols, tile_ref, span_ref, clips, pair_got, mid_got, w, partial, out):
     ch = w.shape[-1] // 3
-    acc[...] = jnp.zeros_like(acc)
+    flag = flags_of(clips, (span_ref[0] + 1) * 2)
+    odd = tile_ref[0] % 2 == 1
+    for f_pair, part, taps in (
+        (odd, slice(0, cols), slice(0, ch)),
+        (jnp.logical_not(odd), slice(cols, 2 * cols), slice(2 * ch, 3 * ch)),
+    ):
+        pick = f_pair.astype(f32)
+        edge = [
+            pair_got[f].astype(f32) * pick + mid_got[f].astype(f32) * (1.0 - pick)
+            for f in range(2)
+        ]
+        last = jnp.concatenate([edge[0] * flag[0][0], edge[1] * flag[1][0]], axis=0).astype(bf16)
+        middle = (edge[1] * flag[0][1]).astype(bf16)
+        far = dot32(last, w[0, taps])
+        near = far[:cols] + dot32(middle, w[1, taps])
+        for f, val in ((0, near), (1, far[cols:])):
+            out[f, part, :] = (shift_add(val, cols, ch) + partial[f, part, :]).astype(bf16)
+
+
+def own_kernel(cols, tile_ref, span_ref, clips, mid, pair_got, mid_got, w, out):
+    ch = mid.shape[-1]
+    flag = flags_of(clips, span_ref[0] * 2)
+    pick = (tile_ref[0] % 2).astype(f32)
     first_row, second_row = slice(0, cols), slice(cols, 2 * cols)
-    for tap, frame, which in work:
-
-        @pl.when(usable_flag(clips, (span_ref[0] + ahead) * 2 + frame, tap))
-        def _(tap=tap, frame=frame, which=which):
-            if use == "edge":
-                above, below = ins
-                acc[frame, first_row] += dot32(above[which], w[tap, :ch])
-                acc[frame, second_row] += dot32(below[which], w[tap, 2 * ch :])
-            else:
-                mid = ins[0]
-                rows = [mid[which, first_row, :], mid[which, second_row, :]]
-                if use == "own":
-                    lhs = jnp.concatenate(rows, axis=1)
-                    acc[frame, first_row] += dot32(lhs, w[tap, ch:])
-                    acc[frame, second_row] += dot32(lhs, w[tap, : 2 * ch])
-                else:
-                    rows = [ins[1][which]] + rows + [ins[2][which]]
-                    lhs = jnp.concatenate(
-                        [jnp.concatenate(rows[r : r + 3], axis=1) for r in range(2)], axis=0
-                    )
-                    acc[frame] += dot32(lhs, w[tap])
-
-    for frame in range(2):
-        for part in (first_row, second_row):
-            val = shift_add(acc[frame, part, :], cols, ch)
-            if partial:
-                val = val + partial[0][frame, part, :]
-            out[frame, part, :] = val.astype(out.dtype)
+    wide = []
+    for f in range(2):
+        pair, other = pair_got[f].astype(f32), mid_got[f].astype(f32)
+        above = (pair * pick + other * (1.0 - pick)).astype(bf16)
+        below = (other * pick + pair * (1.0 - pick)).astype(bf16)
+        rows = [above, mid[f, first_row, :], mid[f, second_row, :], below]
+        wide.append([jnp.concatenate(rows[r : r + 3], axis=1) for r in range(2)])
+    here = dot32(jnp.concatenate(wide[0] + wide[1], axis=0), w[2])
+    back = dot32(jnp.concatenate([weigh(flag[1][1], x) for x in wide[0]], axis=0), w[1])
+    for r in range(2):
+        part = slice(r * cols, (r + 1) * cols)
+        out[0, part, :] = shift_add(here[part], cols, ch)
+        after = here[(2 + r) * cols : (3 + r) * cols]
+        out[1, part, :] = shift_add(after + back[part], cols, ch)
 
 
 def on_device(features, clip_lengths, norm_gain, w_qkv, w_out, conv_gain, w_conv):
@@ -225,18 +279,15 @@
     send_b = lax.dynamic_index_in_dim(x, 1 - low, 0, keepdims=False)
     own_a = lax.ppermute(send_a, both, route_a)
     own_b = lax.ppermute(send_b, both, route_b)
-    w_packed, w_qkv, w_out = call(
-        load_kernel,
-        "load_weights",
-        tuple(
-            pltpu.VMEM(shape, bf16) for shape in ((3, 3 * ch, 3 * ch), w_qkv.shape, w_out.shape)
-        ),
-        [ANY] * 3,
-        [pltpu.SemaphoreType.DMA((29,))],
-        48,
-        size=9 << 20,
-    )(w_conv, w_qkv, w_out)
-    own_a, w_packed = lax.optimization_barrier((own_a, w_packed))
+    w_qkv, w_out = call(
+        load_small_kernel,
+        "load_small",
+        tuple(pltpu.VMEM(w.shape, bf16) for w in (w_qkv, w_out)),
+        [ANY] * 2,
+        [pltpu.SemaphoreType.DMA((2,))],
+        60,
+    )(w_qkv, w_out)
+    own_a, w_qkv = lax.optimization_barrier((own_a, w_qkv))
     other_a = lax.ppermute(own_a, "span", other_core)
     other_b = lax.ppermute(own_b, "span", other_core)
     kv_flops = 2 * 2 * cells * ch * 2 * ch
@@ -260,7 +311,7 @@
         flops=3 * row_flops,
     )(own_b, kv_a, kv_b, norm_gain, w_qkv, w_out)
     got_b = lax.ppermute(att_b, both, route_b)
-    attended, active, top_edge, low_edge = call(
+    attended, active, pair_edge, mid_edge = call(
         functools.partial(activate_kernel, cols),
         "activate",
         (
@@ -271,30 +322,31 @@
         ),
         [SMEM] + [VMEM] * 3,
     )(tile, got_a, got_b, conv_gain)
-    above = lax.ppermute(low_edge, both, shifted_route(tiles, spans, 1, 0))
-    below = lax.ppermute(top_edge, both, shifted_route(tiles, spans, -1, 0))
-    acc = pltpu.VMEM((frames, cells, 3 * ch), f32)
+    pair_got = lax.ppermute(pair_edge, "tile", [(0, 1), (1, 0), (2, 3), (3, 2)])
+    mid_got = lax.ppermute(mid_edge, "tile", [(1, 2), (2, 1)])
     block = struct((frames, cells, ch))
     sums = struct((frames, cells, ch), f32)
     unit = 2 * cells * 9 * ch * ch
-    to_next = [(0, 0, 0), (1, 0, 1), (0, 1, 1)]
-    to_own = [(2, 0, 0), (2, 1, 1), (1, 1, 0)]
-
-    def conv(work, use, ahead, result, name, ins, *partial):
-        share = {"own": 2, "edge": 1, "all": 3}[use]
-        return call(
-            functools.partial(conv_kernel, cols, work, use, len(ins), ahead),
-            name,
-            result,
-            [SMEM, SMEM] + [VMEM] * (len(ins) + 1 + len(partial)),
-            [acc],
-            flops=share * unit,
-        )(span, clip_lengths, *ins, w_packed, *partial)
-
-    started = conv(to_next, "own", 1, sums, "conv_next_own", [active])
-    for_next = conv(to_next, "edge", 1, block, "conv_next_edge", [above, below], started)
+    started, w_packed = call(
+        functools.partial(next_own_kernel, cols),
+        "next_own",
+        (sums, struct((3, 3 * ch, 3 * ch))),
+        [SMEM] * 2 + [VMEM, ANY],
+        [pltpu.SemaphoreType.DMA((27,))],
+        42,
+        flops=2 * unit,
+    )(span, clip_lengths, active, w_conv)
+    for_next = call(
+        functools.partial(next_edge_kernel, cols),
+        "next_edge",
+        block,
+        [SMEM] * 3 + [VMEM] * 4,
+        flops=unit,
+    )(tile, span, clip_lengths, pair_got, mid_got, w_packed, started)
     earlier = lax.ppermute(for_next, both, shifted_route(tiles, spans, 0, 1))
-    own = conv(to_own, "all", 0, sums, "conv_own", [active, above, below])
+    own = call(
+        functools.partial(own_kernel, cols), "own", sums, [SMEM] * 3 + [VMEM] * 4, flops=3 * unit
+    )(tile, span, clip_lengths, active, pair_got, mid_got, w_packed)
     hidden = (own + earlier.astype(f32)).astype(bf16)
     shape = (frames, row_count, cols, ch)
     return attended.reshape(shape), hidden.reshape(shape)

time: 65.3 us -> 62.7 us (0.960)
  the two profiles are of different devices: /device:TPU:1 before, /device:TPU:13 now
where the time goes in v3:
time: 62.7 us; the launch traced here: 61.7 us
  waiting for transfers between devices  23.3 us (37%)
  Pallas kernels  19.8 us (32%)
  starting transfers between devices  15.1 us (24%)
  local copies, waits for them, and re-layouts  1.81 us (3%)
  other arithmetic  0.9 us (1%)
  between operations  0.78 us (1%)
    ppermute x1, waiting for transfers between devices, on_device(): got_b = lax.ppermute(att_b, both, route_b)  7.35 us
    ppermute x1, waiting for transfers between devices, on_device(): own_a = lax.ppermute(send_a, both, route_a)  7.02 us
    pallas_call x1, Pallas kernels, on_device(): call(functools.partial(next_own_kernel, cols), 'next_own', (sums, struct(...  4.8 us
    ppermute x1, starting transfers between devices, on_device(): own_a = lax.ppermute(send_a, both, route_a)  4.78 us
    ppermute x1, starting transfers between devices, on_device(): got_a = lax.ppermute(att_a, both, route_a)  4.1 us
    pallas_call x1, Pallas kernels, on_device(): call(functools.partial(own_kernel, cols), 'own', sums, [SMEM] * 3 + [VMEM...  3.86 us
    ppermute x1, starting transfers between devices, on_device(): earlier = lax.ppermute(for_next, both, shifted_route(tiles, spans, 0, 1))  3.85 us
    pallas_call x1, Pallas kernels, on_device(): call(functools.partial(attend_kernel, cols), 'attend', (struct((2 * cells...  3.14 us
  transfers between devices with their start and end apart: 9, of which 7 were waited for; matrix products, arithmetic and copies ran while one was open for 0% of the time, Pallas kernels for 22%

profile of v3, /device:TPU:13, one launch (start us, length us, event | category | flops | bytes accessed | tf_op | source)
XLA Modules:
  0.0 61.7 jit_solution(10606085709213394820)
XLA Ops:
  0.7 1.1 %dynamic-slice_bitcast_fusion = (bf16[320,384]{1,0:T(8,128)(2,1)S(1)}, bf16[320,384]{1,0:T(8,128)(2,1)S(1)}) fusion(bf16[2,320,384]{2,1,0:T(8,128)(2,1)} %bitcast.9, s32[]{:T(128)S(6)} %select_n.16, s32[]{:T(128)S(6)} %select_n.15), kind=kLoop, calls=%fused_computation.1 | loop fusion | bytes 983048 | tf_op jit(solution)/shard_map/jit(dynamic_index_in_dim)/squeeze | solution.py:278
  1.8 4.8 %collective-permute-start.2 = (bf16[320,384]{1,0:T(8,128)(2,1)S(1)}, bf16[320,384]{1,0:T(8,128)(2,1)S(1)}, u32[]{:S(2)}, u32[]{:S(2)}) collective-permute-start(bf16[320,384]{1,0:T(8,128)(2,1)S(1)} %get-tuple-element.26), channel_id=1, source_target_pairs={{0,0},{1,8},{2,2},{3,10},{4,4},{5,12},{6,6},{7,14},{8,1},{9,9},{10... | collective-permute-start | bytes 737288 | tf_op jit(solution)/shard_map/ppermute | solution.py:280
  6.6 0.1 collective-permute-start
  6.6 1.2 %load_small.1 = (bf16[384,1152]{1,0:T(8,128)(2,1)S(1)}, bf16[384,384]{1,0:T(8,128)(2,1)S(1)}) custom-call(bf16[384,1152]{1,0:T(8,128)(2,1)} %w_qkv.1, bf16[384,384]{1,0:T(8,128)(2,1)} %w_out.1), custom_call_target="tpu_custom_call" | custom-call | bytes 1048576 | tf_op jit(solution)/shard_map/load_small/pallas_call | solution.py:282
  7.9 0.0 copy-start.1
  7.9 7.0 %collective-permute-done.2.own.own_a = bf16[320,384]{1,0:T(8,128)(2,1)S(1)} collective-permute-done((bf16[320,384]{1,0:T(8,128)(2,1)S(1)}, bf16[320,384]{1,0:T(8,128)(2,1)S(1)}, u32[]{:S(2)}, u32[]{:S(2)}) %collective-permute-start.2) | collective-permute-done | bytes 245792 | tf_op jit(solution)/shard_map/ppermute | solution.py:280
  14.9 0.0 copy-start
  14.9 0.0 collective-permute-start.3
  14.9 2.6 %collective-permute-done.own_b = bf16[320,384]{1,0:T(8,128)(2,1)S(1)} collective-permute-done((bf16[320,384]{1,0:T(8,128)(2,1)S(1)}, bf16[320,384]{1,0:T(8,128)(2,1)S(1)}, u32[]{:S(2)}, u32[]{:S(2)}) %collective-permute-start) | collective-permute-done | bytes 245792 | tf_op jit(solution)/shard_map/ppermute | solution.py:281
  17.6 0.0 collective-permute-start.1
  17.6 0.0 collective-permute-done.3.other
  17.6 0.0 copy-start.2
  17.6 0.7 %copy-done.2 = f32[384]{0:T(512)S(1)} copy-done((f32[384]{0:T(512)S(1)}, f32[384]{0:T(512)}, u32[]{:S(2)}) %copy-start.2) | copy-done | bytes 1560
  18.2 0.7 %keys.1.kv_a = bf16[640,768]{1,0:T(8,128)(2,1)S(1)} custom-call(bf16[320,384]{1,0:T(8,128)(2,1)S(1)} %collective-permute-done.2.own.own_a, bf16[320,384]{1,0:T(8,128)(2,1)S(1)} %collective-permute-done.3.other, f32[384]{0:T(512)S(1)} %copy-done.2, bf16[384,1152]{1,0:T(8,128)(2,1)S(1)} %get-tuple-element.16.w_qkv), custom_call_target="tpu_custom_call" | custom-call | flops 377487360 | bytes 1048576 | tf_op jit(solution)/shard_map/keys/pallas_call | solution.py:295
  19.0 0.1 collective-permute-done.1.other_b
  19.1 3.1 %attend.1 = (bf16[640,768]{1,0:T(8,128)(2,1)S(1)}, bf16[320,384]{1,0:T(8,128)(2,1)S(1)}) custom-call(bf16[320,384]{1,0:T(8,128)(2,1)S(1)} %collective-permute-done.own_b, bf16[320,384]{1,0:T(8,128)(2,1)S(1)} %collective-permute-done.1.other_b, bf16[320,384]{1,0:T(8,128)(2,1)S(1)} %collective-permute-done.2.own.own_a, bf16[640,768]{1,0:T(8,128)(2,1)S(1)} %keys.1.kv_a, ...), custom_call_target="tpu_custom_call" | custom-call | flops 1195376640 | bytes 1048576 | tf_op jit(solution)/shard_map/attend/pallas_call | solution.py:298
  22.2 4.1 %collective-permute-start.4 = (bf16[320,384]{1,0:T(8,128)(2,1)S(1)}, bf16[320,384]{1,0:T(8,128)(2,1)S(1)}, u32[]{:S(2)}, u32[]{:S(2)}) collective-permute-start(bf16[320,384]{1,0:T(8,128)(2,1)S(1)} %get-tuple-element.18), channel_id=1, source_target_pairs={{0,0},{1,8},{2,2},{3,10},{4,4},{5,12},{6,6},{7,14},{8,1},{9,9},{10... | collective-permute-start | bytes 737288 | tf_op jit(solution)/shard_map/ppermute | solution.py:305
  26.3 2.6 %attend_rest.1 = bf16[320,384]{1,0:T(8,128)(2,1)S(1)} custom-call(bf16[320,384]{1,0:T(8,128)(2,1)S(1)} %collective-permute-done.own_b, bf16[640,768]{1,0:T(8,128)(2,1)S(1)} %keys.1.kv_a, bf16[640,768]{1,0:T(8,128)(2,1)S(1)} %get-tuple-element.19.kv_b, f32[384]{0:T(512)S(1)} %copy-done.2, bf16[384,1152]{1,0:T(8,128)(2,1)S(1)} %get-tuple-element.16.w_qkv, ...), custom_call_target="tpu_custom_call" | custom-call | flops 2453667840 | bytes 1048576 | tf_op jit(solution)/shard_map/attend_rest/pallas_call | solution.py:306
  28.9 0.4 collective-permute-start.5
  29.3 1.7 %collective-permute-done.4.got_a = bf16[320,384]{1,0:T(8,128)(2,1)S(1)} collective-permute-done((bf16[320,384]{1,0:T(8,128)(2,1)S(1)}, bf16[320,384]{1,0:T(8,128)(2,1)S(1)}, u32[]{:S(2)}, u32[]{:S(2)}) %collective-permute-start.4) | collective-permute-done | bytes 245792 | tf_op jit(solution)/shard_map/ppermute | solution.py:305
  31.0 7.4 %collective-permute-done.5.got_b = bf16[320,384]{1,0:T(8,128)(2,1)S(1)} collective-permute-done((bf16[320,384]{1,0:T(8,128)(2,1)S(1)}, bf16[320,384]{1,0:T(8,128)(2,1)S(1)}, u32[]{:S(2)}, u32[]{:S(2)}) %collective-permute-start.5) | collective-permute-done | bytes 245792 | tf_op jit(solution)/shard_map/ppermute | solution.py:313
  38.4 0.0 copy-done.1
  38.4 1.4 %activate.1 = (bf16[2,320,384]{2,1,0:T(8,128)(2,1)}, bf16[2,320,384]{2,1,0:T(8,128)(2,1)S(1)}, bf16[2,160,384]{2,1,0:T(8,128)(2,1)S(1)}, bf16[2,160,384]{2,1,0:T(8,128)(2,1)S(1)}) custom-call(s32[1]{0:T(128)} %bitcast.tile_ref, bf16[320,384]{1,0:T(8,128)(2,1)S(1)} %collective-permute-done.4.got_a, bf16[320,384]{1,0:T(8,128)(2,1)S(1)} %collective-permute-done.5.got_b, ...), custom_call_target="tpu_custom_call" | custom-call | bytes 1048576 | tf_op jit(solution)/shard_map/activate/pallas_call | solution.py:314
  39.8 0.0 collective-permute-start.6
  39.8 1.9 %collective-permute-start.7 = (bf16[2,160,384]{2,1,0:T(8,128)(2,1)S(1)}, bf16[2,160,384]{2,1,0:T(8,128)(2,1)S(1)}, u32[]{:S(2)}, u32[]{:S(2)}) collective-permute-start(bf16[2,160,384]{2,1,0:T(8,128)(2,1)S(1)} %get-tuple-element.23), channel_id=1, source_target_pairs={{4,8},{8,4},{5,9},{9,5},{6,10},{10,6},{7,11},{11,7},{20,24},{24,20... | collective-permute-start | bytes 737288 | tf_op jit(solution)/shard_map/ppermute | solution.py:326
  41.7 0.0 copy-done
  41.7 4.8 %next_own.1 = (f32[2,320,384]{2,1,0:T(8,128)S(1)}, bf16[3,1152,1152]{2,1,0:T(8,128)(2,1)S(1)}) custom-call(s32[1]{0:T(128)} %bitcast.5.span_ref, s32[4]{0:T(128)S(1)} %copy-done, bf16[2,320,384]{2,1,0:T(8,128)(2,1)S(1)} %get-tuple-element.21.mid, bf16[3,3,3,384,384]{4,3,2,1,0:T(8,128)(2,1)} %w_hbm.1), custom_call_target="tpu_custom_call" | custom-call | flops 1698693120 | bytes 1048576 | tf_op jit(solution)/shard_map/next_own/pallas_call | solution.py:330
  46.5 0.0 collective-permute-done.6.pair_got
  46.5 2.8 %collective-permute-done.7.mid_got = bf16[2,160,384]{2,1,0:T(8,128)(2,1)S(1)} collective-permute-done((bf16[2,160,384]{2,1,0:T(8,128)(2,1)S(1)}, bf16[2,160,384]{2,1,0:T(8,128)(2,1)S(1)}, u32[]{:S(2)}, u32[]{:S(2)}) %collective-permute-start.7) | collective-permute-done | bytes 245792 | tf_op jit(solution)/shard_map/ppermute | solution.py:326
  49.3 2.0 %next_edge.1 = bf16[2,320,384]{2,1,0:T(8,128)(2,1)S(1)} custom-call(s32[1]{0:T(128)} %bitcast.tile_ref, s32[1]{0:T(128)} %bitcast.5.span_ref, s32[4]{0:T(128)S(1)} %copy-done, bf16[2,160,384]{2,1,0:T(8,128)(2,1)S(1)} %collective-permute-done.6.pair_got, bf16[2,160,384]{2,1,0:T(8,128)(2,1)S(1)} %collective-permute-done.7.mid_got, ...), custom_call_target="tpu_custom_call" | custom-call | flops 849346560 | bytes 1048576 | tf_op jit(solution)/shard_map/next_edge/pallas_call | solution.py:339
  51.4 3.8 %collective-permute-start.8 = (bf16[2,320,384]{2,1,0:T(8,128)(2,1)S(1)}, bf16[2,320,384]{2,1,0:T(8,128)(2,1)S(1)}, u32[]{:S(2)}, u32[]{:S(2)}) collective-permute-start(bf16[2,320,384]{2,1,0:T(8,128)(2,1)S(1)} %next_edge.1), channel_id=1, source_target_pairs={{0,1},{1,2},{2,3},{4,5},{5,6},{6,7},{8,9},{9,10},{10,11},{12,13},{... | collective-permute-start | bytes 1474568 | tf_op jit(solution)/shard_map/ppermute | solution.py:346
  55.2 3.9 %own.1 = f32[2,320,384]{2,1,0:T(8,128)S(1)} custom-call(s32[1]{0:T(128)} %bitcast.tile_ref, s32[1]{0:T(128)} %bitcast.5.span_ref, s32[4]{0:T(128)S(1)} %copy-done, bf16[2,320,384]{2,1,0:T(8,128)(2,1)S(1)} %get-tuple-element.21.mid, bf16[2,160,384]{2,1,0:T(8,128)(2,1)S(1)} %collective-permute-done.6.pair_got, ...), custom_call_target="tpu_custom_call" | custom-call | flops 2548039680 | bytes 1048576 | tf_op jit(solution)/shard_map/own/pallas_call | solution.py:347
  59.1 1.7 %collective-permute-done.8 = bf16[2,320,384]{2,1,0:T(8,128)(2,1)S(1)} collective-permute-done((bf16[2,320,384]{2,1,0:T(8,128)(2,1)S(1)}, bf16[2,320,384]{2,1,0:T(8,128)(2,1)S(1)}, u32[]{:S(2)}, u32[]{:S(2)}) %collective-permute-start.8) | collective-permute-done | bytes 491552 | tf_op jit(solution)/shard_map/ppermute | solution.py:346
  60.8 0.9 %add_convert_fusion = bf16[2,320,384]{2,1,0:T(8,128)(2,1)} fusion(f32[2,320,384]{2,1,0:T(8,128)S(1)} %own.1, bf16[2,320,384]{2,1,0:T(8,128)(2,1)S(1)} %collective-permute-done.8), kind=kLoop, calls=%fused_computation | loop fusion | flops 737280 | bytes 1966080 | tf_op jit(solution)/shard_map/convert_element_type | solution.py:350
Async XLA Ops:
  1.8 13.1 %collective-permute-start.2 = (bf16[320,384]{1,0:T(8,128)(2,1)S(1)}, bf16[320,384]{1,0:T(8,128)(2,1)S(1)}, u32[]{:S(2)}, u32[]{:S(2)}) collective-permute-start(bf16[320,384]{1,0:T(8,128)(2,1)S(1)} %get-tuple-element.26), channel_id=1, source_target_pairs={{0,0},{1,8},{2,2},{3,10},{4,4},{5,12},{6,6},{7,14},{8,1},{9,9},{10... | collective-permute-start | bytes 737288 | tf_op jit(solution)/shard_map/ppermute | solution.py:280
  6.6 11.0 %collective-permute-start = (bf16[320,384]{1,0:T(8,128)(2,1)S(1)}, bf16[320,384]{1,0:T(8,128)(2,1)S(1)}, u32[]{:S(2)}, u32[]{:S(2)}) collective-permute-start(bf16[320,384]{1,0:T(8,128)(2,1)S(1)} %get-tuple-element.27), channel_id=1, source_target_pairs={{0,4},{1,12},{2,6},{3,14},{4,0},{5,8},{6,2},{7,10},{8,5},{9,13},{1... | collective-permute-start | bytes 737288 | tf_op jit(solution)/shard_map/ppermute | solution.py:281
  7.9 30.5 %copy-start.1 = (f32[384]{0:T(512)S(1)}, f32[384]{0:T(512)}, u32[]{:S(2)}) copy-start(f32[384]{0:T(512)} %gain.7) | copy-start | bytes 4612
  14.9 26.8 %copy-start = (s32[4]{0:T(128)S(1)}, s32[4]{0:T(128)}, u32[]{:S(2)}) copy-start(s32[4]{0:T(128)} %clips.5) | copy-start | bytes 52
  14.9 2.6 %collective-permute-start.3 = (bf16[320,384]{1,0:T(8,128)(2,1)S(1)}, bf16[320,384]{1,0:T(8,128)(2,1)S(1)}, u32[]{:S(2)}, u32[]{:S(2)}) collective-permute-start(bf16[320,384]{1,0:T(8,128)(2,1)S(1)} %collective-permute-done.2.own.own_a), channel_id=1, source_target_pairs={{0,1},{1,0},{2,3},{3,2},{4,5},{5,4},{6,7},{7,6},{8,9},{9,8},{10,11... | collective-permute-start | bytes 737288 | tf_op jit(solution)/shard_map/ppermute | solution.py:291
  17.6 1.5 %collective-permute-start.1 = (bf16[320,384]{1,0:T(8,128)(2,1)S(1)}, bf16[320,384]{1,0:T(8,128)(2,1)S(1)}, u32[]{:S(2)}, u32[]{:S(2)}) collective-permute-start(bf16[320,384]{1,0:T(8,128)(2,1)S(1)} %collective-permute-done.own_b), channel_id=1, source_target_pairs={{0,1},{1,0},{2,3},{3,2},{4,5},{5,4},{6,7},{7,6},{8,9},{9,8},{10,11... | collective-permute-start | bytes 737288 | tf_op jit(solution)/shard_map/ppermute | solution.py:292
  17.6 0.7 %copy-start.2 = (f32[384]{0:T(512)S(1)}, f32[384]{0:T(512)}, u32[]{:S(2)}) copy-start(f32[384]{0:T(512)} %gain.6) | copy-start | bytes 4612
  22.2 8.8 %collective-permute-start.4 = (bf16[320,384]{1,0:T(8,128)(2,1)S(1)}, bf16[320,384]{1,0:T(8,128)(2,1)S(1)}, u32[]{:S(2)}, u32[]{:S(2)}) collective-permute-start(bf16[320,384]{1,0:T(8,128)(2,1)S(1)} %get-tuple-element.18), channel_id=1, source_target_pairs={{0,0},{1,8},{2,2},{3,10},{4,4},{5,12},{6,6},{7,14},{8,1},{9,9},{10... | collective-permute-start | bytes 737288 | tf_op jit(solution)/shard_map/ppermute | solution.py:305
  28.9 9.4 %collective-permute-start.5 = (bf16[320,384]{1,0:T(8,128)(2,1)S(1)}, bf16[320,384]{1,0:T(8,128)(2,1)S(1)}, u32[]{:S(2)}, u32[]{:S(2)}) collective-permute-start(bf16[320,384]{1,0:T(8,128)(2,1)S(1)} %attend_rest.1), channel_id=1, source_target_pairs={{0,4},{1,12},{2,6},{3,14},{4,0},{5,8},{6,2},{7,10},{8,5},{9,13},{1... | collective-permute-start | bytes 737288 | tf_op jit(solution)/shard_map/ppermute | solution.py:313
  39.8 6.7 %collective-permute-start.6 = (bf16[2,160,384]{2,1,0:T(8,128)(2,1)S(1)}, bf16[2,160,384]{2,1,0:T(8,128)(2,1)S(1)}, u32[]{:S(2)}, u32[]{:S(2)}) collective-permute-start(bf16[2,160,384]{2,1,0:T(8,128)(2,1)S(1)} %get-tuple-element.22), channel_id=1, source_target_pairs={{0,4},{4,0},{8,12},{12,8},{1,5},{5,1},{9,13},{13,9},{2,6},{6,2},{1... | collective-permute-start | bytes 737288 | tf_op jit(solution)/shard_map/ppermute | solution.py:325
  39.8 9.6 %collective-permute-start.7 = (bf16[2,160,384]{2,1,0:T(8,128)(2,1)S(1)}, bf16[2,160,384]{2,1,0:T(8,128)(2,1)S(1)}, u32[]{:S(2)}, u32[]{:S(2)}) collective-permute-start(bf16[2,160,384]{2,1,0:T(8,128)(2,1)S(1)} %get-tuple-element.23), channel_id=1, source_target_pairs={{4,8},{8,4},{5,9},{9,5},{6,10},{10,6},{7,11},{11,7},{20,24},{24,20... | collective-permute-start | bytes 737288 | tf_op jit(solution)/shard_map/ppermute | solution.py:326
  51.4 9.4 %collective-permute-start.8 = (bf16[2,320,384]{2,1,0:T(8,128)(2,1)S(1)}, bf16[2,320,384]{2,1,0:T(8,128)(2,1)S(1)}, u32[]{:S(2)}, u32[]{:S(2)}) collective-permute-start(bf16[2,320,384]{2,1,0:T(8,128)(2,1)S(1)} %next_edge.1), channel_id=1, source_target_pairs={{0,1},{1,2},{2,3},{4,5},{5,6},{6,7},{8,9},{9,10},{10,11},{12,13},{... | collective-permute-start | bytes 1474568 | tf_op jit(solution)/shard_map/ppermute | solution.py:346

commit v4 on v1

--- a/solution.py
+++ b/solution.py
@@ -36,8 +36,9 @@
     return jax.ShapeDtypeStruct(shape, dtype)
 
 
-def call(kernel, name, out_shape, in_specs, scratch=(), limit=24):
+def call(kernel, name, out_shape, in_specs, scratch=(), limit=16, flops=0, size=1 << 20):
     outs = jax.tree.map(lambda _: VMEM, out_shape)
+    cost = pl.CostEstimate(flops=int(flops), transcendentals=0, bytes_accessed=int(size))
     return pl.pallas_call(
         kernel,
         out_shape=out_shape,
@@ -45,6 +46,7 @@
         out_specs=outs,
         scratch_shapes=list(scratch),
         compiler_params=pltpu.CompilerParams(vmem_limit_bytes=limit << 20),
+        cost_estimate=cost,
         name=name,
     )
 
@@ -68,20 +70,14 @@
     ]
 
 
-def pack_kernel(w_hbm, w_out, sem):
-    ch = w_hbm.shape[-1]
+def load_small_kernel(w_qkv, w_out, gain, qkv_vm, out_vm, gain_vm, sem):
     copies = [
-        pltpu.make_async_copy(
-            w_hbm.at[i, j, k],
-            w_out.at[i, j * ch : (j + 1) * ch, k * ch : (k + 1) * ch],
-            sem.at[i, j, k],
-        )
-        for i in range(3)
-        for j in range(3)
-        for k in range(3)
+        pltpu.make_async_copy(w_qkv, qkv_vm, sem.at[0]),
+        pltpu.make_async_copy(w_out, out_vm, sem.at[1]),
     ]
     for copy in copies:
         copy.start()
+    gain_vm[...] = gain[...]
     for copy in copies:
         copy.wait()
 
@@ -92,10 +88,10 @@
     out[place * cells : (place + 1) * cells, :] = dot32(normed, w_qkv[:, ch:]).astype(bf16)
 
 
-def keys_kernel(own, other, gain, w_qkv, kv_out):
-    gain_vec = gain[...].reshape(1, own.shape[1])
-    project_keys(own, gain_vec, w_qkv, kv_out, 0)
-    project_keys(other, gain_vec, w_qkv, kv_out, 1)
+def keys_kernel(own_a, other_a, own_b, gain, w_qkv, kv_out):
+    gain_vec = gain[...].reshape(1, own_a.shape[1])
+    for place, block in enumerate((own_a, other_a, own_b)):
+        project_keys(block, gain_vec, w_qkv, kv_out, place)
 
 
 def attend_rows(cols, source, kv_parts, gain_vec, w_qkv, w_out, att_out):
@@ -122,10 +118,9 @@
         att_out[part, :] = (feats.astype(f32) + dot32(mixture, w_out[...])).astype(bf16)
 
 
-def attend_kernel(cols, own_b, other_b, own_a, kv_a, gain, w_qkv, w_out, kv_b, att_a):
+def attend_kernel(cols, other_b, own_a, kv_a, gain, w_qkv, w_out, kv_b, att_a):
     gain_vec = gain[...].reshape(1, own_a.shape[1])
-    project_keys(own_b, gain_vec, w_qkv, kv_b, 0)
-    project_keys(other_b, gain_vec, w_qkv, kv_b, 1)
+    project_keys(other_b, gain_vec, w_qkv, kv_b, 0)
     attend_rows(cols, own_a, (kv_a, kv_b), gain_vec, w_qkv, w_out, att_a)
 
 
@@ -134,21 +129,31 @@
     attend_rows(cols, own_b, (kv_a, kv_b), gain_vec, w_qkv, w_out, att_b)
 
 
-def activate_kernel(cols, tile_ref, got_a, got_b, gain, attended, active, top_edge, low_edge):
+def activate(cols, low, block, gain, act_out, pair_edge, mid_edge):
+    lifted = rms_scale(block[...], gain[...].reshape(1, block.shape[1]))
+    act = (lifted / (1.0 + jnp.exp(-lifted))).astype(bf16)
+    act_out[...] = act
+
+    @pl.when(low == 0)
+    def _():
+        pair_edge[...] = act[cols:, :]
+        mid_edge[...] = act[:cols, :]
+
+    @pl.when(low == 1)
+    def _():
+        pair_edge[...] = act[:cols, :]
+        mid_edge[...] = act[cols:, :]
+
+
+def activate_a_kernel(cols, tile_ref, got_a, gain, *outs):
+    activate(cols, tile_ref[0] % 2, got_a, gain, *outs)
+
+
+def activate_b_kernel(cols, tile_ref, got_a, got_b, gain, attended, *outs):
     low = tile_ref[0] % 2
-    gain_vec = gain[...].reshape(1, got_a.shape[1])
-
-    def one(block, frame):
-        values = block[...]
-        attended[frame] = values
-        lifted = rms_scale(values, gain_vec)
-        act = (lifted / (1.0 + jnp.exp(-lifted))).astype(bf16)
-        active[frame] = act
-        top_edge[frame] = act[:cols, :]
-        low_edge[frame] = act[cols:, :]
-
-    one(got_a, low)
-    one(got_b, 1 - low)
+    activate(cols, low, got_b, gain, *outs)
+    attended[low] = got_a[...]
+    attended[1 - low] = got_b[...]
 
 
 def usable_flag(clips, frame_at, tap):
@@ -167,30 +172,118 @@
     return part[:, ch : 2 * ch] + left + right
 
 
-def conv_kernel(cols, work, first, span_ref, clips, mid, top, low, w, *refs):
-    if first:
-        out, acc = refs
-    else:
-        partial, out, acc = refs
-    ch = mid.shape[-1]
-    acc[...] = jnp.zeros_like(acc)
-    for tap, frame, which in work:
-
-        @pl.when(usable_flag(clips, span_ref[0] * 2 + frame, tap))
-        def _(tap=tap, frame=frame, which=which):
-            rows = [top[which], mid[which, :cols, :], mid[which, cols:, :], low[which]]
-            lhs = jnp.concatenate(
-                [jnp.concatenate(rows[r : r + 3], axis=1) for r in range(2)], axis=0
-            )
-            acc[frame] += dot32(lhs, w[tap])
-
-    for frame in range(2):
-        for r in range(2):
-            part = slice(r * cols, (r + 1) * cols)
-            val = shift_add(acc[frame, part, :], cols, ch)
-            if not first:
-                val = val + partial[frame, part, :]
-            out[frame, part, :] = val.astype(out.dtype)
+def weigh(flag, block):
+    return (block.astype(f32) * flag).astype(bf16)
+
+
+def flag_at(clips, frame_at, tap):
+    return usable_flag(clips, frame_at, tap).astype(f32)
+
+
+def add_next(cols, frame, at_next, clips, block, part, w, taps, partial, out):
+    ch = out.shape[-1]
+
+    def put(n, value):
+        value = shift_add(value, cols, ch)
+        if partial is not None:
+            value = value + partial[n, part, :]
+        out[n, part, :] = value.astype(out.dtype)
+
+    put(0, dot32(weigh(flag_at(clips, at_next, frame), block), w[frame, taps]))
+
+    @pl.when(frame == 1)
+    def _():
+        put(1, dot32(weigh(flag_at(clips, at_next + 1, 0), block), w[0, taps]))
+
+    @pl.when(frame == 0)
+    def _():
+        if partial is None:
+            out[1, part, :] = jnp.zeros((cols, ch), out.dtype)
+        else:
+            out[1, part, :] = partial[1, part, :].astype(out.dtype)
+
+
+def add_own_rows(cols, frame, at_next, clips, act, w, partial, out):
+    ch = act.shape[-1]
+    block = jnp.concatenate([act[:cols, :], act[cols:, :]], axis=1)
+    for part, taps in (
+        (slice(0, cols), slice(ch, 3 * ch)),
+        (slice(cols, 2 * cols), slice(0, 2 * ch)),
+    ):
+        add_next(cols, frame, at_next, clips, block, part, w, taps, partial, out)
+
+
+def next_a_kernel(cols, tile_ref, span_ref, clips, act, w_hbm, out, w, sem):
+    ch = act.shape[-1]
+    copies = [
+        pltpu.make_async_copy(
+            w_hbm.at[i, j, k],
+            w.at[i, j * ch : (j + 1) * ch, k * ch : (k + 1) * ch],
+            sem.at[9 * i + 3 * j + k],
+        )
+        for i in range(3)
+        for j in range(3)
+        for k in range(3)
+    ]
+    for copy in copies:
+        copy.start()
+    for copy in copies[:18]:
+        copy.wait()
+    low, at_next = tile_ref[0] % 2, (span_ref[0] + 1) * 2
+    add_own_rows(cols, low, at_next, clips, act, w, None, out)
+    for copy in copies[18:]:
+        copy.wait()
+
+
+def next_b_kernel(cols, tile_ref, span_ref, clips, act, w, partial, out):
+    low, at_next = tile_ref[0] % 2, (span_ref[0] + 1) * 2
+    add_own_rows(cols, 1 - low, at_next, clips, act, w, partial, out)
+
+
+def edge_kernel(cols, second, tile_ref, span_ref, clips, pair_got, mid_got, w, partial, out):
+    ch = w.shape[-1] // 3
+    low, at_next = tile_ref[0] % 2, (span_ref[0] + 1) * 2
+    frame = low if second else 1 - low
+    pick = low.astype(f32)
+    pair, mid = pair_got[...].astype(f32), mid_got[...].astype(f32)
+    above = pair * pick + mid * (1.0 - pick)
+    below = mid * pick + pair * (1.0 - pick)
+    for block, part, taps in (
+        (above, slice(0, cols), slice(0, ch)),
+        (below, slice(cols, 2 * cols), slice(2 * ch, 3 * ch)),
+    ):
+        add_next(cols, frame, at_next, clips, block, part, w, taps, partial, out)
+
+
+def own_kernel(
+    cols, tile_ref, span_ref, clips, act_a, act_b, pair_a, mid_a, pair_b, mid_b, w, out, rows
+):
+    ch = act_a.shape[-1]
+    low = tile_ref[0] % 2
+    for frame, act, pair, mid in ((low, act_a, pair_b, mid_b), (1 - low, act_b, pair_a, mid_a)):
+        rows[frame, cols : 3 * cols, :] = act[...]
+
+        @pl.when(low == 0)
+        def _(frame=frame, pair=pair, mid=mid):
+            rows[frame, :cols, :] = mid[...]
+            rows[frame, 3 * cols :, :] = pair[...]
+
+        @pl.when(low == 1)
+        def _(frame=frame, pair=pair, mid=mid):
+            rows[frame, :cols, :] = pair[...]
+            rows[frame, 3 * cols :, :] = mid[...]
+
+    wide = [
+        jnp.concatenate([rows[f, j * cols : (j + 2) * cols, :] for j in range(3)], axis=1)
+        for f in range(2)
+    ]
+    here = dot32(jnp.concatenate(wide, axis=0), w[2])
+    back = dot32(weigh(flag_at(clips, span_ref[0] * 2 + 1, 1), wide[0]), w[1])
+    for r in range(2):
+        part = slice(r * cols, (r + 1) * cols)
+        out[0, part, :] = shift_add(here[part], cols, ch)
+        after = here[(2 + r) * cols : (3 + r) * cols]
+        out[1, part, :] = shift_add(after + back[part], cols, ch)
 
 
 def on_device(features, clip_lengths, norm_gain, w_qkv, w_out, conv_gain, w_conv):
@@ -210,61 +303,93 @@
     send_b = lax.dynamic_index_in_dim(x, 1 - low, 0, keepdims=False)
     own_a = lax.ppermute(send_a, both, route_a)
     own_b = lax.ppermute(send_b, both, route_b)
-    w_packed = call(
-        pack_kernel,
-        "pack_weights",
-        struct((3, 3 * ch, 3 * ch)),
-        [ANY],
-        [pltpu.SemaphoreType.DMA((3, 3, 3))],
-        16,
-    )(w_conv)
+    w_qkv, w_out, norm_gain = call(
+        load_small_kernel,
+        "load_small",
+        (pltpu.VMEM(w_qkv.shape, bf16), pltpu.VMEM(w_out.shape, bf16), struct((ch,), f32)),
+        [ANY, ANY, VMEM],
+        [pltpu.SemaphoreType.DMA((2,))],
+        60,
+    )(w_qkv, w_out, norm_gain)
+    own_a, w_qkv = lax.optimization_barrier((own_a, w_qkv))
     other_a = lax.ppermute(own_a, "span", other_core)
     other_b = lax.ppermute(own_b, "span", other_core)
-    kv_a = call(keys_kernel, "keys", struct((2 * cells, 2 * ch)), [VMEM] * 4)(
-        own_a, other_a, norm_gain, w_qkv
+    kv_flops = 2 * 2 * cells * ch * 2 * ch
+    row_flops = 2 * cells * ch * (2 * ch + 8 * cells)
+    kv_a = call(keys_kernel, "keys", struct((3 * cells, 2 * ch)), [VMEM] * 5, flops=kv_flops)(
+        own_a, other_a, own_b, norm_gain, w_qkv
     )
     kv_b, att_a = call(
         functools.partial(attend_kernel, cols),
         "attend",
-        (struct((2 * cells, 2 * ch)), struct((cells, ch))),
-        [VMEM] * 7,
-    )(own_b, other_b, own_a, kv_a, norm_gain, w_qkv, w_out)
+        (struct((cells, 2 * ch)), struct((cells, ch))),
+        [VMEM] * 6,
+        flops=kv_flops + row_flops,
+    )(other_b, own_a, kv_a, norm_gain, w_qkv, w_out)
     got_a = lax.ppermute(att_a, both, route_a)
     att_b = call(
-        functools.partial(attend_rest_kernel, cols), "attend_rest", struct((cells, ch)), [VMEM] * 6
+        functools.partial(attend_rest_kernel, cols),
+        "attend_rest",
+        struct((cells, ch)),
+        [VMEM] * 6,
+        flops=3 * row_flops,
     )(own_b, kv_a, kv_b, norm_gain, w_qkv, w_out)
     got_b = lax.ppermute(att_b, both, route_b)
-    attended, active, top_edge, low_edge = call(
-        functools.partial(activate_kernel, cols),
-        "activate",
-        (
-            struct((frames, cells, ch)),
-            struct((frames, cells, ch)),
-            struct((frames, cols, ch)),
-            struct((frames, cols, ch)),
-        ),
+    pairs, middle = [(0, 1), (1, 0), (2, 3), (3, 2)], [(1, 2), (2, 1)]
+    one, edge = struct((cells, ch)), struct((cols, ch))
+    sums = struct((frames, cells, ch), f32)
+    unit = 2 * cells * 9 * ch * ch
+    where = (tile, span, clip_lengths)
+    act_a, pair_edge, mid_edge = call(
+        functools.partial(activate_a_kernel, cols), "activate_a", (one, edge, edge), [SMEM, VMEM, VMEM]
+    )(tile, got_a, conv_gain)
+    pair_a = lax.ppermute(pair_edge, "tile", pairs)
+    mid_a = lax.ppermute(mid_edge, "tile", middle)
+    next_a, w_packed = call(
+        functools.partial(next_a_kernel, cols),
+        "next_a",
+        (sums, struct((3, 3 * ch, 3 * ch))),
+        [SMEM] * 3 + [VMEM, ANY],
+        [pltpu.SemaphoreType.DMA((27,))],
+        42,
+        flops=unit,
+    )(*where, act_a, w_conv)
+    got_b, next_a = lax.optimization_barrier((got_b, next_a))
+    attended, act_b, pair_edge, mid_edge = call(
+        functools.partial(activate_b_kernel, cols),
+        "activate_b",
+        (struct((frames, cells, ch)), one, edge, edge),
         [SMEM] + [VMEM] * 3,
     )(tile, got_a, got_b, conv_gain)
-    above = lax.ppermute(low_edge, both, shifted_route(tiles, spans, 1, 0))
-    below = lax.ppermute(top_edge, both, shifted_route(tiles, spans, -1, 0))
-    before = lax.ppermute(active, both, shifted_route(tiles, spans, 0, 1))
-    before_above = lax.ppermute(low_edge, both, shifted_route(tiles, spans, 1, 1))
-    before_below = lax.ppermute(top_edge, both, shifted_route(tiles, spans, -1, 1))
-    acc = pltpu.VMEM((frames, cells, 3 * ch), f32)
-    partial = call(
-        functools.partial(conv_kernel, cols, [(2, 0, 0), (2, 1, 1), (1, 1, 0)], True),
-        "conv_own",
-        struct((frames, cells, ch), f32),
-        [SMEM, SMEM] + [VMEM] * 4,
-        [acc],
-    )(span, clip_lengths, active, above, below, w_packed)
-    hidden = call(
-        functools.partial(conv_kernel, cols, [(0, 0, 0), (1, 0, 1), (0, 1, 1)], False),
-        "conv_before",
+    pair_b = lax.ppermute(pair_edge, "tile", pairs)
+    mid_b = lax.ppermute(mid_edge, "tile", middle)
+    next_b = call(
+        functools.partial(next_b_kernel, cols), "next_b", sums, [SMEM] * 3 + [VMEM] * 3, flops=unit
+    )(*where, act_b, w_packed, next_a)
+    edges_a = call(
+        functools.partial(edge_kernel, cols, False),
+        "edges_a",
+        sums,
+        [SMEM] * 3 + [VMEM] * 4,
+        flops=unit // 2,
+    )(*where, pair_a, mid_a, w_packed, next_b)
+    for_next = call(
+        functools.partial(edge_kernel, cols, True),
+        "edges_b",
         struct((frames, cells, ch)),
-        [SMEM, SMEM] + [VMEM] * 5,
-        [acc],
-    )(span, clip_lengths, before, before_above, before_below, w_packed, partial)
+        [SMEM] * 3 + [VMEM] * 4,
+        flops=unit // 2,
+    )(*where, pair_b, mid_b, w_packed, edges_a)
+    earlier = lax.ppermute(for_next, both, shifted_route(tiles, spans, 0, 1))
+    own = call(
+        functools.partial(own_kernel, cols),
+        "own",
+        sums,
+        [SMEM] * 3 + [VMEM] * 7,
+        [pltpu.VMEM((frames, 4 * cols, ch), bf16)],
+        flops=3 * unit,
+    )(*where, act_a, act_b, pair_a, mid_a, pair_b, mid_b, w_packed)
+    hidden = (own + earlier.astype(f32)).astype(bf16)
     shape = (frames, row_count, cols, ch)
     return attended.reshape(shape), hidden.reshape(shape)
 

time: 71 us -> 64.2 us (0.904); the launches traced: 71 us -> 63.2 us
  waiting for transfers between devices: 20.1 us -> 12.5 us
  local copies, waits for them, and re-layouts: 8.83 us -> 1.81 us
  Pallas kernels: 18 us -> 24.7 us
  starting transfers between devices: 23.3 us -> 22.3 us
  other arithmetic: 0 us -> 0.9 us
    unnamed x16 -> x6, local copies, waits for them, and re-layouts: 7.71 us -> 0.69 us
    pallas_call x6 -> x10, Pallas kernels: 15.4 us -> 22.1 us  [the longest x1 5.29 us: on_device(): call(functools.partial(next_a_kernel, cols), 'next_a', (sums, struct((3,...]
    ppermute x1, waiting for transfers between devices: 6.49 us -> 0.01 us  [on_device(): got_b = lax.ppermute(att_b, both, route_b)]
    ppermute x1, waiting for transfers between devices: 8.28 us -> 5.79 us  [on_device(): own_a = lax.ppermute(send_a, both, route_a)]
    ppermute x5, waiting for transfers between devices: 0.01 us -> 2.37 us  [the longest x1 1.77 us: on_device(): earlier = lax.ppermute(for_next, both, shifted_route(tiles, spans, 0, 1))]
    ppermute x1, starting transfers between devices: 1.91 us -> 4.16 us  [on_device(): got_a = lax.ppermute(att_a, both, route_a)]
    ppermute x1, starting transfers between devices: 2.54 us -> 0.34 us  [on_device(): got_b = lax.ppermute(att_b, both, route_b)]
    ppermute x5, starting transfers between devices: 14 us -> 13 us  [the longest x1 5.35 us: on_device(): earlier = lax.ppermute(for_next, both, shifted_route(tiles, spans, 0, 1))]
  transfers between devices with their start and end apart: 11 -> 11, of which waited for: 4 -> 5; matrix products, arithmetic and copies ran while one was open for 0% -> 0% of each run, Pallas kernels for 9% -> 31%
where the time goes in v4:
time: 64.2 us; the launch traced here: 63.2 us
  Pallas kernels  24.7 us (38%)
  starting transfers between devices  22.3 us (35%)
  waiting for transfers between devices  12.5 us (19%)
  local copies, waits for them, and re-layouts  1.81 us (3%)
  other arithmetic  0.9 us (1%)
  between operations  0.83 us (1%)
    ppermute x1, waiting for transfers between devices, on_device(): own_a = lax.ppermute(send_a, both, route_a)  5.79 us
    ppermute x1, starting transfers between devices, on_device(): earlier = lax.ppermute(for_next, both, shifted_route(tiles, spans, 0, 1))  5.35 us
    pallas_call x1, Pallas kernels, on_device(): call(functools.partial(next_a_kernel, cols), 'next_a', (sums, struct((3,...  5.29 us
    ppermute x1, starting transfers between devices, on_device(): own_a = lax.ppermute(send_a, both, route_a)  4.78 us
    ppermute x1, starting transfers between devices, on_device(): got_a = lax.ppermute(att_a, both, route_a)  4.16 us
    pallas_call x1, Pallas kernels, on_device(): call(functools.partial(own_kernel, cols), 'own', sums, [SMEM] * 3 + [VMEM...  3.97 us
    ppermute x1, starting transfers between devices, on_device(): pair_a = lax.ppermute(pair_edge, 'tile', pairs)  3.38 us
    pallas_call x1, Pallas kernels, on_device(): call(functools.partial(attend_kernel, cols), 'attend', (struct((cells, 2...  2.82 us
  transfers between devices with their start and end apart: 11, of which 5 were waited for; matrix products, arithmetic and copies ran while one was open for 0% of the time, Pallas kernels for 31%

profile of v4, /device:TPU:13, one launch (start us, length us, event | category | flops | bytes accessed | tf_op | source)
XLA Modules:
  0.0 63.2 jit_solution(4288066632666657232)
XLA Ops:
  0.7 1.1 %dynamic-slice_bitcast_fusion = (bf16[320,384]{1,0:T(8,128)(2,1)S(1)}, bf16[320,384]{1,0:T(8,128)(2,1)S(1)}) fusion(bf16[2,320,384]{2,1,0:T(8,128)(2,1)} %bitcast.9, s32[]{:T(128)S(6)} %select_n.16, s32[]{:T(128)S(6)} %select_n.15), kind=kLoop, calls=%fused_computation.1 | loop fusion | bytes 983048 | tf_op jit(solution)/shard_map/jit(dynamic_index_in_dim)/squeeze | solution.py:302
  1.8 4.8 %collective-permute-start.2 = (bf16[320,384]{1,0:T(8,128)(2,1)S(1)}, bf16[320,384]{1,0:T(8,128)(2,1)S(1)}, u32[]{:S(2)}, u32[]{:S(2)}) collective-permute-start(bf16[320,384]{1,0:T(8,128)(2,1)S(1)} %get-tuple-element.38), channel_id=1, source_target_pairs={{0,0},{1,8},{2,2},{3,10},{4,4},{5,12},{6,6},{7,14},{8,1},{9,9},{10... | collective-permute-start | bytes 737288 | tf_op jit(solution)/shard_map/ppermute | solution.py:304
  6.6 0.1 collective-permute-start
  6.6 2.5 %load_small.1 = (bf16[384,1152]{1,0:T(8,128)(2,1)S(1)}, bf16[384,384]{1,0:T(8,128)(2,1)S(1)}, f32[384]{0:T(512)}) custom-call(bf16[384,1152]{1,0:T(8,128)(2,1)} %w_qkv.1, bf16[384,384]{1,0:T(8,128)(2,1)} %w_out.1, f32[384]{0:T(512)} %gain.3), custom_call_target="tpu_custom_call" | custom-call | bytes 1048576 | tf_op jit(solution)/shard_map/load_small/pallas_call | solution.py:306
  9.1 5.8 %collective-permute-done.2.own_a = bf16[320,384]{1,0:T(8,128)(2,1)S(1)} collective-permute-done((bf16[320,384]{1,0:T(8,128)(2,1)S(1)}, bf16[320,384]{1,0:T(8,128)(2,1)S(1)}, u32[]{:S(2)}, u32[]{:S(2)}) %collective-permute-start.2) | collective-permute-done | bytes 245792 | tf_op jit(solution)/shard_map/ppermute | solution.py:304
  14.9 0.0 collective-permute-start.3
  14.9 2.6 %collective-permute-done.own_b = bf16[320,384]{1,0:T(8,128)(2,1)S(1)} collective-permute-done((bf16[320,384]{1,0:T(8,128)(2,1)S(1)}, bf16[320,384]{1,0:T(8,128)(2,1)S(1)}, u32[]{:S(2)}, u32[]{:S(2)}) %collective-permute-start) | collective-permute-done | bytes 245792 | tf_op jit(solution)/shard_map/ppermute | solution.py:305
  17.6 0.0 collective-permute-start.1
  17.6 0.0 collective-permute-done.3.other_a
  17.6 0.0 copy-start.2
  17.6 0.7 %copy-done.2 = f32[384]{0:T(512)S(1)} copy-done((f32[384]{0:T(512)S(1)}, f32[384]{0:T(512)}, u32[]{:S(2)}) %copy-start.2) | copy-done | bytes 1560
  18.2 0.0 copy-start.1
  18.2 0.0 copy-start
  18.2 1.0 %keys.1.kv_a = bf16[960,768]{1,0:T(8,128)(2,1)S(1)} custom-call(bf16[320,384]{1,0:T(8,128)(2,1)S(1)} %collective-permute-done.2.own_a, bf16[320,384]{1,0:T(8,128)(2,1)S(1)} %collective-permute-done.3.other_a, bf16[320,384]{1,0:T(8,128)(2,1)S(1)} %collective-permute-done.own_b, f32[384]{0:T(512)S(1)} %copy-done.2, bf16[384,1152]{1,0:T(8,128)(2,1)S(1)} %get-tuple-element.23.w_qkv), custom_call_target="tpu_custom_call" | custom-call | flops 377487360 | bytes 1048576 | tf_op jit(solution)/shard_map/keys/pallas_call | solution.py:319
  19.3 0.0 collective-permute-done.1.other_b
  19.3 2.8 %attend.1 = (bf16[320,768]{1,0:T(8,128)(2,1)S(1)}, bf16[320,384]{1,0:T(8,128)(2,1)S(1)}) custom-call(bf16[320,384]{1,0:T(8,128)(2,1)S(1)} %collective-permute-done.1.other_b, bf16[320,384]{1,0:T(8,128)(2,1)S(1)} %collective-permute-done.2.own_a, bf16[960,768]{1,0:T(8,128)(2,1)S(1)} %keys.1.kv_a, f32[384]{0:T(512)S(1)} %copy-done.2, ...), custom_call_target="tpu_custom_call" | custom-call | flops 1195376640 | bytes 1048576 | tf_op jit(solution)/shard_map/attend/pallas_call | solution.py:322
  22.1 4.2 %collective-permute-start.4 = (bf16[320,384]{1,0:T(8,128)(2,1)S(1)}, bf16[320,384]{1,0:T(8,128)(2,1)S(1)}, u32[]{:S(2)}, u32[]{:S(2)}) collective-permute-start(bf16[320,384]{1,0:T(8,128)(2,1)S(1)} %get-tuple-element.25), channel_id=1, source_target_pairs={{0,0},{1,8},{2,2},{3,10},{4,4},{5,12},{6,6},{7,14},{8,1},{9,9},{10... | collective-permute-start | bytes 737288 | tf_op jit(solution)/shard_map/ppermute | solution.py:329
  26.3 2.6 %attend_rest.1 = bf16[320,384]{1,0:T(8,128)(2,1)S(1)} custom-call(bf16[320,384]{1,0:T(8,128)(2,1)S(1)} %collective-permute-done.own_b, bf16[960,768]{1,0:T(8,128)(2,1)S(1)} %keys.1.kv_a, bf16[320,768]{1,0:T(8,128)(2,1)S(1)} %get-tuple-element.26.kv_b, f32[384]{0:T(512)S(1)} %copy-done.2, bf16[384,1152]{1,0:T(8,128)(2,1)S(1)} %get-tuple-element.23.w_qkv, ...), custom_call_target="tpu_custom_call" | custom-call | flops 2453667840 | bytes 1048576 | tf_op jit(solution)/shard_map/attend_rest/pallas_call | solution.py:330
  28.9 0.3 collective-permute-start.5
  29.2 1.8 %collective-permute-done.4.got_a = bf16[320,384]{1,0:T(8,128)(2,1)S(1)} collective-permute-done((bf16[320,384]{1,0:T(8,128)(2,1)S(1)}, bf16[320,384]{1,0:T(8,128)(2,1)S(1)}, u32[]{:S(2)}, u32[]{:S(2)}) %collective-permute-start.4) | collective-permute-done | bytes 245792 | tf_op jit(solution)/shard_map/ppermute | solution.py:329
  31.0 0.0 copy-done.1
  31.0 0.3 activate_a.1
  31.3 3.4 %collective-permute-start.6 = (bf16[160,384]{1,0:T(8,128)(2,1)S(1)}, bf16[160,384]{1,0:T(8,128)(2,1)S(1)}, u32[]{:S(2)}, u32[]{:S(2)}) collective-permute-start(bf16[160,384]{1,0:T(8,128)(2,1)S(1)} %get-tuple-element.32), channel_id=1, source_target_pairs={{0,4},{4,0},{8,12},{12,8},{1,5},{5,1},{9,13},{13,9},{2,6},{6,2},{1... | collective-permute-start | bytes 368648 | tf_op jit(solution)/shard_map/ppermute | solution.py:346
  34.6 1.9 %collective-permute-start.7 = (bf16[160,384]{1,0:T(8,128)(2,1)S(1)}, bf16[160,384]{1,0:T(8,128)(2,1)S(1)}, u32[]{:S(2)}, u32[]{:S(2)}) collective-permute-start(bf16[160,384]{1,0:T(8,128)(2,1)S(1)} %get-tuple-element.33), channel_id=1, source_target_pairs={{4,8},{8,4},{5,9},{9,5},{6,10},{10,6},{7,11},{11,7},{20,24},{24,20... | collective-permute-start | bytes 368648 | tf_op jit(solution)/shard_map/ppermute | solution.py:347
  36.6 0.0 copy-done
  36.6 5.3 %next_a.1 = (f32[2,320,384]{2,1,0:T(8,128)S(1)}, bf16[3,1152,1152]{2,1,0:T(8,128)(2,1)S(1)}) custom-call(s32[1]{0:T(128)} %bitcast.tile_ref, s32[1]{0:T(128)} %bitcast.4.span_ref, s32[4]{0:T(128)S(1)} %copy-done, bf16[320,384]{1,0:T(8,128)(2,1)S(1)} %get-tuple-element.27.act.act_a, bf16[3,3,3,384,384]{4,3,2,1,0:T(8,128)(2,1)} %w_hbm.1), custom_call_target="tpu_custom_call" | custom-call | flops 849346560 | bytes 1048576 | tf_op jit(solution)/shard_map/next_a/pallas_call | solution.py:348
  41.9 0.0 collective-permute-done.5.got_b
  41.9 1.1 %activate_b.1 = (bf16[2,320,384]{2,1,0:T(8,128)(2,1)}, bf16[320,384]{1,0:T(8,128)(2,1)S(1)}, bf16[160,384]{1,0:T(8,128)(2,1)S(1)}, bf16[160,384]{1,0:T(8,128)(2,1)S(1)}) custom-call(s32[1]{0:T(128)} %bitcast.tile_ref, bf16[320,384]{1,0:T(8,128)(2,1)S(1)} %collective-permute-done.4.got_a, bf16[320,384]{1,0:T(8,128)(2,1)S(1)} %collective-permute-done.5.got_b, ...), custom_call_target="tpu_custom_call" | custom-call | bytes 1048576 | tf_op jit(solution)/shard_map/activate_b/pallas_call | solution.py:358
  43.0 0.0 collective-permute-start.8
  43.0 2.3 %collective-permute-start.9 = (bf16[160,384]{1,0:T(8,128)(2,1)S(1)}, bf16[160,384]{1,0:T(8,128)(2,1)S(1)}, u32[]{:S(2)}, u32[]{:S(2)}) collective-permute-start(bf16[160,384]{1,0:T(8,128)(2,1)S(1)} %get-tuple-element.35), channel_id=1, source_target_pairs={{4,8},{8,4},{5,9},{9,5},{6,10},{10,6},{7,11},{11,7},{20,24},{24,20... | collective-permute-start | bytes 368648 | tf_op jit(solution)/shard_map/ppermute | solution.py:365
  45.4 1.6 %next_b.1.partial = f32[2,320,384]{2,1,0:T(8,128)S(1)} custom-call(s32[1]{0:T(128)} %bitcast.tile_ref, s32[1]{0:T(128)} %bitcast.4.span_ref, s32[4]{0:T(128)S(1)} %copy-done, bf16[320,384]{1,0:T(8,128)(2,1)S(1)} %get-tuple-element.31.act_b.act, bf16[3,1152,1152]{2,1,0:T(8,128)(2,1)S(1)} %get-tuple-element.36.w, f32[2,320,384]{2,1,0:T(8,128)S(1)} %get-tuple-element.37.partial), custom_call_target="tpu_custom_call" | custom-call | flops 849346560 | bytes 1048576 | tf_op jit(solution)/shard_map/next_b/pallas_call | solution.py:366
  47.0 0.0 collective-permute-done.6.pair_a.pair_got
  47.0 0.0 collective-permute-done.7.mid_a.mid_got
  47.0 1.3 %edges_a.1.partial = f32[2,320,384]{2,1,0:T(8,128)S(1)} custom-call(s32[1]{0:T(128)} %bitcast.tile_ref, s32[1]{0:T(128)} %bitcast.4.span_ref, s32[4]{0:T(128)S(1)} %copy-done, bf16[160,384]{1,0:T(8,128)(2,1)S(1)} %collective-permute-done.6.pair_a.pair_got, bf16[160,384]{1,0:T(8,128)(2,1)S(1)} %collective-permute-done.7.mid_a.mid_got, ...), custom_call_target="tpu_custom_call" | custom-call | flops 424673280 | bytes 1048576 | tf_op jit(solution)/shard_map/edges_a/pallas_call | solution.py:369
  48.3 0.0 collective-permute-done.8.pair_b.pair_got
  48.3 0.6 collective-permute-done.9.mid_b.mid_got
  48.9 2.2 %edges_b.1 = bf16[2,320,384]{2,1,0:T(8,128)(2,1)S(1)} custom-call(s32[1]{0:T(128)} %bitcast.tile_ref, s32[1]{0:T(128)} %bitcast.4.span_ref, s32[4]{0:T(128)S(1)} %copy-done, bf16[160,384]{1,0:T(8,128)(2,1)S(1)} %collective-permute-done.8.pair_b.pair_got, bf16[160,384]{1,0:T(8,128)(2,1)S(1)} %collective-permute-done.9.mid_b.mid_got, ...), custom_call_target="tpu_custom_call" | custom-call | flops 424673280 | bytes 1048576 | tf_op jit(solution)/shard_map/edges_b/pallas_call | solution.py:376
  51.1 5.4 %collective-permute-start.10 = (bf16[2,320,384]{2,1,0:T(8,128)(2,1)S(1)}, bf16[2,320,384]{2,1,0:T(8,128)(2,1)S(1)}, u32[]{:S(2)}, u32[]{:S(2)}) collective-permute-start(bf16[2,320,384]{2,1,0:T(8,128)(2,1)S(1)} %edges_b.1), channel_id=1, source_target_pairs={{0,1},{1,2},{2,3},{4,5},{5,6},{6,7},{8,9},{9,10},{10,11},{12,13},{... | collective-permute-start | bytes 1474568 | tf_op jit(solution)/shard_map/ppermute | solution.py:383
  56.5 4.0 %own.1 = f32[2,320,384]{2,1,0:T(8,128)S(1)} custom-call(s32[1]{0:T(128)} %bitcast.tile_ref, s32[1]{0:T(128)} %bitcast.4.span_ref, s32[4]{0:T(128)S(1)} %copy-done, bf16[320,384]{1,0:T(8,128)(2,1)S(1)} %get-tuple-element.27.act.act_a, bf16[320,384]{1,0:T(8,128)(2,1)S(1)} %get-tuple-element.31.act_b.act, ...), custom_call_target="tpu_custom_call" | custom-call | flops 2548039680 | bytes 1048576 | tf_op jit(solution)/shard_map/own/pallas_call | solution.py:384
  60.5 1.8 %collective-permute-done.10 = bf16[2,320,384]{2,1,0:T(8,128)(2,1)S(1)} collective-permute-done((bf16[2,320,384]{2,1,0:T(8,128)(2,1)S(1)}, bf16[2,320,384]{2,1,0:T(8,128)(2,1)S(1)}, u32[]{:S(2)}, u32[]{:S(2)}) %collective-permute-start.10) | collective-permute-done | bytes 491552 | tf_op jit(solution)/shard_map/ppermute | solution.py:383
  62.3 0.9 %add_convert_fusion = bf16[2,320,384]{2,1,0:T(8,128)(2,1)} fusion(f32[2,320,384]{2,1,0:T(8,128)S(1)} %own.1, bf16[2,320,384]{2,1,0:T(8,128)(2,1)S(1)} %collective-permute-done.10), kind=kLoop, calls=%fused_computation | loop fusion | flops 737280 | bytes 1966080 | tf_op jit(solution)/shard_map/convert_element_type | solution.py:392
Async XLA Ops:
  1.8 13.1 %collective-permute-start.2 = (bf16[320,384]{1,0:T(8,128)(2,1)S(1)}, bf16[320,384]{1,0:T(8,128)(2,1)S(1)}, u32[]{:S(2)}, u32[]{:S(2)}) collective-permute-start(bf16[320,384]{1,0:T(8,128)(2,1)S(1)} %get-tuple-element.38), channel_id=1, source_target_pairs={{0,0},{1,8},{2,2},{3,10},{4,4},{5,12},{6,6},{7,14},{8,1},{9,9},{10... | collective-permute-start | bytes 737288 | tf_op jit(solution)/shard_map/ppermute | solution.py:304
  6.6 11.0 %collective-permute-start = (bf16[320,384]{1,0:T(8,128)(2,1)S(1)}, bf16[320,384]{1,0:T(8,128)(2,1)S(1)}, u32[]{:S(2)}, u32[]{:S(2)}) collective-permute-start(bf16[320,384]{1,0:T(8,128)(2,1)S(1)} %get-tuple-element.39), channel_id=1, source_target_pairs={{0,4},{1,12},{2,6},{3,14},{4,0},{5,8},{6,2},{7,10},{8,5},{9,13},{1... | collective-permute-start | bytes 737288 | tf_op jit(solution)/shard_map/ppermute | solution.py:305
  14.9 2.6 %collective-permute-start.3 = (bf16[320,384]{1,0:T(8,128)(2,1)S(1)}, bf16[320,384]{1,0:T(8,128)(2,1)S(1)}, u32[]{:S(2)}, u32[]{:S(2)}) collective-permute-start(bf16[320,384]{1,0:T(8,128)(2,1)S(1)} %collective-permute-done.2.own_a), channel_id=1, source_target_pairs={{0,1},{1,0},{2,3},{3,2},{4,5},{5,4},{6,7},{7,6},{8,9},{9,8},{10,11... | collective-permute-start | bytes 737288 | tf_op jit(solution)/shard_map/ppermute | solution.py:315
  17.6 1.7 %collective-permute-start.1 = (bf16[320,384]{1,0:T(8,128)(2,1)S(1)}, bf16[320,384]{1,0:T(8,128)(2,1)S(1)}, u32[]{:S(2)}, u32[]{:S(2)}) collective-permute-start(bf16[320,384]{1,0:T(8,128)(2,1)S(1)} %collective-permute-done.own_b), channel_id=1, source_target_pairs={{0,1},{1,0},{2,3},{3,2},{4,5},{5,4},{6,7},{7,6},{8,9},{9,8},{10,11... | collective-permute-start | bytes 737288 | tf_op jit(solution)/shard_map/ppermute | solution.py:316
  17.6 0.7 %copy-start.2 = (f32[384]{0:T(512)S(1)}, f32[384]{0:T(512)}, u32[]{:S(2)}) copy-start(f32[384]{0:T(512)} %get-tuple-element.22.gain) | copy-start | bytes 4612
  18.2 12.7 %copy-start.1 = (f32[384]{0:T(512)S(1)}, f32[384]{0:T(512)}, u32[]{:S(2)}) copy-start(f32[384]{0:T(512)} %gain.5) | copy-start | bytes 4612
  18.2 18.3 %copy-start = (s32[4]{0:T(128)S(1)}, s32[4]{0:T(128)}, u32[]{:S(2)}) copy-start(s32[4]{0:T(128)} %clips.9) | copy-start | bytes 52
  22.1 8.9 %collective-permute-start.4 = (bf16[320,384]{1,0:T(8,128)(2,1)S(1)}, bf16[320,384]{1,0:T(8,128)(2,1)S(1)}, u32[]{:S(2)}, u32[]{:S(2)}) collective-permute-start(bf16[320,384]{1,0:T(8,128)(2,1)S(1)} %get-tuple-element.25), channel_id=1, source_target_pairs={{0,0},{1,8},{2,2},{3,10},{4,4},{5,12},{6,6},{7,14},{8,1},{9,9},{10... | collective-permute-start | bytes 737288 | tf_op jit(solution)/shard_map/ppermute | solution.py:329
  28.9 13.0 %collective-permute-start.5 = (bf16[320,384]{1,0:T(8,128)(2,1)S(1)}, bf16[320,384]{1,0:T(8,128)(2,1)S(1)}, u32[]{:S(2)}, u32[]{:S(2)}) collective-permute-start(bf16[320,384]{1,0:T(8,128)(2,1)S(1)} %attend_rest.1), channel_id=1, source_target_pairs={{0,4},{1,12},{2,6},{3,14},{4,0},{5,8},{6,2},{7,10},{8,5},{9,13},{1... | collective-permute-start | bytes 737288 | tf_op jit(solution)/shard_map/ppermute | solution.py:337
  31.3 15.7 %collective-permute-start.6 = (bf16[160,384]{1,0:T(8,128)(2,1)S(1)}, bf16[160,384]{1,0:T(8,128)(2,1)S(1)}, u32[]{:S(2)}, u32[]{:S(2)}) collective-permute-start(bf16[160,384]{1,0:T(8,128)(2,1)S(1)} %get-tuple-element.32), channel_id=1, source_target_pairs={{0,4},{4,0},{8,12},{12,8},{1,5},{5,1},{9,13},{13,9},{2,6},{6,2},{1... | collective-permute-start | bytes 368648 | tf_op jit(solution)/shard_map/ppermute | solution.py:346
  34.6 12.3 %collective-permute-start.7 = (bf16[160,384]{1,0:T(8,128)(2,1)S(1)}, bf16[160,384]{1,0:T(8,128)(2,1)S(1)}, u32[]{:S(2)}, u32[]{:S(2)}) collective-permute-start(bf16[160,384]{1,0:T(8,128)(2,1)S(1)} %get-tuple-element.33), channel_id=1, source_target_pairs={{4,8},{8,4},{5,9},{9,5},{6,10},{10,6},{7,11},{11,7},{20,24},{24,20... | collective-permute-start | bytes 368648 | tf_op jit(solution)/shard_map/ppermute | solution.py:347
  43.0 5.3 %collective-permute-start.8 = (bf16[160,384]{1,0:T(8,128)(2,1)S(1)}, bf16[160,384]{1,0:T(8,128)(2,1)S(1)}, u32[]{:S(2)}, u32[]{:S(2)}) collective-permute-start(bf16[160,384]{1,0:T(8,128)(2,1)S(1)} %get-tuple-element.34), channel_id=1, source_target_pairs={{0,4},{4,0},{8,12},{12,8},{1,5},{5,1},{9,13},{13,9},{2,6},{6,2},{1... | collective-permute-start | bytes 368648 | tf_op jit(solution)/shard_map/ppermute | solution.py:364
  43.0 5.9 %collective-permute-start.9 = (bf16[160,384]{1,0:T(8,128)(2,1)S(1)}, bf16[160,384]{1,0:T(8,128)(2,1)S(1)}, u32[]{:S(2)}, u32[]{:S(2)}) collective-permute-start(bf16[160,384]{1,0:T(8,128)(2,1)S(1)} %get-tuple-element.35), channel_id=1, source_target_pairs={{4,8},{8,4},{5,9},{9,5},{6,10},{10,6},{7,11},{11,7},{20,24},{24,20... | collective-permute-start | bytes 368648 | tf_op jit(solution)/shard_map/ppermute | solution.py:365
  51.1 11.1 %collective-permute-start.10 = (bf16[2,320,384]{2,1,0:T(8,128)(2,1)S(1)}, bf16[2,320,384]{2,1,0:T(8,128)(2,1)S(1)}, u32[]{:S(2)}, u32[]{:S(2)}) collective-permute-start(bf16[2,320,384]{2,1,0:T(8,128)(2,1)S(1)} %edges_b.1), channel_id=1, source_target_pairs={{0,1},{1,2},{2,3},{4,5},{5,6},{6,7},{8,9},{9,10},{10,11},{12,13},{... | collective-permute-start | bytes 1474568 | tf_op jit(solution)/shard_map/ppermute | solution.py:383

commit v5 on v4

--- a/solution.py
+++ b/solution.py
@@ -129,96 +129,12 @@
     attend_rows(cols, own_b, (kv_a, kv_b), gain_vec, w_qkv, w_out, att_b)
 
 
-def activate(cols, low, block, gain, act_out, pair_edge, mid_edge):
-    lifted = rms_scale(block[...], gain[...].reshape(1, block.shape[1]))
-    act = (lifted / (1.0 + jnp.exp(-lifted))).astype(bf16)
-    act_out[...] = act
-
-    @pl.when(low == 0)
-    def _():
-        pair_edge[...] = act[cols:, :]
-        mid_edge[...] = act[:cols, :]
-
-    @pl.when(low == 1)
-    def _():
-        pair_edge[...] = act[:cols, :]
-        mid_edge[...] = act[cols:, :]
-
-
-def activate_a_kernel(cols, tile_ref, got_a, gain, *outs):
-    activate(cols, tile_ref[0] % 2, got_a, gain, *outs)
-
-
-def activate_b_kernel(cols, tile_ref, got_a, got_b, gain, attended, *outs):
-    low = tile_ref[0] % 2
-    activate(cols, low, got_b, gain, *outs)
-    attended[low] = got_a[...]
-    attended[1 - low] = got_b[...]
-
-
-def usable_flag(clips, frame_at, tap):
-    end = jnp.int32(0)
-    start = jnp.int32(0)
-    for i in range(clips.shape[0]):
-        end = end + clips[i]
-        start = start + jnp.where(end <= frame_at, clips[i], 0)
-    return frame_at - (2 - tap) >= start
-
-
-def shift_add(part, cols, ch):
-    at = lax.broadcasted_iota(jnp.int32, (cols, ch), 0)
-    left = jnp.where(at == 0, 0.0, pltpu.roll(part[:, :ch], 1, 0))
-    right = jnp.where(at == cols - 1, 0.0, pltpu.roll(part[:, 2 * ch :], cols - 1, 0))
-    return part[:, ch : 2 * ch] + left + right
-
-
-def weigh(flag, block):
-    return (block.astype(f32) * flag).astype(bf16)
-
-
-def flag_at(clips, frame_at, tap):
-    return usable_flag(clips, frame_at, tap).astype(f32)
-
-
-def add_next(cols, frame, at_next, clips, block, part, w, taps, partial, out):
-    ch = out.shape[-1]
-
-    def put(n, value):
-        value = shift_add(value, cols, ch)
-        if partial is not None:
-            value = value + partial[n, part, :]
-        out[n, part, :] = value.astype(out.dtype)
-
-    put(0, dot32(weigh(flag_at(clips, at_next, frame), block), w[frame, taps]))
-
-    @pl.when(frame == 1)
-    def _():
-        put(1, dot32(weigh(flag_at(clips, at_next + 1, 0), block), w[0, taps]))
-
-    @pl.when(frame == 0)
-    def _():
-        if partial is None:
-            out[1, part, :] = jnp.zeros((cols, ch), out.dtype)
-        else:
-            out[1, part, :] = partial[1, part, :].astype(out.dtype)
-
-
-def add_own_rows(cols, frame, at_next, clips, act, w, partial, out):
-    ch = act.shape[-1]
-    block = jnp.concatenate([act[:cols, :], act[cols:, :]], axis=1)
-    for part, taps in (
-        (slice(0, cols), slice(ch, 3 * ch)),
-        (slice(cols, 2 * cols), slice(0, 2 * ch)),
-    ):
-        add_next(cols, frame, at_next, clips, block, part, w, taps, partial, out)
-
-
-def next_a_kernel(cols, tile_ref, span_ref, clips, act, w_hbm, out, w, sem):
-    ch = act.shape[-1]
+def load_kernel(_, w_hbm, w_vm, sem):
+    ch = w_hbm.shape[-1]
     copies = [
         pltpu.make_async_copy(
             w_hbm.at[i, j, k],
-            w.at[i, j * ch : (j + 1) * ch, k * ch : (k + 1) * ch],
+            w_vm.at[i, j * ch : (j + 1) * ch, k * ch : (k + 1) * ch],
             sem.at[9 * i + 3 * j + k],
         )
         for i in range(3)
@@ -227,58 +143,120 @@
     ]
     for copy in copies:
         copy.start()
-    for copy in copies[:18]:
+    for copy in copies:
         copy.wait()
-    low, at_next = tile_ref[0] % 2, (span_ref[0] + 1) * 2
-    add_own_rows(cols, low, at_next, clips, act, w, None, out)
-    for copy in copies[18:]:
-        copy.wait()
-
-
-def next_b_kernel(cols, tile_ref, span_ref, clips, act, w, partial, out):
-    low, at_next = tile_ref[0] % 2, (span_ref[0] + 1) * 2
-    add_own_rows(cols, 1 - low, at_next, clips, act, w, partial, out)
-
-
-def edge_kernel(cols, second, tile_ref, span_ref, clips, pair_got, mid_got, w, partial, out):
+
+
+def activate(cols, low, block, gain, act_out, pair_edge, mid_edge):
+    lifted = rms_scale(block[...], gain[...].reshape(1, block.shape[1]))
+    act = (lifted / (1.0 + jnp.exp(-lifted))).astype(bf16)
+    act_out[...] = act
+
+    @pl.when(low == 0)
+    def _():
+        pair_edge[...] = act[cols:, :]
+        mid_edge[...] = act[:cols, :]
+
+    @pl.when(low == 1)
+    def _():
+        pair_edge[...] = act[:cols, :]
+        mid_edge[...] = act[cols:, :]
+
+
+def activate_a_kernel(cols, tile_ref, got_a, gain, *outs):
+    activate(cols, tile_ref[0] % 2, got_a, gain, *outs)
+
+
+def activate_b_kernel(
+    cols, tile_ref, got_a, got_b, act_a, gain, _, attended, active, pair_edge, mid_edge
+):
+    low = tile_ref[0] % 2
+    activate(cols, low, got_b, gain, active.at[1 - low], pair_edge, mid_edge)
+    active[low] = act_a[...]
+    attended[low] = got_a[...]
+    attended[1 - low] = got_b[...]
+
+
+def usable_flag(clips, frame_at, tap):
+    end = jnp.int32(0)
+    start = jnp.int32(0)
+    for i in range(clips.shape[0]):
+        end = end + clips[i]
+        start = start + jnp.where(end <= frame_at, clips[i], 0)
+    return frame_at - (2 - tap) >= start
+
+
+def shift_add(part, cols, ch):
+    at = lax.broadcasted_iota(jnp.int32, (cols, ch), 0)
+    left = jnp.where(at == 0, 0.0, pltpu.roll(part[:, :ch], 1, 0))
+    right = jnp.where(at == cols - 1, 0.0, pltpu.roll(part[:, 2 * ch :], cols - 1, 0))
+    return part[:, ch : 2 * ch] + left + right
+
+
+def weigh(flag, block):
+    return (block.astype(f32) * flag).astype(bf16)
+
+
+def flags_of(clips, frame_at):
+    return [
+        [usable_flag(clips, frame_at + f, tap).astype(f32) for tap in range(3)] for f in range(2)
+    ]
+
+
+def edge_rows(tile_ref, pair_a, mid_a, pair_b, mid_b):
+    odd = (tile_ref[0] % 2).astype(f32)
+
+    def pick(if_odd, if_even):
+        return if_odd[...].astype(f32) * odd + if_even[...].astype(f32) * (1.0 - odd)
+
+    above = [pick(pair_a, mid_b), pick(pair_b, mid_a)]
+    below = [pick(mid_a, pair_b), pick(mid_b, pair_a)]
+    return above, below
+
+
+def next_own_kernel(cols, span_ref, clips, mid, w, out):
+    ch = mid.shape[-1]
+    flag = flags_of(clips, (span_ref[0] + 1) * 2)
+    first_row, second_row = slice(0, cols), slice(cols, 2 * cols)
+    pair = [
+        jnp.concatenate([mid[f, first_row, :], mid[f, second_row, :]], axis=1) for f in range(2)
+    ]
+    last = jnp.concatenate([weigh(flag[0][0], pair[0]), weigh(flag[1][0], pair[1])], axis=0)
+    middle = weigh(flag[0][1], pair[1])
+    for part, taps in ((first_row, slice(ch, 3 * ch)), (second_row, slice(0, 2 * ch))):
+        far = dot32(last, w[0, taps])
+        out[0, part, :] = shift_add(far[:cols] + dot32(middle, w[1, taps]), cols, ch)
+        out[1, part, :] = shift_add(far[cols:], cols, ch)
+
+
+def next_edge_kernel(
+    cols, tile_ref, span_ref, clips, pair_a, mid_a, pair_b, mid_b, w, partial, out
+):
     ch = w.shape[-1] // 3
-    low, at_next = tile_ref[0] % 2, (span_ref[0] + 1) * 2
-    frame = low if second else 1 - low
-    pick = low.astype(f32)
-    pair, mid = pair_got[...].astype(f32), mid_got[...].astype(f32)
-    above = pair * pick + mid * (1.0 - pick)
-    below = mid * pick + pair * (1.0 - pick)
-    for block, part, taps in (
+    flag = flags_of(clips, (span_ref[0] + 1) * 2)
+    above, below = edge_rows(tile_ref, pair_a, mid_a, pair_b, mid_b)
+    for edge, part, taps in (
         (above, slice(0, cols), slice(0, ch)),
         (below, slice(cols, 2 * cols), slice(2 * ch, 3 * ch)),
     ):
-        add_next(cols, frame, at_next, clips, block, part, w, taps, partial, out)
-
-
-def own_kernel(
-    cols, tile_ref, span_ref, clips, act_a, act_b, pair_a, mid_a, pair_b, mid_b, w, out, rows
-):
-    ch = act_a.shape[-1]
-    low = tile_ref[0] % 2
-    for frame, act, pair, mid in ((low, act_a, pair_b, mid_b), (1 - low, act_b, pair_a, mid_a)):
-        rows[frame, cols : 3 * cols, :] = act[...]
-
-        @pl.when(low == 0)
-        def _(frame=frame, pair=pair, mid=mid):
-            rows[frame, :cols, :] = mid[...]
-            rows[frame, 3 * cols :, :] = pair[...]
-
-        @pl.when(low == 1)
-        def _(frame=frame, pair=pair, mid=mid):
-            rows[frame, :cols, :] = pair[...]
-            rows[frame, 3 * cols :, :] = mid[...]
-
-    wide = [
-        jnp.concatenate([rows[f, j * cols : (j + 2) * cols, :] for j in range(3)], axis=1)
-        for f in range(2)
-    ]
+        last = jnp.concatenate([edge[0] * flag[0][0], edge[1] * flag[1][0]], axis=0).astype(bf16)
+        middle = (edge[1] * flag[0][1]).astype(bf16)
+        far = dot32(last, w[0, taps])
+        near = far[:cols] + dot32(middle, w[1, taps])
+        for f, val in ((0, near), (1, far[cols:])):
+            out[f, part, :] = (shift_add(val, cols, ch) + partial[f, part, :]).astype(bf16)
+
+
+def own_kernel(cols, tile_ref, span_ref, clips, mid, pair_a, mid_a, pair_b, mid_b, w, out):
+    ch = mid.shape[-1]
+    above, below = edge_rows(tile_ref, pair_a, mid_a, pair_b, mid_b)
+    wide = []
+    for f in range(2):
+        rows = [above[f].astype(bf16), mid[f, :cols, :], mid[f, cols:, :], below[f].astype(bf16)]
+        wide += [jnp.concatenate(rows[r : r + 3], axis=1) for r in range(2)]
     here = dot32(jnp.concatenate(wide, axis=0), w[2])
-    back = dot32(weigh(flag_at(clips, span_ref[0] * 2 + 1, 1), wide[0]), w[1])
+    flag = usable_flag(clips, span_ref[0] * 2 + 1, 1).astype(f32)
+    back = dot32(weigh(flag, jnp.concatenate(wide[:2], axis=0)), w[1])
     for r in range(2):
         part = slice(r * cols, (r + 1) * cols)
         out[0, part, :] = shift_add(here[part], cols, ch)
@@ -306,7 +284,7 @@
     w_qkv, w_out, norm_gain = call(
         load_small_kernel,
         "load_small",
-        (pltpu.VMEM(w_qkv.shape, bf16), pltpu.VMEM(w_out.shape, bf16), struct((ch,), f32)),
+        (pltpu.VMEM(w_qkv.shape, bf16), pltpu.VMEM(w_out.shape, bf16), pltpu.VMEM((ch,), f32)),
         [ANY, ANY, VMEM],
         [pltpu.SemaphoreType.DMA((2,))],
         60,
@@ -345,50 +323,42 @@
     )(tile, got_a, conv_gain)
     pair_a = lax.ppermute(pair_edge, "tile", pairs)
     mid_a = lax.ppermute(mid_edge, "tile", middle)
-    next_a, w_packed = call(
-        functools.partial(next_a_kernel, cols),
-        "next_a",
-        (sums, struct((3, 3 * ch, 3 * ch))),
-        [SMEM] * 3 + [VMEM, ANY],
+    w_packed = call(
+        load_kernel,
+        "load_conv",
+        struct((3, 3 * ch, 3 * ch)),
+        [ANY, ANY],
         [pltpu.SemaphoreType.DMA((27,))],
         42,
-        flops=unit,
-    )(*where, act_a, w_conv)
-    got_b, next_a = lax.optimization_barrier((got_b, next_a))
-    attended, act_b, pair_edge, mid_edge = call(
+        size=1 << 12,
+    )(act_a, w_conv)
+    attended, active, pair_edge, mid_edge = call(
         functools.partial(activate_b_kernel, cols),
         "activate_b",
-        (struct((frames, cells, ch)), one, edge, edge),
-        [SMEM] + [VMEM] * 3,
-    )(tile, got_a, got_b, conv_gain)
+        (struct((frames, cells, ch)), struct((frames, cells, ch)), edge, edge),
+        [SMEM] + [VMEM] * 4 + [ANY],
+    )(tile, got_a, got_b, act_a, conv_gain, w_packed)
     pair_b = lax.ppermute(pair_edge, "tile", pairs)
     mid_b = lax.ppermute(mid_edge, "tile", middle)
-    next_b = call(
-        functools.partial(next_b_kernel, cols), "next_b", sums, [SMEM] * 3 + [VMEM] * 3, flops=unit
-    )(*where, act_b, w_packed, next_a)
-    edges_a = call(
-        functools.partial(edge_kernel, cols, False),
-        "edges_a",
+    edges = (pair_a, mid_a, pair_b, mid_b)
+    started = call(
+        functools.partial(next_own_kernel, cols),
+        "next_own",
         sums,
-        [SMEM] * 3 + [VMEM] * 4,
-        flops=unit // 2,
-    )(*where, pair_a, mid_a, w_packed, next_b)
+        [SMEM] * 2 + [VMEM] * 2,
+        flops=2 * unit,
+    )(span, clip_lengths, active, w_packed)
     for_next = call(
-        functools.partial(edge_kernel, cols, True),
-        "edges_b",
+        functools.partial(next_edge_kernel, cols),
+        "next_edge",
         struct((frames, cells, ch)),
-        [SMEM] * 3 + [VMEM] * 4,
-        flops=unit // 2,
-    )(*where, pair_b, mid_b, w_packed, edges_a)
+        [SMEM] * 3 + [VMEM] * 6,
+        flops=unit,
+    )(*where, *edges, w_packed, started)
     earlier = lax.ppermute(for_next, both, shifted_route(tiles, spans, 0, 1))
     own = call(
-        functools.partial(own_kernel, cols),
-        "own",
-        sums,
-        [SMEM] * 3 + [VMEM] * 7,
-        [pltpu.VMEM((frames, 4 * cols, ch), bf16)],
-        flops=3 * unit,
-    )(*where, act_a, act_b, pair_a, mid_a, pair_b, mid_b, w_packed)
+        functools.partial(own_kernel, cols), "own", sums, [SMEM] * 3 + [VMEM] * 6, flops=3 * unit
+    )(*where, active, *edges, w_packed)
     hidden = (own + earlier.astype(f32)).astype(bf16)
     shape = (frames, row_count, cols, ch)
     return attended.reshape(shape), hidden.reshape(shape)

time: 64.2 us -> 62.2 us (0.969)
  Pallas kernels: 24.7 us -> 21.7 us
  starting transfers between devices: 22.3 us -> 23.3 us
  waiting for transfers between devices: 12.5 us -> 13.3 us
  local copies, waits for them, and re-layouts: 1.81 us -> 1.13 us
    pallas_call x4 -> x3, Pallas kernels: 10.4 us -> 8.1 us  [the longest x1 3.48 us: on_device(): call(load_kernel, 'load_conv', struct((3, 3 * ch, 3 * ch)), [ANY, ANY], [...]
    ppermute x1, starting transfers between devices: 2.35 us -> 3.33 us  [on_device(): mid_b = lax.ppermute(mid_edge, 'tile', middle)]
    unnamed x6 -> x4, local copies, waits for them, and re-layouts: 0.69 us -> 0.01 us
  transfers between devices with their start and end apart: 11 -> 11, of which waited for: 5 -> 5; matrix products, arithmetic and copies ran while one was open for 0% -> 0% of each run, Pallas kernels for 31% -> 28%
where the time goes in v5:
time: 62.2 us; the launch traced here: 61.2 us
  starting transfers between devices  23.3 us (37%)
  Pallas kernels  21.7 us (35%)
  waiting for transfers between devices  13.3 us (21%)
  local copies, waits for them, and re-layouts  1.13 us (2%)
  other arithmetic  0.88 us (1%)
  between operations  0.83 us (1%)
    ppermute x1, waiting for transfers between devices, on_device(): own_a = lax.ppermute(send_a, both, route_a)  6.35 us
    ppermute x1, starting transfers between devices, on_device(): earlier = lax.ppermute(for_next, both, shifted_route(tiles, spans, 0, 1))  5.68 us
    ppermute x1, starting transfers between devices, on_device(): own_a = lax.ppermute(send_a, both, route_a)  4.78 us
    pallas_call x1, Pallas kernels, on_device(): call(functools.partial(own_kernel, cols), 'own', sums, [SMEM] * 3 + [VMEM...  3.84 us
    ppermute x1, starting transfers between devices, on_device(): got_a = lax.ppermute(att_a, both, route_a)  3.67 us
    pallas_call x1, Pallas kernels, on_device(): call(load_kernel, 'load_conv', struct((3, 3 * ch, 3 * ch)), [ANY, ANY], [...  3.48 us
    ppermute x1, starting transfers between devices, on_device(): mid_b = lax.ppermute(mid_edge, 'tile', middle)  3.33 us
    ppermute x1, starting transfers between devices, on_device(): pair_a = lax.ppermute(pair_edge, 'tile', pairs)  3.09 us
  transfers between devices with their start and end apart: 11, of which 5 were waited for; matrix products, arithmetic and copies ran while one was open for 0% of the time, Pallas kernels for 28%

profile of v5, /device:TPU:13, one launch (start us, length us, event | category | flops | bytes accessed | tf_op | source)
XLA Modules:
  0.0 61.2 jit_solution(7141016112600501482)
XLA Ops:
  0.7 1.1 %dynamic-slice_bitcast_fusion = (bf16[320,384]{1,0:T(8,128)(2,1)S(1)}, bf16[320,384]{1,0:T(8,128)(2,1)S(1)}) fusion(bf16[2,320,384]{2,1,0:T(8,128)(2,1)} %bitcast.9, s32[]{:T(128)S(6)} %select_n.16, s32[]{:T(128)S(6)} %select_n.15), kind=kLoop, calls=%fused_computation.1 | loop fusion | bytes 983048 | tf_op jit(solution)/shard_map/jit(dynamic_index_in_dim)/squeeze | solution.py:280
  1.8 4.8 %collective-permute-start.2 = (bf16[320,384]{1,0:T(8,128)(2,1)S(1)}, bf16[320,384]{1,0:T(8,128)(2,1)S(1)}, u32[]{:S(2)}, u32[]{:S(2)}) collective-permute-start(bf16[320,384]{1,0:T(8,128)(2,1)S(1)} %get-tuple-element.30), channel_id=1, source_target_pairs={{0,0},{1,8},{2,2},{3,10},{4,4},{5,12},{6,6},{7,14},{8,1},{9,9},{10... | collective-permute-start | bytes 737288 | tf_op jit(solution)/shard_map/ppermute | solution.py:282
  6.6 0.1 collective-permute-start
  6.6 1.9 %load_small.1 = (bf16[384,1152]{1,0:T(8,128)(2,1)S(1)}, bf16[384,384]{1,0:T(8,128)(2,1)S(1)}, f32[384]{0:T(512)S(1)}) custom-call(bf16[384,1152]{1,0:T(8,128)(2,1)} %w_qkv.1, bf16[384,384]{1,0:T(8,128)(2,1)} %w_out.1, f32[384]{0:T(512)} %gain.3), custom_call_target="tpu_custom_call" | custom-call | bytes 1048576 | tf_op jit(solution)/shard_map/load_small/pallas_call | solution.py:284
  8.6 6.3 %collective-permute-done.2.own_a = bf16[320,384]{1,0:T(8,128)(2,1)S(1)} collective-permute-done((bf16[320,384]{1,0:T(8,128)(2,1)S(1)}, bf16[320,384]{1,0:T(8,128)(2,1)S(1)}, u32[]{:S(2)}, u32[]{:S(2)}) %collective-permute-start.2) | collective-permute-done | bytes 245792 | tf_op jit(solution)/shard_map/ppermute | solution.py:282
  14.9 0.0 collective-permute-start.3
  14.9 2.6 %collective-permute-done.own_b = bf16[320,384]{1,0:T(8,128)(2,1)S(1)} collective-permute-done((bf16[320,384]{1,0:T(8,128)(2,1)S(1)}, bf16[320,384]{1,0:T(8,128)(2,1)S(1)}, u32[]{:S(2)}, u32[]{:S(2)}) %collective-permute-start) | collective-permute-done | bytes 245792 | tf_op jit(solution)/shard_map/ppermute | solution.py:283
  17.6 0.0 collective-permute-start.1
  17.6 0.0 collective-permute-done.3.other_a
  17.6 0.0 copy-start
  17.6 1.0 %keys.1.kv_a = bf16[960,768]{1,0:T(8,128)(2,1)S(1)} custom-call(bf16[320,384]{1,0:T(8,128)(2,1)S(1)} %collective-permute-done.2.own_a, bf16[320,384]{1,0:T(8,128)(2,1)S(1)} %collective-permute-done.3.other_a, bf16[320,384]{1,0:T(8,128)(2,1)S(1)} %collective-permute-done.own_b, f32[384]{0:T(512)S(1)} %get-tuple-element.18.gain, ...), custom_call_target="tpu_custom_call" | custom-call | flops 377487360 | bytes 1048576 | tf_op jit(solution)/shard_map/keys/pallas_call | solution.py:297
  18.6 0.5 collective-permute-done.1.other_b
  19.1 2.8 %attend.1 = (bf16[320,768]{1,0:T(8,128)(2,1)S(1)}, bf16[320,384]{1,0:T(8,128)(2,1)S(1)}) custom-call(bf16[320,384]{1,0:T(8,128)(2,1)S(1)} %collective-permute-done.1.other_b, bf16[320,384]{1,0:T(8,128)(2,1)S(1)} %collective-permute-done.2.own_a, bf16[960,768]{1,0:T(8,128)(2,1)S(1)} %keys.1.kv_a, f32[384]{0:T(512)S(1)} %get-tuple-element.18.gain, ...), custom_call_target="tpu_custom_call" | custom-call | flops 1195376640 | bytes 1048576 | tf_op jit(solution)/shard_map/attend/pallas_call | solution.py:300
  21.9 3.7 %collective-permute-start.4 = (bf16[320,384]{1,0:T(8,128)(2,1)S(1)}, bf16[320,384]{1,0:T(8,128)(2,1)S(1)}, u32[]{:S(2)}, u32[]{:S(2)}) collective-permute-start(bf16[320,384]{1,0:T(8,128)(2,1)S(1)} %get-tuple-element.21), channel_id=1, source_target_pairs={{0,0},{1,8},{2,2},{3,10},{4,4},{5,12},{6,6},{7,14},{8,1},{9,9},{10... | collective-permute-start | bytes 737288 | tf_op jit(solution)/shard_map/ppermute | solution.py:307
  25.6 2.6 %attend_rest.1 = bf16[320,384]{1,0:T(8,128)(2,1)S(1)} custom-call(bf16[320,384]{1,0:T(8,128)(2,1)S(1)} %collective-permute-done.own_b, bf16[960,768]{1,0:T(8,128)(2,1)S(1)} %keys.1.kv_a, bf16[320,768]{1,0:T(8,128)(2,1)S(1)} %get-tuple-element.22.kv_b, f32[384]{0:T(512)S(1)} %get-tuple-element.18.gain, bf16[384,1152]{1,0:T(8,128)(2,1)S(1)} %get-tuple-element.19.w_qkv, ...), custom_call_target="tpu_custom_call" | custom-call | flops 2453667840 | bytes 1048576 | tf_op jit(solution)/shard_map/attend_rest/pallas_call | solution.py:308
  28.2 0.8 %collective-permute-start.5 = (bf16[320,384]{1,0:T(8,128)(2,1)S(1)}, bf16[320,384]{1,0:T(8,128)(2,1)S(1)}, u32[]{:S(2)}, u32[]{:S(2)}) collective-permute-start(bf16[320,384]{1,0:T(8,128)(2,1)S(1)} %attend_rest.1), channel_id=1, source_target_pairs={{0,4},{1,12},{2,6},{3,14},{4,0},{5,8},{6,2},{7,10},{8,5},{9,13},{1... | collective-permute-start | bytes 737288 | tf_op jit(solution)/shard_map/ppermute | solution.py:315
  29.0 2.1 %collective-permute-done.4.got_a = bf16[320,384]{1,0:T(8,128)(2,1)S(1)} collective-permute-done((bf16[320,384]{1,0:T(8,128)(2,1)S(1)}, bf16[320,384]{1,0:T(8,128)(2,1)S(1)}, u32[]{:S(2)}, u32[]{:S(2)}) %collective-permute-start.4) | collective-permute-done | bytes 245792 | tf_op jit(solution)/shard_map/ppermute | solution.py:307
  31.0 0.0 copy-done
  31.0 0.3 activate_a.1
  31.3 3.1 %collective-permute-start.6 = (bf16[160,384]{1,0:T(8,128)(2,1)S(1)}, bf16[160,384]{1,0:T(8,128)(2,1)S(1)}, u32[]{:S(2)}, u32[]{:S(2)}) collective-permute-start(bf16[160,384]{1,0:T(8,128)(2,1)S(1)} %get-tuple-element.26), channel_id=1, source_target_pairs={{0,4},{4,0},{8,12},{12,8},{1,5},{5,1},{9,13},{13,9},{2,6},{6,2},{1... | collective-permute-start | bytes 368648 | tf_op jit(solution)/shard_map/ppermute | solution.py:324
  34.4 1.9 %collective-permute-start.7 = (bf16[160,384]{1,0:T(8,128)(2,1)S(1)}, bf16[160,384]{1,0:T(8,128)(2,1)S(1)}, u32[]{:S(2)}, u32[]{:S(2)}) collective-permute-start(bf16[160,384]{1,0:T(8,128)(2,1)S(1)} %get-tuple-element.27), channel_id=1, source_target_pairs={{4,8},{8,4},{5,9},{9,5},{6,10},{10,6},{7,11},{11,7},{20,24},{24,20... | collective-permute-start | bytes 368648 | tf_op jit(solution)/shard_map/ppermute | solution.py:325
  36.4 3.5 %load_conv.1._.w = bf16[3,1152,1152]{2,1,0:T(8,128)(2,1)S(1)} custom-call(bf16[320,384]{1,0:T(8,128)(2,1)S(1)} %get-tuple-element.23._.act_a, bf16[3,3,3,384,384]{4,3,2,1,0:T(8,128)(2,1)} %w_hbm.1), custom_call_target="tpu_custom_call" | custom-call | bytes 4096 | tf_op jit(solution)/shard_map/load_conv/pallas_call | solution.py:326
  39.8 0.0 copy-start.1
  39.9 0.0 collective-permute-done.5.got_b
  39.9 1.1 %activate_b.1 = (bf16[2,320,384]{2,1,0:T(8,128)(2,1)}, bf16[2,320,384]{2,1,0:T(8,128)(2,1)S(1)}, bf16[160,384]{1,0:T(8,128)(2,1)S(1)}, bf16[160,384]{1,0:T(8,128)(2,1)S(1)}) custom-call(s32[1]{0:T(128)} %bitcast.tile_ref, bf16[320,384]{1,0:T(8,128)(2,1)S(1)} %collective-permute-done.4.got_a, bf16[320,384]{1,0:T(8,128)(2,1)S(1)} %collective-permute-done.5.got_b, ...), custom_call_target="tpu_custom_call" | custom-call | bytes 1048576 | tf_op jit(solution)/shard_map/activate_b/pallas_call | solution.py:335
  41.0 0.0 collective-permute-start.8
  41.0 3.3 %collective-permute-start.9 = (bf16[160,384]{1,0:T(8,128)(2,1)S(1)}, bf16[160,384]{1,0:T(8,128)(2,1)S(1)}, u32[]{:S(2)}, u32[]{:S(2)}) collective-permute-start(bf16[160,384]{1,0:T(8,128)(2,1)S(1)} %get-tuple-element.29), channel_id=1, source_target_pairs={{4,8},{8,4},{5,9},{9,5},{6,10},{10,6},{7,11},{11,7},{20,24},{24,20... | collective-permute-start | bytes 368648 | tf_op jit(solution)/shard_map/ppermute | solution.py:342
  44.3 0.0 copy-done.1
  44.4 2.6 %next_own.1.partial = f32[2,320,384]{2,1,0:T(8,128)S(1)} custom-call(s32[1]{0:T(128)} %bitcast.5.span_ref, s32[4]{0:T(128)S(1)} %copy-done.1, bf16[2,320,384]{2,1,0:T(8,128)(2,1)S(1)} %get-tuple-element.25.mid, bf16[3,1152,1152]{2,1,0:T(8,128)(2,1)S(1)} %load_conv.1._.w), custom_call_target="tpu_custom_call" | custom-call | flops 1698693120 | bytes 1048576 | tf_op jit(solution)/shard_map/next_own/pallas_call | solution.py:344
  47.0 0.0 collective-permute-done.6.pair_a
  47.0 0.0 collective-permute-done.7.mid_a
  47.0 0.0 collective-permute-done.8.pair_b
  47.0 0.0 collective-permute-done.9.mid_b
  47.0 2.0 %next_edge.1 = bf16[2,320,384]{2,1,0:T(8,128)(2,1)S(1)} custom-call(s32[1]{0:T(128)} %bitcast.tile_ref, s32[1]{0:T(128)} %bitcast.5.span_ref, s32[4]{0:T(128)S(1)} %copy-done.1, bf16[160,384]{1,0:T(8,128)(2,1)S(1)} %collective-permute-done.6.pair_a, bf16[160,384]{1,0:T(8,128)(2,1)S(1)} %collective-permute-done.7.mid_a, ...), custom_call_target="tpu_custom_call" | custom-call | flops 849346560 | bytes 1048576 | tf_op jit(solution)/shard_map/next_edge/pallas_call | solution.py:351
  49.0 5.7 %collective-permute-start.10 = (bf16[2,320,384]{2,1,0:T(8,128)(2,1)S(1)}, bf16[2,320,384]{2,1,0:T(8,128)(2,1)S(1)}, u32[]{:S(2)}, u32[]{:S(2)}) collective-permute-start(bf16[2,320,384]{2,1,0:T(8,128)(2,1)S(1)} %next_edge.1), channel_id=1, source_target_pairs={{0,1},{1,2},{2,3},{4,5},{5,6},{6,7},{8,9},{9,10},{10,11},{12,13},{... | collective-permute-start | bytes 1474568 | tf_op jit(solution)/shard_map/ppermute | solution.py:358
  54.7 3.8 %own.1 = f32[2,320,384]{2,1,0:T(8,128)S(1)} custom-call(s32[1]{0:T(128)} %bitcast.tile_ref, s32[1]{0:T(128)} %bitcast.5.span_ref, s32[4]{0:T(128)S(1)} %copy-done.1, bf16[2,320,384]{2,1,0:T(8,128)(2,1)S(1)} %get-tuple-element.25.mid, bf16[160,384]{1,0:T(8,128)(2,1)S(1)} %collective-permute-done.6.pair_a, bf16[160,384]{1,0:T(8,128)(2,1)S(1)} %collective-permute-done.7.mid_a, ...), custom_call_target="tpu_custom_call" | custom-call | flops 2548039680 | bytes 1048576 | tf_op jit(solution)/shard_map/own/pallas_call | solution.py:359
  58.6 1.7 %collective-permute-done.10 = bf16[2,320,384]{2,1,0:T(8,128)(2,1)S(1)} collective-permute-done((bf16[2,320,384]{2,1,0:T(8,128)(2,1)S(1)}, bf16[2,320,384]{2,1,0:T(8,128)(2,1)S(1)}, u32[]{:S(2)}, u32[]{:S(2)}) %collective-permute-start.10) | collective-permute-done | bytes 491552 | tf_op jit(solution)/shard_map/ppermute | solution.py:358
  60.3 0.9 %add_convert_fusion = bf16[2,320,384]{2,1,0:T(8,128)(2,1)} fusion(f32[2,320,384]{2,1,0:T(8,128)S(1)} %own.1, bf16[2,320,384]{2,1,0:T(8,128)(2,1)S(1)} %collective-permute-done.10), kind=kLoop, calls=%fused_computation | loop fusion | flops 737280 | bytes 1966080 | tf_op jit(solution)/shard_map/convert_element_type | solution.py:362
Async XLA Ops:
  1.8 13.1 %collective-permute-start.2 = (bf16[320,384]{1,0:T(8,128)(2,1)S(1)}, bf16[320,384]{1,0:T(8,128)(2,1)S(1)}, u32[]{:S(2)}, u32[]{:S(2)}) collective-permute-start(bf16[320,384]{1,0:T(8,128)(2,1)S(1)} %get-tuple-element.30), channel_id=1, source_target_pairs={{0,0},{1,8},{2,2},{3,10},{4,4},{5,12},{6,6},{7,14},{8,1},{9,9},{10... | collective-permute-start | bytes 737288 | tf_op jit(solution)/shard_map/ppermute | solution.py:282
  6.6 11.0 %collective-permute-start = (bf16[320,384]{1,0:T(8,128)(2,1)S(1)}, bf16[320,384]{1,0:T(8,128)(2,1)S(1)}, u32[]{:S(2)}, u32[]{:S(2)}) collective-permute-start(bf16[320,384]{1,0:T(8,128)(2,1)S(1)} %get-tuple-element.31), channel_id=1, source_target_pairs={{0,4},{1,12},{2,6},{3,14},{4,0},{5,8},{6,2},{7,10},{8,5},{9,13},{1... | collective-permute-start | bytes 737288 | tf_op jit(solution)/shard_map/ppermute | solution.py:283
  14.9 2.6 %collective-permute-start.3 = (bf16[320,384]{1,0:T(8,128)(2,1)S(1)}, bf16[320,384]{1,0:T(8,128)(2,1)S(1)}, u32[]{:S(2)}, u32[]{:S(2)}) collective-permute-start(bf16[320,384]{1,0:T(8,128)(2,1)S(1)} %collective-permute-done.2.own_a), channel_id=1, source_target_pairs={{0,1},{1,0},{2,3},{3,2},{4,5},{5,4},{6,7},{7,6},{8,9},{9,8},{10,11... | collective-permute-start | bytes 737288 | tf_op jit(solution)/shard_map/ppermute | solution.py:293
  17.6 1.5 %collective-permute-start.1 = (bf16[320,384]{1,0:T(8,128)(2,1)S(1)}, bf16[320,384]{1,0:T(8,128)(2,1)S(1)}, u32[]{:S(2)}, u32[]{:S(2)}) collective-permute-start(bf16[320,384]{1,0:T(8,128)(2,1)S(1)} %collective-permute-done.own_b), channel_id=1, source_target_pairs={{0,1},{1,0},{2,3},{3,2},{4,5},{5,4},{6,7},{7,6},{8,9},{9,8},{10,11... | collective-permute-start | bytes 737288 | tf_op jit(solution)/shard_map/ppermute | solution.py:294
  17.6 13.5 %copy-start = (f32[384]{0:T(512)S(1)}, f32[384]{0:T(512)}, u32[]{:S(2)}) copy-start(f32[384]{0:T(512)} %gain.5) | copy-start | bytes 4612
  21.9 9.1 %collective-permute-start.4 = (bf16[320,384]{1,0:T(8,128)(2,1)S(1)}, bf16[320,384]{1,0:T(8,128)(2,1)S(1)}, u32[]{:S(2)}, u32[]{:S(2)}) collective-permute-start(bf16[320,384]{1,0:T(8,128)(2,1)S(1)} %get-tuple-element.21), channel_id=1, source_target_pairs={{0,0},{1,8},{2,2},{3,10},{4,4},{5,12},{6,6},{7,14},{8,1},{9,9},{10... | collective-permute-start | bytes 737288 | tf_op jit(solution)/shard_map/ppermute | solution.py:307
  28.2 11.7 %collective-permute-start.5 = (bf16[320,384]{1,0:T(8,128)(2,1)S(1)}, bf16[320,384]{1,0:T(8,128)(2,1)S(1)}, u32[]{:S(2)}, u32[]{:S(2)}) collective-permute-start(bf16[320,384]{1,0:T(8,128)(2,1)S(1)} %attend_rest.1), channel_id=1, source_target_pairs={{0,4},{1,12},{2,6},{3,14},{4,0},{5,8},{6,2},{7,10},{8,5},{9,13},{1... | collective-permute-start | bytes 737288 | tf_op jit(solution)/shard_map/ppermute | solution.py:315
  31.3 15.7 %collective-permute-start.6 = (bf16[160,384]{1,0:T(8,128)(2,1)S(1)}, bf16[160,384]{1,0:T(8,128)(2,1)S(1)}, u32[]{:S(2)}, u32[]{:S(2)}) collective-permute-start(bf16[160,384]{1,0:T(8,128)(2,1)S(1)} %get-tuple-element.26), channel_id=1, source_target_pairs={{0,4},{4,0},{8,12},{12,8},{1,5},{5,1},{9,13},{13,9},{2,6},{6,2},{1... | collective-permute-start | bytes 368648 | tf_op jit(solution)/shard_map/ppermute | solution.py:324
  34.4 12.6 %collective-permute-start.7 = (bf16[160,384]{1,0:T(8,128)(2,1)S(1)}, bf16[160,384]{1,0:T(8,128)(2,1)S(1)}, u32[]{:S(2)}, u32[]{:S(2)}) collective-permute-start(bf16[160,384]{1,0:T(8,128)(2,1)S(1)} %get-tuple-element.27), channel_id=1, source_target_pairs={{4,8},{8,4},{5,9},{9,5},{6,10},{10,6},{7,11},{11,7},{20,24},{24,20... | collective-permute-start | bytes 368648 | tf_op jit(solution)/shard_map/ppermute | solution.py:325
  39.8 4.5 %copy-start.1 = (s32[4]{0:T(128)S(1)}, s32[4]{0:T(128)}, u32[]{:S(2)}) copy-start(s32[4]{0:T(128)} %clips.5) | copy-start | bytes 52
  41.0 6.0 %collective-permute-start.8 = (bf16[160,384]{1,0:T(8,128)(2,1)S(1)}, bf16[160,384]{1,0:T(8,128)(2,1)S(1)}, u32[]{:S(2)}, u32[]{:S(2)}) collective-permute-start(bf16[160,384]{1,0:T(8,128)(2,1)S(1)} %get-tuple-element.28), channel_id=1, source_target_pairs={{0,4},{4,0},{8,12},{12,8},{1,5},{5,1},{9,13},{13,9},{2,6},{6,2},{1... | collective-permute-start | bytes 368648 | tf_op jit(solution)/shard_map/ppermute | solution.py:341
  41.0 6.0 %collective-permute-start.9 = (bf16[160,384]{1,0:T(8,128)(2,1)S(1)}, bf16[160,384]{1,0:T(8,128)(2,1)S(1)}, u32[]{:S(2)}, u32[]{:S(2)}) collective-permute-start(bf16[160,384]{1,0:T(8,128)(2,1)S(1)} %get-tuple-element.29), channel_id=1, source_target_pairs={{4,8},{8,4},{5,9},{9,5},{6,10},{10,6},{7,11},{11,7},{20,24},{24,20... | collective-permute-start | bytes 368648 | tf_op jit(solution)/shard_map/ppermute | solution.py:342
  49.0 11.3 %collective-permute-start.10 = (bf16[2,320,384]{2,1,0:T(8,128)(2,1)S(1)}, bf16[2,320,384]{2,1,0:T(8,128)(2,1)S(1)}, u32[]{:S(2)}, u32[]{:S(2)}) collective-permute-start(bf16[2,320,384]{2,1,0:T(8,128)(2,1)S(1)} %next_edge.1), channel_id=1, source_target_pairs={{0,1},{1,2},{2,3},{4,5},{5,6},{6,7},{8,9},{9,10},{10,11},{12,13},{... | collective-permute-start | bytes 1474568 | tf_op jit(solution)/shard_map/ppermute | solution.py:358

commit v6 on v5

--- a/solution.py
+++ b/solution.py
@@ -59,15 +59,6 @@
             there = (2 * core + (low ^ flip)) * spans + 2 * column + high
             route.append((tile * spans + span, there))
     return route
-
-
-def shifted_route(tiles, spans, down, ahead):
-    return [
-        (t * spans + s, (t + down) * spans + s + ahead)
-        for t in range(tiles)
-        for s in range(spans)
-        if 0 <= t + down < tiles and s + ahead < spans
-    ]
 
 
 def load_small_kernel(w_qkv, w_out, gain, qkv_vm, out_vm, gain_vm, sem):
@@ -163,7 +154,7 @@
         mid_edge[...] = act[cols:, :]
 
 
-def activate_a_kernel(cols, tile_ref, got_a, gain, *outs):
+def activate_a_kernel(cols, tile_ref, got_a, gain, _, *outs):
     activate(cols, tile_ref[0] % 2, got_a, gain, *outs)
 
 
@@ -318,11 +309,6 @@
     sums = struct((frames, cells, ch), f32)
     unit = 2 * cells * 9 * ch * ch
     where = (tile, span, clip_lengths)
-    act_a, pair_edge, mid_edge = call(
-        functools.partial(activate_a_kernel, cols), "activate_a", (one, edge, edge), [SMEM, VMEM, VMEM]
-    )(tile, got_a, conv_gain)
-    pair_a = lax.ppermute(pair_edge, "tile", pairs)
-    mid_a = lax.ppermute(mid_edge, "tile", middle)
     w_packed = call(
         load_kernel,
         "load_conv",
@@ -331,7 +317,12 @@
         [pltpu.SemaphoreType.DMA((27,))],
         42,
         size=1 << 12,
-    )(act_a, w_conv)
+    )(att_b, w_conv)
+    act_a, pair_edge, mid_edge = call(
+        functools.partial(activate_a_kernel, cols), "activate_a", (one, edge, edge), [SMEM, VMEM, VMEM, ANY]
+    )(tile, got_a, conv_gain, w_packed)
+    pair_a = lax.ppermute(pair_edge, "tile", pairs)
+    mid_a = lax.ppermute(mid_edge, "tile", middle)
     attended, active, pair_edge, mid_edge = call(
         functools.partial(activate_b_kernel, cols),
         "activate_b",
@@ -355,11 +346,12 @@
         [SMEM] * 3 + [VMEM] * 6,
         flops=unit,
     )(*where, *edges, w_packed, started)
-    earlier = lax.ppermute(for_next, both, shifted_route(tiles, spans, 0, 1))
+    from_odd = lax.ppermute(for_next, "span", [(s, s + 1) for s in range(1, spans - 1, 2)])
+    from_even = lax.ppermute(for_next, "span", [(s, s + 1) for s in range(0, spans, 2)])
     own = call(
         functools.partial(own_kernel, cols), "own", sums, [SMEM] * 3 + [VMEM] * 6, flops=3 * unit
     )(*where, active, *edges, w_packed)
-    hidden = (own + earlier.astype(f32)).astype(bf16)
+    hidden = (own + from_odd.astype(f32) + from_even.astype(f32)).astype(bf16)
     shape = (frames, row_count, cols, ch)
     return attended.reshape(shape), hidden.reshape(shape)
 

time: 62.2 us -> 61.6 us (level)
  starting transfers between devices: 23.3 us -> 21.3 us
  waiting for transfers between devices: 13.3 us -> 14.7 us
    ppermute x1, waiting for transfers between devices: 2.06 us -> 0.01 us  [on_device(): got_a = lax.ppermute(att_a, both, route_a)]
    ppermute x1, waiting for transfers between devices: 0.01 us -> 1.81 us  [on_device(): got_b = lax.ppermute(att_b, both, route_b)]
    ppermute x1, waiting for transfers between devices: 0.01 us -> 1.67 us  [on_device(): mid_b = lax.ppermute(mid_edge, 'tile', middle)]
    ppermute x1, starting transfers between devices: 3.09 us -> 1.52 us  [on_device(): pair_a = lax.ppermute(pair_edge, 'tile', pairs)]
    ppermute x1, starting transfers between devices: 3.33 us -> 1.91 us  [on_device(): mid_b = lax.ppermute(mid_edge, 'tile', middle)]
    ppermute x1, starting transfers between devices: 0.01 us -> 0.72 us  [on_device(): pair_b = lax.ppermute(pair_edge, 'tile', pairs)]
    ppermute x1 -> x2, starting transfers between devices: 5.68 us -> 5.9 us  [the longest x1 4.61 us: on_device(): lax.ppermute(for_next, 'span', [(s, s + 1) for s in range(1, spans - 1, 2)])]
    ppermute x1 -> x2, waiting for transfers between devices: 1.72 us -> 1.7 us  [the longest x1 1.7 us: on_device(): lax.ppermute(for_next, 'span', [(s, s + 1) for s in range(1, spans - 1, 2)])]
  transfers between devices with their start and end apart: 11 -> 12, of which waited for: 5 -> 6; matrix products, arithmetic and copies ran while one was open for 0% -> 0% of each run, Pallas kernels for 28% -> 28%
where the time goes in v6:
time: 61.6 us; the launch traced here: 60.6 us
  Pallas kernels  21.7 us (35%)
  starting transfers between devices  21.3 us (35%)
  waiting for transfers between devices  14.7 us (24%)
  local copies, waits for them, and re-layouts  1.13 us (2%)
  other arithmetic  0.95 us (2%)
  between operations  0.84 us (1%)
    ppermute x1, waiting for transfers between devices, on_device(): own_a = lax.ppermute(send_a, both, route_a)  6.35 us
    ppermute x1, starting transfers between devices, on_device(): own_a = lax.ppermute(send_a, both, route_a)  4.78 us
    ppermute x1, starting transfers between devices, on_device(): lax.ppermute(for_next, 'span', [(s, s + 1) for s in range(1, spans - 1, 2)])  4.61 us
    pallas_call x1, Pallas kernels, on_device(): call(functools.partial(own_kernel, cols), 'own', sums, [SMEM] * 3 + [VMEM...  3.83 us
    ppermute x1, starting transfers between devices, on_device(): got_a = lax.ppermute(att_a, both, route_a)  3.67 us
    pallas_call x1, Pallas kernels, on_device(): call(load_kernel, 'load_conv', struct((3, 3 * ch, 3 * ch)), [ANY, ANY], [...  3.48 us
    pallas_call x1, Pallas kernels, on_device(): call(functools.partial(attend_kernel, cols), 'attend', (struct((cells, 2...  2.83 us
    ppermute x1, waiting for transfers between devices, on_device(): own_b = lax.ppermute(send_b, both, route_b)  2.63 us
  transfers between devices with their start and end apart: 12, of which 6 were waited for; matrix products, arithmetic and copies ran while one was open for 0% of the time, Pallas kernels for 28%

profile of v6, /device:TPU:13, one launch (start us, length us, event | category | flops | bytes accessed | tf_op | source)
XLA Modules:
  0.0 60.6 jit_solution(16192750047191720779)
XLA Ops:
  0.7 1.1 %dynamic-slice_bitcast_fusion = (bf16[320,384]{1,0:T(8,128)(2,1)S(1)}, bf16[320,384]{1,0:T(8,128)(2,1)S(1)}) fusion(bf16[2,320,384]{2,1,0:T(8,128)(2,1)} %bitcast.10, s32[]{:T(128)S(6)} %select_n.16, s32[]{:T(128)S(6)} %select_n.15), kind=kLoop, calls=%fused_computation.1 | loop fusion | bytes 983048 | tf_op jit(solution)/shard_map/jit(dynamic_index_in_dim)/squeeze | solution.py:271
  1.8 4.8 %collective-permute-start.2 = (bf16[320,384]{1,0:T(8,128)(2,1)S(1)}, bf16[320,384]{1,0:T(8,128)(2,1)S(1)}, u32[]{:S(2)}, u32[]{:S(2)}) collective-permute-start(bf16[320,384]{1,0:T(8,128)(2,1)S(1)} %get-tuple-element.30), channel_id=1, source_target_pairs={{0,0},{1,8},{2,2},{3,10},{4,4},{5,12},{6,6},{7,14},{8,1},{9,9},{10... | collective-permute-start | bytes 737288 | tf_op jit(solution)/shard_map/ppermute | solution.py:273
  6.6 0.1 collective-permute-start
  6.6 1.9 %load_small.1 = (bf16[384,1152]{1,0:T(8,128)(2,1)S(1)}, bf16[384,384]{1,0:T(8,128)(2,1)S(1)}, f32[384]{0:T(512)S(1)}) custom-call(bf16[384,1152]{1,0:T(8,128)(2,1)} %w_qkv.1, bf16[384,384]{1,0:T(8,128)(2,1)} %w_out.1, f32[384]{0:T(512)} %gain.3), custom_call_target="tpu_custom_call" | custom-call | bytes 1048576 | tf_op jit(solution)/shard_map/load_small/pallas_call | solution.py:275
  8.6 6.3 %collective-permute-done.2.own_a = bf16[320,384]{1,0:T(8,128)(2,1)S(1)} collective-permute-done((bf16[320,384]{1,0:T(8,128)(2,1)S(1)}, bf16[320,384]{1,0:T(8,128)(2,1)S(1)}, u32[]{:S(2)}, u32[]{:S(2)}) %collective-permute-start.2) | collective-permute-done | bytes 245792 | tf_op jit(solution)/shard_map/ppermute | solution.py:273
  14.9 0.0 collective-permute-start.3
  14.9 2.6 %collective-permute-done.own_b = bf16[320,384]{1,0:T(8,128)(2,1)S(1)} collective-permute-done((bf16[320,384]{1,0:T(8,128)(2,1)S(1)}, bf16[320,384]{1,0:T(8,128)(2,1)S(1)}, u32[]{:S(2)}, u32[]{:S(2)}) %collective-permute-start) | collective-permute-done | bytes 245792 | tf_op jit(solution)/shard_map/ppermute | solution.py:274
  17.6 0.0 collective-permute-start.1
  17.6 0.0 collective-permute-done.3.other_a
  17.6 1.0 %keys.1.kv_a = bf16[960,768]{1,0:T(8,128)(2,1)S(1)} custom-call(bf16[320,384]{1,0:T(8,128)(2,1)S(1)} %collective-permute-done.2.own_a, bf16[320,384]{1,0:T(8,128)(2,1)S(1)} %collective-permute-done.3.other_a, bf16[320,384]{1,0:T(8,128)(2,1)S(1)} %collective-permute-done.own_b, f32[384]{0:T(512)S(1)} %get-tuple-element.18.gain, ...), custom_call_target="tpu_custom_call" | custom-call | flops 377487360 | bytes 1048576 | tf_op jit(solution)/shard_map/keys/pallas_call | solution.py:288
  18.6 0.5 collective-permute-done.1.other_b
  19.1 2.8 %attend.1 = (bf16[320,768]{1,0:T(8,128)(2,1)S(1)}, bf16[320,384]{1,0:T(8,128)(2,1)S(1)}) custom-call(bf16[320,384]{1,0:T(8,128)(2,1)S(1)} %collective-permute-done.1.other_b, bf16[320,384]{1,0:T(8,128)(2,1)S(1)} %collective-permute-done.2.own_a, bf16[960,768]{1,0:T(8,128)(2,1)S(1)} %keys.1.kv_a, f32[384]{0:T(512)S(1)} %get-tuple-element.18.gain, ...), custom_call_target="tpu_custom_call" | custom-call | flops 1195376640 | bytes 1048576 | tf_op jit(solution)/shard_map/attend/pallas_call | solution.py:291
  21.9 3.7 %collective-permute-start.4 = (bf16[320,384]{1,0:T(8,128)(2,1)S(1)}, bf16[320,384]{1,0:T(8,128)(2,1)S(1)}, u32[]{:S(2)}, u32[]{:S(2)}) collective-permute-start(bf16[320,384]{1,0:T(8,128)(2,1)S(1)} %get-tuple-element.21), channel_id=1, source_target_pairs={{0,0},{1,8},{2,2},{3,10},{4,4},{5,12},{6,6},{7,14},{8,1},{9,9},{10... | collective-permute-start | bytes 737288 | tf_op jit(solution)/shard_map/ppermute | solution.py:298
  25.6 2.6 %attend_rest.1._ = bf16[320,384]{1,0:T(8,128)(2,1)S(1)} custom-call(bf16[320,384]{1,0:T(8,128)(2,1)S(1)} %collective-permute-done.own_b, bf16[960,768]{1,0:T(8,128)(2,1)S(1)} %keys.1.kv_a, bf16[320,768]{1,0:T(8,128)(2,1)S(1)} %get-tuple-element.22.kv_b, f32[384]{0:T(512)S(1)} %get-tuple-element.18.gain, bf16[384,1152]{1,0:T(8,128)(2,1)S(1)} %get-tuple-element.19.w_qkv, ...), custom_call_target="tpu_custom_call" | custom-call | flops 2453667840 | bytes 1048576 | tf_op jit(solution)/shard_map/attend_rest/pallas_call | solution.py:299
  28.2 0.8 %collective-permute-start.5 = (bf16[320,384]{1,0:T(8,128)(2,1)S(1)}, bf16[320,384]{1,0:T(8,128)(2,1)S(1)}, u32[]{:S(2)}, u32[]{:S(2)}) collective-permute-start(bf16[320,384]{1,0:T(8,128)(2,1)S(1)} %attend_rest.1._), channel_id=1, source_target_pairs={{0,4},{1,12},{2,6},{3,14},{4,0},{5,8},{6,2},{7,10},{8,5},{9,13},{1... | collective-permute-start | bytes 737288 | tf_op jit(solution)/shard_map/ppermute | solution.py:306
  29.0 0.0 copy-start
  29.0 3.5 %load_conv.1._.w = bf16[3,1152,1152]{2,1,0:T(8,128)(2,1)S(1)} custom-call(bf16[320,384]{1,0:T(8,128)(2,1)S(1)} %attend_rest.1._, bf16[3,3,3,384,384]{4,3,2,1,0:T(8,128)(2,1)} %w_hbm.1), custom_call_target="tpu_custom_call" | custom-call | bytes 4096 | tf_op jit(solution)/shard_map/load_conv/pallas_call | solution.py:312
  32.5 0.0 collective-permute-done.4.got_a
  32.5 0.0 copy-done
  32.5 0.0 copy-start.1
  32.5 0.3 activate_a.1
  32.8 1.5 %collective-permute-start.6 = (bf16[160,384]{1,0:T(8,128)(2,1)S(1)}, bf16[160,384]{1,0:T(8,128)(2,1)S(1)}, u32[]{:S(2)}, u32[]{:S(2)}) collective-permute-start(bf16[160,384]{1,0:T(8,128)(2,1)S(1)} %get-tuple-element.26), channel_id=1, source_target_pairs={{0,4},{4,0},{8,12},{12,8},{1,5},{5,1},{9,13},{13,9},{2,6},{6,2},{1... | collective-permute-start | bytes 368648 | tf_op jit(solution)/shard_map/ppermute | solution.py:324
  34.3 1.9 %collective-permute-start.7 = (bf16[160,384]{1,0:T(8,128)(2,1)S(1)}, bf16[160,384]{1,0:T(8,128)(2,1)S(1)}, u32[]{:S(2)}, u32[]{:S(2)}) collective-permute-start(bf16[160,384]{1,0:T(8,128)(2,1)S(1)} %get-tuple-element.27), channel_id=1, source_target_pairs={{4,8},{8,4},{5,9},{9,5},{6,10},{10,6},{7,11},{11,7},{20,24},{24,20... | collective-permute-start | bytes 368648 | tf_op jit(solution)/shard_map/ppermute | solution.py:325
  36.3 1.8 %collective-permute-done.5.got_b = bf16[320,384]{1,0:T(8,128)(2,1)S(1)} collective-permute-done((bf16[320,384]{1,0:T(8,128)(2,1)S(1)}, bf16[320,384]{1,0:T(8,128)(2,1)S(1)}, u32[]{:S(2)}, u32[]{:S(2)}) %collective-permute-start.5) | collective-permute-done | bytes 245792 | tf_op jit(solution)/shard_map/ppermute | solution.py:306
  38.1 1.1 %activate_b.1 = (bf16[2,320,384]{2,1,0:T(8,128)(2,1)}, bf16[2,320,384]{2,1,0:T(8,128)(2,1)S(1)}, bf16[160,384]{1,0:T(8,128)(2,1)S(1)}, bf16[160,384]{1,0:T(8,128)(2,1)S(1)}) custom-call(s32[1]{0:T(128)} %bitcast.tile_ref, bf16[320,384]{1,0:T(8,128)(2,1)S(1)} %collective-permute-done.4.got_a, bf16[320,384]{1,0:T(8,128)(2,1)S(1)} %collective-permute-done.5.got_b, ...), custom_call_target="tpu_custom_call" | custom-call | bytes 1048576 | tf_op jit(solution)/shard_map/activate_b/pallas_call | solution.py:326
  39.2 0.7 %collective-permute-start.8 = (bf16[160,384]{1,0:T(8,128)(2,1)S(1)}, bf16[160,384]{1,0:T(8,128)(2,1)S(1)}, u32[]{:S(2)}, u32[]{:S(2)}) collective-permute-start(bf16[160,384]{1,0:T(8,128)(2,1)S(1)} %get-tuple-element.28), channel_id=1, source_target_pairs={{0,4},{4,0},{8,12},{12,8},{1,5},{5,1},{9,13},{13,9},{2,6},{6,2},{1... | collective-permute-start | bytes 368648 | tf_op jit(solution)/shard_map/ppermute | solution.py:332
  39.9 1.9 %collective-permute-start.9 = (bf16[160,384]{1,0:T(8,128)(2,1)S(1)}, bf16[160,384]{1,0:T(8,128)(2,1)S(1)}, u32[]{:S(2)}, u32[]{:S(2)}) collective-permute-start(bf16[160,384]{1,0:T(8,128)(2,1)S(1)} %get-tuple-element.29), channel_id=1, source_target_pairs={{4,8},{8,4},{5,9},{9,5},{6,10},{10,6},{7,11},{11,7},{20,24},{24,20... | collective-permute-start | bytes 368648 | tf_op jit(solution)/shard_map/ppermute | solution.py:333
  41.8 0.0 copy-done.1
  41.8 2.6 %next_own.1.partial = f32[2,320,384]{2,1,0:T(8,128)S(1)} custom-call(s32[1]{0:T(128)} %bitcast.5.span_ref, s32[4]{0:T(128)S(1)} %copy-done.1, bf16[2,320,384]{2,1,0:T(8,128)(2,1)S(1)} %get-tuple-element.25.mid, bf16[3,1152,1152]{2,1,0:T(8,128)(2,1)S(1)} %load_conv.1._.w), custom_call_target="tpu_custom_call" | custom-call | flops 1698693120 | bytes 1048576 | tf_op jit(solution)/shard_map/next_own/pallas_call | solution.py:335
  44.5 0.0 collective-permute-done.6.pair_a
  44.5 0.0 collective-permute-done.7.mid_a
  44.5 0.0 collective-permute-done.8.pair_b
  44.5 1.7 %collective-permute-done.9.mid_b = bf16[160,384]{1,0:T(8,128)(2,1)S(1)} collective-permute-done((bf16[160,384]{1,0:T(8,128)(2,1)S(1)}, bf16[160,384]{1,0:T(8,128)(2,1)S(1)}, u32[]{:S(2)}, u32[]{:S(2)}) %collective-permute-start.9) | collective-permute-done | bytes 122912 | tf_op jit(solution)/shard_map/ppermute | solution.py:333
  46.2 2.0 %next_edge.1 = bf16[2,320,384]{2,1,0:T(8,128)(2,1)S(1)} custom-call(s32[1]{0:T(128)} %bitcast.tile_ref, s32[1]{0:T(128)} %bitcast.5.span_ref, s32[4]{0:T(128)S(1)} %copy-done.1, bf16[160,384]{1,0:T(8,128)(2,1)S(1)} %collective-permute-done.6.pair_a, bf16[160,384]{1,0:T(8,128)(2,1)S(1)} %collective-permute-done.7.mid_a, ...), custom_call_target="tpu_custom_call" | custom-call | flops 849346560 | bytes 1048576 | tf_op jit(solution)/shard_map/next_edge/pallas_call | solution.py:342
  48.2 1.3 %collective-permute-start.11 = (bf16[2,320,384]{2,1,0:T(8,128)(2,1)S(1)}, bf16[2,320,384]{2,1,0:T(8,128)(2,1)S(1)}, u32[]{:S(2)}, u32[]{:S(2)}) collective-permute-start(bf16[2,320,384]{2,1,0:T(8,128)(2,1)S(1)} %next_edge.1), channel_id=1, source_target_pairs={{0,1},{2,3},{4,5},{6,7},{8,9},{10,11},{12,13},{14,15},{16,17},{18,... | collective-permute-start | bytes 1474568 | tf_op jit(solution)/shard_map/ppermute | solution.py:350
  49.5 4.6 %collective-permute-start.10 = (bf16[2,320,384]{2,1,0:T(8,128)(2,1)S(1)}, bf16[2,320,384]{2,1,0:T(8,128)(2,1)S(1)}, u32[]{:S(2)}, u32[]{:S(2)}) collective-permute-start(bf16[2,320,384]{2,1,0:T(8,128)(2,1)S(1)} %next_edge.1), channel_id=1, source_target_pairs={{1,2},{5,6},{9,10},{13,14},{17,18},{21,22},{25,26},{29,30}} | collective-permute-start | bytes 1474568 | tf_op jit(solution)/shard_map/ppermute | solution.py:349
  54.1 3.8 %own.1 = f32[2,320,384]{2,1,0:T(8,128)S(1)} custom-call(s32[1]{0:T(128)} %bitcast.tile_ref, s32[1]{0:T(128)} %bitcast.5.span_ref, s32[4]{0:T(128)S(1)} %copy-done.1, bf16[2,320,384]{2,1,0:T(8,128)(2,1)S(1)} %get-tuple-element.25.mid, bf16[160,384]{1,0:T(8,128)(2,1)S(1)} %collective-permute-done.6.pair_a, bf16[160,384]{1,0:T(8,128)(2,1)S(1)} %collective-permute-done.7.mid_a, ...), custom_call_target="tpu_custom_call" | custom-call | flops 2548039680 | bytes 1048576 | tf_op jit(solution)/shard_map/own/pallas_call | solution.py:351
  57.9 0.0 collective-permute-done.11
  57.9 1.7 %collective-permute-done.10 = bf16[2,320,384]{2,1,0:T(8,128)(2,1)S(1)} collective-permute-done((bf16[2,320,384]{2,1,0:T(8,128)(2,1)S(1)}, bf16[2,320,384]{2,1,0:T(8,128)(2,1)S(1)}, u32[]{:S(2)}, u32[]{:S(2)}) %collective-permute-start.10) | collective-permute-done | bytes 491552 | tf_op jit(solution)/shard_map/ppermute | solution.py:349
  59.6 1.0 %add_convert_fusion = bf16[2,320,384]{2,1,0:T(8,128)(2,1)} fusion(bf16[2,320,384]{2,1,0:T(8,128)(2,1)S(1)} %collective-permute-done.11, f32[2,320,384]{2,1,0:T(8,128)S(1)} %own.1, bf16[2,320,384]{2,1,0:T(8,128)(2,1)S(1)} %collective-permute-done.10), kind=kLoop, calls=%fused_computation | loop fusion | flops 1228800 | bytes 2457600 | tf_op jit(solution)/shard_map/convert_element_type | solution.py:354
Async XLA Ops:
  1.8 13.1 %collective-permute-start.2 = (bf16[320,384]{1,0:T(8,128)(2,1)S(1)}, bf16[320,384]{1,0:T(8,128)(2,1)S(1)}, u32[]{:S(2)}, u32[]{:S(2)}) collective-permute-start(bf16[320,384]{1,0:T(8,128)(2,1)S(1)} %get-tuple-element.30), channel_id=1, source_target_pairs={{0,0},{1,8},{2,2},{3,10},{4,4},{5,12},{6,6},{7,14},{8,1},{9,9},{10... | collective-permute-start | bytes 737288 | tf_op jit(solution)/shard_map/ppermute | solution.py:273
  6.6 11.0 %collective-permute-start = (bf16[320,384]{1,0:T(8,128)(2,1)S(1)}, bf16[320,384]{1,0:T(8,128)(2,1)S(1)}, u32[]{:S(2)}, u32[]{:S(2)}) collective-permute-start(bf16[320,384]{1,0:T(8,128)(2,1)S(1)} %get-tuple-element.31), channel_id=1, source_target_pairs={{0,4},{1,12},{2,6},{3,14},{4,0},{5,8},{6,2},{7,10},{8,5},{9,13},{1... | collective-permute-start | bytes 737288 | tf_op jit(solution)/shard_map/ppermute | solution.py:274
  14.9 2.6 %collective-permute-start.3 = (bf16[320,384]{1,0:T(8,128)(2,1)S(1)}, bf16[320,384]{1,0:T(8,128)(2,1)S(1)}, u32[]{:S(2)}, u32[]{:S(2)}) collective-permute-start(bf16[320,384]{1,0:T(8,128)(2,1)S(1)} %collective-permute-done.2.own_a), channel_id=1, source_target_pairs={{0,1},{1,0},{2,3},{3,2},{4,5},{5,4},{6,7},{7,6},{8,9},{9,8},{10,11... | collective-permute-start | bytes 737288 | tf_op jit(solution)/shard_map/ppermute | solution.py:284
  17.6 1.5 %collective-permute-start.1 = (bf16[320,384]{1,0:T(8,128)(2,1)S(1)}, bf16[320,384]{1,0:T(8,128)(2,1)S(1)}, u32[]{:S(2)}, u32[]{:S(2)}) collective-permute-start(bf16[320,384]{1,0:T(8,128)(2,1)S(1)} %collective-permute-done.own_b), channel_id=1, source_target_pairs={{0,1},{1,0},{2,3},{3,2},{4,5},{5,4},{6,7},{7,6},{8,9},{9,8},{10,11... | collective-permute-start | bytes 737288 | tf_op jit(solution)/shard_map/ppermute | solution.py:285
  21.9 10.6 %collective-permute-start.4 = (bf16[320,384]{1,0:T(8,128)(2,1)S(1)}, bf16[320,384]{1,0:T(8,128)(2,1)S(1)}, u32[]{:S(2)}, u32[]{:S(2)}) collective-permute-start(bf16[320,384]{1,0:T(8,128)(2,1)S(1)} %get-tuple-element.21), channel_id=1, source_target_pairs={{0,0},{1,8},{2,2},{3,10},{4,4},{5,12},{6,6},{7,14},{8,1},{9,9},{10... | collective-permute-start | bytes 737288 | tf_op jit(solution)/shard_map/ppermute | solution.py:298
  28.2 9.9 %collective-permute-start.5 = (bf16[320,384]{1,0:T(8,128)(2,1)S(1)}, bf16[320,384]{1,0:T(8,128)(2,1)S(1)}, u32[]{:S(2)}, u32[]{:S(2)}) collective-permute-start(bf16[320,384]{1,0:T(8,128)(2,1)S(1)} %attend_rest.1._), channel_id=1, source_target_pairs={{0,4},{1,12},{2,6},{3,14},{4,0},{5,8},{6,2},{7,10},{8,5},{9,13},{1... | collective-permute-start | bytes 737288 | tf_op jit(solution)/shard_map/ppermute | solution.py:306
  29.0 3.5 %copy-start = (f32[384]{0:T(512)S(1)}, f32[384]{0:T(512)}, u32[]{:S(2)}) copy-start(f32[384]{0:T(512)} %gain.5) | copy-start | bytes 4612
  32.5 9.3 %copy-start.1 = (s32[4]{0:T(128)S(1)}, s32[4]{0:T(128)}, u32[]{:S(2)}) copy-start(s32[4]{0:T(128)} %clips.5) | copy-start | bytes 52
  32.8 11.7 %collective-permute-start.6 = (bf16[160,384]{1,0:T(8,128)(2,1)S(1)}, bf16[160,384]{1,0:T(8,128)(2,1)S(1)}, u32[]{:S(2)}, u32[]{:S(2)}) collective-permute-start(bf16[160,384]{1,0:T(8,128)(2,1)S(1)} %get-tuple-element.26), channel_id=1, source_target_pairs={{0,4},{4,0},{8,12},{12,8},{1,5},{5,1},{9,13},{13,9},{2,6},{6,2},{1... | collective-permute-start | bytes 368648 | tf_op jit(solution)/shard_map/ppermute | solution.py:324
  34.3 10.2 %collective-permute-start.7 = (bf16[160,384]{1,0:T(8,128)(2,1)S(1)}, bf16[160,384]{1,0:T(8,128)(2,1)S(1)}, u32[]{:S(2)}, u32[]{:S(2)}) collective-permute-start(bf16[160,384]{1,0:T(8,128)(2,1)S(1)} %get-tuple-element.27), channel_id=1, source_target_pairs={{4,8},{8,4},{5,9},{9,5},{6,10},{10,6},{7,11},{11,7},{20,24},{24,20... | collective-permute-start | bytes 368648 | tf_op jit(solution)/shard_map/ppermute | solution.py:325
  39.2 5.3 %collective-permute-start.8 = (bf16[160,384]{1,0:T(8,128)(2,1)S(1)}, bf16[160,384]{1,0:T(8,128)(2,1)S(1)}, u32[]{:S(2)}, u32[]{:S(2)}) collective-permute-start(bf16[160,384]{1,0:T(8,128)(2,1)S(1)} %get-tuple-element.28), channel_id=1, source_target_pairs={{0,4},{4,0},{8,12},{12,8},{1,5},{5,1},{9,13},{13,9},{2,6},{6,2},{1... | collective-permute-start | bytes 368648 | tf_op jit(solution)/shard_map/ppermute | solution.py:332
  39.9 6.3 %collective-permute-start.9 = (bf16[160,384]{1,0:T(8,128)(2,1)S(1)}, bf16[160,384]{1,0:T(8,128)(2,1)S(1)}, u32[]{:S(2)}, u32[]{:S(2)}) collective-permute-start(bf16[160,384]{1,0:T(8,128)(2,1)S(1)} %get-tuple-element.29), channel_id=1, source_target_pairs={{4,8},{8,4},{5,9},{9,5},{6,10},{10,6},{7,11},{11,7},{20,24},{24,20... | collective-permute-start | bytes 368648 | tf_op jit(solution)/shard_map/ppermute | solution.py:333
  48.2 9.8 %collective-permute-start.11 = (bf16[2,320,384]{2,1,0:T(8,128)(2,1)S(1)}, bf16[2,320,384]{2,1,0:T(8,128)(2,1)S(1)}, u32[]{:S(2)}, u32[]{:S(2)}) collective-permute-start(bf16[2,320,384]{2,1,0:T(8,128)(2,1)S(1)} %next_edge.1), channel_id=1, source_target_pairs={{0,1},{2,3},{4,5},{6,7},{8,9},{10,11},{12,13},{14,15},{16,17},{18,... | collective-permute-start | bytes 1474568 | tf_op jit(solution)/shard_map/ppermute | solution.py:350
  49.5 10.2 %collective-permute-start.10 = (bf16[2,320,384]{2,1,0:T(8,128)(2,1)S(1)}, bf16[2,320,384]{2,1,0:T(8,128)(2,1)S(1)}, u32[]{:S(2)}, u32[]{:S(2)}) collective-permute-start(bf16[2,320,384]{2,1,0:T(8,128)(2,1)S(1)} %next_edge.1), channel_id=1, source_target_pairs={{1,2},{5,6},{9,10},{13,14},{17,18},{21,22},{25,26},{29,30}} | collective-permute-start | bytes 1474568 | tf_op jit(solution)/shard_map/ppermute | solution.py:349

commit v7 on v6

--- a/solution.py
+++ b/solution.py
@@ -61,6 +61,28 @@
     return route
 
 
+def pick_kernel(tile_ref, x_hbm, first, second, sem):
+    low = tile_ref[0] % 2
+
+    def move(a, b):
+        copies = [
+            pltpu.make_async_copy(x_hbm.at[a], first, sem.at[0]),
+            pltpu.make_async_copy(x_hbm.at[b], second, sem.at[1]),
+        ]
+        for copy in copies:
+            copy.start()
+        for copy in copies:
+            copy.wait()
+
+    @pl.when(low == 0)
+    def _():
+        move(0, 1)
+
+    @pl.when(low == 1)
+    def _():
+        move(1, 0)
+
+
 def load_small_kernel(w_qkv, w_out, gain, qkv_vm, out_vm, gain_vm, sem):
     copies = [
         pltpu.make_async_copy(w_qkv, qkv_vm, sem.at[0]),
@@ -85,39 +107,35 @@
         project_keys(block, gain_vec, w_qkv, kv_out, place)
 
 
-def attend_rows(cols, source, kv_parts, gain_vec, w_qkv, w_out, att_out):
+def attend_rows(source, kv_parts, gain_vec, w_qkv, w_out, att_out):
     ch = source.shape[1]
-    for row in range(source.shape[0] // cols):
-        part = slice(row * cols, (row + 1) * cols)
-        feats = source[part, :]
-        normed = rms_scale(feats, gain_vec).astype(bf16)
-        queries = dot32(normed, w_qkv[:, :ch]).astype(bf16)
-        scores = [
-            lax.dot_general(
-                queries, kv[:, :ch], (((1,), (1,)), ((), ())), preferred_element_type=f32
-            )
-            * (ch ** (-0.5) * LOG2E)
-            for kv in kv_parts
-        ]
-        top = functools.reduce(
-            jnp.maximum, [jnp.max(s, axis=1, keepdims=True) for s in scores]
+    feats = source[...]
+    normed = rms_scale(feats, gain_vec).astype(bf16)
+    queries = dot32(normed, w_qkv[:, :ch]).astype(bf16)
+    scores = [
+        lax.dot_general(
+            queries, kv[:, :ch], (((1,), (1,)), ((), ())), preferred_element_type=f32
         )
-        raised = [jnp.exp2(s - top) for s in scores]
-        total = sum(jnp.sum(r, axis=1, keepdims=True) for r in raised)
-        mixed = sum(dot32(r.astype(bf16), kv[:, ch:]) for r, kv in zip(raised, kv_parts))
-        mixture = (mixed / total).astype(bf16)
-        att_out[part, :] = (feats.astype(f32) + dot32(mixture, w_out[...])).astype(bf16)
-
-
-def attend_kernel(cols, other_b, own_a, kv_a, gain, w_qkv, w_out, kv_b, att_a):
+        * (ch ** (-0.5) * LOG2E)
+        for kv in kv_parts
+    ]
+    top = functools.reduce(jnp.maximum, [jnp.max(s, axis=1, keepdims=True) for s in scores])
+    raised = [jnp.exp2(s - top) for s in scores]
+    total = sum(jnp.sum(r, axis=1, keepdims=True) for r in raised)
+    mixed = sum(dot32(r.astype(bf16), kv[:, ch:]) for r, kv in zip(raised, kv_parts))
+    mixture = (mixed / total).astype(bf16)
+    att_out[...] = (feats.astype(f32) + dot32(mixture, w_out[...])).astype(bf16)
+
+
+def attend_kernel(other_b, own_a, kv_a, gain, w_qkv, w_out, kv_b, att_a):
     gain_vec = gain[...].reshape(1, own_a.shape[1])
     project_keys(other_b, gain_vec, w_qkv, kv_b, 0)
-    attend_rows(cols, own_a, (kv_a, kv_b), gain_vec, w_qkv, w_out, att_a)
-
-
-def attend_rest_kernel(cols, own_b, kv_a, kv_b, gain, w_qkv, w_out, att_b):
+    attend_rows(own_a, (kv_a, kv_b), gain_vec, w_qkv, w_out, att_a)
+
+
+def attend_rest_kernel(own_b, kv_a, kv_b, gain, w_qkv, w_out, att_b):
     gain_vec = gain[...].reshape(1, own_b.shape[1])
-    attend_rows(cols, own_b, (kv_a, kv_b), gain_vec, w_qkv, w_out, att_b)
+    attend_rows(own_b, (kv_a, kv_b), gain_vec, w_qkv, w_out, att_b)
 
 
 def load_kernel(_, w_hbm, w_vm, sem):
@@ -158,14 +176,10 @@
     activate(cols, tile_ref[0] % 2, got_a, gain, *outs)
 
 
-def activate_b_kernel(
-    cols, tile_ref, got_a, got_b, act_a, gain, _, attended, active, pair_edge, mid_edge
-):
+def activate_b_kernel(cols, tile_ref, got_b, act_a, gain, _, active, pair_edge, mid_edge):
     low = tile_ref[0] % 2
     activate(cols, low, got_b, gain, active.at[1 - low], pair_edge, mid_edge)
     active[low] = act_a[...]
-    attended[low] = got_a[...]
-    attended[1 - low] = got_b[...]
 
 
 def usable_flag(clips, frame_at, tap):
@@ -238,7 +252,25 @@
             out[f, part, :] = (shift_add(val, cols, ch) + partial[f, part, :]).astype(bf16)
 
 
-def own_kernel(cols, tile_ref, span_ref, clips, mid, pair_a, mid_a, pair_b, mid_b, w, out):
+def own_kernel(
+    cols,
+    tile_ref,
+    span_ref,
+    clips,
+    mid,
+    pair_a,
+    mid_a,
+    pair_b,
+    mid_b,
+    w,
+    got_a,
+    got_b,
+    out,
+    attended,
+):
+    low = tile_ref[0] % 2
+    attended[low] = got_a[...]
+    attended[1 - low] = got_b[...]
     ch = mid.shape[-1]
     above, below = edge_rows(tile_ref, pair_a, mid_a, pair_b, mid_b)
     wide = []
@@ -255,6 +287,22 @@
         out[1, part, :] = shift_add(after + back[part], cols, ch)
 
 
+def finish_kernel(span_ref, own, link_got, core_got, out):
+    span = span_ref[0]
+
+    @pl.when(span == 0)
+    def _():
+        out[...] = own[...].astype(bf16)
+
+    @pl.when(span % 2 == 1)
+    def _():
+        out[...] = (own[...] + core_got[...].astype(f32)).astype(bf16)
+
+    @pl.when(jnp.logical_and(span % 2 == 0, span > 0))
+    def _():
+        out[...] = (own[...] + link_got[...].astype(f32)).astype(bf16)
+
+
 def on_device(features, clip_lengths, norm_gain, w_qkv, w_out, conv_gain, w_conv):
     frames, row_count, cols, ch = features.shape
     tiles, spans = lax.axis_size("tile"), lax.axis_size("span")
@@ -266,10 +314,15 @@
     span = lax.axis_index("span").astype(jnp.int32).reshape(1)
     other_core = [(i, i ^ 1) for i in range(spans)]
     route_a, route_b = frame_route(spans, 0), frame_route(spans, 1)
-    low = tile[0] % 2
     x = features.reshape(frames, cells, ch)
-    send_a = lax.dynamic_index_in_dim(x, low, 0, keepdims=False)
-    send_b = lax.dynamic_index_in_dim(x, 1 - low, 0, keepdims=False)
+    send_a, send_b = call(
+        pick_kernel,
+        "pick",
+        (pltpu.VMEM((cells, ch), bf16), pltpu.VMEM((cells, ch), bf16)),
+        [SMEM, ANY],
+        [pltpu.SemaphoreType.DMA((2,))],
+        62,
+    )(tile, x)
     own_a = lax.ppermute(send_a, both, route_a)
     own_b = lax.ppermute(send_b, both, route_b)
     w_qkv, w_out, norm_gain = call(
@@ -289,7 +342,7 @@
         own_a, other_a, own_b, norm_gain, w_qkv
     )
     kv_b, att_a = call(
-        functools.partial(attend_kernel, cols),
+        attend_kernel,
         "attend",
         (struct((cells, 2 * ch)), struct((cells, ch))),
         [VMEM] * 6,
@@ -297,7 +350,7 @@
     )(other_b, own_a, kv_a, norm_gain, w_qkv, w_out)
     got_a = lax.ppermute(att_a, both, route_a)
     att_b = call(
-        functools.partial(attend_rest_kernel, cols),
+        attend_rest_kernel,
         "attend_rest",
         struct((cells, ch)),
         [VMEM] * 6,
@@ -323,12 +376,12 @@
     )(tile, got_a, conv_gain, w_packed)
     pair_a = lax.ppermute(pair_edge, "tile", pairs)
     mid_a = lax.ppermute(mid_edge, "tile", middle)
-    attended, active, pair_edge, mid_edge = call(
+    active, pair_edge, mid_edge = call(
         functools.partial(activate_b_kernel, cols),
         "activate_b",
-        (struct((frames, cells, ch)), struct((frames, cells, ch)), edge, edge),
-        [SMEM] + [VMEM] * 4 + [ANY],
-    )(tile, got_a, got_b, act_a, conv_gain, w_packed)
+        (struct((frames, cells, ch)), edge, edge),
+        [SMEM] + [VMEM] * 3 + [ANY],
+    )(tile, got_b, act_a, conv_gain, w_packed)
     pair_b = lax.ppermute(pair_edge, "tile", pairs)
     mid_b = lax.ppermute(mid_edge, "tile", middle)
     edges = (pair_a, mid_a, pair_b, mid_b)
@@ -346,12 +399,19 @@
         [SMEM] * 3 + [VMEM] * 6,
         flops=unit,
     )(*where, *edges, w_packed, started)
-    from_odd = lax.ppermute(for_next, "span", [(s, s + 1) for s in range(1, spans - 1, 2)])
-    from_even = lax.ppermute(for_next, "span", [(s, s + 1) for s in range(0, spans, 2)])
-    own = call(
-        functools.partial(own_kernel, cols), "own", sums, [SMEM] * 3 + [VMEM] * 6, flops=3 * unit
-    )(*where, active, *edges, w_packed)
-    hidden = (own + from_odd.astype(f32) + from_even.astype(f32)).astype(bf16)
+    link = [(s + d, s + 1 - d) for s in range(1, spans - 1, 2) for d in range(2)]
+    link_got = lax.ppermute(for_next, "span", link)
+    core_got = lax.ppermute(for_next, "span", other_core)
+    own, attended = call(
+        functools.partial(own_kernel, cols),
+        "own",
+        (sums, struct((frames, cells, ch))),
+        [SMEM] * 3 + [VMEM] * 8,
+        flops=3 * unit,
+    )(*where, active, *edges, w_packed, got_a, got_b)
+    hidden = call(
+        finish_kernel, "finish", struct((frames, cells, ch)), [SMEM] + [VMEM] * 3
+    )(span, own, link_got, core_got)
     shape = (frames, row_count, cols, ch)
     return attended.reshape(shape), hidden.reshape(shape)
 

time: 61.6 us -> 58.3 us (0.946); the launches traced: 60.6 us -> 58.1 us
  starting transfers between devices: 21.3 us -> 19.9 us
  local copies, waits for them, and re-layouts: 1.13 us -> 0.01 us
  other arithmetic: 0.95 us -> 0 us
  Pallas kernels: 21.7 us -> 22.6 us
    pallas_call x3 -> x5, Pallas kernels: 9.26 us -> 10.9 us  [the longest x1 4.62 us: on_device(): call(functools.partial(own_kernel, cols), 'own', (sums, struct((frames, c...]
    ppermute x2, starting transfers between devices: 5.9 us -> 4.4 us  [the longest x1 4.33 us: on_device(): link_got = lax.ppermute(for_next, 'span', link)]
    squeeze x1 -> x0, local copies, waits for them, and re-layouts: 1.12 us -> none  [on_device(): send_a = lax.dynamic_index_in_dim(x, low, 0, keepdims=False)]
    convert_element_type x1 -> x0, other arithmetic: 0.95 us -> none  [on_device(): hidden = (own + from_odd.astype(f32) + from_even.astype(f32)).astype(bf16)]
    pallas_call x1, Pallas kernels: 1.14 us -> 0.31 us  [on_device(): call(functools.partial(activate_b_kernel, cols), 'activate_b', (struct((f...]
where the time goes in v7:
time: 58.3 us; the launch traced here: 58.1 us
  Pallas kernels  22.6 us (39%)
  starting transfers between devices  19.9 us (34%)
  waiting for transfers between devices  14.7 us (25%)
  between operations  0.82 us (1%)
    ppermute x1, waiting for transfers between devices, on_device(): own_a = lax.ppermute(send_a, both, route_a)  6.34 us
    ppermute x1, starting transfers between devices, on_device(): own_a = lax.ppermute(send_a, both, route_a)  4.78 us
    pallas_call x1, Pallas kernels, on_device(): call(functools.partial(own_kernel, cols), 'own', (sums, struct((frames, c...  4.62 us
    ppermute x1, starting transfers between devices, on_device(): link_got = lax.ppermute(for_next, 'span', link)  4.33 us
    ppermute x1, starting transfers between devices, on_device(): got_a = lax.ppermute(att_a, both, route_a)  3.67 us
    pallas_call x1, Pallas kernels, on_device(): call(load_kernel, 'load_conv', struct((3, 3 * ch, 3 * ch)), [ANY, ANY], [...  3.48 us
    pallas_call x1, Pallas kernels, on_device(): call(functools.partial(next_own_kernel, cols), 'next_own', sums, [SMEM] *...  2.63 us
    ppermute x1, waiting for transfers between devices, on_device(): own_b = lax.ppermute(send_b, both, route_b)  2.63 us
  transfers between devices with their start and end apart: 12, of which 6 were waited for; matrix products, arithmetic and copies ran while one was open for 0% of the time, Pallas kernels for 28%

profile of v7, /device:TPU:13, one launch (start us, length us, event | category | flops | bytes accessed | tf_op | source)
XLA Modules:
  0.0 58.1 jit_solution(5358586268243672628)
XLA Ops:
  0.6 1.1 %pick.1 = (bf16[320,384]{1,0:T(8,128)(2,1)S(1)}, bf16[320,384]{1,0:T(8,128)(2,1)S(1)}) custom-call(s32[1]{0:T(128)} %bitcast.tile_ref, bf16[2,320,384]{2,1,0:T(8,128)(2,1)} %bitcast.5), custom_call_target="tpu_custom_call" | custom-call | bytes 1048576 | tf_op jit(solution)/shard_map/pick/pallas_call | solution.py:318
  1.7 4.8 %collective-permute-start.1 = (bf16[320,384]{1,0:T(8,128)(2,1)S(1)}, bf16[320,384]{1,0:T(8,128)(2,1)S(1)}, u32[]{:S(2)}, u32[]{:S(2)}) collective-permute-start(bf16[320,384]{1,0:T(8,128)(2,1)S(1)} %get-tuple-element.20), channel_id=1, source_target_pairs={{0,0},{1,8},{2,2},{3,10},{4,4},{5,12},{6,6},{7,14},{8,1},{9,9},{10... | collective-permute-start | bytes 737288 | tf_op jit(solution)/shard_map/ppermute | solution.py:326
  6.5 0.1 collective-permute-start
  6.6 1.9 %load_small.1 = (bf16[384,1152]{1,0:T(8,128)(2,1)S(1)}, bf16[384,384]{1,0:T(8,128)(2,1)S(1)}, f32[384]{0:T(512)S(1)}) custom-call(bf16[384,1152]{1,0:T(8,128)(2,1)} %w_qkv.1, bf16[384,384]{1,0:T(8,128)(2,1)} %w_out.1, f32[384]{0:T(512)} %gain.3), custom_call_target="tpu_custom_call" | custom-call | bytes 1048576 | tf_op jit(solution)/shard_map/load_small/pallas_call | solution.py:328
  8.5 6.3 %collective-permute-done.1.own_a = bf16[320,384]{1,0:T(8,128)(2,1)S(1)} collective-permute-done((bf16[320,384]{1,0:T(8,128)(2,1)S(1)}, bf16[320,384]{1,0:T(8,128)(2,1)S(1)}, u32[]{:S(2)}, u32[]{:S(2)}) %collective-permute-start.1) | collective-permute-done | bytes 245792 | tf_op jit(solution)/shard_map/ppermute | solution.py:326
  14.9 0.0 collective-permute-start.2
  14.9 2.6 %collective-permute-done.own_b = bf16[320,384]{1,0:T(8,128)(2,1)S(1)} collective-permute-done((bf16[320,384]{1,0:T(8,128)(2,1)S(1)}, bf16[320,384]{1,0:T(8,128)(2,1)S(1)}, u32[]{:S(2)}, u32[]{:S(2)}) %collective-permute-start) | collective-permute-done | bytes 245792 | tf_op jit(solution)/shard_map/ppermute | solution.py:327
  17.5 0.0 collective-permute-start.3
  17.5 0.0 collective-permute-done.2.other_a
  17.5 1.0 %keys.1.kv_a = bf16[960,768]{1,0:T(8,128)(2,1)S(1)} custom-call(bf16[320,384]{1,0:T(8,128)(2,1)S(1)} %collective-permute-done.1.own_a, bf16[320,384]{1,0:T(8,128)(2,1)S(1)} %collective-permute-done.2.other_a, bf16[320,384]{1,0:T(8,128)(2,1)S(1)} %collective-permute-done.own_b, f32[384]{0:T(512)S(1)} %get-tuple-element.23.gain, ...), custom_call_target="tpu_custom_call" | custom-call | flops 377487360 | bytes 1048576 | tf_op jit(solution)/shard_map/keys/pallas_call | solution.py:341
  18.5 0.5 collective-permute-done.3.other_b
  19.0 2.3 %attend.1 = (bf16[320,768]{1,0:T(8,128)(2,1)S(1)}, bf16[320,384]{1,0:T(8,128)(2,1)S(1)}) custom-call(bf16[320,384]{1,0:T(8,128)(2,1)S(1)} %collective-permute-done.3.other_b, bf16[320,384]{1,0:T(8,128)(2,1)S(1)} %collective-permute-done.1.own_a, bf16[960,768]{1,0:T(8,128)(2,1)S(1)} %keys.1.kv_a, f32[384]{0:T(512)S(1)} %get-tuple-element.23.gain, ...), custom_call_target="tpu_custom_call" | custom-call | flops 1195376640 | bytes 1048576 | tf_op jit(solution)/shard_map/attend/pallas_call | solution.py:344
  21.3 3.7 %collective-permute-start.5 = (bf16[320,384]{1,0:T(8,128)(2,1)S(1)}, bf16[320,384]{1,0:T(8,128)(2,1)S(1)}, u32[]{:S(2)}, u32[]{:S(2)}) collective-permute-start(bf16[320,384]{1,0:T(8,128)(2,1)S(1)} %get-tuple-element.27), channel_id=1, source_target_pairs={{0,0},{1,8},{2,2},{3,10},{4,4},{5,12},{6,6},{7,14},{8,1},{9,9},{10... | collective-permute-start | bytes 737288 | tf_op jit(solution)/shard_map/ppermute | solution.py:351
  25.0 2.1 %attend_rest.1._ = bf16[320,384]{1,0:T(8,128)(2,1)S(1)} custom-call(bf16[320,384]{1,0:T(8,128)(2,1)S(1)} %collective-permute-done.own_b, bf16[960,768]{1,0:T(8,128)(2,1)S(1)} %keys.1.kv_a, bf16[320,768]{1,0:T(8,128)(2,1)S(1)} %get-tuple-element.26.kv_b, f32[384]{0:T(512)S(1)} %get-tuple-element.23.gain, bf16[384,1152]{1,0:T(8,128)(2,1)S(1)} %get-tuple-element.24.w_qkv, ...), custom_call_target="tpu_custom_call" | custom-call | flops 2453667840 | bytes 1048576 | tf_op jit(solution)/shard_map/attend_rest/pallas_call | solution.py:352
  27.1 0.8 %collective-permute-start.4 = (bf16[320,384]{1,0:T(8,128)(2,1)S(1)}, bf16[320,384]{1,0:T(8,128)(2,1)S(1)}, u32[]{:S(2)}, u32[]{:S(2)}) collective-permute-start(bf16[320,384]{1,0:T(8,128)(2,1)S(1)} %attend_rest.1._), channel_id=1, source_target_pairs={{0,4},{1,12},{2,6},{3,14},{4,0},{5,8},{6,2},{7,10},{8,5},{9,13},{1... | collective-permute-start | bytes 737288 | tf_op jit(solution)/shard_map/ppermute | solution.py:359
  27.8 0.0 copy-start
  27.8 3.5 %load_conv.1._.w = bf16[3,1152,1152]{2,1,0:T(8,128)(2,1)S(1)} custom-call(bf16[320,384]{1,0:T(8,128)(2,1)S(1)} %attend_rest.1._, bf16[3,3,3,384,384]{4,3,2,1,0:T(8,128)(2,1)} %w_hbm.1), custom_call_target="tpu_custom_call" | custom-call | bytes 4096 | tf_op jit(solution)/shard_map/load_conv/pallas_call | solution.py:365
  31.3 0.0 copy-start.1
  31.3 0.0 collective-permute-done.5.got_a
  31.4 0.0 copy-done
  31.4 0.3 activate_a.1
  31.7 2.1 %collective-permute-start.6 = (bf16[160,384]{1,0:T(8,128)(2,1)S(1)}, bf16[160,384]{1,0:T(8,128)(2,1)S(1)}, u32[]{:S(2)}, u32[]{:S(2)}) collective-permute-start(bf16[160,384]{1,0:T(8,128)(2,1)S(1)} %get-tuple-element.30), channel_id=1, source_target_pairs={{0,4},{4,0},{8,12},{12,8},{1,5},{5,1},{9,13},{13,9},{2,6},{6,2},{1... | collective-permute-start | bytes 368648 | tf_op jit(solution)/shard_map/ppermute | solution.py:377
  33.8 1.9 %collective-permute-start.7 = (bf16[160,384]{1,0:T(8,128)(2,1)S(1)}, bf16[160,384]{1,0:T(8,128)(2,1)S(1)}, u32[]{:S(2)}, u32[]{:S(2)}) collective-permute-start(bf16[160,384]{1,0:T(8,128)(2,1)S(1)} %get-tuple-element.31), channel_id=1, source_target_pairs={{4,8},{8,4},{5,9},{9,5},{6,10},{10,6},{7,11},{11,7},{20,24},{24,20... | collective-permute-start | bytes 368648 | tf_op jit(solution)/shard_map/ppermute | solution.py:378
  35.7 1.7 %collective-permute-done.4.got_b = bf16[320,384]{1,0:T(8,128)(2,1)S(1)} collective-permute-done((bf16[320,384]{1,0:T(8,128)(2,1)S(1)}, bf16[320,384]{1,0:T(8,128)(2,1)S(1)}, u32[]{:S(2)}, u32[]{:S(2)}) %collective-permute-start.4) | collective-permute-done | bytes 245792 | tf_op jit(solution)/shard_map/ppermute | solution.py:359
  37.5 0.3 activate_b.1
  37.8 0.3 collective-permute-start.8
  38.1 1.9 %collective-permute-start.9 = (bf16[160,384]{1,0:T(8,128)(2,1)S(1)}, bf16[160,384]{1,0:T(8,128)(2,1)S(1)}, u32[]{:S(2)}, u32[]{:S(2)}) collective-permute-start(bf16[160,384]{1,0:T(8,128)(2,1)S(1)} %get-tuple-element.33), channel_id=1, source_target_pairs={{4,8},{8,4},{5,9},{9,5},{6,10},{10,6},{7,11},{11,7},{20,24},{24,20... | collective-permute-start | bytes 368648 | tf_op jit(solution)/shard_map/ppermute | solution.py:386
  40.0 0.0 copy-done.1
  40.0 2.6 %next_own.1.partial = f32[2,320,384]{2,1,0:T(8,128)S(1)} custom-call(s32[1]{0:T(128)} %bitcast.1.span_ref, s32[4]{0:T(128)S(1)} %copy-done.1, bf16[2,320,384]{2,1,0:T(8,128)(2,1)S(1)} %get-tuple-element.29.mid, bf16[3,1152,1152]{2,1,0:T(8,128)(2,1)S(1)} %load_conv.1._.w), custom_call_target="tpu_custom_call" | custom-call | flops 1698693120 | bytes 1048576 | tf_op jit(solution)/shard_map/next_own/pallas_call | solution.py:388
  42.6 0.0 collective-permute-done.6.pair_a
  42.6 0.0 collective-permute-done.7.mid_a
  42.7 0.0 collective-permute-done.8.pair_b
  42.7 1.7 %collective-permute-done.9.mid_b = bf16[160,384]{1,0:T(8,128)(2,1)S(1)} collective-permute-done((bf16[160,384]{1,0:T(8,128)(2,1)S(1)}, bf16[160,384]{1,0:T(8,128)(2,1)S(1)}, u32[]{:S(2)}, u32[]{:S(2)}) %collective-permute-start.9) | collective-permute-done | bytes 122912 | tf_op jit(solution)/shard_map/ppermute | solution.py:386
  44.3 2.0 %next_edge.1 = bf16[2,320,384]{2,1,0:T(8,128)(2,1)S(1)} custom-call(s32[1]{0:T(128)} %bitcast.tile_ref, s32[1]{0:T(128)} %bitcast.1.span_ref, s32[4]{0:T(128)S(1)} %copy-done.1, bf16[160,384]{1,0:T(8,128)(2,1)S(1)} %collective-permute-done.6.pair_a, bf16[160,384]{1,0:T(8,128)(2,1)S(1)} %collective-permute-done.7.mid_a, ...), custom_call_target="tpu_custom_call" | custom-call | flops 849346560 | bytes 1048576 | tf_op jit(solution)/shard_map/next_edge/pallas_call | solution.py:395
  46.3 4.3 %collective-permute-start.10 = (bf16[2,320,384]{2,1,0:T(8,128)(2,1)S(1)}, bf16[2,320,384]{2,1,0:T(8,128)(2,1)S(1)}, u32[]{:S(2)}, u32[]{:S(2)}) collective-permute-start(bf16[2,320,384]{2,1,0:T(8,128)(2,1)S(1)} %next_edge.1), channel_id=1, source_target_pairs={{1,2},{2,1},{5,6},{6,5},{9,10},{10,9},{13,14},{14,13},{17,18},{18,... | collective-permute-start | bytes 1474568 | tf_op jit(solution)/shard_map/ppermute | solution.py:403
  50.7 0.1 collective-permute-start.11
  50.8 4.6 %own.1 = (f32[2,320,384]{2,1,0:T(8,128)S(1)}, bf16[2,320,384]{2,1,0:T(8,128)(2,1)}) custom-call(s32[1]{0:T(128)} %bitcast.tile_ref, s32[1]{0:T(128)} %bitcast.1.span_ref, s32[4]{0:T(128)S(1)} %copy-done.1, bf16[2,320,384]{2,1,0:T(8,128)(2,1)S(1)} %get-tuple-element.29.mid, bf16[160,384]{1,0:T(8,128)(2,1)S(1)} %collective-permute-done.6.pair_a, ...), custom_call_target="tpu_custom_call" | custom-call | flops 2548039680 | bytes 1048576 | tf_op jit(solution)/shard_map/own/pallas_call | solution.py:405
  55.4 1.8 %collective-permute-done.10.link_got = bf16[2,320,384]{2,1,0:T(8,128)(2,1)S(1)} collective-permute-done((bf16[2,320,384]{2,1,0:T(8,128)(2,1)S(1)}, bf16[2,320,384]{2,1,0:T(8,128)(2,1)S(1)}, u32[]{:S(2)}, u32[]{:S(2)}) %collective-permute-start.10) | collective-permute-done | bytes 491552 | tf_op jit(solution)/shard_map/ppermute | solution.py:403
  57.2 0.0 collective-permute-done.11.core_got
  57.2 0.9 %finish.1 = bf16[2,320,384]{2,1,0:T(8,128)(2,1)} custom-call(s32[1]{0:T(128)} %bitcast.1.span_ref, f32[2,320,384]{2,1,0:T(8,128)S(1)} %get-tuple-element.35.own, bf16[2,320,384]{2,1,0:T(8,128)(2,1)S(1)} %collective-permute-done.10.link_got, bf16[2,320,384]{2,1,0:T(8,128)(2,1)S(1)} %collective-permute-done.11.core_got), custom_call_target="tpu_custom_call" | custom-call | bytes 1048576 | tf_op jit(solution)/shard_map/finish/pallas_call | solution.py:412
Async XLA Ops:
  1.7 13.1 %collective-permute-start.1 = (bf16[320,384]{1,0:T(8,128)(2,1)S(1)}, bf16[320,384]{1,0:T(8,128)(2,1)S(1)}, u32[]{:S(2)}, u32[]{:S(2)}) collective-permute-start(bf16[320,384]{1,0:T(8,128)(2,1)S(1)} %get-tuple-element.20), channel_id=1, source_target_pairs={{0,0},{1,8},{2,2},{3,10},{4,4},{5,12},{6,6},{7,14},{8,1},{9,9},{10... | collective-permute-start | bytes 737288 | tf_op jit(solution)/shard_map/ppermute | solution.py:326
  6.5 11.0 %collective-permute-start = (bf16[320,384]{1,0:T(8,128)(2,1)S(1)}, bf16[320,384]{1,0:T(8,128)(2,1)S(1)}, u32[]{:S(2)}, u32[]{:S(2)}) collective-permute-start(bf16[320,384]{1,0:T(8,128)(2,1)S(1)} %get-tuple-element.19), channel_id=1, source_target_pairs={{0,4},{1,12},{2,6},{3,14},{4,0},{5,8},{6,2},{7,10},{8,5},{9,13},{1... | collective-permute-start | bytes 737288 | tf_op jit(solution)/shard_map/ppermute | solution.py:327
  14.9 2.6 %collective-permute-start.2 = (bf16[320,384]{1,0:T(8,128)(2,1)S(1)}, bf16[320,384]{1,0:T(8,128)(2,1)S(1)}, u32[]{:S(2)}, u32[]{:S(2)}) collective-permute-start(bf16[320,384]{1,0:T(8,128)(2,1)S(1)} %collective-permute-done.1.own_a), channel_id=1, source_target_pairs={{0,1},{1,0},{2,3},{3,2},{4,5},{5,4},{6,7},{7,6},{8,9},{9,8},{10,11... | collective-permute-start | bytes 737288 | tf_op jit(solution)/shard_map/ppermute | solution.py:337
  17.5 1.5 %collective-permute-start.3 = (bf16[320,384]{1,0:T(8,128)(2,1)S(1)}, bf16[320,384]{1,0:T(8,128)(2,1)S(1)}, u32[]{:S(2)}, u32[]{:S(2)}) collective-permute-start(bf16[320,384]{1,0:T(8,128)(2,1)S(1)} %collective-permute-done.own_b), channel_id=1, source_target_pairs={{0,1},{1,0},{2,3},{3,2},{4,5},{5,4},{6,7},{7,6},{8,9},{9,8},{10,11... | collective-permute-start | bytes 737288 | tf_op jit(solution)/shard_map/ppermute | solution.py:338
  21.3 10.0 %collective-permute-start.5 = (bf16[320,384]{1,0:T(8,128)(2,1)S(1)}, bf16[320,384]{1,0:T(8,128)(2,1)S(1)}, u32[]{:S(2)}, u32[]{:S(2)}) collective-permute-start(bf16[320,384]{1,0:T(8,128)(2,1)S(1)} %get-tuple-element.27), channel_id=1, source_target_pairs={{0,0},{1,8},{2,2},{3,10},{4,4},{5,12},{6,6},{7,14},{8,1},{9,9},{10... | collective-permute-start | bytes 737288 | tf_op jit(solution)/shard_map/ppermute | solution.py:351
  27.1 10.4 %collective-permute-start.4 = (bf16[320,384]{1,0:T(8,128)(2,1)S(1)}, bf16[320,384]{1,0:T(8,128)(2,1)S(1)}, u32[]{:S(2)}, u32[]{:S(2)}) collective-permute-start(bf16[320,384]{1,0:T(8,128)(2,1)S(1)} %attend_rest.1._), channel_id=1, source_target_pairs={{0,4},{1,12},{2,6},{3,14},{4,0},{5,8},{6,2},{7,10},{8,5},{9,13},{1... | collective-permute-start | bytes 737288 | tf_op jit(solution)/shard_map/ppermute | solution.py:359
  27.8 3.5 %copy-start = (f32[384]{0:T(512)S(1)}, f32[384]{0:T(512)}, u32[]{:S(2)}) copy-start(f32[384]{0:T(512)} %gain.5) | copy-start | bytes 4612
  31.3 8.6 %copy-start.1 = (s32[4]{0:T(128)S(1)}, s32[4]{0:T(128)}, u32[]{:S(2)}) copy-start(s32[4]{0:T(128)} %clips.5) | copy-start | bytes 52
  31.7 11.0 %collective-permute-start.6 = (bf16[160,384]{1,0:T(8,128)(2,1)S(1)}, bf16[160,384]{1,0:T(8,128)(2,1)S(1)}, u32[]{:S(2)}, u32[]{:S(2)}) collective-permute-start(bf16[160,384]{1,0:T(8,128)(2,1)S(1)} %get-tuple-element.30), channel_id=1, source_target_pairs={{0,4},{4,0},{8,12},{12,8},{1,5},{5,1},{9,13},{13,9},{2,6},{6,2},{1... | collective-permute-start | bytes 368648 | tf_op jit(solution)/shard_map/ppermute | solution.py:377
  33.8 8.9 %collective-permute-start.7 = (bf16[160,384]{1,0:T(8,128)(2,1)S(1)}, bf16[160,384]{1,0:T(8,128)(2,1)S(1)}, u32[]{:S(2)}, u32[]{:S(2)}) collective-permute-start(bf16[160,384]{1,0:T(8,128)(2,1)S(1)} %get-tuple-element.31), channel_id=1, source_target_pairs={{4,8},{8,4},{5,9},{9,5},{6,10},{10,6},{7,11},{11,7},{20,24},{24,20... | collective-permute-start | bytes 368648 | tf_op jit(solution)/shard_map/ppermute | solution.py:378
  37.8 4.9 %collective-permute-start.8 = (bf16[160,384]{1,0:T(8,128)(2,1)S(1)}, bf16[160,384]{1,0:T(8,128)(2,1)S(1)}, u32[]{:S(2)}, u32[]{:S(2)}) collective-permute-start(bf16[160,384]{1,0:T(8,128)(2,1)S(1)} %get-tuple-element.32), channel_id=1, source_target_pairs={{0,4},{4,0},{8,12},{12,8},{1,5},{5,1},{9,13},{13,9},{2,6},{6,2},{1... | collective-permute-start | bytes 368648 | tf_op jit(solution)/shard_map/ppermute | solution.py:385
  38.1 6.3 %collective-permute-start.9 = (bf16[160,384]{1,0:T(8,128)(2,1)S(1)}, bf16[160,384]{1,0:T(8,128)(2,1)S(1)}, u32[]{:S(2)}, u32[]{:S(2)}) collective-permute-start(bf16[160,384]{1,0:T(8,128)(2,1)S(1)} %get-tuple-element.33), channel_id=1, source_target_pairs={{4,8},{8,4},{5,9},{9,5},{6,10},{10,6},{7,11},{11,7},{20,24},{24,20... | collective-permute-start | bytes 368648 | tf_op jit(solution)/shard_map/ppermute | solution.py:386
  46.3 10.8 %collective-permute-start.10 = (bf16[2,320,384]{2,1,0:T(8,128)(2,1)S(1)}, bf16[2,320,384]{2,1,0:T(8,128)(2,1)S(1)}, u32[]{:S(2)}, u32[]{:S(2)}) collective-permute-start(bf16[2,320,384]{2,1,0:T(8,128)(2,1)S(1)} %next_edge.1), channel_id=1, source_target_pairs={{1,2},{2,1},{5,6},{6,5},{9,10},{10,9},{13,14},{14,13},{17,18},{18,... | collective-permute-start | bytes 1474568 | tf_op jit(solution)/shard_map/ppermute | solution.py:403
  50.7 6.5 %collective-permute-start.11 = (bf16[2,320,384]{2,1,0:T(8,128)(2,1)S(1)}, bf16[2,320,384]{2,1,0:T(8,128)(2,1)S(1)}, u32[]{:S(2)}, u32[]{:S(2)}) collective-permute-start(bf16[2,320,384]{2,1,0:T(8,128)(2,1)S(1)} %next_edge.1), channel_id=1, source_target_pairs={{0,1},{1,0},{2,3},{3,2},{4,5},{5,4},{6,7},{7,6},{8,9},{9,8},{10,11... | collective-permute-start | bytes 1474568 | tf_op jit(solution)/shard_map/ppermute | solution.py:404

commit v8 on v7

--- a/solution.py
+++ b/solution.py
@@ -156,7 +156,7 @@
         copy.wait()
 
 
-def activate(cols, low, block, gain, act_out, pair_edge, mid_edge):
+def activate(cols, low, block, gain, act_out, mid_edge, pair_edge):
     lifted = rms_scale(block[...], gain[...].reshape(1, block.shape[1]))
     act = (lifted / (1.0 + jnp.exp(-lifted))).astype(bf16)
     act_out[...] = act
@@ -176,9 +176,9 @@
     activate(cols, tile_ref[0] % 2, got_a, gain, *outs)
 
 
-def activate_b_kernel(cols, tile_ref, got_b, act_a, gain, _, active, pair_edge, mid_edge):
+def activate_b_kernel(cols, tile_ref, got_b, act_a, gain, _, active, mid_edge, pair_edge):
     low = tile_ref[0] % 2
-    activate(cols, low, got_b, gain, active.at[1 - low], pair_edge, mid_edge)
+    activate(cols, low, got_b, gain, active.at[1 - low], mid_edge, pair_edge)
     active[low] = act_a[...]
 
 
@@ -208,15 +208,16 @@
     ]
 
 
-def edge_rows(tile_ref, pair_a, mid_a, pair_b, mid_b):
-    odd = (tile_ref[0] % 2).astype(f32)
-
-    def pick(if_odd, if_even):
-        return if_odd[...].astype(f32) * odd + if_even[...].astype(f32) * (1.0 - odd)
-
-    above = [pick(pair_a, mid_b), pick(pair_b, mid_a)]
-    below = [pick(mid_a, pair_b), pick(mid_b, pair_a)]
-    return above, below
+def with_edges(tile_ref, pair_a, mid_a, pair_b, mid_b, body):
+    odd = tile_ref[0] % 2 == 1
+
+    @pl.when(odd)
+    def _():
+        body((pair_a, pair_b), (mid_a, mid_b))
+
+    @pl.when(jnp.logical_not(odd))
+    def _():
+        body((mid_b, mid_a), (pair_b, pair_a))
 
 
 def next_own_kernel(cols, span_ref, clips, mid, w, out):
@@ -235,21 +236,24 @@
 
 
 def next_edge_kernel(
-    cols, tile_ref, span_ref, clips, pair_a, mid_a, pair_b, mid_b, w, partial, out
+    cols, tile_ref, span_ref, clips, mid_a, pair_a, mid_b, pair_b, w, partial, out
 ):
     ch = w.shape[-1] // 3
     flag = flags_of(clips, (span_ref[0] + 1) * 2)
-    above, below = edge_rows(tile_ref, pair_a, mid_a, pair_b, mid_b)
-    for edge, part, taps in (
-        (above, slice(0, cols), slice(0, ch)),
-        (below, slice(cols, 2 * cols), slice(2 * ch, 3 * ch)),
-    ):
-        last = jnp.concatenate([edge[0] * flag[0][0], edge[1] * flag[1][0]], axis=0).astype(bf16)
-        middle = (edge[1] * flag[0][1]).astype(bf16)
-        far = dot32(last, w[0, taps])
-        near = far[:cols] + dot32(middle, w[1, taps])
-        for f, val in ((0, near), (1, far[cols:])):
-            out[f, part, :] = (shift_add(val, cols, ch) + partial[f, part, :]).astype(bf16)
+
+    def body(above, below):
+        for edge, part, taps in (
+            (above, slice(0, cols), slice(0, ch)),
+            (below, slice(cols, 2 * cols), slice(2 * ch, 3 * ch)),
+        ):
+            first, second = edge[0][...], edge[1][...]
+            last = jnp.concatenate([weigh(flag[0][0], first), weigh(flag[1][0], second)], axis=0)
+            far = dot32(last, w[0, taps])
+            near = far[:cols] + dot32(weigh(flag[0][1], second), w[1, taps])
+            for f, val in ((0, near), (1, far[cols:])):
+                out[f, part, :] = (shift_add(val, cols, ch) + partial[f, part, :]).astype(bf16)
+
+    with_edges(tile_ref, pair_a, mid_a, pair_b, mid_b, body)
 
 
 def own_kernel(
@@ -258,10 +262,10 @@
     span_ref,
     clips,
     mid,
+    mid_a,
     pair_a,
-    mid_a,
+    mid_b,
     pair_b,
-    mid_b,
     w,
     got_a,
     got_b,
@@ -272,19 +276,22 @@
     attended[low] = got_a[...]
     attended[1 - low] = got_b[...]
     ch = mid.shape[-1]
-    above, below = edge_rows(tile_ref, pair_a, mid_a, pair_b, mid_b)
-    wide = []
-    for f in range(2):
-        rows = [above[f].astype(bf16), mid[f, :cols, :], mid[f, cols:, :], below[f].astype(bf16)]
-        wide += [jnp.concatenate(rows[r : r + 3], axis=1) for r in range(2)]
-    here = dot32(jnp.concatenate(wide, axis=0), w[2])
     flag = usable_flag(clips, span_ref[0] * 2 + 1, 1).astype(f32)
-    back = dot32(weigh(flag, jnp.concatenate(wide[:2], axis=0)), w[1])
-    for r in range(2):
-        part = slice(r * cols, (r + 1) * cols)
-        out[0, part, :] = shift_add(here[part], cols, ch)
-        after = here[(2 + r) * cols : (3 + r) * cols]
-        out[1, part, :] = shift_add(after + back[part], cols, ch)
+
+    def body(above, below):
+        wide = []
+        for f in range(2):
+            rows = [above[f][...], mid[f, :cols, :], mid[f, cols:, :], below[f][...]]
+            wide += [jnp.concatenate(rows[r : r + 3], axis=1) for r in range(2)]
+        here = dot32(jnp.concatenate(wide, axis=0), w[2])
+        back = dot32(weigh(flag, jnp.concatenate(wide[:2], axis=0)), w[1])
+        for r in range(2):
+            part = slice(r * cols, (r + 1) * cols)
+            out[0, part, :] = shift_add(here[part], cols, ch)
+            after = here[(2 + r) * cols : (3 + r) * cols]
+            out[1, part, :] = shift_add(after + back[part], cols, ch)
+
+    with_edges(tile_ref, pair_a, mid_a, pair_b, mid_b, body)
 
 
 def finish_kernel(span_ref, own, link_got, core_got, out):
@@ -371,20 +378,20 @@
         42,
         size=1 << 12,
     )(att_b, w_conv)
-    act_a, pair_edge, mid_edge = call(
+    act_a, mid_edge, pair_edge = call(
         functools.partial(activate_a_kernel, cols), "activate_a", (one, edge, edge), [SMEM, VMEM, VMEM, ANY]
     )(tile, got_a, conv_gain, w_packed)
+    mid_a = lax.ppermute(mid_edge, "tile", middle)
     pair_a = lax.ppermute(pair_edge, "tile", pairs)
-    mid_a = lax.ppermute(mid_edge, "tile", middle)
-    active, pair_edge, mid_edge = call(
+    active, mid_edge, pair_edge = call(
         functools.partial(activate_b_kernel, cols),
         "activate_b",
         (struct((frames, cells, ch)), edge, edge),
         [SMEM] + [VMEM] * 3 + [ANY],
     )(tile, got_b, act_a, conv_gain, w_packed)
+    mid_b = lax.ppermute(mid_edge, "tile", middle)
     pair_b = lax.ppermute(pair_edge, "tile", pairs)
-    mid_b = lax.ppermute(mid_edge, "tile", middle)
-    edges = (pair_a, mid_a, pair_b, mid_b)
+    edges = (mid_a, pair_a, mid_b, pair_b)
     started = call(
         functools.partial(next_own_kernel, cols),
         "next_own",

time: 58.3 us -> 60.2 us (1.033); the launches traced: 58.1 us -> 59.2 us
  waiting for transfers between devices: 14.7 us -> 17.4 us
  starting transfers between devices: 19.9 us -> 18.1 us
    ppermute x1, waiting for transfers between devices: 1.75 us -> 4.37 us  [on_device(): got_b = lax.ppermute(att_b, both, route_b)]
    ppermute x1, starting transfers between devices: 2.12 us -> 0.81 us  [on_device(): pair_a = lax.ppermute(pair_edge, 'tile', pairs)]
    ppermute x1, waiting for transfers between devices: 0.01 us -> 0.8 us  [on_device(): pair_b = lax.ppermute(pair_edge, 'tile', pairs)]
  transfers between devices with their start and end apart: 12 -> 12, of which waited for: 6 -> 7; matrix products, arithmetic and copies ran while one was open for 0% -> 0% of each run, Pallas kernels for 28% -> 28%
where the time goes in v8:
time: 60.2 us; the launch traced here: 59.2 us
  Pallas kernels  22.8 us (38%)
  starting transfers between devices  18.1 us (30%)
  waiting for transfers between devices  17.4 us (29%)
  between operations  0.82 us (1%)
    ppermute x1, waiting for transfers between devices, on_device(): own_a = lax.ppermute(send_a, both, route_a)  6.34 us
    pallas_call x1, Pallas kernels, on_device(): call(functools.partial(own_kernel, cols), 'own', (sums, struct((frames, c...  4.87 us
    ppermute x1, starting transfers between devices, on_device(): own_a = lax.ppermute(send_a, both, route_a)  4.78 us
    ppermute x1, waiting for transfers between devices, on_device(): got_b = lax.ppermute(att_b, both, route_b)  4.37 us
    ppermute x1, starting transfers between devices, on_device(): link_got = lax.ppermute(for_next, 'span', link)  4.02 us
    ppermute x1, starting transfers between devices, on_device(): got_a = lax.ppermute(att_a, both, route_a)  3.68 us
    pallas_call x1, Pallas kernels, on_device(): call(load_kernel, 'load_conv', struct((3, 3 * ch, 3 * ch)), [ANY, ANY], [...  3.48 us
    ppermute x1, waiting for transfers between devices, on_device(): own_b = lax.ppermute(send_b, both, route_b)  2.63 us
  transfers between devices with their start and end apart: 12, of which 7 were waited for; matrix products, arithmetic and copies ran while one was open for 0% of the time, Pallas kernels for 28%

profile of v8, /device:TPU:13, one launch (start us, length us, event | category | flops | bytes accessed | tf_op | source)
XLA Modules:
  0.0 59.2 jit_solution(8661539267564514855)
XLA Ops:
  0.6 1.1 %pick.1 = (bf16[320,384]{1,0:T(8,128)(2,1)S(1)}, bf16[320,384]{1,0:T(8,128)(2,1)S(1)}) custom-call(s32[1]{0:T(128)} %bitcast.tile_ref, bf16[2,320,384]{2,1,0:T(8,128)(2,1)} %bitcast.5), custom_call_target="tpu_custom_call" | custom-call | bytes 1048576 | tf_op jit(solution)/shard_map/pick/pallas_call | solution.py:325
  1.7 4.8 %collective-permute-start.1 = (bf16[320,384]{1,0:T(8,128)(2,1)S(1)}, bf16[320,384]{1,0:T(8,128)(2,1)S(1)}, u32[]{:S(2)}, u32[]{:S(2)}) collective-permute-start(bf16[320,384]{1,0:T(8,128)(2,1)S(1)} %get-tuple-element.20), channel_id=1, source_target_pairs={{0,0},{1,8},{2,2},{3,10},{4,4},{5,12},{6,6},{7,14},{8,1},{9,9},{10... | collective-permute-start | bytes 737288 | tf_op jit(solution)/shard_map/ppermute | solution.py:333
  6.5 0.1 collective-permute-start
  6.6 1.9 %load_small.1 = (bf16[384,1152]{1,0:T(8,128)(2,1)S(1)}, bf16[384,384]{1,0:T(8,128)(2,1)S(1)}, f32[384]{0:T(512)S(1)}) custom-call(bf16[384,1152]{1,0:T(8,128)(2,1)} %w_qkv.1, bf16[384,384]{1,0:T(8,128)(2,1)} %w_out.1, f32[384]{0:T(512)} %gain.3), custom_call_target="tpu_custom_call" | custom-call | bytes 1048576 | tf_op jit(solution)/shard_map/load_small/pallas_call | solution.py:335
  8.5 6.3 %collective-permute-done.1.own_a = bf16[320,384]{1,0:T(8,128)(2,1)S(1)} collective-permute-done((bf16[320,384]{1,0:T(8,128)(2,1)S(1)}, bf16[320,384]{1,0:T(8,128)(2,1)S(1)}, u32[]{:S(2)}, u32[]{:S(2)}) %collective-permute-start.1) | collective-permute-done | bytes 245792 | tf_op jit(solution)/shard_map/ppermute | solution.py:333
  14.9 0.0 collective-permute-start.2
  14.9 2.6 %collective-permute-done.own_b = bf16[320,384]{1,0:T(8,128)(2,1)S(1)} collective-permute-done((bf16[320,384]{1,0:T(8,128)(2,1)S(1)}, bf16[320,384]{1,0:T(8,128)(2,1)S(1)}, u32[]{:S(2)}, u32[]{:S(2)}) %collective-permute-start) | collective-permute-done | bytes 245792 | tf_op jit(solution)/shard_map/ppermute | solution.py:334
  17.5 0.0 collective-permute-start.3
  17.5 0.0 collective-permute-done.2.other_a
  17.5 1.0 %keys.1.kv_a = bf16[960,768]{1,0:T(8,128)(2,1)S(1)} custom-call(bf16[320,384]{1,0:T(8,128)(2,1)S(1)} %collective-permute-done.1.own_a, bf16[320,384]{1,0:T(8,128)(2,1)S(1)} %collective-permute-done.2.other_a, bf16[320,384]{1,0:T(8,128)(2,1)S(1)} %collective-permute-done.own_b, f32[384]{0:T(512)S(1)} %get-tuple-element.23.gain, ...), custom_call_target="tpu_custom_call" | custom-call | flops 377487360 | bytes 1048576 | tf_op jit(solution)/shard_map/keys/pallas_call | solution.py:348
  18.5 0.5 collective-permute-done.3.other_b
  19.0 2.3 %attend.1 = (bf16[320,768]{1,0:T(8,128)(2,1)S(1)}, bf16[320,384]{1,0:T(8,128)(2,1)S(1)}) custom-call(bf16[320,384]{1,0:T(8,128)(2,1)S(1)} %collective-permute-done.3.other_b, bf16[320,384]{1,0:T(8,128)(2,1)S(1)} %collective-permute-done.1.own_a, bf16[960,768]{1,0:T(8,128)(2,1)S(1)} %keys.1.kv_a, f32[384]{0:T(512)S(1)} %get-tuple-element.23.gain, ...), custom_call_target="tpu_custom_call" | custom-call | flops 1195376640 | bytes 1048576 | tf_op jit(solution)/shard_map/attend/pallas_call | solution.py:351
  21.3 3.7 %collective-permute-start.5 = (bf16[320,384]{1,0:T(8,128)(2,1)S(1)}, bf16[320,384]{1,0:T(8,128)(2,1)S(1)}, u32[]{:S(2)}, u32[]{:S(2)}) collective-permute-start(bf16[320,384]{1,0:T(8,128)(2,1)S(1)} %get-tuple-element.27), channel_id=1, source_target_pairs={{0,0},{1,8},{2,2},{3,10},{4,4},{5,12},{6,6},{7,14},{8,1},{9,9},{10... | collective-permute-start | bytes 737288 | tf_op jit(solution)/shard_map/ppermute | solution.py:358
  25.0 2.1 %attend_rest.1._ = bf16[320,384]{1,0:T(8,128)(2,1)S(1)} custom-call(bf16[320,384]{1,0:T(8,128)(2,1)S(1)} %collective-permute-done.own_b, bf16[960,768]{1,0:T(8,128)(2,1)S(1)} %keys.1.kv_a, bf16[320,768]{1,0:T(8,128)(2,1)S(1)} %get-tuple-element.26.kv_b, f32[384]{0:T(512)S(1)} %get-tuple-element.23.gain, bf16[384,1152]{1,0:T(8,128)(2,1)S(1)} %get-tuple-element.24.w_qkv, ...), custom_call_target="tpu_custom_call" | custom-call | flops 2453667840 | bytes 1048576 | tf_op jit(solution)/shard_map/attend_rest/pallas_call | solution.py:359
  27.1 0.8 %collective-permute-start.4 = (bf16[320,384]{1,0:T(8,128)(2,1)S(1)}, bf16[320,384]{1,0:T(8,128)(2,1)S(1)}, u32[]{:S(2)}, u32[]{:S(2)}) collective-permute-start(bf16[320,384]{1,0:T(8,128)(2,1)S(1)} %attend_rest.1._), channel_id=1, source_target_pairs={{0,4},{1,12},{2,6},{3,14},{4,0},{5,8},{6,2},{7,10},{8,5},{9,13},{1... | collective-permute-start | bytes 737288 | tf_op jit(solution)/shard_map/ppermute | solution.py:366
  27.8 0.0 copy-start
  27.8 3.5 %load_conv.1._.w = bf16[3,1152,1152]{2,1,0:T(8,128)(2,1)S(1)} custom-call(bf16[320,384]{1,0:T(8,128)(2,1)S(1)} %attend_rest.1._, bf16[3,3,3,384,384]{4,3,2,1,0:T(8,128)(2,1)} %w_hbm.1), custom_call_target="tpu_custom_call" | custom-call | bytes 4096 | tf_op jit(solution)/shard_map/load_conv/pallas_call | solution.py:372
  31.3 0.0 copy-start.1
  31.3 0.0 collective-permute-done.5.got_a
  31.4 0.0 copy-done
  31.4 0.3 activate_a.1
  31.7 1.9 %collective-permute-start.6 = (bf16[160,384]{1,0:T(8,128)(2,1)S(1)}, bf16[160,384]{1,0:T(8,128)(2,1)S(1)}, u32[]{:S(2)}, u32[]{:S(2)}) collective-permute-start(bf16[160,384]{1,0:T(8,128)(2,1)S(1)} %get-tuple-element.30), channel_id=1, source_target_pairs={{4,8},{8,4},{5,9},{9,5},{6,10},{10,6},{7,11},{11,7},{20,24},{24,20... | collective-permute-start | bytes 368648 | tf_op jit(solution)/shard_map/ppermute | solution.py:384
  33.6 0.8 %collective-permute-start.7 = (bf16[160,384]{1,0:T(8,128)(2,1)S(1)}, bf16[160,384]{1,0:T(8,128)(2,1)S(1)}, u32[]{:S(2)}, u32[]{:S(2)}) collective-permute-start(bf16[160,384]{1,0:T(8,128)(2,1)S(1)} %get-tuple-element.31), channel_id=1, source_target_pairs={{0,4},{4,0},{8,12},{12,8},{1,5},{5,1},{9,13},{13,9},{2,6},{6,2},{1... | collective-permute-start | bytes 368648 | tf_op jit(solution)/shard_map/ppermute | solution.py:385
  34.4 4.4 %collective-permute-done.4.got_b = bf16[320,384]{1,0:T(8,128)(2,1)S(1)} collective-permute-done((bf16[320,384]{1,0:T(8,128)(2,1)S(1)}, bf16[320,384]{1,0:T(8,128)(2,1)S(1)}, u32[]{:S(2)}, u32[]{:S(2)}) %collective-permute-start.4) | collective-permute-done | bytes 245792 | tf_op jit(solution)/shard_map/ppermute | solution.py:366
  38.8 0.3 activate_b.1
  39.1 1.9 %collective-permute-start.8 = (bf16[160,384]{1,0:T(8,128)(2,1)S(1)}, bf16[160,384]{1,0:T(8,128)(2,1)S(1)}, u32[]{:S(2)}, u32[]{:S(2)}) collective-permute-start(bf16[160,384]{1,0:T(8,128)(2,1)S(1)} %get-tuple-element.32), channel_id=1, source_target_pairs={{4,8},{8,4},{5,9},{9,5},{6,10},{10,6},{7,11},{11,7},{20,24},{24,20... | collective-permute-start | bytes 368648 | tf_op jit(solution)/shard_map/ppermute | solution.py:392
  41.0 0.1 collective-permute-start.9
  41.1 0.0 copy-done.1
  41.1 2.6 %next_own.1.partial = f32[2,320,384]{2,1,0:T(8,128)S(1)} custom-call(s32[1]{0:T(128)} %bitcast.1.span_ref, s32[4]{0:T(128)S(1)} %copy-done.1, bf16[2,320,384]{2,1,0:T(8,128)(2,1)S(1)} %get-tuple-element.29.mid, bf16[3,1152,1152]{2,1,0:T(8,128)(2,1)S(1)} %load_conv.1._.w), custom_call_target="tpu_custom_call" | custom-call | flops 1698693120 | bytes 1048576 | tf_op jit(solution)/shard_map/next_own/pallas_call | solution.py:395
  43.8 0.0 collective-permute-done.6.mid_a
  43.8 0.0 collective-permute-done.7.pair_a
  43.8 1.2 %collective-permute-done.8.mid_b = bf16[160,384]{1,0:T(8,128)(2,1)S(1)} collective-permute-done((bf16[160,384]{1,0:T(8,128)(2,1)S(1)}, bf16[160,384]{1,0:T(8,128)(2,1)S(1)}, u32[]{:S(2)}, u32[]{:S(2)}) %collective-permute-start.8) | collective-permute-done | bytes 122912 | tf_op jit(solution)/shard_map/ppermute | solution.py:392
  45.0 0.8 %collective-permute-done.9.pair_b = bf16[160,384]{1,0:T(8,128)(2,1)S(1)} collective-permute-done((bf16[160,384]{1,0:T(8,128)(2,1)S(1)}, bf16[160,384]{1,0:T(8,128)(2,1)S(1)}, u32[]{:S(2)}, u32[]{:S(2)}) %collective-permute-start.9) | collective-permute-done | bytes 122912 | tf_op jit(solution)/shard_map/ppermute | solution.py:393
  45.8 2.0 %next_edge.1 = bf16[2,320,384]{2,1,0:T(8,128)(2,1)S(1)} custom-call(s32[1]{0:T(128)} %bitcast.tile_ref, s32[1]{0:T(128)} %bitcast.1.span_ref, s32[4]{0:T(128)S(1)} %copy-done.1, bf16[160,384]{1,0:T(8,128)(2,1)S(1)} %collective-permute-done.6.mid_a, bf16[160,384]{1,0:T(8,128)(2,1)S(1)} %collective-permute-done.7.pair_a, ...), custom_call_target="tpu_custom_call" | custom-call | flops 849346560 | bytes 1048576 | tf_op jit(solution)/shard_map/next_edge/pallas_call | solution.py:402
  47.8 4.0 %collective-permute-start.10 = (bf16[2,320,384]{2,1,0:T(8,128)(2,1)S(1)}, bf16[2,320,384]{2,1,0:T(8,128)(2,1)S(1)}, u32[]{:S(2)}, u32[]{:S(2)}) collective-permute-start(bf16[2,320,384]{2,1,0:T(8,128)(2,1)S(1)} %next_edge.1), channel_id=1, source_target_pairs={{1,2},{2,1},{5,6},{6,5},{9,10},{10,9},{13,14},{14,13},{17,18},{18,... | collective-permute-start | bytes 1474568 | tf_op jit(solution)/shard_map/ppermute | solution.py:410
  51.9 0.1 collective-permute-start.11
  51.9 4.9 %own.1 = (f32[2,320,384]{2,1,0:T(8,128)S(1)}, bf16[2,320,384]{2,1,0:T(8,128)(2,1)}) custom-call(s32[1]{0:T(128)} %bitcast.tile_ref, s32[1]{0:T(128)} %bitcast.1.span_ref, s32[4]{0:T(128)S(1)} %copy-done.1, bf16[2,320,384]{2,1,0:T(8,128)(2,1)S(1)} %get-tuple-element.29.mid, bf16[160,384]{1,0:T(8,128)(2,1)S(1)} %collective-permute-done.6.mid_a, ...), custom_call_target="tpu_custom_call" | custom-call | flops 2548039680 | bytes 1048576 | tf_op jit(solution)/shard_map/own/pallas_call | solution.py:412
  56.8 1.6 %collective-permute-done.10.link_got = bf16[2,320,384]{2,1,0:T(8,128)(2,1)S(1)} collective-permute-done((bf16[2,320,384]{2,1,0:T(8,128)(2,1)S(1)}, bf16[2,320,384]{2,1,0:T(8,128)(2,1)S(1)}, u32[]{:S(2)}, u32[]{:S(2)}) %collective-permute-start.10) | collective-permute-done | bytes 491552 | tf_op jit(solution)/shard_map/ppermute | solution.py:410
  58.4 0.0 collective-permute-done.11.core_got
  58.4 0.9 %finish.1 = bf16[2,320,384]{2,1,0:T(8,128)(2,1)} custom-call(s32[1]{0:T(128)} %bitcast.1.span_ref, f32[2,320,384]{2,1,0:T(8,128)S(1)} %get-tuple-element.35.own, bf16[2,320,384]{2,1,0:T(8,128)(2,1)S(1)} %collective-permute-done.10.link_got, bf16[2,320,384]{2,1,0:T(8,128)(2,1)S(1)} %collective-permute-done.11.core_got), custom_call_target="tpu_custom_call" | custom-call | bytes 1048576 | tf_op jit(solution)/shard_map/finish/pallas_call | solution.py:419
Async XLA Ops:
  1.7 13.1 %collective-permute-start.1 = (bf16[320,384]{1,0:T(8,128)(2,1)S(1)}, bf16[320,384]{1,0:T(8,128)(2,1)S(1)}, u32[]{:S(2)}, u32[]{:S(2)}) collective-permute-start(bf16[320,384]{1,0:T(8,128)(2,1)S(1)} %get-tuple-element.20), channel_id=1, source_target_pairs={{0,0},{1,8},{2,2},{3,10},{4,4},{5,12},{6,6},{7,14},{8,1},{9,9},{10... | collective-permute-start | bytes 737288 | tf_op jit(solution)/shard_map/ppermute | solution.py:333
  6.5 11.0 %collective-permute-start = (bf16[320,384]{1,0:T(8,128)(2,1)S(1)}, bf16[320,384]{1,0:T(8,128)(2,1)S(1)}, u32[]{:S(2)}, u32[]{:S(2)}) collective-permute-start(bf16[320,384]{1,0:T(8,128)(2,1)S(1)} %get-tuple-element.19), channel_id=1, source_target_pairs={{0,4},{1,12},{2,6},{3,14},{4,0},{5,8},{6,2},{7,10},{8,5},{9,13},{1... | collective-permute-start | bytes 737288 | tf_op jit(solution)/shard_map/ppermute | solution.py:334
  14.9 2.6 %collective-permute-start.2 = (bf16[320,384]{1,0:T(8,128)(2,1)S(1)}, bf16[320,384]{1,0:T(8,128)(2,1)S(1)}, u32[]{:S(2)}, u32[]{:S(2)}) collective-permute-start(bf16[320,384]{1,0:T(8,128)(2,1)S(1)} %collective-permute-done.1.own_a), channel_id=1, source_target_pairs={{0,1},{1,0},{2,3},{3,2},{4,5},{5,4},{6,7},{7,6},{8,9},{9,8},{10,11... | collective-permute-start | bytes 737288 | tf_op jit(solution)/shard_map/ppermute | solution.py:344
  17.5 1.5 %collective-permute-start.3 = (bf16[320,384]{1,0:T(8,128)(2,1)S(1)}, bf16[320,384]{1,0:T(8,128)(2,1)S(1)}, u32[]{:S(2)}, u32[]{:S(2)}) collective-permute-start(bf16[320,384]{1,0:T(8,128)(2,1)S(1)} %collective-permute-done.own_b), channel_id=1, source_target_pairs={{0,1},{1,0},{2,3},{3,2},{4,5},{5,4},{6,7},{7,6},{8,9},{9,8},{10,11... | collective-permute-start | bytes 737288 | tf_op jit(solution)/shard_map/ppermute | solution.py:345
  21.3 10.0 %collective-permute-start.5 = (bf16[320,384]{1,0:T(8,128)(2,1)S(1)}, bf16[320,384]{1,0:T(8,128)(2,1)S(1)}, u32[]{:S(2)}, u32[]{:S(2)}) collective-permute-start(bf16[320,384]{1,0:T(8,128)(2,1)S(1)} %get-tuple-element.27), channel_id=1, source_target_pairs={{0,0},{1,8},{2,2},{3,10},{4,4},{5,12},{6,6},{7,14},{8,1},{9,9},{10... | collective-permute-start | bytes 737288 | tf_op jit(solution)/shard_map/ppermute | solution.py:358
  27.1 11.7 %collective-permute-start.4 = (bf16[320,384]{1,0:T(8,128)(2,1)S(1)}, bf16[320,384]{1,0:T(8,128)(2,1)S(1)}, u32[]{:S(2)}, u32[]{:S(2)}) collective-permute-start(bf16[320,384]{1,0:T(8,128)(2,1)S(1)} %attend_rest.1._), channel_id=1, source_target_pairs={{0,4},{1,12},{2,6},{3,14},{4,0},{5,8},{6,2},{7,10},{8,5},{9,13},{1... | collective-permute-start | bytes 737288 | tf_op jit(solution)/shard_map/ppermute | solution.py:366
  27.8 3.5 %copy-start = (f32[384]{0:T(512)S(1)}, f32[384]{0:T(512)}, u32[]{:S(2)}) copy-start(f32[384]{0:T(512)} %gain.5) | copy-start | bytes 4612
  31.3 9.8 %copy-start.1 = (s32[4]{0:T(128)S(1)}, s32[4]{0:T(128)}, u32[]{:S(2)}) copy-start(s32[4]{0:T(128)} %clips.5) | copy-start | bytes 52
  31.7 12.1 %collective-permute-start.6 = (bf16[160,384]{1,0:T(8,128)(2,1)S(1)}, bf16[160,384]{1,0:T(8,128)(2,1)S(1)}, u32[]{:S(2)}, u32[]{:S(2)}) collective-permute-start(bf16[160,384]{1,0:T(8,128)(2,1)S(1)} %get-tuple-element.30), channel_id=1, source_target_pairs={{4,8},{8,4},{5,9},{9,5},{6,10},{10,6},{7,11},{11,7},{20,24},{24,20... | collective-permute-start | bytes 368648 | tf_op jit(solution)/shard_map/ppermute | solution.py:384
  33.6 10.2 %collective-permute-start.7 = (bf16[160,384]{1,0:T(8,128)(2,1)S(1)}, bf16[160,384]{1,0:T(8,128)(2,1)S(1)}, u32[]{:S(2)}, u32[]{:S(2)}) collective-permute-start(bf16[160,384]{1,0:T(8,128)(2,1)S(1)} %get-tuple-element.31), channel_id=1, source_target_pairs={{0,4},{4,0},{8,12},{12,8},{1,5},{5,1},{9,13},{13,9},{2,6},{6,2},{1... | collective-permute-start | bytes 368648 | tf_op jit(solution)/shard_map/ppermute | solution.py:385
  39.1 5.9 %collective-permute-start.8 = (bf16[160,384]{1,0:T(8,128)(2,1)S(1)}, bf16[160,384]{1,0:T(8,128)(2,1)S(1)}, u32[]{:S(2)}, u32[]{:S(2)}) collective-permute-start(bf16[160,384]{1,0:T(8,128)(2,1)S(1)} %get-tuple-element.32), channel_id=1, source_target_pairs={{4,8},{8,4},{5,9},{9,5},{6,10},{10,6},{7,11},{11,7},{20,24},{24,20... | collective-permute-start | bytes 368648 | tf_op jit(solution)/shard_map/ppermute | solution.py:392
  41.0 4.8 %collective-permute-start.9 = (bf16[160,384]{1,0:T(8,128)(2,1)S(1)}, bf16[160,384]{1,0:T(8,128)(2,1)S(1)}, u32[]{:S(2)}, u32[]{:S(2)}) collective-permute-start(bf16[160,384]{1,0:T(8,128)(2,1)S(1)} %get-tuple-element.33), channel_id=1, source_target_pairs={{0,4},{4,0},{8,12},{12,8},{1,5},{5,1},{9,13},{13,9},{2,6},{6,2},{1... | collective-permute-start | bytes 368648 | tf_op jit(solution)/shard_map/ppermute | solution.py:393
  47.8 10.5 %collective-permute-start.10 = (bf16[2,320,384]{2,1,0:T(8,128)(2,1)S(1)}, bf16[2,320,384]{2,1,0:T(8,128)(2,1)S(1)}, u32[]{:S(2)}, u32[]{:S(2)}) collective-permute-start(bf16[2,320,384]{2,1,0:T(8,128)(2,1)S(1)} %next_edge.1), channel_id=1, source_target_pairs={{1,2},{2,1},{5,6},{6,5},{9,10},{10,9},{13,14},{14,13},{17,18},{18,... | collective-permute-start | bytes 1474568 | tf_op jit(solution)/shard_map/ppermute | solution.py:410
  51.9 6.5 %collective-permute-start.11 = (bf16[2,320,384]{2,1,0:T(8,128)(2,1)S(1)}, bf16[2,320,384]{2,1,0:T(8,128)(2,1)S(1)}, u32[]{:S(2)}, u32[]{:S(2)}) collective-permute-start(bf16[2,320,384]{2,1,0:T(8,128)(2,1)S(1)} %next_edge.1), channel_id=1, source_target_pairs={{0,1},{1,0},{2,3},{3,2},{4,5},{5,4},{6,7},{7,6},{8,9},{9,8},{10,11... | collective-permute-start | bytes 1474568 | tf_op jit(solution)/shard_map/ppermute | solution.py:411

commit v9 on v7

--- a/solution.py
+++ b/solution.py
@@ -234,22 +234,47 @@
         out[1, part, :] = shift_add(far[cols:], cols, ch)
 
 
-def next_edge_kernel(
-    cols, tile_ref, span_ref, clips, pair_a, mid_a, pair_b, mid_b, w, partial, out
-):
+def edge_part(cols, flag, first, second, above, w, partial, put):
     ch = w.shape[-1] // 3
+    part = slice(0, cols) if above else slice(cols, 2 * cols)
+    taps = slice(0, ch) if above else slice(2 * ch, 3 * ch)
+    last = jnp.concatenate([weigh(flag[0][0], first), weigh(flag[1][0], second)], axis=0)
+    far = dot32(last, w[0, taps])
+    near = far[:cols] + dot32(weigh(flag[0][1], second), w[1, taps])
+    for f, val in ((0, near), (1, far[cols:])):
+        put(f, part, (shift_add(val, cols, ch) + partial[f, part, :]).astype(bf16))
+
+
+def pair_edge_kernel(cols, tile_ref, span_ref, clips, pair_a, pair_b, w, partial, out):
     flag = flags_of(clips, (span_ref[0] + 1) * 2)
-    above, below = edge_rows(tile_ref, pair_a, mid_a, pair_b, mid_b)
-    for edge, part, taps in (
-        (above, slice(0, cols), slice(0, ch)),
-        (below, slice(cols, 2 * cols), slice(2 * ch, 3 * ch)),
-    ):
-        last = jnp.concatenate([edge[0] * flag[0][0], edge[1] * flag[1][0]], axis=0).astype(bf16)
-        middle = (edge[1] * flag[0][1]).astype(bf16)
-        far = dot32(last, w[0, taps])
-        near = far[:cols] + dot32(middle, w[1, taps])
-        for f, val in ((0, near), (1, far[cols:])):
-            out[f, part, :] = (shift_add(val, cols, ch) + partial[f, part, :]).astype(bf16)
+
+    def put(f, part, val):
+        out[f] = val
+
+    @pl.when(tile_ref[0] % 2 == 1)
+    def _():
+        edge_part(cols, flag, pair_a[...], pair_b[...], True, w, partial, put)
+
+    @pl.when(tile_ref[0] % 2 == 0)
+    def _():
+        edge_part(cols, flag, pair_b[...], pair_a[...], False, w, partial, put)
+
+
+def mid_edge_kernel(cols, tile_ref, span_ref, clips, mid_a, mid_b, w, partial, pair_rows, out):
+    flag = flags_of(clips, (span_ref[0] + 1) * 2)
+
+    def put(f, part, val):
+        out[f, part, :] = val
+
+    @pl.when(tile_ref[0] % 2 == 1)
+    def _():
+        out[:, :cols, :] = pair_rows[...]
+        edge_part(cols, flag, mid_a[...], mid_b[...], False, w, partial, put)
+
+    @pl.when(tile_ref[0] % 2 == 0)
+    def _():
+        out[:, cols:, :] = pair_rows[...]
+        edge_part(cols, flag, mid_b[...], mid_a[...], True, w, partial, put)
 
 
 def own_kernel(
@@ -287,20 +312,34 @@
         out[1, part, :] = shift_add(after + back[part], cols, ch)
 
 
-def finish_kernel(span_ref, own, link_got, core_got, out):
+def finish_kernel(cols, span_ref, own, link_got, core_got, out_hbm, held, sem):
     span = span_ref[0]
-
-    @pl.when(span == 0)
-    def _():
-        out[...] = own[...].astype(bf16)
-
-    @pl.when(span % 2 == 1)
-    def _():
-        out[...] = (own[...] + core_got[...].astype(f32)).astype(bf16)
-
-    @pl.when(jnp.logical_and(span % 2 == 0, span > 0))
-    def _():
-        out[...] = (own[...] + link_got[...].astype(f32)).astype(bf16)
+    copies = []
+    for f in range(2):
+        for r in range(2):
+            part = slice(r * cols, (r + 1) * cols)
+
+            @pl.when(span == 0)
+            def _(f=f, part=part):
+                held[f, part, :] = own[f, part, :].astype(bf16)
+
+            @pl.when(span % 2 == 1)
+            def _(f=f, part=part):
+                total = own[f, part, :] + core_got[f, part, :].astype(f32)
+                held[f, part, :] = total.astype(bf16)
+
+            @pl.when(jnp.logical_and(span % 2 == 0, span > 0))
+            def _(f=f, part=part):
+                total = own[f, part, :] + link_got[f, part, :].astype(f32)
+                held[f, part, :] = total.astype(bf16)
+
+            copy = pltpu.make_async_copy(
+                held.at[f, part], out_hbm.at[f, part], sem.at[2 * f + r]
+            )
+            copy.start()
+            copies.append(copy)
+    for copy in copies:
+        copy.wait()
 
 
 def on_device(features, clip_lengths, norm_gain, w_qkv, w_out, conv_gain, w_conv):
@@ -392,13 +431,20 @@
         [SMEM] * 2 + [VMEM] * 2,
         flops=2 * unit,
     )(span, clip_lengths, active, w_packed)
+    pair_rows = call(
+        functools.partial(pair_edge_kernel, cols),
+        "pair_edge",
+        struct((frames, cols, ch)),
+        [SMEM] * 3 + [VMEM] * 4,
+        flops=unit // 2,
+    )(*where, pair_a, pair_b, w_packed, started)
     for_next = call(
-        functools.partial(next_edge_kernel, cols),
-        "next_edge",
+        functools.partial(mid_edge_kernel, cols),
+        "mid_edge",
         struct((frames, cells, ch)),
-        [SMEM] * 3 + [VMEM] * 6,
-        flops=unit,
-    )(*where, *edges, w_packed, started)
+        [SMEM] * 3 + [VMEM] * 5,
+        flops=unit // 2,
+    )(*where, mid_a, mid_b, w_packed, started, pair_rows)
     link = [(s + d, s + 1 - d) for s in range(1, spans - 1, 2) for d in range(2)]
     link_got = lax.ppermute(for_next, "span", link)
     core_got = lax.ppermute(for_next, "span", other_core)
@@ -409,8 +455,17 @@
         [SMEM] * 3 + [VMEM] * 8,
         flops=3 * unit,
     )(*where, active, *edges, w_packed, got_a, got_b)
-    hidden = call(
-        finish_kernel, "finish", struct((frames, cells, ch)), [SMEM] + [VMEM] * 3
+    hidden = pl.pallas_call(
+        functools.partial(finish_kernel, cols),
+        out_shape=struct((frames, cells, ch)),
+        in_specs=[SMEM] + [VMEM] * 3,
+        out_specs=ANY,
+        scratch_shapes=[
+            pltpu.VMEM((frames, cells, ch), bf16),
+            pltpu.SemaphoreType.DMA((4,)),
+        ],
+        compiler_params=pltpu.CompilerParams(vmem_limit_bytes=16 << 20),
+        name="finish",
     )(span, own, link_got, core_got)
     shape = (frames, row_count, cols, ch)
     return attended.reshape(shape), hidden.reshape(shape)

time: 58.3 us -> 58.6 us (level)
  waiting for transfers between devices: 14.7 us -> 13.2 us
  starting transfers between devices: 19.9 us -> 20.9 us
  Pallas kernels: 22.6 us -> 23.3 us
    ppermute x1, waiting for transfers between devices: 1.69 us -> 0.3 us  [on_device(): mid_b = lax.ppermute(mid_edge, 'tile', middle)]
    ppermute x1, starting transfers between devices: 4.33 us -> 5.26 us  [on_device(): link_got = lax.ppermute(for_next, 'span', link)]
    pallas_call x2 -> x3, Pallas kernels: 2.86 us -> 3.59 us  [the longest x1 1.39 us: on_device(): call(functools.partial(mid_edge_kernel, cols), 'mid_edge', struct((frames...]
  transfers between devices with their start and end apart: 12 -> 12, of which waited for: 6 -> 6; matrix products, arithmetic and copies ran while one was open for 0% -> 0% of each run, Pallas kernels for 28% -> 30%
where the time goes in v9:
time: 58.6 us; the launch traced here: 58.3 us
  Pallas kernels  23.3 us (40%)
  starting transfers between devices  20.9 us (36%)
  waiting for transfers between devices  13.2 us (23%)
  between operations  0.99 us (2%)
    ppermute x1, waiting for transfers between devices, on_device(): own_a = lax.ppermute(send_a, both, route_a)  6.34 us
    ppermute x1, starting transfers between devices, on_device(): link_got = lax.ppermute(for_next, 'span', link)  5.26 us
    ppermute x1, starting transfers between devices, on_device(): own_a = lax.ppermute(send_a, both, route_a)  4.78 us
    pallas_call x1, Pallas kernels, on_device(): call(functools.partial(own_kernel, cols), 'own', (sums, struct((frames, c...  4.62 us
    ppermute x1, starting transfers between devices, on_device(): got_a = lax.ppermute(att_a, both, route_a)  3.68 us
    pallas_call x1, Pallas kernels, on_device(): call(load_kernel, 'load_conv', struct((3, 3 * ch, 3 * ch)), [ANY, ANY], [...  3.48 us
    pallas_call x1, Pallas kernels, on_device(): call(functools.partial(next_own_kernel, cols), 'next_own', sums, [SMEM] *...  2.63 us
    ppermute x1, waiting for transfers between devices, on_device(): own_b = lax.ppermute(send_b, both, route_b)  2.63 us
  transfers between devices with their start and end apart: 12, of which 6 were waited for; matrix products, arithmetic and copies ran while one was open for 0% of the time, Pallas kernels for 30%

profile of v9, /device:TPU:13, one launch (start us, length us, event | category | flops | bytes accessed | tf_op | source)
XLA Modules:
  0.0 58.3 jit_solution(13240097723228312916)
XLA Ops:
  0.6 1.1 %pick.1 = (bf16[320,384]{1,0:T(8,128)(2,1)S(1)}, bf16[320,384]{1,0:T(8,128)(2,1)S(1)}) custom-call(s32[1]{0:T(128)} %bitcast.tile_ref, bf16[2,320,384]{2,1,0:T(8,128)(2,1)} %bitcast.5), custom_call_target="tpu_custom_call" | custom-call | bytes 1048576 | tf_op jit(solution)/shard_map/pick/pallas_call | solution.py:357
  1.7 4.8 %collective-permute-start.1 = (bf16[320,384]{1,0:T(8,128)(2,1)S(1)}, bf16[320,384]{1,0:T(8,128)(2,1)S(1)}, u32[]{:S(2)}, u32[]{:S(2)}) collective-permute-start(bf16[320,384]{1,0:T(8,128)(2,1)S(1)} %get-tuple-element.20), channel_id=1, source_target_pairs={{0,0},{1,8},{2,2},{3,10},{4,4},{5,12},{6,6},{7,14},{8,1},{9,9},{10... | collective-permute-start | bytes 737288 | tf_op jit(solution)/shard_map/ppermute | solution.py:365
  6.5 0.1 collective-permute-start
  6.6 1.9 %load_small.1 = (bf16[384,1152]{1,0:T(8,128)(2,1)S(1)}, bf16[384,384]{1,0:T(8,128)(2,1)S(1)}, f32[384]{0:T(512)S(1)}) custom-call(bf16[384,1152]{1,0:T(8,128)(2,1)} %w_qkv.1, bf16[384,384]{1,0:T(8,128)(2,1)} %w_out.1, f32[384]{0:T(512)} %gain.3), custom_call_target="tpu_custom_call" | custom-call | bytes 1048576 | tf_op jit(solution)/shard_map/load_small/pallas_call | solution.py:367
  8.5 6.3 %collective-permute-done.1.own_a = bf16[320,384]{1,0:T(8,128)(2,1)S(1)} collective-permute-done((bf16[320,384]{1,0:T(8,128)(2,1)S(1)}, bf16[320,384]{1,0:T(8,128)(2,1)S(1)}, u32[]{:S(2)}, u32[]{:S(2)}) %collective-permute-start.1) | collective-permute-done | bytes 245792 | tf_op jit(solution)/shard_map/ppermute | solution.py:365
  14.9 0.0 collective-permute-start.2
  14.9 2.6 %collective-permute-done.own_b = bf16[320,384]{1,0:T(8,128)(2,1)S(1)} collective-permute-done((bf16[320,384]{1,0:T(8,128)(2,1)S(1)}, bf16[320,384]{1,0:T(8,128)(2,1)S(1)}, u32[]{:S(2)}, u32[]{:S(2)}) %collective-permute-start) | collective-permute-done | bytes 245792 | tf_op jit(solution)/shard_map/ppermute | solution.py:366
  17.5 0.0 collective-permute-start.3
  17.5 0.0 collective-permute-done.2.other_a
  17.5 1.0 %keys.1.kv_a = bf16[960,768]{1,0:T(8,128)(2,1)S(1)} custom-call(bf16[320,384]{1,0:T(8,128)(2,1)S(1)} %collective-permute-done.1.own_a, bf16[320,384]{1,0:T(8,128)(2,1)S(1)} %collective-permute-done.2.other_a, bf16[320,384]{1,0:T(8,128)(2,1)S(1)} %collective-permute-done.own_b, f32[384]{0:T(512)S(1)} %get-tuple-element.23.gain, ...), custom_call_target="tpu_custom_call" | custom-call | flops 377487360 | bytes 1048576 | tf_op jit(solution)/shard_map/keys/pallas_call | solution.py:380
  18.5 0.5 collective-permute-done.3.other_b
  19.0 2.3 %attend.1 = (bf16[320,768]{1,0:T(8,128)(2,1)S(1)}, bf16[320,384]{1,0:T(8,128)(2,1)S(1)}) custom-call(bf16[320,384]{1,0:T(8,128)(2,1)S(1)} %collective-permute-done.3.other_b, bf16[320,384]{1,0:T(8,128)(2,1)S(1)} %collective-permute-done.1.own_a, bf16[960,768]{1,0:T(8,128)(2,1)S(1)} %keys.1.kv_a, f32[384]{0:T(512)S(1)} %get-tuple-element.23.gain, ...), custom_call_target="tpu_custom_call" | custom-call | flops 1195376640 | bytes 1048576 | tf_op jit(solution)/shard_map/attend/pallas_call | solution.py:383
  21.3 3.7 %collective-permute-start.5 = (bf16[320,384]{1,0:T(8,128)(2,1)S(1)}, bf16[320,384]{1,0:T(8,128)(2,1)S(1)}, u32[]{:S(2)}, u32[]{:S(2)}) collective-permute-start(bf16[320,384]{1,0:T(8,128)(2,1)S(1)} %get-tuple-element.27), channel_id=1, source_target_pairs={{0,0},{1,8},{2,2},{3,10},{4,4},{5,12},{6,6},{7,14},{8,1},{9,9},{10... | collective-permute-start | bytes 737288 | tf_op jit(solution)/shard_map/ppermute | solution.py:390
  25.0 2.1 %attend_rest.1._ = bf16[320,384]{1,0:T(8,128)(2,1)S(1)} custom-call(bf16[320,384]{1,0:T(8,128)(2,1)S(1)} %collective-permute-done.own_b, bf16[960,768]{1,0:T(8,128)(2,1)S(1)} %keys.1.kv_a, bf16[320,768]{1,0:T(8,128)(2,1)S(1)} %get-tuple-element.26.kv_b, f32[384]{0:T(512)S(1)} %get-tuple-element.23.gain, bf16[384,1152]{1,0:T(8,128)(2,1)S(1)} %get-tuple-element.24.w_qkv, ...), custom_call_target="tpu_custom_call" | custom-call | flops 2453667840 | bytes 1048576 | tf_op jit(solution)/shard_map/attend_rest/pallas_call | solution.py:391
  27.1 0.8 %collective-permute-start.4 = (bf16[320,384]{1,0:T(8,128)(2,1)S(1)}, bf16[320,384]{1,0:T(8,128)(2,1)S(1)}, u32[]{:S(2)}, u32[]{:S(2)}) collective-permute-start(bf16[320,384]{1,0:T(8,128)(2,1)S(1)} %attend_rest.1._), channel_id=1, source_target_pairs={{0,4},{1,12},{2,6},{3,14},{4,0},{5,8},{6,2},{7,10},{8,5},{9,13},{1... | collective-permute-start | bytes 737288 | tf_op jit(solution)/shard_map/ppermute | solution.py:398
  27.8 0.0 copy-start
  27.8 3.5 %load_conv.1._.w = bf16[3,1152,1152]{2,1,0:T(8,128)(2,1)S(1)} custom-call(bf16[320,384]{1,0:T(8,128)(2,1)S(1)} %attend_rest.1._, bf16[3,3,3,384,384]{4,3,2,1,0:T(8,128)(2,1)} %w_hbm.1), custom_call_target="tpu_custom_call" | custom-call | bytes 4096 | tf_op jit(solution)/shard_map/load_conv/pallas_call | solution.py:404
  31.3 0.0 copy-start.1
  31.3 0.0 collective-permute-done.5.got_a
  31.4 0.0 copy-done
  31.4 0.3 activate_a.1
  31.7 2.1 %collective-permute-start.6 = (bf16[160,384]{1,0:T(8,128)(2,1)S(1)}, bf16[160,384]{1,0:T(8,128)(2,1)S(1)}, u32[]{:S(2)}, u32[]{:S(2)}) collective-permute-start(bf16[160,384]{1,0:T(8,128)(2,1)S(1)} %get-tuple-element.30), channel_id=1, source_target_pairs={{0,4},{4,0},{8,12},{12,8},{1,5},{5,1},{9,13},{13,9},{2,6},{6,2},{1... | collective-permute-start | bytes 368648 | tf_op jit(solution)/shard_map/ppermute | solution.py:416
  33.8 1.9 %collective-permute-start.7 = (bf16[160,384]{1,0:T(8,128)(2,1)S(1)}, bf16[160,384]{1,0:T(8,128)(2,1)S(1)}, u32[]{:S(2)}, u32[]{:S(2)}) collective-permute-start(bf16[160,384]{1,0:T(8,128)(2,1)S(1)} %get-tuple-element.31), channel_id=1, source_target_pairs={{4,8},{8,4},{5,9},{9,5},{6,10},{10,6},{7,11},{11,7},{20,24},{24,20... | collective-permute-start | bytes 368648 | tf_op jit(solution)/shard_map/ppermute | solution.py:417
  35.7 1.7 %collective-permute-done.4.got_b = bf16[320,384]{1,0:T(8,128)(2,1)S(1)} collective-permute-done((bf16[320,384]{1,0:T(8,128)(2,1)S(1)}, bf16[320,384]{1,0:T(8,128)(2,1)S(1)}, u32[]{:S(2)}, u32[]{:S(2)}) %collective-permute-start.4) | collective-permute-done | bytes 245792 | tf_op jit(solution)/shard_map/ppermute | solution.py:398
  37.5 0.3 activate_b.1
  37.8 0.3 collective-permute-start.8
  38.1 1.9 %collective-permute-start.9 = (bf16[160,384]{1,0:T(8,128)(2,1)S(1)}, bf16[160,384]{1,0:T(8,128)(2,1)S(1)}, u32[]{:S(2)}, u32[]{:S(2)}) collective-permute-start(bf16[160,384]{1,0:T(8,128)(2,1)S(1)} %get-tuple-element.33), channel_id=1, source_target_pairs={{4,8},{8,4},{5,9},{9,5},{6,10},{10,6},{7,11},{11,7},{20,24},{24,20... | collective-permute-start | bytes 368648 | tf_op jit(solution)/shard_map/ppermute | solution.py:425
  40.0 0.0 copy-done.1
  40.0 2.6 %next_own.1.partial = f32[2,320,384]{2,1,0:T(8,128)S(1)} custom-call(s32[1]{0:T(128)} %bitcast.1.span_ref, s32[4]{0:T(128)S(1)} %copy-done.1, bf16[2,320,384]{2,1,0:T(8,128)(2,1)S(1)} %get-tuple-element.29.mid, bf16[3,1152,1152]{2,1,0:T(8,128)(2,1)S(1)} %load_conv.1._.w), custom_call_target="tpu_custom_call" | custom-call | flops 1698693120 | bytes 1048576 | tf_op jit(solution)/shard_map/next_own/pallas_call | solution.py:427
  42.6 0.0 collective-permute-done.6.pair_a
  42.6 0.0 collective-permute-done.8.pair_b
  42.6 1.4 %pair_edge.1.pair_rows = bf16[2,160,384]{2,1,0:T(8,128)(2,1)S(1)} custom-call(s32[1]{0:T(128)} %bitcast.tile_ref, s32[1]{0:T(128)} %bitcast.1.span_ref, s32[4]{0:T(128)S(1)} %copy-done.1, bf16[160,384]{1,0:T(8,128)(2,1)S(1)} %collective-permute-done.6.pair_a, bf16[160,384]{1,0:T(8,128)(2,1)S(1)} %collective-permute-done.8.pair_b, ...), custom_call_target="tpu_custom_call" | custom-call | flops 424673280 | bytes 1048576 | tf_op jit(solution)/shard_map/pair_edge/pallas_call | solution.py:434
  44.0 0.0 collective-permute-done.7.mid_a
  44.0 0.3 collective-permute-done.9.mid_b
  44.3 1.4 %mid_edge.1 = bf16[2,320,384]{2,1,0:T(8,128)(2,1)S(1)} custom-call(s32[1]{0:T(128)} %bitcast.tile_ref, s32[1]{0:T(128)} %bitcast.1.span_ref, s32[4]{0:T(128)S(1)} %copy-done.1, bf16[160,384]{1,0:T(8,128)(2,1)S(1)} %collective-permute-done.7.mid_a, bf16[160,384]{1,0:T(8,128)(2,1)S(1)} %collective-permute-done.9.mid_b, ...), custom_call_target="tpu_custom_call" | custom-call | flops 424673280 | bytes 1048576 | tf_op jit(solution)/shard_map/mid_edge/pallas_call | solution.py:441
  45.7 5.3 %collective-permute-start.10 = (bf16[2,320,384]{2,1,0:T(8,128)(2,1)S(1)}, bf16[2,320,384]{2,1,0:T(8,128)(2,1)S(1)}, u32[]{:S(2)}, u32[]{:S(2)}) collective-permute-start(bf16[2,320,384]{2,1,0:T(8,128)(2,1)S(1)} %mid_edge.1), channel_id=1, source_target_pairs={{1,2},{2,1},{5,6},{6,5},{9,10},{10,9},{13,14},{14,13},{17,18},{18,... | collective-permute-start | bytes 1474568 | tf_op jit(solution)/shard_map/ppermute | solution.py:449
  51.0 0.1 collective-permute-start.11
  51.1 4.6 %own.1 = (f32[2,320,384]{2,1,0:T(8,128)S(1)}, bf16[2,320,384]{2,1,0:T(8,128)(2,1)}) custom-call(s32[1]{0:T(128)} %bitcast.tile_ref, s32[1]{0:T(128)} %bitcast.1.span_ref, s32[4]{0:T(128)S(1)} %copy-done.1, bf16[2,320,384]{2,1,0:T(8,128)(2,1)S(1)} %get-tuple-element.29.mid, bf16[160,384]{1,0:T(8,128)(2,1)S(1)} %collective-permute-done.6.pair_a, ...), custom_call_target="tpu_custom_call" | custom-call | flops 2548039680 | bytes 1048576 | tf_op jit(solution)/shard_map/own/pallas_call | solution.py:451
  55.7 1.6 %collective-permute-done.10.link_got = bf16[2,320,384]{2,1,0:T(8,128)(2,1)S(1)} collective-permute-done((bf16[2,320,384]{2,1,0:T(8,128)(2,1)S(1)}, bf16[2,320,384]{2,1,0:T(8,128)(2,1)S(1)}, u32[]{:S(2)}, u32[]{:S(2)}) %collective-permute-start.10) | collective-permute-done | bytes 491552 | tf_op jit(solution)/shard_map/ppermute | solution.py:449
  57.3 0.0 collective-permute-done.11.core_got
  57.3 0.8 %finish.1 = bf16[2,320,384]{2,1,0:T(8,128)(2,1)} custom-call(s32[1]{0:T(128)} %bitcast.1.span_ref, f32[2,320,384]{2,1,0:T(8,128)S(1)} %get-tuple-element.35.own, bf16[2,320,384]{2,1,0:T(8,128)(2,1)S(1)} %collective-permute-done.10.link_got, bf16[2,320,384]{2,1,0:T(8,128)(2,1)S(1)} %collective-permute-done.11.core_got), custom_call_target="tpu_custom_call" | custom-call | tf_op jit(solution)/shard_map/finish/pallas_call | solution.py:458
Async XLA Ops:
  1.7 13.1 %collective-permute-start.1 = (bf16[320,384]{1,0:T(8,128)(2,1)S(1)}, bf16[320,384]{1,0:T(8,128)(2,1)S(1)}, u32[]{:S(2)}, u32[]{:S(2)}) collective-permute-start(bf16[320,384]{1,0:T(8,128)(2,1)S(1)} %get-tuple-element.20), channel_id=1, source_target_pairs={{0,0},{1,8},{2,2},{3,10},{4,4},{5,12},{6,6},{7,14},{8,1},{9,9},{10... | collective-permute-start | bytes 737288 | tf_op jit(solution)/shard_map/ppermute | solution.py:365
  6.5 11.0 %collective-permute-start = (bf16[320,384]{1,0:T(8,128)(2,1)S(1)}, bf16[320,384]{1,0:T(8,128)(2,1)S(1)}, u32[]{:S(2)}, u32[]{:S(2)}) collective-permute-start(bf16[320,384]{1,0:T(8,128)(2,1)S(1)} %get-tuple-element.19), channel_id=1, source_target_pairs={{0,4},{1,12},{2,6},{3,14},{4,0},{5,8},{6,2},{7,10},{8,5},{9,13},{1... | collective-permute-start | bytes 737288 | tf_op jit(solution)/shard_map/ppermute | solution.py:366
  14.9 2.6 %collective-permute-start.2 = (bf16[320,384]{1,0:T(8,128)(2,1)S(1)}, bf16[320,384]{1,0:T(8,128)(2,1)S(1)}, u32[]{:S(2)}, u32[]{:S(2)}) collective-permute-start(bf16[320,384]{1,0:T(8,128)(2,1)S(1)} %collective-permute-done.1.own_a), channel_id=1, source_target_pairs={{0,1},{1,0},{2,3},{3,2},{4,5},{5,4},{6,7},{7,6},{8,9},{9,8},{10,11... | collective-permute-start | bytes 737288 | tf_op jit(solution)/shard_map/ppermute | solution.py:376
  17.5 1.5 %collective-permute-start.3 = (bf16[320,384]{1,0:T(8,128)(2,1)S(1)}, bf16[320,384]{1,0:T(8,128)(2,1)S(1)}, u32[]{:S(2)}, u32[]{:S(2)}) collective-permute-start(bf16[320,384]{1,0:T(8,128)(2,1)S(1)} %collective-permute-done.own_b), channel_id=1, source_target_pairs={{0,1},{1,0},{2,3},{3,2},{4,5},{5,4},{6,7},{7,6},{8,9},{9,8},{10,11... | collective-permute-start | bytes 737288 | tf_op jit(solution)/shard_map/ppermute | solution.py:377
  21.3 10.0 %collective-permute-start.5 = (bf16[320,384]{1,0:T(8,128)(2,1)S(1)}, bf16[320,384]{1,0:T(8,128)(2,1)S(1)}, u32[]{:S(2)}, u32[]{:S(2)}) collective-permute-start(bf16[320,384]{1,0:T(8,128)(2,1)S(1)} %get-tuple-element.27), channel_id=1, source_target_pairs={{0,0},{1,8},{2,2},{3,10},{4,4},{5,12},{6,6},{7,14},{8,1},{9,9},{10... | collective-permute-start | bytes 737288 | tf_op jit(solution)/shard_map/ppermute | solution.py:390
  27.1 10.4 %collective-permute-start.4 = (bf16[320,384]{1,0:T(8,128)(2,1)S(1)}, bf16[320,384]{1,0:T(8,128)(2,1)S(1)}, u32[]{:S(2)}, u32[]{:S(2)}) collective-permute-start(bf16[320,384]{1,0:T(8,128)(2,1)S(1)} %attend_rest.1._), channel_id=1, source_target_pairs={{0,4},{1,12},{2,6},{3,14},{4,0},{5,8},{6,2},{7,10},{8,5},{9,13},{1... | collective-permute-start | bytes 737288 | tf_op jit(solution)/shard_map/ppermute | solution.py:398
  27.8 3.5 %copy-start = (f32[384]{0:T(512)S(1)}, f32[384]{0:T(512)}, u32[]{:S(2)}) copy-start(f32[384]{0:T(512)} %gain.5) | copy-start | bytes 4612
  31.3 8.6 %copy-start.1 = (s32[4]{0:T(128)S(1)}, s32[4]{0:T(128)}, u32[]{:S(2)}) copy-start(s32[4]{0:T(128)} %clips.7) | copy-start | bytes 52
  31.7 11.0 %collective-permute-start.6 = (bf16[160,384]{1,0:T(8,128)(2,1)S(1)}, bf16[160,384]{1,0:T(8,128)(2,1)S(1)}, u32[]{:S(2)}, u32[]{:S(2)}) collective-permute-start(bf16[160,384]{1,0:T(8,128)(2,1)S(1)} %get-tuple-element.30), channel_id=1, source_target_pairs={{0,4},{4,0},{8,12},{12,8},{1,5},{5,1},{9,13},{13,9},{2,6},{6,2},{1... | collective-permute-start | bytes 368648 | tf_op jit(solution)/shard_map/ppermute | solution.py:416
  33.8 10.2 %collective-permute-start.7 = (bf16[160,384]{1,0:T(8,128)(2,1)S(1)}, bf16[160,384]{1,0:T(8,128)(2,1)S(1)}, u32[]{:S(2)}, u32[]{:S(2)}) collective-permute-start(bf16[160,384]{1,0:T(8,128)(2,1)S(1)} %get-tuple-element.31), channel_id=1, source_target_pairs={{4,8},{8,4},{5,9},{9,5},{6,10},{10,6},{7,11},{11,7},{20,24},{24,20... | collective-permute-start | bytes 368648 | tf_op jit(solution)/shard_map/ppermute | solution.py:417
  37.8 4.9 %collective-permute-start.8 = (bf16[160,384]{1,0:T(8,128)(2,1)S(1)}, bf16[160,384]{1,0:T(8,128)(2,1)S(1)}, u32[]{:S(2)}, u32[]{:S(2)}) collective-permute-start(bf16[160,384]{1,0:T(8,128)(2,1)S(1)} %get-tuple-element.32), channel_id=1, source_target_pairs={{0,4},{4,0},{8,12},{12,8},{1,5},{5,1},{9,13},{13,9},{2,6},{6,2},{1... | collective-permute-start | bytes 368648 | tf_op jit(solution)/shard_map/ppermute | solution.py:424
  38.1 6.3 %collective-permute-start.9 = (bf16[160,384]{1,0:T(8,128)(2,1)S(1)}, bf16[160,384]{1,0:T(8,128)(2,1)S(1)}, u32[]{:S(2)}, u32[]{:S(2)}) collective-permute-start(bf16[160,384]{1,0:T(8,128)(2,1)S(1)} %get-tuple-element.33), channel_id=1, source_target_pairs={{4,8},{8,4},{5,9},{9,5},{6,10},{10,6},{7,11},{11,7},{20,24},{24,20... | collective-permute-start | bytes 368648 | tf_op jit(solution)/shard_map/ppermute | solution.py:425
  45.7 11.6 %collective-permute-start.10 = (bf16[2,320,384]{2,1,0:T(8,128)(2,1)S(1)}, bf16[2,320,384]{2,1,0:T(8,128)(2,1)S(1)}, u32[]{:S(2)}, u32[]{:S(2)}) collective-permute-start(bf16[2,320,384]{2,1,0:T(8,128)(2,1)S(1)} %mid_edge.1), channel_id=1, source_target_pairs={{1,2},{2,1},{5,6},{6,5},{9,10},{10,9},{13,14},{14,13},{17,18},{18,... | collective-permute-start | bytes 1474568 | tf_op jit(solution)/shard_map/ppermute | solution.py:449
  51.0 6.3 %collective-permute-start.11 = (bf16[2,320,384]{2,1,0:T(8,128)(2,1)S(1)}, bf16[2,320,384]{2,1,0:T(8,128)(2,1)S(1)}, u32[]{:S(2)}, u32[]{:S(2)}) collective-permute-start(bf16[2,320,384]{2,1,0:T(8,128)(2,1)S(1)} %mid_edge.1), channel_id=1, source_target_pairs={{0,1},{1,0},{2,3},{3,2},{4,5},{5,4},{6,7},{7,6},{8,9},{9,8},{10,11... | collective-permute-start | bytes 1474568 | tf_op jit(solution)/shard_map/ppermute | solution.py:450

commit v10 on v7

--- a/solution.py
+++ b/solution.py
@@ -222,34 +222,57 @@
 def next_own_kernel(cols, span_ref, clips, mid, w, out):
     ch = mid.shape[-1]
     flag = flags_of(clips, (span_ref[0] + 1) * 2)
-    first_row, second_row = slice(0, cols), slice(cols, 2 * cols)
-    pair = [
-        jnp.concatenate([mid[f, first_row, :], mid[f, second_row, :]], axis=1) for f in range(2)
-    ]
-    last = jnp.concatenate([weigh(flag[0][0], pair[0]), weigh(flag[1][0], pair[1])], axis=0)
-    middle = weigh(flag[0][1], pair[1])
-    for part, taps in ((first_row, slice(ch, 3 * ch)), (second_row, slice(0, 2 * ch))):
-        far = dot32(last, w[0, taps])
-        out[0, part, :] = shift_add(far[:cols] + dot32(middle, w[1, taps]), cols, ch)
-        out[1, part, :] = shift_add(far[cols:], cols, ch)
+    use_far, use_near = flag[0][0] + flag[1][0] > 0.0, flag[0][1] > 0.0
+    parts = ((slice(0, cols), slice(ch, 3 * ch)), (slice(cols, 2 * cols), slice(0, 2 * ch)))
+
+    def pair(f):
+        return jnp.concatenate([mid[f, :cols, :], mid[f, cols:, :]], axis=1)
+
+    @pl.when(use_far)
+    def _():
+        last = jnp.concatenate([weigh(flag[f][0], pair(f)) for f in range(2)], axis=0)
+        for part, taps in parts:
+            far = dot32(last, w[0, taps])
+            out[0, part, :] = shift_add(far[:cols], cols, ch)
+            out[1, part, :] = shift_add(far[cols:], cols, ch)
+
+    @pl.when(jnp.logical_not(use_far))
+    def _():
+        out[...] = jnp.zeros_like(out)
+
+    @pl.when(use_near)
+    def _():
+        middle = pair(1)
+        for part, taps in parts:
+            out[0, part, :] += shift_add(dot32(middle, w[1, taps]), cols, ch)
 
 
 def next_edge_kernel(
-    cols, tile_ref, span_ref, clips, pair_a, mid_a, pair_b, mid_b, w, partial, out
+    cols, tile_ref, span_ref, clips, pair_a, mid_a, pair_b, mid_b, w, partial, out, total
 ):
     ch = w.shape[-1] // 3
     flag = flags_of(clips, (span_ref[0] + 1) * 2)
-    above, below = edge_rows(tile_ref, pair_a, mid_a, pair_b, mid_b)
-    for edge, part, taps in (
-        (above, slice(0, cols), slice(0, ch)),
-        (below, slice(cols, 2 * cols), slice(2 * ch, 3 * ch)),
-    ):
-        last = jnp.concatenate([edge[0] * flag[0][0], edge[1] * flag[1][0]], axis=0).astype(bf16)
-        middle = (edge[1] * flag[0][1]).astype(bf16)
-        far = dot32(last, w[0, taps])
-        near = far[:cols] + dot32(middle, w[1, taps])
-        for f, val in ((0, near), (1, far[cols:])):
-            out[f, part, :] = (shift_add(val, cols, ch) + partial[f, part, :]).astype(bf16)
+    use_far, use_near = flag[0][0] + flag[1][0] > 0.0, flag[0][1] > 0.0
+    parts = ((slice(0, cols), slice(0, ch)), (slice(cols, 2 * cols), slice(2 * ch, 3 * ch)))
+    total[...] = partial[...]
+
+    @pl.when(use_far)
+    def _():
+        edges = edge_rows(tile_ref, pair_a, mid_a, pair_b, mid_b)
+        for edge, (part, taps) in zip(edges, parts):
+            last = jnp.concatenate([edge[f] * flag[f][0] for f in range(2)], axis=0)
+            far = dot32(last.astype(bf16), w[0, taps])
+            total[0, part, :] += shift_add(far[:cols], cols, ch)
+            total[1, part, :] += shift_add(far[cols:], cols, ch)
+
+    @pl.when(use_near)
+    def _():
+        edges = edge_rows(tile_ref, pair_a, mid_a, pair_b, mid_b)
+        for edge, (part, taps) in zip(edges, parts):
+            near = dot32(edge[1].astype(bf16), w[1, taps])
+            total[0, part, :] += shift_add(near, cols, ch)
+
+    out[...] = total[...].astype(bf16)
 
 
 def own_kernel(
@@ -397,6 +420,7 @@
         "next_edge",
         struct((frames, cells, ch)),
         [SMEM] * 3 + [VMEM] * 6,
+        [pltpu.VMEM((frames, cells, ch), f32)],
         flops=unit,
     )(*where, *edges, w_packed, started)
     link = [(s + d, s + 1 - d) for s in range(1, spans - 1, 2) for d in range(2)]

time: 58.3 us -> 58.6 us (level)
  Pallas kernels: 22.6 us -> 19.2 us
  starting transfers between devices: 19.9 us -> 21.7 us
  waiting for transfers between devices: 14.7 us -> 16.5 us
    pallas_call x1, Pallas kernels: 2.63 us -> 0.63 us  [on_device(): call(functools.partial(next_own_kernel, cols), 'next_own', sums, [SMEM] *...]
    ppermute x1, starting transfers between devices: 4.33 us -> 6.13 us  [on_device(): link_got = lax.ppermute(for_next, 'span', link)]
    ppermute x1, waiting for transfers between devices: 0.01 us -> 1.38 us  [on_device(): pair_b = lax.ppermute(pair_edge, 'tile', pairs)]
    pallas_call x1, Pallas kernels: 1.99 us -> 0.66 us  [on_device(): call(functools.partial(next_edge_kernel, cols), 'next_edge', struct((fram...]
    ppermute x1, waiting for transfers between devices: 1.69 us -> 2.31 us  [on_device(): mid_b = lax.ppermute(mid_edge, 'tile', middle)]
  transfers between devices with their start and end apart: 12 -> 12, of which waited for: 6 -> 7; matrix products, arithmetic and copies ran while one was open for 0% -> 0% of each run, Pallas kernels for 28% -> 25%
where the time goes in v10:
time: 58.6 us; the launch traced here: 58.3 us
  starting transfers between devices  21.7 us (37%)
  Pallas kernels  19.2 us (33%)
  waiting for transfers between devices  16.5 us (28%)
  between operations  0.81 us (1%)
    ppermute x1, waiting for transfers between devices, on_device(): own_a = lax.ppermute(send_a, both, route_a)  6.34 us
    ppermute x1, starting transfers between devices, on_device(): link_got = lax.ppermute(for_next, 'span', link)  6.13 us
    ppermute x1, starting transfers between devices, on_device(): own_a = lax.ppermute(send_a, both, route_a)  4.78 us
    pallas_call x1, Pallas kernels, on_device(): call(functools.partial(own_kernel, cols), 'own', (sums, struct((frames, c...  4.61 us
    ppermute x1, starting transfers between devices, on_device(): got_a = lax.ppermute(att_a, both, route_a)  3.68 us
    pallas_call x1, Pallas kernels, on_device(): call(load_kernel, 'load_conv', struct((3, 3 * ch, 3 * ch)), [ANY, ANY], [...  3.48 us
    ppermute x1, waiting for transfers between devices, on_device(): own_b = lax.ppermute(send_b, both, route_b)  2.63 us
    ppermute x1, waiting for transfers between devices, on_device(): mid_b = lax.ppermute(mid_edge, 'tile', middle)  2.31 us
  transfers between devices with their start and end apart: 12, of which 7 were waited for; matrix products, arithmetic and copies ran while one was open for 0% of the time, Pallas kernels for 25%

profile of v10, /device:TPU:13, one launch (start us, length us, event | category | flops | bytes accessed | tf_op | source)
XLA Modules:
  0.0 58.3 jit_solution(15733478512939719696)
XLA Ops:
  0.6 1.1 %pick.1 = (bf16[320,384]{1,0:T(8,128)(2,1)S(1)}, bf16[320,384]{1,0:T(8,128)(2,1)S(1)}) custom-call(s32[1]{0:T(128)} %bitcast.tile_ref, bf16[2,320,384]{2,1,0:T(8,128)(2,1)} %bitcast.5), custom_call_target="tpu_custom_call" | custom-call | bytes 1048576 | tf_op jit(solution)/shard_map/pick/pallas_call | solution.py:341
  1.7 4.8 %collective-permute-start.1 = (bf16[320,384]{1,0:T(8,128)(2,1)S(1)}, bf16[320,384]{1,0:T(8,128)(2,1)S(1)}, u32[]{:S(2)}, u32[]{:S(2)}) collective-permute-start(bf16[320,384]{1,0:T(8,128)(2,1)S(1)} %get-tuple-element.20), channel_id=1, source_target_pairs={{0,0},{1,8},{2,2},{3,10},{4,4},{5,12},{6,6},{7,14},{8,1},{9,9},{10... | collective-permute-start | bytes 737288 | tf_op jit(solution)/shard_map/ppermute | solution.py:349
  6.5 0.1 collective-permute-start
  6.6 1.9 %load_small.1 = (bf16[384,1152]{1,0:T(8,128)(2,1)S(1)}, bf16[384,384]{1,0:T(8,128)(2,1)S(1)}, f32[384]{0:T(512)S(1)}) custom-call(bf16[384,1152]{1,0:T(8,128)(2,1)} %w_qkv.1, bf16[384,384]{1,0:T(8,128)(2,1)} %w_out.1, f32[384]{0:T(512)} %gain.3), custom_call_target="tpu_custom_call" | custom-call | bytes 1048576 | tf_op jit(solution)/shard_map/load_small/pallas_call | solution.py:351
  8.5 6.3 %collective-permute-done.1.own_a = bf16[320,384]{1,0:T(8,128)(2,1)S(1)} collective-permute-done((bf16[320,384]{1,0:T(8,128)(2,1)S(1)}, bf16[320,384]{1,0:T(8,128)(2,1)S(1)}, u32[]{:S(2)}, u32[]{:S(2)}) %collective-permute-start.1) | collective-permute-done | bytes 245792 | tf_op jit(solution)/shard_map/ppermute | solution.py:349
  14.9 0.0 collective-permute-start.2
  14.9 2.6 %collective-permute-done.own_b = bf16[320,384]{1,0:T(8,128)(2,1)S(1)} collective-permute-done((bf16[320,384]{1,0:T(8,128)(2,1)S(1)}, bf16[320,384]{1,0:T(8,128)(2,1)S(1)}, u32[]{:S(2)}, u32[]{:S(2)}) %collective-permute-start) | collective-permute-done | bytes 245792 | tf_op jit(solution)/shard_map/ppermute | solution.py:350
  17.5 0.0 collective-permute-start.3
  17.5 0.0 collective-permute-done.2.other_a
  17.5 1.0 %keys.1.kv_a = bf16[960,768]{1,0:T(8,128)(2,1)S(1)} custom-call(bf16[320,384]{1,0:T(8,128)(2,1)S(1)} %collective-permute-done.1.own_a, bf16[320,384]{1,0:T(8,128)(2,1)S(1)} %collective-permute-done.2.other_a, bf16[320,384]{1,0:T(8,128)(2,1)S(1)} %collective-permute-done.own_b, f32[384]{0:T(512)S(1)} %get-tuple-element.23.gain, ...), custom_call_target="tpu_custom_call" | custom-call | flops 377487360 | bytes 1048576 | tf_op jit(solution)/shard_map/keys/pallas_call | solution.py:364
  18.5 0.5 collective-permute-done.3.other_b
  19.0 2.3 %attend.1 = (bf16[320,768]{1,0:T(8,128)(2,1)S(1)}, bf16[320,384]{1,0:T(8,128)(2,1)S(1)}) custom-call(bf16[320,384]{1,0:T(8,128)(2,1)S(1)} %collective-permute-done.3.other_b, bf16[320,384]{1,0:T(8,128)(2,1)S(1)} %collective-permute-done.1.own_a, bf16[960,768]{1,0:T(8,128)(2,1)S(1)} %keys.1.kv_a, f32[384]{0:T(512)S(1)} %get-tuple-element.23.gain, ...), custom_call_target="tpu_custom_call" | custom-call | flops 1195376640 | bytes 1048576 | tf_op jit(solution)/shard_map/attend/pallas_call | solution.py:367
  21.3 3.7 %collective-permute-start.5 = (bf16[320,384]{1,0:T(8,128)(2,1)S(1)}, bf16[320,384]{1,0:T(8,128)(2,1)S(1)}, u32[]{:S(2)}, u32[]{:S(2)}) collective-permute-start(bf16[320,384]{1,0:T(8,128)(2,1)S(1)} %get-tuple-element.27), channel_id=1, source_target_pairs={{0,0},{1,8},{2,2},{3,10},{4,4},{5,12},{6,6},{7,14},{8,1},{9,9},{10... | collective-permute-start | bytes 737288 | tf_op jit(solution)/shard_map/ppermute | solution.py:374
  25.0 2.1 %attend_rest.1._ = bf16[320,384]{1,0:T(8,128)(2,1)S(1)} custom-call(bf16[320,384]{1,0:T(8,128)(2,1)S(1)} %collective-permute-done.own_b, bf16[960,768]{1,0:T(8,128)(2,1)S(1)} %keys.1.kv_a, bf16[320,768]{1,0:T(8,128)(2,1)S(1)} %get-tuple-element.26.kv_b, f32[384]{0:T(512)S(1)} %get-tuple-element.23.gain, bf16[384,1152]{1,0:T(8,128)(2,1)S(1)} %get-tuple-element.24.w_qkv, ...), custom_call_target="tpu_custom_call" | custom-call | flops 2453667840 | bytes 1048576 | tf_op jit(solution)/shard_map/attend_rest/pallas_call | solution.py:375
  27.1 0.8 %collective-permute-start.4 = (bf16[320,384]{1,0:T(8,128)(2,1)S(1)}, bf16[320,384]{1,0:T(8,128)(2,1)S(1)}, u32[]{:S(2)}, u32[]{:S(2)}) collective-permute-start(bf16[320,384]{1,0:T(8,128)(2,1)S(1)} %attend_rest.1._), channel_id=1, source_target_pairs={{0,4},{1,12},{2,6},{3,14},{4,0},{5,8},{6,2},{7,10},{8,5},{9,13},{1... | collective-permute-start | bytes 737288 | tf_op jit(solution)/shard_map/ppermute | solution.py:382
  27.8 0.0 copy-start
  27.8 3.5 %load_conv.1._.w = bf16[3,1152,1152]{2,1,0:T(8,128)(2,1)S(1)} custom-call(bf16[320,384]{1,0:T(8,128)(2,1)S(1)} %attend_rest.1._, bf16[3,3,3,384,384]{4,3,2,1,0:T(8,128)(2,1)} %w_hbm.1), custom_call_target="tpu_custom_call" | custom-call | bytes 4096 | tf_op jit(solution)/shard_map/load_conv/pallas_call | solution.py:388
  31.3 0.0 copy-start.1
  31.3 0.0 collective-permute-done.5.got_a
  31.4 0.0 copy-done
  31.4 0.3 activate_a.1
  31.7 2.1 %collective-permute-start.6 = (bf16[160,384]{1,0:T(8,128)(2,1)S(1)}, bf16[160,384]{1,0:T(8,128)(2,1)S(1)}, u32[]{:S(2)}, u32[]{:S(2)}) collective-permute-start(bf16[160,384]{1,0:T(8,128)(2,1)S(1)} %get-tuple-element.30), channel_id=1, source_target_pairs={{0,4},{4,0},{8,12},{12,8},{1,5},{5,1},{9,13},{13,9},{2,6},{6,2},{1... | collective-permute-start | bytes 368648 | tf_op jit(solution)/shard_map/ppermute | solution.py:400
  33.8 1.9 %collective-permute-start.7 = (bf16[160,384]{1,0:T(8,128)(2,1)S(1)}, bf16[160,384]{1,0:T(8,128)(2,1)S(1)}, u32[]{:S(2)}, u32[]{:S(2)}) collective-permute-start(bf16[160,384]{1,0:T(8,128)(2,1)S(1)} %get-tuple-element.31), channel_id=1, source_target_pairs={{4,8},{8,4},{5,9},{9,5},{6,10},{10,6},{7,11},{11,7},{20,24},{24,20... | collective-permute-start | bytes 368648 | tf_op jit(solution)/shard_map/ppermute | solution.py:401
  35.7 1.7 %collective-permute-done.4.got_b = bf16[320,384]{1,0:T(8,128)(2,1)S(1)} collective-permute-done((bf16[320,384]{1,0:T(8,128)(2,1)S(1)}, bf16[320,384]{1,0:T(8,128)(2,1)S(1)}, u32[]{:S(2)}, u32[]{:S(2)}) %collective-permute-start.4) | collective-permute-done | bytes 245792 | tf_op jit(solution)/shard_map/ppermute | solution.py:382
  37.5 0.3 activate_b.1
  37.8 0.3 collective-permute-start.8
  38.1 1.9 %collective-permute-start.9 = (bf16[160,384]{1,0:T(8,128)(2,1)S(1)}, bf16[160,384]{1,0:T(8,128)(2,1)S(1)}, u32[]{:S(2)}, u32[]{:S(2)}) collective-permute-start(bf16[160,384]{1,0:T(8,128)(2,1)S(1)} %get-tuple-element.33), channel_id=1, source_target_pairs={{4,8},{8,4},{5,9},{9,5},{6,10},{10,6},{7,11},{11,7},{20,24},{24,20... | collective-permute-start | bytes 368648 | tf_op jit(solution)/shard_map/ppermute | solution.py:409
  40.0 0.0 copy-done.1
  40.0 0.6 %next_own.1.partial = f32[2,320,384]{2,1,0:T(8,128)S(1)} custom-call(s32[1]{0:T(128)} %bitcast.1.span_ref, s32[4]{0:T(128)S(1)} %copy-done.1, bf16[2,320,384]{2,1,0:T(8,128)(2,1)S(1)} %get-tuple-element.29.mid, bf16[3,1152,1152]{2,1,0:T(8,128)(2,1)S(1)} %load_conv.1._.w), custom_call_target="tpu_custom_call" | custom-call | flops 1698693120 | bytes 1048576 | tf_op jit(solution)/shard_map/next_own/pallas_call | solution.py:411
  40.6 0.0 collective-permute-done.6.pair_a
  40.6 0.0 collective-permute-done.7.mid_a
  40.7 1.4 %collective-permute-done.8.pair_b = bf16[160,384]{1,0:T(8,128)(2,1)S(1)} collective-permute-done((bf16[160,384]{1,0:T(8,128)(2,1)S(1)}, bf16[160,384]{1,0:T(8,128)(2,1)S(1)}, u32[]{:S(2)}, u32[]{:S(2)}) %collective-permute-start.8) | collective-permute-done | bytes 122912 | tf_op jit(solution)/shard_map/ppermute | solution.py:408
  42.0 2.3 %collective-permute-done.9.mid_b = bf16[160,384]{1,0:T(8,128)(2,1)S(1)} collective-permute-done((bf16[160,384]{1,0:T(8,128)(2,1)S(1)}, bf16[160,384]{1,0:T(8,128)(2,1)S(1)}, u32[]{:S(2)}, u32[]{:S(2)}) %collective-permute-start.9) | collective-permute-done | bytes 122912 | tf_op jit(solution)/shard_map/ppermute | solution.py:409
  44.3 0.7 %next_edge.1 = bf16[2,320,384]{2,1,0:T(8,128)(2,1)S(1)} custom-call(s32[1]{0:T(128)} %bitcast.tile_ref, s32[1]{0:T(128)} %bitcast.1.span_ref, s32[4]{0:T(128)S(1)} %copy-done.1, bf16[160,384]{1,0:T(8,128)(2,1)S(1)} %collective-permute-done.6.pair_a, bf16[160,384]{1,0:T(8,128)(2,1)S(1)} %collective-permute-done.7.mid_a, ...), custom_call_target="tpu_custom_call" | custom-call | flops 849346560 | bytes 1048576 | tf_op jit(solution)/shard_map/next_edge/pallas_call | solution.py:418
  45.0 6.1 %collective-permute-start.10 = (bf16[2,320,384]{2,1,0:T(8,128)(2,1)S(1)}, bf16[2,320,384]{2,1,0:T(8,128)(2,1)S(1)}, u32[]{:S(2)}, u32[]{:S(2)}) collective-permute-start(bf16[2,320,384]{2,1,0:T(8,128)(2,1)S(1)} %next_edge.1), channel_id=1, source_target_pairs={{1,2},{2,1},{5,6},{6,5},{9,10},{10,9},{13,14},{14,13},{17,18},{18,... | collective-permute-start | bytes 1474568 | tf_op jit(solution)/shard_map/ppermute | solution.py:427
  51.2 0.1 collective-permute-start.11
  51.2 4.6 %own.1 = (f32[2,320,384]{2,1,0:T(8,128)S(1)}, bf16[2,320,384]{2,1,0:T(8,128)(2,1)}) custom-call(s32[1]{0:T(128)} %bitcast.tile_ref, s32[1]{0:T(128)} %bitcast.1.span_ref, s32[4]{0:T(128)S(1)} %copy-done.1, bf16[2,320,384]{2,1,0:T(8,128)(2,1)S(1)} %get-tuple-element.29.mid, bf16[160,384]{1,0:T(8,128)(2,1)S(1)} %collective-permute-done.6.pair_a, ...), custom_call_target="tpu_custom_call" | custom-call | flops 2548039680 | bytes 1048576 | tf_op jit(solution)/shard_map/own/pallas_call | solution.py:429
  55.8 1.6 %collective-permute-done.10.link_got = bf16[2,320,384]{2,1,0:T(8,128)(2,1)S(1)} collective-permute-done((bf16[2,320,384]{2,1,0:T(8,128)(2,1)S(1)}, bf16[2,320,384]{2,1,0:T(8,128)(2,1)S(1)}, u32[]{:S(2)}, u32[]{:S(2)}) %collective-permute-start.10) | collective-permute-done | bytes 491552 | tf_op jit(solution)/shard_map/ppermute | solution.py:427
  57.5 0.0 collective-permute-done.11.core_got
  57.5 0.9 %finish.1 = bf16[2,320,384]{2,1,0:T(8,128)(2,1)} custom-call(s32[1]{0:T(128)} %bitcast.1.span_ref, f32[2,320,384]{2,1,0:T(8,128)S(1)} %get-tuple-element.35.own, bf16[2,320,384]{2,1,0:T(8,128)(2,1)S(1)} %collective-permute-done.10.link_got, bf16[2,320,384]{2,1,0:T(8,128)(2,1)S(1)} %collective-permute-done.11.core_got), custom_call_target="tpu_custom_call" | custom-call | bytes 1048576 | tf_op jit(solution)/shard_map/finish/pallas_call | solution.py:436
Async XLA Ops:
  1.7 13.1 %collective-permute-start.1 = (bf16[320,384]{1,0:T(8,128)(2,1)S(1)}, bf16[320,384]{1,0:T(8,128)(2,1)S(1)}, u32[]{:S(2)}, u32[]{:S(2)}) collective-permute-start(bf16[320,384]{1,0:T(8,128)(2,1)S(1)} %get-tuple-element.20), channel_id=1, source_target_pairs={{0,0},{1,8},{2,2},{3,10},{4,4},{5,12},{6,6},{7,14},{8,1},{9,9},{10... | collective-permute-start | bytes 737288 | tf_op jit(solution)/shard_map/ppermute | solution.py:349
  6.5 11.0 %collective-permute-start = (bf16[320,384]{1,0:T(8,128)(2,1)S(1)}, bf16[320,384]{1,0:T(8,128)(2,1)S(1)}, u32[]{:S(2)}, u32[]{:S(2)}) collective-permute-start(bf16[320,384]{1,0:T(8,128)(2,1)S(1)} %get-tuple-element.19), channel_id=1, source_target_pairs={{0,4},{1,12},{2,6},{3,14},{4,0},{5,8},{6,2},{7,10},{8,5},{9,13},{1... | collective-permute-start | bytes 737288 | tf_op jit(solution)/shard_map/ppermute | solution.py:350
  14.9 2.6 %collective-permute-start.2 = (bf16[320,384]{1,0:T(8,128)(2,1)S(1)}, bf16[320,384]{1,0:T(8,128)(2,1)S(1)}, u32[]{:S(2)}, u32[]{:S(2)}) collective-permute-start(bf16[320,384]{1,0:T(8,128)(2,1)S(1)} %collective-permute-done.1.own_a), channel_id=1, source_target_pairs={{0,1},{1,0},{2,3},{3,2},{4,5},{5,4},{6,7},{7,6},{8,9},{9,8},{10,11... | collective-permute-start | bytes 737288 | tf_op jit(solution)/shard_map/ppermute | solution.py:360
  17.5 1.5 %collective-permute-start.3 = (bf16[320,384]{1,0:T(8,128)(2,1)S(1)}, bf16[320,384]{1,0:T(8,128)(2,1)S(1)}, u32[]{:S(2)}, u32[]{:S(2)}) collective-permute-start(bf16[320,384]{1,0:T(8,128)(2,1)S(1)} %collective-permute-done.own_b), channel_id=1, source_target_pairs={{0,1},{1,0},{2,3},{3,2},{4,5},{5,4},{6,7},{7,6},{8,9},{9,8},{10,11... | collective-permute-start | bytes 737288 | tf_op jit(solution)/shard_map/ppermute | solution.py:361
  21.3 10.0 %collective-permute-start.5 = (bf16[320,384]{1,0:T(8,128)(2,1)S(1)}, bf16[320,384]{1,0:T(8,128)(2,1)S(1)}, u32[]{:S(2)}, u32[]{:S(2)}) collective-permute-start(bf16[320,384]{1,0:T(8,128)(2,1)S(1)} %get-tuple-element.27), channel_id=1, source_target_pairs={{0,0},{1,8},{2,2},{3,10},{4,4},{5,12},{6,6},{7,14},{8,1},{9,9},{10... | collective-permute-start | bytes 737288 | tf_op jit(solution)/shard_map/ppermute | solution.py:374
  27.1 10.4 %collective-permute-start.4 = (bf16[320,384]{1,0:T(8,128)(2,1)S(1)}, bf16[320,384]{1,0:T(8,128)(2,1)S(1)}, u32[]{:S(2)}, u32[]{:S(2)}) collective-permute-start(bf16[320,384]{1,0:T(8,128)(2,1)S(1)} %attend_rest.1._), channel_id=1, source_target_pairs={{0,4},{1,12},{2,6},{3,14},{4,0},{5,8},{6,2},{7,10},{8,5},{9,13},{1... | collective-permute-start | bytes 737288 | tf_op jit(solution)/shard_map/ppermute | solution.py:382
  27.8 3.5 %copy-start = (f32[384]{0:T(512)S(1)}, f32[384]{0:T(512)}, u32[]{:S(2)}) copy-start(f32[384]{0:T(512)} %gain.5) | copy-start | bytes 4612
  31.3 8.6 %copy-start.1 = (s32[4]{0:T(128)S(1)}, s32[4]{0:T(128)}, u32[]{:S(2)}) copy-start(s32[4]{0:T(128)} %clips.5) | copy-start | bytes 52
  31.7 9.0 %collective-permute-start.6 = (bf16[160,384]{1,0:T(8,128)(2,1)S(1)}, bf16[160,384]{1,0:T(8,128)(2,1)S(1)}, u32[]{:S(2)}, u32[]{:S(2)}) collective-permute-start(bf16[160,384]{1,0:T(8,128)(2,1)S(1)} %get-tuple-element.30), channel_id=1, source_target_pairs={{0,4},{4,0},{8,12},{12,8},{1,5},{5,1},{9,13},{13,9},{2,6},{6,2},{1... | collective-permute-start | bytes 368648 | tf_op jit(solution)/shard_map/ppermute | solution.py:400
  33.8 6.8 %collective-permute-start.7 = (bf16[160,384]{1,0:T(8,128)(2,1)S(1)}, bf16[160,384]{1,0:T(8,128)(2,1)S(1)}, u32[]{:S(2)}, u32[]{:S(2)}) collective-permute-start(bf16[160,384]{1,0:T(8,128)(2,1)S(1)} %get-tuple-element.31), channel_id=1, source_target_pairs={{4,8},{8,4},{5,9},{9,5},{6,10},{10,6},{7,11},{11,7},{20,24},{24,20... | collective-permute-start | bytes 368648 | tf_op jit(solution)/shard_map/ppermute | solution.py:401
  37.8 4.2 %collective-permute-start.8 = (bf16[160,384]{1,0:T(8,128)(2,1)S(1)}, bf16[160,384]{1,0:T(8,128)(2,1)S(1)}, u32[]{:S(2)}, u32[]{:S(2)}) collective-permute-start(bf16[160,384]{1,0:T(8,128)(2,1)S(1)} %get-tuple-element.32), channel_id=1, source_target_pairs={{0,4},{4,0},{8,12},{12,8},{1,5},{5,1},{9,13},{13,9},{2,6},{6,2},{1... | collective-permute-start | bytes 368648 | tf_op jit(solution)/shard_map/ppermute | solution.py:408
  38.1 6.3 %collective-permute-start.9 = (bf16[160,384]{1,0:T(8,128)(2,1)S(1)}, bf16[160,384]{1,0:T(8,128)(2,1)S(1)}, u32[]{:S(2)}, u32[]{:S(2)}) collective-permute-start(bf16[160,384]{1,0:T(8,128)(2,1)S(1)} %get-tuple-element.33), channel_id=1, source_target_pairs={{4,8},{8,4},{5,9},{9,5},{6,10},{10,6},{7,11},{11,7},{20,24},{24,20... | collective-permute-start | bytes 368648 | tf_op jit(solution)/shard_map/ppermute | solution.py:409
  45.0 12.5 %collective-permute-start.10 = (bf16[2,320,384]{2,1,0:T(8,128)(2,1)S(1)}, bf16[2,320,384]{2,1,0:T(8,128)(2,1)S(1)}, u32[]{:S(2)}, u32[]{:S(2)}) collective-permute-start(bf16[2,320,384]{2,1,0:T(8,128)(2,1)S(1)} %next_edge.1), channel_id=1, source_target_pairs={{1,2},{2,1},{5,6},{6,5},{9,10},{10,9},{13,14},{14,13},{17,18},{18,... | collective-permute-start | bytes 1474568 | tf_op jit(solution)/shard_map/ppermute | solution.py:427
  51.2 6.3 %collective-permute-start.11 = (bf16[2,320,384]{2,1,0:T(8,128)(2,1)S(1)}, bf16[2,320,384]{2,1,0:T(8,128)(2,1)S(1)}, u32[]{:S(2)}, u32[]{:S(2)}) collective-permute-start(bf16[2,320,384]{2,1,0:T(8,128)(2,1)S(1)} %next_edge.1), channel_id=1, source_target_pairs={{0,1},{1,0},{2,3},{3,2},{4,5},{5,4},{6,7},{7,6},{8,9},{9,8},{10,11... | collective-permute-start | bytes 1474568 | tf_op jit(solution)/shard_map/ppermute | solution.py:428

commit v11 on v10

--- a/solution.py
+++ b/solution.py
@@ -247,32 +247,56 @@
             out[0, part, :] += shift_add(dot32(middle, w[1, taps]), cols, ch)
 
 
-def next_edge_kernel(
-    cols, tile_ref, span_ref, clips, pair_a, mid_a, pair_b, mid_b, w, partial, out, total
+def edge_part(cols, flag, first, second, above, w, partial, total):
+    ch = w.shape[-1] // 3
+    part = slice(0, cols) if above else slice(cols, 2 * cols)
+    taps = slice(0, ch) if above else slice(2 * ch, 3 * ch)
+    total[...] = partial[:, part, :]
+
+    @pl.when(flag[0][0] + flag[1][0] > 0.0)
+    def _():
+        last = jnp.concatenate(
+            [weigh(flag[0][0], first[...]), weigh(flag[1][0], second[...])], axis=0
+        )
+        far = dot32(last, w[0, taps])
+        total[0] += shift_add(far[:cols], cols, ch)
+        total[1] += shift_add(far[cols:], cols, ch)
+
+    @pl.when(flag[0][1] > 0.0)
+    def _():
+        total[0] += shift_add(dot32(second[...], w[1, taps]), cols, ch)
+
+
+def pair_edge_kernel(cols, tile_ref, span_ref, clips, pair_a, pair_b, w, partial, out, total):
+    flag = flags_of(clips, (span_ref[0] + 1) * 2)
+
+    @pl.when(tile_ref[0] % 2 == 1)
+    def _():
+        edge_part(cols, flag, pair_a, pair_b, True, w, partial, total)
+
+    @pl.when(tile_ref[0] % 2 == 0)
+    def _():
+        edge_part(cols, flag, pair_b, pair_a, False, w, partial, total)
+
+    out[...] = total[...].astype(bf16)
+
+
+def mid_edge_kernel(
+    cols, tile_ref, span_ref, clips, mid_a, mid_b, w, partial, pair_rows, out, total
 ):
-    ch = w.shape[-1] // 3
     flag = flags_of(clips, (span_ref[0] + 1) * 2)
-    use_far, use_near = flag[0][0] + flag[1][0] > 0.0, flag[0][1] > 0.0
-    parts = ((slice(0, cols), slice(0, ch)), (slice(cols, 2 * cols), slice(2 * ch, 3 * ch)))
-    total[...] = partial[...]
-
-    @pl.when(use_far)
-    def _():
-        edges = edge_rows(tile_ref, pair_a, mid_a, pair_b, mid_b)
-        for edge, (part, taps) in zip(edges, parts):
-            last = jnp.concatenate([edge[f] * flag[f][0] for f in range(2)], axis=0)
-            far = dot32(last.astype(bf16), w[0, taps])
-            total[0, part, :] += shift_add(far[:cols], cols, ch)
-            total[1, part, :] += shift_add(far[cols:], cols, ch)
-
-    @pl.when(use_near)
-    def _():
-        edges = edge_rows(tile_ref, pair_a, mid_a, pair_b, mid_b)
-        for edge, (part, taps) in zip(edges, parts):
-            near = dot32(edge[1].astype(bf16), w[1, taps])
-            total[0, part, :] += shift_add(near, cols, ch)
-
-    out[...] = total[...].astype(bf16)
+
+    @pl.when(tile_ref[0] % 2 == 1)
+    def _():
+        edge_part(cols, flag, mid_a, mid_b, False, w, partial, total)
+        out[:, :cols, :] = pair_rows[...]
+        out[:, cols:, :] = total[...].astype(bf16)
+
+    @pl.when(tile_ref[0] % 2 == 0)
+    def _():
+        edge_part(cols, flag, mid_b, mid_a, True, w, partial, total)
+        out[:, cols:, :] = pair_rows[...]
+        out[:, :cols, :] = total[...].astype(bf16)
 
 
 def own_kernel(
@@ -415,14 +439,23 @@
         [SMEM] * 2 + [VMEM] * 2,
         flops=2 * unit,
     )(span, clip_lengths, active, w_packed)
+    rows_sum = pltpu.VMEM((frames, cols, ch), f32)
+    pair_rows = call(
+        functools.partial(pair_edge_kernel, cols),
+        "pair_edge",
+        struct((frames, cols, ch)),
+        [SMEM] * 3 + [VMEM] * 4,
+        [rows_sum],
+        flops=unit // 2,
+    )(*where, pair_a, pair_b, w_packed, started)
     for_next = call(
-        functools.partial(next_edge_kernel, cols),
-        "next_edge",
+        functools.partial(mid_edge_kernel, cols),
+        "mid_edge",
         struct((frames, cells, ch)),
-        [SMEM] * 3 + [VMEM] * 6,
-        [pltpu.VMEM((frames, cells, ch), f32)],
-        flops=unit,
-    )(*where, *edges, w_packed, started)
+        [SMEM] * 3 + [VMEM] * 5,
+        [rows_sum],
+        flops=unit // 2,
+    )(*where, mid_a, mid_b, w_packed, started, pair_rows)
     link = [(s + d, s + 1 - d) for s in range(1, spans - 1, 2) for d in range(2)]
     link_got = lax.ppermute(for_next, "span", link)
     core_got = lax.ppermute(for_next, "span", other_core)

time: 58.6 us -> 59.1 us (level)
  the two profiles are of different devices: /device:TPU:13 before, /device:TPU:9 now
where the time goes in v11:
time: 59.1 us; the launch traced here: 58.9 us
  Pallas kernels  24 us (41%)
  starting transfers between devices  21.2 us (36%)
  waiting for transfers between devices  12.8 us (22%)
  between operations  0.84 us (1%)
    ppermute x1, waiting for transfers between devices, on_device(): own_a = lax.ppermute(send_a, both, route_a)  6.34 us
    ppermute x1, starting transfers between devices, on_device(): link_got = lax.ppermute(for_next, 'span', link)  5.55 us
    ppermute x1, starting transfers between devices, on_device(): own_a = lax.ppermute(send_a, both, route_a)  4.78 us
    pallas_call x1, Pallas kernels, on_device(): call(functools.partial(own_kernel, cols), 'own', (sums, struct((frames, c...  4.62 us
    ppermute x1, starting transfers between devices, on_device(): got_a = lax.ppermute(att_a, both, route_a)  3.68 us
    pallas_call x1, Pallas kernels, on_device(): call(load_kernel, 'load_conv', struct((3, 3 * ch, 3 * ch)), [ANY, ANY], [...  3.48 us
    pallas_call x1, Pallas kernels, on_device(): call(functools.partial(next_own_kernel, cols), 'next_own', sums, [SMEM] *...  2.87 us
    ppermute x1, waiting for transfers between devices, on_device(): own_b = lax.ppermute(send_b, both, route_b)  2.63 us
  transfers between devices with their start and end apart: 12, of which 5 were waited for; matrix products, arithmetic and copies ran while one was open for 0% of the time, Pallas kernels for 31%

profile of v11, /device:TPU:9, one launch (start us, length us, event | category | flops | bytes accessed | tf_op | source)
XLA Modules:
  0.0 58.9 jit_solution(16460771711001620054)
XLA Ops:
  0.6 1.1 %pick.1 = (bf16[320,384]{1,0:T(8,128)(2,1)S(1)}, bf16[320,384]{1,0:T(8,128)(2,1)S(1)}) custom-call(s32[1]{0:T(128)} %bitcast.tile_ref, bf16[2,320,384]{2,1,0:T(8,128)(2,1)} %bitcast.5), custom_call_target="tpu_custom_call" | custom-call | bytes 1048576 | tf_op jit(solution)/shard_map/pick/pallas_call | solution.py:365
  1.7 4.8 %collective-permute-start.1 = (bf16[320,384]{1,0:T(8,128)(2,1)S(1)}, bf16[320,384]{1,0:T(8,128)(2,1)S(1)}, u32[]{:S(2)}, u32[]{:S(2)}) collective-permute-start(bf16[320,384]{1,0:T(8,128)(2,1)S(1)} %get-tuple-element.20), channel_id=1, source_target_pairs={{0,0},{1,8},{2,2},{3,10},{4,4},{5,12},{6,6},{7,14},{8,1},{9,9},{10... | collective-permute-start | bytes 737288 | tf_op jit(solution)/shard_map/ppermute | solution.py:373
  6.5 0.1 collective-permute-start
  6.6 1.9 %load_small.1 = (bf16[384,1152]{1,0:T(8,128)(2,1)S(1)}, bf16[384,384]{1,0:T(8,128)(2,1)S(1)}, f32[384]{0:T(512)S(1)}) custom-call(bf16[384,1152]{1,0:T(8,128)(2,1)} %w_qkv.1, bf16[384,384]{1,0:T(8,128)(2,1)} %w_out.1, f32[384]{0:T(512)} %gain.3), custom_call_target="tpu_custom_call" | custom-call | bytes 1048576 | tf_op jit(solution)/shard_map/load_small/pallas_call | solution.py:375
  8.5 6.3 %collective-permute-done.1.own_a = bf16[320,384]{1,0:T(8,128)(2,1)S(1)} collective-permute-done((bf16[320,384]{1,0:T(8,128)(2,1)S(1)}, bf16[320,384]{1,0:T(8,128)(2,1)S(1)}, u32[]{:S(2)}, u32[]{:S(2)}) %collective-permute-start.1) | collective-permute-done | bytes 245792 | tf_op jit(solution)/shard_map/ppermute | solution.py:373
  14.9 0.0 collective-permute-start.2
  14.9 2.6 %collective-permute-done.own_b = bf16[320,384]{1,0:T(8,128)(2,1)S(1)} collective-permute-done((bf16[320,384]{1,0:T(8,128)(2,1)S(1)}, bf16[320,384]{1,0:T(8,128)(2,1)S(1)}, u32[]{:S(2)}, u32[]{:S(2)}) %collective-permute-start) | collective-permute-done | bytes 245792 | tf_op jit(solution)/shard_map/ppermute | solution.py:374
  17.5 0.0 collective-permute-start.3
  17.5 0.0 collective-permute-done.2.other_a
  17.5 1.0 %keys.1.kv_a = bf16[960,768]{1,0:T(8,128)(2,1)S(1)} custom-call(bf16[320,384]{1,0:T(8,128)(2,1)S(1)} %collective-permute-done.1.own_a, bf16[320,384]{1,0:T(8,128)(2,1)S(1)} %collective-permute-done.2.other_a, bf16[320,384]{1,0:T(8,128)(2,1)S(1)} %collective-permute-done.own_b, f32[384]{0:T(512)S(1)} %get-tuple-element.23.gain, ...), custom_call_target="tpu_custom_call" | custom-call | flops 377487360 | bytes 1048576 | tf_op jit(solution)/shard_map/keys/pallas_call | solution.py:388
  18.5 0.5 collective-permute-done.3.other_b
  19.0 2.3 %attend.1 = (bf16[320,768]{1,0:T(8,128)(2,1)S(1)}, bf16[320,384]{1,0:T(8,128)(2,1)S(1)}) custom-call(bf16[320,384]{1,0:T(8,128)(2,1)S(1)} %collective-permute-done.3.other_b, bf16[320,384]{1,0:T(8,128)(2,1)S(1)} %collective-permute-done.1.own_a, bf16[960,768]{1,0:T(8,128)(2,1)S(1)} %keys.1.kv_a, f32[384]{0:T(512)S(1)} %get-tuple-element.23.gain, ...), custom_call_target="tpu_custom_call" | custom-call | flops 1195376640 | bytes 1048576 | tf_op jit(solution)/shard_map/attend/pallas_call | solution.py:391
  21.3 3.7 %collective-permute-start.5 = (bf16[320,384]{1,0:T(8,128)(2,1)S(1)}, bf16[320,384]{1,0:T(8,128)(2,1)S(1)}, u32[]{:S(2)}, u32[]{:S(2)}) collective-permute-start(bf16[320,384]{1,0:T(8,128)(2,1)S(1)} %get-tuple-element.27), channel_id=1, source_target_pairs={{0,0},{1,8},{2,2},{3,10},{4,4},{5,12},{6,6},{7,14},{8,1},{9,9},{10... | collective-permute-start | bytes 737288 | tf_op jit(solution)/shard_map/ppermute | solution.py:398
  25.0 2.1 %attend_rest.1._ = bf16[320,384]{1,0:T(8,128)(2,1)S(1)} custom-call(bf16[320,384]{1,0:T(8,128)(2,1)S(1)} %collective-permute-done.own_b, bf16[960,768]{1,0:T(8,128)(2,1)S(1)} %keys.1.kv_a, bf16[320,768]{1,0:T(8,128)(2,1)S(1)} %get-tuple-element.26.kv_b, f32[384]{0:T(512)S(1)} %get-tuple-element.23.gain, bf16[384,1152]{1,0:T(8,128)(2,1)S(1)} %get-tuple-element.24.w_qkv, ...), custom_call_target="tpu_custom_call" | custom-call | flops 2453667840 | bytes 1048576 | tf_op jit(solution)/shard_map/attend_rest/pallas_call | solution.py:399
  27.1 0.8 %collective-permute-start.4 = (bf16[320,384]{1,0:T(8,128)(2,1)S(1)}, bf16[320,384]{1,0:T(8,128)(2,1)S(1)}, u32[]{:S(2)}, u32[]{:S(2)}) collective-permute-start(bf16[320,384]{1,0:T(8,128)(2,1)S(1)} %attend_rest.1._), channel_id=1, source_target_pairs={{0,4},{1,12},{2,6},{3,14},{4,0},{5,8},{6,2},{7,10},{8,5},{9,13},{1... | collective-permute-start | bytes 737288 | tf_op jit(solution)/shard_map/ppermute | solution.py:406
  27.8 0.0 copy-start
  27.8 3.5 %load_conv.1._.w = bf16[3,1152,1152]{2,1,0:T(8,128)(2,1)S(1)} custom-call(bf16[320,384]{1,0:T(8,128)(2,1)S(1)} %attend_rest.1._, bf16[3,3,3,384,384]{4,3,2,1,0:T(8,128)(2,1)} %w_hbm.1), custom_call_target="tpu_custom_call" | custom-call | bytes 4096 | tf_op jit(solution)/shard_map/load_conv/pallas_call | solution.py:412
  31.3 0.0 copy-start.1
  31.4 0.0 collective-permute-done.5.got_a
  31.4 0.0 copy-done
  31.4 0.3 activate_a.1
  31.7 2.1 %collective-permute-start.6 = (bf16[160,384]{1,0:T(8,128)(2,1)S(1)}, bf16[160,384]{1,0:T(8,128)(2,1)S(1)}, u32[]{:S(2)}, u32[]{:S(2)}) collective-permute-start(bf16[160,384]{1,0:T(8,128)(2,1)S(1)} %get-tuple-element.30), channel_id=1, source_target_pairs={{0,4},{4,0},{8,12},{12,8},{1,5},{5,1},{9,13},{13,9},{2,6},{6,2},{1... | collective-permute-start | bytes 368648 | tf_op jit(solution)/shard_map/ppermute | solution.py:424
  33.8 1.9 %collective-permute-start.7 = (bf16[160,384]{1,0:T(8,128)(2,1)S(1)}, bf16[160,384]{1,0:T(8,128)(2,1)S(1)}, u32[]{:S(2)}, u32[]{:S(2)}) collective-permute-start(bf16[160,384]{1,0:T(8,128)(2,1)S(1)} %get-tuple-element.31), channel_id=1, source_target_pairs={{4,8},{8,4},{5,9},{9,5},{6,10},{10,6},{7,11},{11,7},{20,24},{24,20... | collective-permute-start | bytes 368648 | tf_op jit(solution)/shard_map/ppermute | solution.py:425
  35.7 1.7 %collective-permute-done.4.got_b = bf16[320,384]{1,0:T(8,128)(2,1)S(1)} collective-permute-done((bf16[320,384]{1,0:T(8,128)(2,1)S(1)}, bf16[320,384]{1,0:T(8,128)(2,1)S(1)}, u32[]{:S(2)}, u32[]{:S(2)}) %collective-permute-start.4) | collective-permute-done | bytes 245792 | tf_op jit(solution)/shard_map/ppermute | solution.py:406
  37.5 0.3 activate_b.1
  37.8 0.3 collective-permute-start.8
  38.1 1.9 %collective-permute-start.9 = (bf16[160,384]{1,0:T(8,128)(2,1)S(1)}, bf16[160,384]{1,0:T(8,128)(2,1)S(1)}, u32[]{:S(2)}, u32[]{:S(2)}) collective-permute-start(bf16[160,384]{1,0:T(8,128)(2,1)S(1)} %get-tuple-element.33), channel_id=1, source_target_pairs={{4,8},{8,4},{5,9},{9,5},{6,10},{10,6},{7,11},{11,7},{20,24},{24,20... | collective-permute-start | bytes 368648 | tf_op jit(solution)/shard_map/ppermute | solution.py:433
  40.0 0.0 copy-done.1
  40.0 2.9 %next_own.1.partial = f32[2,320,384]{2,1,0:T(8,128)S(1)} custom-call(s32[1]{0:T(128)} %bitcast.1.span_ref, s32[4]{0:T(128)S(1)} %copy-done.1, bf16[2,320,384]{2,1,0:T(8,128)(2,1)S(1)} %get-tuple-element.29.mid, bf16[3,1152,1152]{2,1,0:T(8,128)(2,1)S(1)} %load_conv.1._.w), custom_call_target="tpu_custom_call" | custom-call | flops 1698693120 | bytes 1048576 | tf_op jit(solution)/shard_map/next_own/pallas_call | solution.py:435
  42.9 0.0 collective-permute-done.6.pair_a
  42.9 0.0 collective-permute-done.8.pair_b
  42.9 1.6 %pair_edge.1.pair_rows = bf16[2,160,384]{2,1,0:T(8,128)(2,1)S(1)} custom-call(s32[1]{0:T(128)} %bitcast.tile_ref, s32[1]{0:T(128)} %bitcast.1.span_ref, s32[4]{0:T(128)S(1)} %copy-done.1, bf16[160,384]{1,0:T(8,128)(2,1)S(1)} %collective-permute-done.6.pair_a, bf16[160,384]{1,0:T(8,128)(2,1)S(1)} %collective-permute-done.8.pair_b, ...), custom_call_target="tpu_custom_call" | custom-call | flops 424673280 | bytes 1048576 | tf_op jit(solution)/shard_map/pair_edge/pallas_call | solution.py:443
  44.5 0.0 collective-permute-done.7.mid_a
  44.5 0.0 collective-permute-done.9.mid_b
  44.5 1.6 %mid_edge.1 = bf16[2,320,384]{2,1,0:T(8,128)(2,1)S(1)} custom-call(s32[1]{0:T(128)} %bitcast.tile_ref, s32[1]{0:T(128)} %bitcast.1.span_ref, s32[4]{0:T(128)S(1)} %copy-done.1, bf16[160,384]{1,0:T(8,128)(2,1)S(1)} %collective-permute-done.7.mid_a, bf16[160,384]{1,0:T(8,128)(2,1)S(1)} %collective-permute-done.9.mid_b, ...), custom_call_target="tpu_custom_call" | custom-call | flops 424673280 | bytes 1048576 | tf_op jit(solution)/shard_map/mid_edge/pallas_call | solution.py:451
  46.1 5.5 %collective-permute-start.10 = (bf16[2,320,384]{2,1,0:T(8,128)(2,1)S(1)}, bf16[2,320,384]{2,1,0:T(8,128)(2,1)S(1)}, u32[]{:S(2)}, u32[]{:S(2)}) collective-permute-start(bf16[2,320,384]{2,1,0:T(8,128)(2,1)S(1)} %mid_edge.1), channel_id=1, source_target_pairs={{1,2},{2,1},{5,6},{6,5},{9,10},{10,9},{13,14},{14,13},{17,18},{18,... | collective-permute-start | bytes 1474568 | tf_op jit(solution)/shard_map/ppermute | solution.py:460
  51.7 0.1 collective-permute-start.11
  51.7 4.6 %own.1 = (f32[2,320,384]{2,1,0:T(8,128)S(1)}, bf16[2,320,384]{2,1,0:T(8,128)(2,1)}) custom-call(s32[1]{0:T(128)} %bitcast.tile_ref, s32[1]{0:T(128)} %bitcast.1.span_ref, s32[4]{0:T(128)S(1)} %copy-done.1, bf16[2,320,384]{2,1,0:T(8,128)(2,1)S(1)} %get-tuple-element.29.mid, bf16[160,384]{1,0:T(8,128)(2,1)S(1)} %collective-permute-done.6.pair_a, ...), custom_call_target="tpu_custom_call" | custom-call | flops 2548039680 | bytes 1048576 | tf_op jit(solution)/shard_map/own/pallas_call | solution.py:462
  56.4 1.6 %collective-permute-done.10.link_got = bf16[2,320,384]{2,1,0:T(8,128)(2,1)S(1)} collective-permute-done((bf16[2,320,384]{2,1,0:T(8,128)(2,1)S(1)}, bf16[2,320,384]{2,1,0:T(8,128)(2,1)S(1)}, u32[]{:S(2)}, u32[]{:S(2)}) %collective-permute-start.10) | collective-permute-done | bytes 491552 | tf_op jit(solution)/shard_map/ppermute | solution.py:460
  58.0 0.0 collective-permute-done.11.core_got
  58.0 0.9 %finish.1 = bf16[2,320,384]{2,1,0:T(8,128)(2,1)} custom-call(s32[1]{0:T(128)} %bitcast.1.span_ref, f32[2,320,384]{2,1,0:T(8,128)S(1)} %get-tuple-element.35.own, bf16[2,320,384]{2,1,0:T(8,128)(2,1)S(1)} %collective-permute-done.10.link_got, bf16[2,320,384]{2,1,0:T(8,128)(2,1)S(1)} %collective-permute-done.11.core_got), custom_call_target="tpu_custom_call" | custom-call | bytes 1048576 | tf_op jit(solution)/shard_map/finish/pallas_call | solution.py:469
Async XLA Ops:
  1.7 13.1 %collective-permute-start.1 = (bf16[320,384]{1,0:T(8,128)(2,1)S(1)}, bf16[320,384]{1,0:T(8,128)(2,1)S(1)}, u32[]{:S(2)}, u32[]{:S(2)}) collective-permute-start(bf16[320,384]{1,0:T(8,128)(2,1)S(1)} %get-tuple-element.20), channel_id=1, source_target_pairs={{0,0},{1,8},{2,2},{3,10},{4,4},{5,12},{6,6},{7,14},{8,1},{9,9},{10... | collective-permute-start | bytes 737288 | tf_op jit(solution)/shard_map/ppermute | solution.py:373
  6.5 11.0 %collective-permute-start = (bf16[320,384]{1,0:T(8,128)(2,1)S(1)}, bf16[320,384]{1,0:T(8,128)(2,1)S(1)}, u32[]{:S(2)}, u32[]{:S(2)}) collective-permute-start(bf16[320,384]{1,0:T(8,128)(2,1)S(1)} %get-tuple-element.19), channel_id=1, source_target_pairs={{0,4},{1,12},{2,6},{3,14},{4,0},{5,8},{6,2},{7,10},{8,5},{9,13},{1... | collective-permute-start | bytes 737288 | tf_op jit(solution)/shard_map/ppermute | solution.py:374
  14.9 2.6 %collective-permute-start.2 = (bf16[320,384]{1,0:T(8,128)(2,1)S(1)}, bf16[320,384]{1,0:T(8,128)(2,1)S(1)}, u32[]{:S(2)}, u32[]{:S(2)}) collective-permute-start(bf16[320,384]{1,0:T(8,128)(2,1)S(1)} %collective-permute-done.1.own_a), channel_id=1, source_target_pairs={{0,1},{1,0},{2,3},{3,2},{4,5},{5,4},{6,7},{7,6},{8,9},{9,8},{10,11... | collective-permute-start | bytes 737288 | tf_op jit(solution)/shard_map/ppermute | solution.py:384
  17.5 1.5 %collective-permute-start.3 = (bf16[320,384]{1,0:T(8,128)(2,1)S(1)}, bf16[320,384]{1,0:T(8,128)(2,1)S(1)}, u32[]{:S(2)}, u32[]{:S(2)}) collective-permute-start(bf16[320,384]{1,0:T(8,128)(2,1)S(1)} %collective-permute-done.own_b), channel_id=1, source_target_pairs={{0,1},{1,0},{2,3},{3,2},{4,5},{5,4},{6,7},{7,6},{8,9},{9,8},{10,11... | collective-permute-start | bytes 737288 | tf_op jit(solution)/shard_map/ppermute | solution.py:385
  21.3 10.1 %collective-permute-start.5 = (bf16[320,384]{1,0:T(8,128)(2,1)S(1)}, bf16[320,384]{1,0:T(8,128)(2,1)S(1)}, u32[]{:S(2)}, u32[]{:S(2)}) collective-permute-start(bf16[320,384]{1,0:T(8,128)(2,1)S(1)} %get-tuple-element.27), channel_id=1, source_target_pairs={{0,0},{1,8},{2,2},{3,10},{4,4},{5,12},{6,6},{7,14},{8,1},{9,9},{10... | collective-permute-start | bytes 737288 | tf_op jit(solution)/shard_map/ppermute | solution.py:398
  27.1 10.4 %collective-permute-start.4 = (bf16[320,384]{1,0:T(8,128)(2,1)S(1)}, bf16[320,384]{1,0:T(8,128)(2,1)S(1)}, u32[]{:S(2)}, u32[]{:S(2)}) collective-permute-start(bf16[320,384]{1,0:T(8,128)(2,1)S(1)} %attend_rest.1._), channel_id=1, source_target_pairs={{0,4},{1,12},{2,6},{3,14},{4,0},{5,8},{6,2},{7,10},{8,5},{9,13},{1... | collective-permute-start | bytes 737288 | tf_op jit(solution)/shard_map/ppermute | solution.py:406
  27.8 3.5 %copy-start = (f32[384]{0:T(512)S(1)}, f32[384]{0:T(512)}, u32[]{:S(2)}) copy-start(f32[384]{0:T(512)} %gain.5) | copy-start | bytes 4612
  31.3 8.6 %copy-start.1 = (s32[4]{0:T(128)S(1)}, s32[4]{0:T(128)}, u32[]{:S(2)}) copy-start(s32[4]{0:T(128)} %clips.7) | copy-start | bytes 52
  31.7 11.2 %collective-permute-start.6 = (bf16[160,384]{1,0:T(8,128)(2,1)S(1)}, bf16[160,384]{1,0:T(8,128)(2,1)S(1)}, u32[]{:S(2)}, u32[]{:S(2)}) collective-permute-start(bf16[160,384]{1,0:T(8,128)(2,1)S(1)} %get-tuple-element.30), channel_id=1, source_target_pairs={{0,4},{4,0},{8,12},{12,8},{1,5},{5,1},{9,13},{13,9},{2,6},{6,2},{1... | collective-permute-start | bytes 368648 | tf_op jit(solution)/shard_map/ppermute | solution.py:424
  33.8 10.7 %collective-permute-start.7 = (bf16[160,384]{1,0:T(8,128)(2,1)S(1)}, bf16[160,384]{1,0:T(8,128)(2,1)S(1)}, u32[]{:S(2)}, u32[]{:S(2)}) collective-permute-start(bf16[160,384]{1,0:T(8,128)(2,1)S(1)} %get-tuple-element.31), channel_id=1, source_target_pairs={{4,8},{8,4},{5,9},{9,5},{6,10},{10,6},{7,11},{11,7},{20,24},{24,20... | collective-permute-start | bytes 368648 | tf_op jit(solution)/shard_map/ppermute | solution.py:425
  37.8 5.1 %collective-permute-start.8 = (bf16[160,384]{1,0:T(8,128)(2,1)S(1)}, bf16[160,384]{1,0:T(8,128)(2,1)S(1)}, u32[]{:S(2)}, u32[]{:S(2)}) collective-permute-start(bf16[160,384]{1,0:T(8,128)(2,1)S(1)} %get-tuple-element.32), channel_id=1, source_target_pairs={{0,4},{4,0},{8,12},{12,8},{1,5},{5,1},{9,13},{13,9},{2,6},{6,2},{1... | collective-permute-start | bytes 368648 | tf_op jit(solution)/shard_map/ppermute | solution.py:432
  38.1 6.4 %collective-permute-start.9 = (bf16[160,384]{1,0:T(8,128)(2,1)S(1)}, bf16[160,384]{1,0:T(8,128)(2,1)S(1)}, u32[]{:S(2)}, u32[]{:S(2)}) collective-permute-start(bf16[160,384]{1,0:T(8,128)(2,1)S(1)} %get-tuple-element.33), channel_id=1, source_target_pairs={{4,8},{8,4},{5,9},{9,5},{6,10},{10,6},{7,11},{11,7},{20,24},{24,20... | collective-permute-start | bytes 368648 | tf_op jit(solution)/shard_map/ppermute | solution.py:433
  46.1 11.9 %collective-permute-start.10 = (bf16[2,320,384]{2,1,0:T(8,128)(2,1)S(1)}, bf16[2,320,384]{2,1,0:T(8,128)(2,1)S(1)}, u32[]{:S(2)}, u32[]{:S(2)}) collective-permute-start(bf16[2,320,384]{2,1,0:T(8,128)(2,1)S(1)} %mid_edge.1), channel_id=1, source_target_pairs={{1,2},{2,1},{5,6},{6,5},{9,10},{10,9},{13,14},{14,13},{17,18},{18,... | collective-permute-start | bytes 1474568 | tf_op jit(solution)/shard_map/ppermute | solution.py:460
  51.7 6.3 %collective-permute-start.11 = (bf16[2,320,384]{2,1,0:T(8,128)(2,1)S(1)}, bf16[2,320,384]{2,1,0:T(8,128)(2,1)S(1)}, u32[]{:S(2)}, u32[]{:S(2)}) collective-permute-start(bf16[2,320,384]{2,1,0:T(8,128)(2,1)S(1)} %mid_edge.1), channel_id=1, source_target_pairs={{0,1},{1,0},{2,3},{3,2},{4,5},{5,4},{6,7},{7,6},{8,9},{9,8},{10,11... | collective-permute-start | bytes 1474568 | tf_op jit(solution)/shard_map/ppermute | solution.py:461

commit v12 on v11

--- a/solution.py
+++ b/solution.py
@@ -101,17 +101,19 @@
     out[place * cells : (place + 1) * cells, :] = dot32(normed, w_qkv[:, ch:]).astype(bf16)
 
 
-def keys_kernel(own_a, other_a, own_b, gain, w_qkv, kv_out):
-    gain_vec = gain[...].reshape(1, own_a.shape[1])
-    for place, block in enumerate((own_a, other_a, own_b)):
-        project_keys(block, gain_vec, w_qkv, kv_out, place)
-
-
-def attend_rows(source, kv_parts, gain_vec, w_qkv, w_out, att_out):
+def keys_kernel(own_a, other_a, own_b, gain, w_qkv, kv_out, q_out):
+    cells, ch = own_a.shape
+    gain_vec = gain[...].reshape(1, ch)
+    project_keys(other_a, gain_vec, w_qkv, kv_out, 1)
+    for place, block in ((0, own_a), (2, own_b)):
+        normed = rms_scale(block[...], gain_vec).astype(bf16)
+        qkv = dot32(normed, w_qkv[...]).astype(bf16)
+        q_out[place // 2] = qkv[:, :ch]
+        kv_out[place * cells : (place + 1) * cells, :] = qkv[:, ch:]
+
+
+def attend_rows(source, queries, kv_parts, w_out, att_out):
     ch = source.shape[1]
-    feats = source[...]
-    normed = rms_scale(feats, gain_vec).astype(bf16)
-    queries = dot32(normed, w_qkv[:, :ch]).astype(bf16)
     scores = [
         lax.dot_general(
             queries, kv[:, :ch], (((1,), (1,)), ((), ())), preferred_element_type=f32
@@ -124,18 +126,16 @@
     total = sum(jnp.sum(r, axis=1, keepdims=True) for r in raised)
     mixed = sum(dot32(r.astype(bf16), kv[:, ch:]) for r, kv in zip(raised, kv_parts))
     mixture = (mixed / total).astype(bf16)
-    att_out[...] = (feats.astype(f32) + dot32(mixture, w_out[...])).astype(bf16)
-
-
-def attend_kernel(other_b, own_a, kv_a, gain, w_qkv, w_out, kv_b, att_a):
-    gain_vec = gain[...].reshape(1, own_a.shape[1])
-    project_keys(other_b, gain_vec, w_qkv, kv_b, 0)
-    attend_rows(own_a, (kv_a, kv_b), gain_vec, w_qkv, w_out, att_a)
-
-
-def attend_rest_kernel(own_b, kv_a, kv_b, gain, w_qkv, w_out, att_b):
-    gain_vec = gain[...].reshape(1, own_b.shape[1])
-    attend_rows(own_b, (kv_a, kv_b), gain_vec, w_qkv, w_out, att_b)
+    att_out[...] = (source[...].astype(f32) + dot32(mixture, w_out[...])).astype(bf16)
+
+
+def attend_kernel(other_b, own_a, queries, kv_a, gain, w_qkv, w_out, kv_b, att_a):
+    project_keys(other_b, gain[...].reshape(1, own_a.shape[1]), w_qkv, kv_b, 0)
+    attend_rows(own_a, queries[0], (kv_a, kv_b), w_out, att_a)
+
+
+def attend_rest_kernel(own_b, queries, kv_a, kv_b, w_out, att_b):
+    attend_rows(own_b, queries[1], (kv_a, kv_b), w_out, att_b)
 
 
 def load_kernel(_, w_hbm, w_vm, sem):
@@ -385,24 +385,24 @@
     other_b = lax.ppermute(own_b, "span", other_core)
     kv_flops = 2 * 2 * cells * ch * 2 * ch
     row_flops = 2 * cells * ch * (2 * ch + 8 * cells)
-    kv_a = call(keys_kernel, "keys", struct((3 * cells, 2 * ch)), [VMEM] * 5, flops=kv_flops)(
-        own_a, other_a, own_b, norm_gain, w_qkv
-    )
+    kv_a, queries = call(
+        keys_kernel,
+        "keys",
+        (struct((3 * cells, 2 * ch)), struct((2, cells, ch))),
+        [VMEM] * 5,
+        flops=kv_flops,
+    )(own_a, other_a, own_b, norm_gain, w_qkv)
     kv_b, att_a = call(
         attend_kernel,
         "attend",
         (struct((cells, 2 * ch)), struct((cells, ch))),
-        [VMEM] * 6,
+        [VMEM] * 7,
         flops=kv_flops + row_flops,
-    )(other_b, own_a, kv_a, norm_gain, w_qkv, w_out)
+    )(other_b, own_a, queries, kv_a, norm_gain, w_qkv, w_out)
     got_a = lax.ppermute(att_a, both, route_a)
     att_b = call(
-        attend_rest_kernel,
-        "attend_rest",
-        struct((cells, ch)),
-        [VMEM] * 6,
-        flops=3 * row_flops,
-    )(own_b, kv_a, kv_b, norm_gain, w_qkv, w_out)
+        attend_rest_kernel, "attend_rest", struct((cells, ch)), [VMEM] * 5, flops=3 * row_flops
+    )(own_b, queries, kv_a, kv_b, w_out)
     got_b = lax.ppermute(att_b, both, route_b)
     pairs, middle = [(0, 1), (1, 0), (2, 3), (3, 2)], [(1, 2), (2, 1)]
     one, edge = struct((cells, ch)), struct((cols, ch))

time: 59.1 us -> 58.9 us (level)
  the two profiles are of different devices: /device:TPU:9 before, /device:TPU:13 now
where the time goes in v12:
time: 58.9 us; the launch traced here: 58.6 us
  starting transfers between devices  22.3 us (38%)
  Pallas kernels  19.7 us (33%)
  waiting for transfers between devices  15.8 us (27%)
  between operations  0.82 us (1%)
    ppermute x1, starting transfers between devices, on_device(): link_got = lax.ppermute(for_next, 'span', link)  6.44 us
    ppermute x1, waiting for transfers between devices, on_device(): own_a = lax.ppermute(send_a, both, route_a)  6.34 us
    ppermute x1, starting transfers between devices, on_device(): own_a = lax.ppermute(send_a, both, route_a)  4.78 us
    pallas_call x1, Pallas kernels, on_device(): call(functools.partial(own_kernel, cols), 'own', (sums, struct((frames, c...  4.62 us
    ppermute x1, starting transfers between devices, on_device(): got_a = lax.ppermute(att_a, both, route_a)  3.98 us
    pallas_call x1, Pallas kernels, on_device(): call(load_kernel, 'load_conv', struct((3, 3 * ch, 3 * ch)), [ANY, ANY], [...  3.48 us
    ppermute x1, waiting for transfers between devices, on_device(): own_b = lax.ppermute(send_b, both, route_b)  2.63 us
    ppermute x1, starting transfers between devices, on_device(): pair_a = lax.ppermute(pair_edge, 'tile', pairs)  2.36 us
  transfers between devices with their start and end apart: 12, of which 7 were waited for; matrix products, arithmetic and copies ran while one was open for 0% of the time, Pallas kernels for 26%

profile of v12, /device:TPU:13, one launch (start us, length us, event | category | flops | bytes accessed | tf_op | source)
XLA Modules:
  0.0 58.6 jit_solution(15736523805525978561)
XLA Ops:
  0.6 1.1 %pick.1 = (bf16[320,384]{1,0:T(8,128)(2,1)S(1)}, bf16[320,384]{1,0:T(8,128)(2,1)S(1)}) custom-call(s32[1]{0:T(128)} %bitcast.tile_ref, bf16[2,320,384]{2,1,0:T(8,128)(2,1)} %bitcast.5), custom_call_target="tpu_custom_call" | custom-call | bytes 1048576 | tf_op jit(solution)/shard_map/pick/pallas_call | solution.py:365
  1.7 4.8 %collective-permute-start.1 = (bf16[320,384]{1,0:T(8,128)(2,1)S(1)}, bf16[320,384]{1,0:T(8,128)(2,1)S(1)}, u32[]{:S(2)}, u32[]{:S(2)}) collective-permute-start(bf16[320,384]{1,0:T(8,128)(2,1)S(1)} %get-tuple-element.22), channel_id=1, source_target_pairs={{0,0},{1,8},{2,2},{3,10},{4,4},{5,12},{6,6},{7,14},{8,1},{9,9},{10... | collective-permute-start | bytes 737288 | tf_op jit(solution)/shard_map/ppermute | solution.py:373
  6.5 0.1 collective-permute-start
  6.6 1.9 %load_small.1 = (bf16[384,1152]{1,0:T(8,128)(2,1)S(1)}, bf16[384,384]{1,0:T(8,128)(2,1)S(1)}, f32[384]{0:T(512)S(1)}) custom-call(bf16[384,1152]{1,0:T(8,128)(2,1)} %w_qkv.1, bf16[384,384]{1,0:T(8,128)(2,1)} %w_out.1, f32[384]{0:T(512)} %gain.3), custom_call_target="tpu_custom_call" | custom-call | bytes 1048576 | tf_op jit(solution)/shard_map/load_small/pallas_call | solution.py:375
  8.5 6.3 %collective-permute-done.1.own_a = bf16[320,384]{1,0:T(8,128)(2,1)S(1)} collective-permute-done((bf16[320,384]{1,0:T(8,128)(2,1)S(1)}, bf16[320,384]{1,0:T(8,128)(2,1)S(1)}, u32[]{:S(2)}, u32[]{:S(2)}) %collective-permute-start.1) | collective-permute-done | bytes 245792 | tf_op jit(solution)/shard_map/ppermute | solution.py:373
  14.9 0.0 collective-permute-start.2
  14.9 2.6 %collective-permute-done.own_b = bf16[320,384]{1,0:T(8,128)(2,1)S(1)} collective-permute-done((bf16[320,384]{1,0:T(8,128)(2,1)S(1)}, bf16[320,384]{1,0:T(8,128)(2,1)S(1)}, u32[]{:S(2)}, u32[]{:S(2)}) %collective-permute-start) | collective-permute-done | bytes 245792 | tf_op jit(solution)/shard_map/ppermute | solution.py:374
  17.5 0.0 collective-permute-start.3
  17.5 0.0 collective-permute-done.2.other_a
  17.5 1.3 %keys.1 = (bf16[960,768]{1,0:T(8,128)(2,1)S(1)}, bf16[2,320,384]{2,1,0:T(8,128)(2,1)S(1)}) custom-call(bf16[320,384]{1,0:T(8,128)(2,1)S(1)} %collective-permute-done.1.own_a, bf16[320,384]{1,0:T(8,128)(2,1)S(1)} %collective-permute-done.2.other_a, bf16[320,384]{1,0:T(8,128)(2,1)S(1)} %collective-permute-done.own_b, f32[384]{0:T(512)S(1)} %get-tuple-element.25.gain, ...), custom_call_target="tpu_custom_call" | custom-call | flops 377487360 | bytes 1048576 | tf_op jit(solution)/shard_map/keys/pallas_call | solution.py:388
  18.8 0.2 collective-permute-done.3.other_b
  19.0 2.1 %attend.1 = (bf16[320,768]{1,0:T(8,128)(2,1)S(1)}, bf16[320,384]{1,0:T(8,128)(2,1)S(1)}) custom-call(bf16[320,384]{1,0:T(8,128)(2,1)S(1)} %collective-permute-done.3.other_b, bf16[320,384]{1,0:T(8,128)(2,1)S(1)} %collective-permute-done.1.own_a, bf16[2,320,384]{2,1,0:T(8,128)(2,1)S(1)} %get-tuple-element.27.queries, ...), custom_call_target="tpu_custom_call" | custom-call | flops 1195376640 | bytes 1048576 | tf_op jit(solution)/shard_map/attend/pallas_call | solution.py:395
  21.1 4.0 %collective-permute-start.5 = (bf16[320,384]{1,0:T(8,128)(2,1)S(1)}, bf16[320,384]{1,0:T(8,128)(2,1)S(1)}, u32[]{:S(2)}, u32[]{:S(2)}) collective-permute-start(bf16[320,384]{1,0:T(8,128)(2,1)S(1)} %get-tuple-element.31), channel_id=1, source_target_pairs={{0,0},{1,8},{2,2},{3,10},{4,4},{5,12},{6,6},{7,14},{8,1},{9,9},{10... | collective-permute-start | bytes 737288 | tf_op jit(solution)/shard_map/ppermute | solution.py:402
  25.1 1.8 %attend_rest.1._ = bf16[320,384]{1,0:T(8,128)(2,1)S(1)} custom-call(bf16[320,384]{1,0:T(8,128)(2,1)S(1)} %collective-permute-done.own_b, bf16[2,320,384]{2,1,0:T(8,128)(2,1)S(1)} %get-tuple-element.27.queries, bf16[960,768]{1,0:T(8,128)(2,1)S(1)} %get-tuple-element.28.kv_a, bf16[320,768]{1,0:T(8,128)(2,1)S(1)} %get-tuple-element.30.kv_b, ...), custom_call_target="tpu_custom_call" | custom-call | flops 2453667840 | bytes 1048576 | tf_op jit(solution)/shard_map/attend_rest/pallas_call | solution.py:403
  26.9 0.5 collective-permute-start.4
  27.4 0.0 copy-start
  27.4 3.5 %load_conv.1._.w = bf16[3,1152,1152]{2,1,0:T(8,128)(2,1)S(1)} custom-call(bf16[320,384]{1,0:T(8,128)(2,1)S(1)} %attend_rest.1._, bf16[3,3,3,384,384]{4,3,2,1,0:T(8,128)(2,1)} %w_hbm.1), custom_call_target="tpu_custom_call" | custom-call | bytes 4096 | tf_op jit(solution)/shard_map/load_conv/pallas_call | solution.py:412
  30.9 0.0 copy-start.1
  30.9 0.0 collective-permute-done.5.got_a
  31.0 0.0 copy-done
  31.0 0.3 activate_a.1
  31.3 2.4 %collective-permute-start.6 = (bf16[160,384]{1,0:T(8,128)(2,1)S(1)}, bf16[160,384]{1,0:T(8,128)(2,1)S(1)}, u32[]{:S(2)}, u32[]{:S(2)}) collective-permute-start(bf16[160,384]{1,0:T(8,128)(2,1)S(1)} %get-tuple-element.34), channel_id=1, source_target_pairs={{0,4},{4,0},{8,12},{12,8},{1,5},{5,1},{9,13},{13,9},{2,6},{6,2},{1... | collective-permute-start | bytes 368648 | tf_op jit(solution)/shard_map/ppermute | solution.py:424
  33.6 1.9 %collective-permute-start.7 = (bf16[160,384]{1,0:T(8,128)(2,1)S(1)}, bf16[160,384]{1,0:T(8,128)(2,1)S(1)}, u32[]{:S(2)}, u32[]{:S(2)}) collective-permute-start(bf16[160,384]{1,0:T(8,128)(2,1)S(1)} %get-tuple-element.35), channel_id=1, source_target_pairs={{4,8},{8,4},{5,9},{9,5},{6,10},{10,6},{7,11},{11,7},{20,24},{24,20... | collective-permute-start | bytes 368648 | tf_op jit(solution)/shard_map/ppermute | solution.py:425
  35.5 1.7 %collective-permute-done.4.got_b = bf16[320,384]{1,0:T(8,128)(2,1)S(1)} collective-permute-done((bf16[320,384]{1,0:T(8,128)(2,1)S(1)}, bf16[320,384]{1,0:T(8,128)(2,1)S(1)}, u32[]{:S(2)}, u32[]{:S(2)}) %collective-permute-start.4) | collective-permute-done | bytes 245792 | tf_op jit(solution)/shard_map/ppermute | solution.py:406
  37.3 0.3 activate_b.1
  37.6 0.3 collective-permute-start.8
  37.9 1.9 %collective-permute-start.9 = (bf16[160,384]{1,0:T(8,128)(2,1)S(1)}, bf16[160,384]{1,0:T(8,128)(2,1)S(1)}, u32[]{:S(2)}, u32[]{:S(2)}) collective-permute-start(bf16[160,384]{1,0:T(8,128)(2,1)S(1)} %get-tuple-element.37), channel_id=1, source_target_pairs={{4,8},{8,4},{5,9},{9,5},{6,10},{10,6},{7,11},{11,7},{20,24},{24,20... | collective-permute-start | bytes 368648 | tf_op jit(solution)/shard_map/ppermute | solution.py:433
  39.8 0.0 copy-done.1
  39.8 0.6 %next_own.1.partial = f32[2,320,384]{2,1,0:T(8,128)S(1)} custom-call(s32[1]{0:T(128)} %bitcast.1.span_ref, s32[4]{0:T(128)S(1)} %copy-done.1, bf16[2,320,384]{2,1,0:T(8,128)(2,1)S(1)} %get-tuple-element.33.mid, bf16[3,1152,1152]{2,1,0:T(8,128)(2,1)S(1)} %load_conv.1._.w), custom_call_target="tpu_custom_call" | custom-call | flops 1698693120 | bytes 1048576 | tf_op jit(solution)/shard_map/next_own/pallas_call | solution.py:435
  40.4 0.0 collective-permute-done.6.pair_a
  40.5 1.7 %collective-permute-done.8.pair_b = bf16[160,384]{1,0:T(8,128)(2,1)S(1)} collective-permute-done((bf16[160,384]{1,0:T(8,128)(2,1)S(1)}, bf16[160,384]{1,0:T(8,128)(2,1)S(1)}, u32[]{:S(2)}, u32[]{:S(2)}) %collective-permute-start.8) | collective-permute-done | bytes 122912 | tf_op jit(solution)/shard_map/ppermute | solution.py:432
  42.1 0.6 %pair_edge.1.pair_rows = bf16[2,160,384]{2,1,0:T(8,128)(2,1)S(1)} custom-call(s32[1]{0:T(128)} %bitcast.tile_ref, s32[1]{0:T(128)} %bitcast.1.span_ref, s32[4]{0:T(128)S(1)} %copy-done.1, bf16[160,384]{1,0:T(8,128)(2,1)S(1)} %collective-permute-done.6.pair_a, bf16[160,384]{1,0:T(8,128)(2,1)S(1)} %collective-permute-done.8.pair_b, ...), custom_call_target="tpu_custom_call" | custom-call | flops 424673280 | bytes 1048576 | tf_op jit(solution)/shard_map/pair_edge/pallas_call | solution.py:443
  42.8 0.0 collective-permute-done.7.mid_a
  42.8 1.6 %collective-permute-done.9.mid_b = bf16[160,384]{1,0:T(8,128)(2,1)S(1)} collective-permute-done((bf16[160,384]{1,0:T(8,128)(2,1)S(1)}, bf16[160,384]{1,0:T(8,128)(2,1)S(1)}, u32[]{:S(2)}, u32[]{:S(2)}) %collective-permute-start.9) | collective-permute-done | bytes 122912 | tf_op jit(solution)/shard_map/ppermute | solution.py:433
  44.3 0.7 %mid_edge.1 = bf16[2,320,384]{2,1,0:T(8,128)(2,1)S(1)} custom-call(s32[1]{0:T(128)} %bitcast.tile_ref, s32[1]{0:T(128)} %bitcast.1.span_ref, s32[4]{0:T(128)S(1)} %copy-done.1, bf16[160,384]{1,0:T(8,128)(2,1)S(1)} %collective-permute-done.7.mid_a, bf16[160,384]{1,0:T(8,128)(2,1)S(1)} %collective-permute-done.9.mid_b, ...), custom_call_target="tpu_custom_call" | custom-call | flops 424673280 | bytes 1048576 | tf_op jit(solution)/shard_map/mid_edge/pallas_call | solution.py:451
  45.0 6.4 %collective-permute-start.10 = (bf16[2,320,384]{2,1,0:T(8,128)(2,1)S(1)}, bf16[2,320,384]{2,1,0:T(8,128)(2,1)S(1)}, u32[]{:S(2)}, u32[]{:S(2)}) collective-permute-start(bf16[2,320,384]{2,1,0:T(8,128)(2,1)S(1)} %mid_edge.1), channel_id=1, source_target_pairs={{1,2},{2,1},{5,6},{6,5},{9,10},{10,9},{13,14},{14,13},{17,18},{18,... | collective-permute-start | bytes 1474568 | tf_op jit(solution)/shard_map/ppermute | solution.py:460
  51.5 0.1 collective-permute-start.11
  51.5 4.6 %own.1 = (f32[2,320,384]{2,1,0:T(8,128)S(1)}, bf16[2,320,384]{2,1,0:T(8,128)(2,1)}) custom-call(s32[1]{0:T(128)} %bitcast.tile_ref, s32[1]{0:T(128)} %bitcast.1.span_ref, s32[4]{0:T(128)S(1)} %copy-done.1, bf16[2,320,384]{2,1,0:T(8,128)(2,1)S(1)} %get-tuple-element.33.mid, bf16[160,384]{1,0:T(8,128)(2,1)S(1)} %collective-permute-done.6.pair_a, ...), custom_call_target="tpu_custom_call" | custom-call | flops 2548039680 | bytes 1048576 | tf_op jit(solution)/shard_map/own/pallas_call | solution.py:462
  56.1 1.6 %collective-permute-done.10.link_got = bf16[2,320,384]{2,1,0:T(8,128)(2,1)S(1)} collective-permute-done((bf16[2,320,384]{2,1,0:T(8,128)(2,1)S(1)}, bf16[2,320,384]{2,1,0:T(8,128)(2,1)S(1)}, u32[]{:S(2)}, u32[]{:S(2)}) %collective-permute-start.10) | collective-permute-done | bytes 491552 | tf_op jit(solution)/shard_map/ppermute | solution.py:460
  57.8 0.0 collective-permute-done.11.core_got
  57.8 0.9 %finish.1 = bf16[2,320,384]{2,1,0:T(8,128)(2,1)} custom-call(s32[1]{0:T(128)} %bitcast.1.span_ref, f32[2,320,384]{2,1,0:T(8,128)S(1)} %get-tuple-element.39.own, bf16[2,320,384]{2,1,0:T(8,128)(2,1)S(1)} %collective-permute-done.10.link_got, bf16[2,320,384]{2,1,0:T(8,128)(2,1)S(1)} %collective-permute-done.11.core_got), custom_call_target="tpu_custom_call" | custom-call | bytes 1048576 | tf_op jit(solution)/shard_map/finish/pallas_call | solution.py:469
Async XLA Ops:
  1.7 13.1 %collective-permute-start.1 = (bf16[320,384]{1,0:T(8,128)(2,1)S(1)}, bf16[320,384]{1,0:T(8,128)(2,1)S(1)}, u32[]{:S(2)}, u32[]{:S(2)}) collective-permute-start(bf16[320,384]{1,0:T(8,128)(2,1)S(1)} %get-tuple-element.22), channel_id=1, source_target_pairs={{0,0},{1,8},{2,2},{3,10},{4,4},{5,12},{6,6},{7,14},{8,1},{9,9},{10... | collective-permute-start | bytes 737288 | tf_op jit(solution)/shard_map/ppermute | solution.py:373
  6.5 11.0 %collective-permute-start = (bf16[320,384]{1,0:T(8,128)(2,1)S(1)}, bf16[320,384]{1,0:T(8,128)(2,1)S(1)}, u32[]{:S(2)}, u32[]{:S(2)}) collective-permute-start(bf16[320,384]{1,0:T(8,128)(2,1)S(1)} %get-tuple-element.21), channel_id=1, source_target_pairs={{0,4},{1,12},{2,6},{3,14},{4,0},{5,8},{6,2},{7,10},{8,5},{9,13},{1... | collective-permute-start | bytes 737288 | tf_op jit(solution)/shard_map/ppermute | solution.py:374
  14.9 2.6 %collective-permute-start.2 = (bf16[320,384]{1,0:T(8,128)(2,1)S(1)}, bf16[320,384]{1,0:T(8,128)(2,1)S(1)}, u32[]{:S(2)}, u32[]{:S(2)}) collective-permute-start(bf16[320,384]{1,0:T(8,128)(2,1)S(1)} %collective-permute-done.1.own_a), channel_id=1, source_target_pairs={{0,1},{1,0},{2,3},{3,2},{4,5},{5,4},{6,7},{7,6},{8,9},{9,8},{10,11... | collective-permute-start | bytes 737288 | tf_op jit(solution)/shard_map/ppermute | solution.py:384
  17.5 1.5 %collective-permute-start.3 = (bf16[320,384]{1,0:T(8,128)(2,1)S(1)}, bf16[320,384]{1,0:T(8,128)(2,1)S(1)}, u32[]{:S(2)}, u32[]{:S(2)}) collective-permute-start(bf16[320,384]{1,0:T(8,128)(2,1)S(1)} %collective-permute-done.own_b), channel_id=1, source_target_pairs={{0,1},{1,0},{2,3},{3,2},{4,5},{5,4},{6,7},{7,6},{8,9},{9,8},{10,11... | collective-permute-start | bytes 737288 | tf_op jit(solution)/shard_map/ppermute | solution.py:385
  21.1 9.8 %collective-permute-start.5 = (bf16[320,384]{1,0:T(8,128)(2,1)S(1)}, bf16[320,384]{1,0:T(8,128)(2,1)S(1)}, u32[]{:S(2)}, u32[]{:S(2)}) collective-permute-start(bf16[320,384]{1,0:T(8,128)(2,1)S(1)} %get-tuple-element.31), channel_id=1, source_target_pairs={{0,0},{1,8},{2,2},{3,10},{4,4},{5,12},{6,6},{7,14},{8,1},{9,9},{10... | collective-permute-start | bytes 737288 | tf_op jit(solution)/shard_map/ppermute | solution.py:402
  26.9 10.3 %collective-permute-start.4 = (bf16[320,384]{1,0:T(8,128)(2,1)S(1)}, bf16[320,384]{1,0:T(8,128)(2,1)S(1)}, u32[]{:S(2)}, u32[]{:S(2)}) collective-permute-start(bf16[320,384]{1,0:T(8,128)(2,1)S(1)} %attend_rest.1._), channel_id=1, source_target_pairs={{0,4},{1,12},{2,6},{3,14},{4,0},{5,8},{6,2},{7,10},{8,5},{9,13},{1... | collective-permute-start | bytes 737288 | tf_op jit(solution)/shard_map/ppermute | solution.py:406
  27.4 3.5 %copy-start = (f32[384]{0:T(512)S(1)}, f32[384]{0:T(512)}, u32[]{:S(2)}) copy-start(f32[384]{0:T(512)} %gain.5) | copy-start | bytes 4612
  30.9 8.9 %copy-start.1 = (s32[4]{0:T(128)S(1)}, s32[4]{0:T(128)}, u32[]{:S(2)}) copy-start(s32[4]{0:T(128)} %clips.7) | copy-start | bytes 52
  31.3 9.2 %collective-permute-start.6 = (bf16[160,384]{1,0:T(8,128)(2,1)S(1)}, bf16[160,384]{1,0:T(8,128)(2,1)S(1)}, u32[]{:S(2)}, u32[]{:S(2)}) collective-permute-start(bf16[160,384]{1,0:T(8,128)(2,1)S(1)} %get-tuple-element.34), channel_id=1, source_target_pairs={{0,4},{4,0},{8,12},{12,8},{1,5},{5,1},{9,13},{13,9},{2,6},{6,2},{1... | collective-permute-start | bytes 368648 | tf_op jit(solution)/shard_map/ppermute | solution.py:424
  33.6 9.1 %collective-permute-start.7 = (bf16[160,384]{1,0:T(8,128)(2,1)S(1)}, bf16[160,384]{1,0:T(8,128)(2,1)S(1)}, u32[]{:S(2)}, u32[]{:S(2)}) collective-permute-start(bf16[160,384]{1,0:T(8,128)(2,1)S(1)} %get-tuple-element.35), channel_id=1, source_target_pairs={{4,8},{8,4},{5,9},{9,5},{6,10},{10,6},{7,11},{11,7},{20,24},{24,20... | collective-permute-start | bytes 368648 | tf_op jit(solution)/shard_map/ppermute | solution.py:425
  37.6 4.5 %collective-permute-start.8 = (bf16[160,384]{1,0:T(8,128)(2,1)S(1)}, bf16[160,384]{1,0:T(8,128)(2,1)S(1)}, u32[]{:S(2)}, u32[]{:S(2)}) collective-permute-start(bf16[160,384]{1,0:T(8,128)(2,1)S(1)} %get-tuple-element.36), channel_id=1, source_target_pairs={{0,4},{4,0},{8,12},{12,8},{1,5},{5,1},{9,13},{13,9},{2,6},{6,2},{1... | collective-permute-start | bytes 368648 | tf_op jit(solution)/shard_map/ppermute | solution.py:432
  37.9 6.5 %collective-permute-start.9 = (bf16[160,384]{1,0:T(8,128)(2,1)S(1)}, bf16[160,384]{1,0:T(8,128)(2,1)S(1)}, u32[]{:S(2)}, u32[]{:S(2)}) collective-permute-start(bf16[160,384]{1,0:T(8,128)(2,1)S(1)} %get-tuple-element.37), channel_id=1, source_target_pairs={{4,8},{8,4},{5,9},{9,5},{6,10},{10,6},{7,11},{11,7},{20,24},{24,20... | collective-permute-start | bytes 368648 | tf_op jit(solution)/shard_map/ppermute | solution.py:433
  45.0 12.8 %collective-permute-start.10 = (bf16[2,320,384]{2,1,0:T(8,128)(2,1)S(1)}, bf16[2,320,384]{2,1,0:T(8,128)(2,1)S(1)}, u32[]{:S(2)}, u32[]{:S(2)}) collective-permute-start(bf16[2,320,384]{2,1,0:T(8,128)(2,1)S(1)} %mid_edge.1), channel_id=1, source_target_pairs={{1,2},{2,1},{5,6},{6,5},{9,10},{10,9},{13,14},{14,13},{17,18},{18,... | collective-permute-start | bytes 1474568 | tf_op jit(solution)/shard_map/ppermute | solution.py:460
  51.5 6.3 %collective-permute-start.11 = (bf16[2,320,384]{2,1,0:T(8,128)(2,1)S(1)}, bf16[2,320,384]{2,1,0:T(8,128)(2,1)S(1)}, u32[]{:S(2)}, u32[]{:S(2)}) collective-permute-start(bf16[2,320,384]{2,1,0:T(8,128)(2,1)S(1)} %mid_edge.1), channel_id=1, source_target_pairs={{0,1},{1,0},{2,3},{3,2},{4,5},{5,4},{6,7},{7,6},{8,9},{9,8},{10,11... | collective-permute-start | bytes 1474568 | tf_op jit(solution)/shard_map/ppermute | solution.py:461

commit v13 on v7

--- a/solution.py
+++ b/solution.py
@@ -101,17 +101,19 @@
     out[place * cells : (place + 1) * cells, :] = dot32(normed, w_qkv[:, ch:]).astype(bf16)
 
 
-def keys_kernel(own_a, other_a, own_b, gain, w_qkv, kv_out):
-    gain_vec = gain[...].reshape(1, own_a.shape[1])
-    for place, block in enumerate((own_a, other_a, own_b)):
-        project_keys(block, gain_vec, w_qkv, kv_out, place)
-
-
-def attend_rows(source, kv_parts, gain_vec, w_qkv, w_out, att_out):
+def keys_kernel(own_a, other_a, own_b, gain, w_qkv, kv_out, q_out):
+    cells, ch = own_a.shape
+    gain_vec = gain[...].reshape(1, ch)
+    project_keys(other_a, gain_vec, w_qkv, kv_out, 1)
+    for place, block in ((0, own_a), (2, own_b)):
+        normed = rms_scale(block[...], gain_vec).astype(bf16)
+        qkv = dot32(normed, w_qkv[...]).astype(bf16)
+        q_out[place // 2] = qkv[:, :ch]
+        kv_out[place * cells : (place + 1) * cells, :] = qkv[:, ch:]
+
+
+def attend_rows(source, queries, kv_parts, w_out, att_out):
     ch = source.shape[1]
-    feats = source[...]
-    normed = rms_scale(feats, gain_vec).astype(bf16)
-    queries = dot32(normed, w_qkv[:, :ch]).astype(bf16)
     scores = [
         lax.dot_general(
             queries, kv[:, :ch], (((1,), (1,)), ((), ())), preferred_element_type=f32
@@ -124,18 +126,16 @@
     total = sum(jnp.sum(r, axis=1, keepdims=True) for r in raised)
     mixed = sum(dot32(r.astype(bf16), kv[:, ch:]) for r, kv in zip(raised, kv_parts))
     mixture = (mixed / total).astype(bf16)
-    att_out[...] = (feats.astype(f32) + dot32(mixture, w_out[...])).astype(bf16)
-
-
-def attend_kernel(other_b, own_a, kv_a, gain, w_qkv, w_out, kv_b, att_a):
-    gain_vec = gain[...].reshape(1, own_a.shape[1])
-    project_keys(other_b, gain_vec, w_qkv, kv_b, 0)
-    attend_rows(own_a, (kv_a, kv_b), gain_vec, w_qkv, w_out, att_a)
-
-
-def attend_rest_kernel(own_b, kv_a, kv_b, gain, w_qkv, w_out, att_b):
-    gain_vec = gain[...].reshape(1, own_b.shape[1])
-    attend_rows(own_b, (kv_a, kv_b), gain_vec, w_qkv, w_out, att_b)
+    att_out[...] = (source[...].astype(f32) + dot32(mixture, w_out[...])).astype(bf16)
+
+
+def attend_kernel(other_b, own_a, queries, kv_a, gain, w_qkv, w_out, kv_b, att_a):
+    project_keys(other_b, gain[...].reshape(1, own_a.shape[1]), w_qkv, kv_b, 0)
+    attend_rows(own_a, queries[0], (kv_a, kv_b), w_out, att_a)
+
+
+def attend_rest_kernel(own_b, queries, kv_a, kv_b, w_out, att_b):
+    attend_rows(own_b, queries[1], (kv_a, kv_b), w_out, att_b)
 
 
 def load_kernel(_, w_hbm, w_vm, sem):
@@ -338,24 +338,24 @@
     other_b = lax.ppermute(own_b, "span", other_core)
     kv_flops = 2 * 2 * cells * ch * 2 * ch
     row_flops = 2 * cells * ch * (2 * ch + 8 * cells)
-    kv_a = call(keys_kernel, "keys", struct((3 * cells, 2 * ch)), [VMEM] * 5, flops=kv_flops)(
-        own_a, other_a, own_b, norm_gain, w_qkv
-    )
+    kv_a, queries = call(
+        keys_kernel,
+        "keys",
+        (struct((3 * cells, 2 * ch)), struct((2, cells, ch))),
+        [VMEM] * 5,
+        flops=kv_flops,
+    )(own_a, other_a, own_b, norm_gain, w_qkv)
     kv_b, att_a = call(
         attend_kernel,
         "attend",
         (struct((cells, 2 * ch)), struct((cells, ch))),
-        [VMEM] * 6,
+        [VMEM] * 7,
         flops=kv_flops + row_flops,
-    )(other_b, own_a, kv_a, norm_gain, w_qkv, w_out)
+    )(other_b, own_a, queries, kv_a, norm_gain, w_qkv, w_out)
     got_a = lax.ppermute(att_a, both, route_a)
     att_b = call(
-        attend_rest_kernel,
-        "attend_rest",
-        struct((cells, ch)),
-        [VMEM] * 6,
-        flops=3 * row_flops,
-    )(own_b, kv_a, kv_b, norm_gain, w_qkv, w_out)
+        attend_rest_kernel, "attend_rest", struct((cells, ch)), [VMEM] * 5, flops=3 * row_flops
+    )(own_b, queries, kv_a, kv_b, w_out)
     got_b = lax.ppermute(att_b, both, route_b)
     pairs, middle = [(0, 1), (1, 0), (2, 3), (3, 2)], [(1, 2), (2, 1)]
     one, edge = struct((cells, ch)), struct((cols, ch))

time: 58.3 us -> 58.2 us (level)
  no operation moved by 1% of the time
where the time goes in v13:
time: 58.2 us; the launch traced here: 57.9 us
  Pallas kernels  22.4 us (38%)
  starting transfers between devices  20 us (34%)
  waiting for transfers between devices  14.6 us (25%)
  between operations  0.82 us (1%)
    ppermute x1, waiting for transfers between devices, on_device(): own_a = lax.ppermute(send_a, both, route_a)  6.34 us
    ppermute x1, starting transfers between devices, on_device(): own_a = lax.ppermute(send_a, both, route_a)  4.78 us
    pallas_call x1, Pallas kernels, on_device(): call(functools.partial(own_kernel, cols), 'own', (sums, struct((frames, c...  4.61 us
    ppermute x1, starting transfers between devices, on_device(): link_got = lax.ppermute(for_next, 'span', link)  4.17 us
    ppermute x1, starting transfers between devices, on_device(): got_a = lax.ppermute(att_a, both, route_a)  3.98 us
    pallas_call x1, Pallas kernels, on_device(): call(load_kernel, 'load_conv', struct((3, 3 * ch, 3 * ch)), [ANY, ANY], [...  3.48 us
    pallas_call x1, Pallas kernels, on_device(): call(functools.partial(next_own_kernel, cols), 'next_own', sums, [SMEM] *...  2.63 us
    ppermute x1, waiting for transfers between devices, on_device(): own_b = lax.ppermute(send_b, both, route_b)  2.63 us
  transfers between devices with their start and end apart: 12, of which 6 were waited for; matrix products, arithmetic and copies ran while one was open for 0% of the time, Pallas kernels for 28%

profile of v13, /device:TPU:13, one launch (start us, length us, event | category | flops | bytes accessed | tf_op | source)
XLA Modules:
  0.0 57.9 jit_solution(11609225678397079683)
XLA Ops:
  0.6 1.1 %pick.1 = (bf16[320,384]{1,0:T(8,128)(2,1)S(1)}, bf16[320,384]{1,0:T(8,128)(2,1)S(1)}) custom-call(s32[1]{0:T(128)} %bitcast.tile_ref, bf16[2,320,384]{2,1,0:T(8,128)(2,1)} %bitcast.5), custom_call_target="tpu_custom_call" | custom-call | bytes 1048576 | tf_op jit(solution)/shard_map/pick/pallas_call | solution.py:318
  1.7 4.8 %collective-permute-start.1 = (bf16[320,384]{1,0:T(8,128)(2,1)S(1)}, bf16[320,384]{1,0:T(8,128)(2,1)S(1)}, u32[]{:S(2)}, u32[]{:S(2)}) collective-permute-start(bf16[320,384]{1,0:T(8,128)(2,1)S(1)} %get-tuple-element.22), channel_id=1, source_target_pairs={{0,0},{1,8},{2,2},{3,10},{4,4},{5,12},{6,6},{7,14},{8,1},{9,9},{10... | collective-permute-start | bytes 737288 | tf_op jit(solution)/shard_map/ppermute | solution.py:326
  6.5 0.1 collective-permute-start
  6.6 1.9 %load_small.1 = (bf16[384,1152]{1,0:T(8,128)(2,1)S(1)}, bf16[384,384]{1,0:T(8,128)(2,1)S(1)}, f32[384]{0:T(512)S(1)}) custom-call(bf16[384,1152]{1,0:T(8,128)(2,1)} %w_qkv.1, bf16[384,384]{1,0:T(8,128)(2,1)} %w_out.1, f32[384]{0:T(512)} %gain.3), custom_call_target="tpu_custom_call" | custom-call | bytes 1048576 | tf_op jit(solution)/shard_map/load_small/pallas_call | solution.py:328
  8.5 6.3 %collective-permute-done.1.own_a = bf16[320,384]{1,0:T(8,128)(2,1)S(1)} collective-permute-done((bf16[320,384]{1,0:T(8,128)(2,1)S(1)}, bf16[320,384]{1,0:T(8,128)(2,1)S(1)}, u32[]{:S(2)}, u32[]{:S(2)}) %collective-permute-start.1) | collective-permute-done | bytes 245792 | tf_op jit(solution)/shard_map/ppermute | solution.py:326
  14.9 0.0 collective-permute-start.2
  14.9 2.6 %collective-permute-done.own_b = bf16[320,384]{1,0:T(8,128)(2,1)S(1)} collective-permute-done((bf16[320,384]{1,0:T(8,128)(2,1)S(1)}, bf16[320,384]{1,0:T(8,128)(2,1)S(1)}, u32[]{:S(2)}, u32[]{:S(2)}) %collective-permute-start) | collective-permute-done | bytes 245792 | tf_op jit(solution)/shard_map/ppermute | solution.py:327
  17.5 0.0 collective-permute-start.3
  17.5 0.0 collective-permute-done.2.other_a
  17.5 1.3 %keys.1 = (bf16[960,768]{1,0:T(8,128)(2,1)S(1)}, bf16[2,320,384]{2,1,0:T(8,128)(2,1)S(1)}) custom-call(bf16[320,384]{1,0:T(8,128)(2,1)S(1)} %collective-permute-done.1.own_a, bf16[320,384]{1,0:T(8,128)(2,1)S(1)} %collective-permute-done.2.other_a, bf16[320,384]{1,0:T(8,128)(2,1)S(1)} %collective-permute-done.own_b, f32[384]{0:T(512)S(1)} %get-tuple-element.25.gain, ...), custom_call_target="tpu_custom_call" | custom-call | flops 377487360 | bytes 1048576 | tf_op jit(solution)/shard_map/keys/pallas_call | solution.py:341
  18.8 0.2 collective-permute-done.3.other_b
  19.0 2.1 %attend.1 = (bf16[320,768]{1,0:T(8,128)(2,1)S(1)}, bf16[320,384]{1,0:T(8,128)(2,1)S(1)}) custom-call(bf16[320,384]{1,0:T(8,128)(2,1)S(1)} %collective-permute-done.3.other_b, bf16[320,384]{1,0:T(8,128)(2,1)S(1)} %collective-permute-done.1.own_a, bf16[2,320,384]{2,1,0:T(8,128)(2,1)S(1)} %get-tuple-element.27.queries, ...), custom_call_target="tpu_custom_call" | custom-call | flops 1195376640 | bytes 1048576 | tf_op jit(solution)/shard_map/attend/pallas_call | solution.py:348
  21.1 4.0 %collective-permute-start.5 = (bf16[320,384]{1,0:T(8,128)(2,1)S(1)}, bf16[320,384]{1,0:T(8,128)(2,1)S(1)}, u32[]{:S(2)}, u32[]{:S(2)}) collective-permute-start(bf16[320,384]{1,0:T(8,128)(2,1)S(1)} %get-tuple-element.31), channel_id=1, source_target_pairs={{0,0},{1,8},{2,2},{3,10},{4,4},{5,12},{6,6},{7,14},{8,1},{9,9},{10... | collective-permute-start | bytes 737288 | tf_op jit(solution)/shard_map/ppermute | solution.py:355
  25.1 1.8 %attend_rest.1._ = bf16[320,384]{1,0:T(8,128)(2,1)S(1)} custom-call(bf16[320,384]{1,0:T(8,128)(2,1)S(1)} %collective-permute-done.own_b, bf16[2,320,384]{2,1,0:T(8,128)(2,1)S(1)} %get-tuple-element.27.queries, bf16[960,768]{1,0:T(8,128)(2,1)S(1)} %get-tuple-element.28.kv_a, bf16[320,768]{1,0:T(8,128)(2,1)S(1)} %get-tuple-element.30.kv_b, ...), custom_call_target="tpu_custom_call" | custom-call | flops 2453667840 | bytes 1048576 | tf_op jit(solution)/shard_map/attend_rest/pallas_call | solution.py:356
  26.9 0.5 collective-permute-start.4
  27.4 0.0 copy-start
  27.4 3.5 %load_conv.1._.w = bf16[3,1152,1152]{2,1,0:T(8,128)(2,1)S(1)} custom-call(bf16[320,384]{1,0:T(8,128)(2,1)S(1)} %attend_rest.1._, bf16[3,3,3,384,384]{4,3,2,1,0:T(8,128)(2,1)} %w_hbm.1), custom_call_target="tpu_custom_call" | custom-call | bytes 4096 | tf_op jit(solution)/shard_map/load_conv/pallas_call | solution.py:365
  30.9 0.0 copy-start.1
  30.9 0.0 collective-permute-done.5.got_a
  30.9 0.0 copy-done
  31.0 0.3 activate_a.1
  31.3 2.4 %collective-permute-start.6 = (bf16[160,384]{1,0:T(8,128)(2,1)S(1)}, bf16[160,384]{1,0:T(8,128)(2,1)S(1)}, u32[]{:S(2)}, u32[]{:S(2)}) collective-permute-start(bf16[160,384]{1,0:T(8,128)(2,1)S(1)} %get-tuple-element.34), channel_id=1, source_target_pairs={{0,4},{4,0},{8,12},{12,8},{1,5},{5,1},{9,13},{13,9},{2,6},{6,2},{1... | collective-permute-start | bytes 368648 | tf_op jit(solution)/shard_map/ppermute | solution.py:377
  33.6 1.9 %collective-permute-start.7 = (bf16[160,384]{1,0:T(8,128)(2,1)S(1)}, bf16[160,384]{1,0:T(8,128)(2,1)S(1)}, u32[]{:S(2)}, u32[]{:S(2)}) collective-permute-start(bf16[160,384]{1,0:T(8,128)(2,1)S(1)} %get-tuple-element.35), channel_id=1, source_target_pairs={{4,8},{8,4},{5,9},{9,5},{6,10},{10,6},{7,11},{11,7},{20,24},{24,20... | collective-permute-start | bytes 368648 | tf_op jit(solution)/shard_map/ppermute | solution.py:378
  35.5 1.7 %collective-permute-done.4.got_b = bf16[320,384]{1,0:T(8,128)(2,1)S(1)} collective-permute-done((bf16[320,384]{1,0:T(8,128)(2,1)S(1)}, bf16[320,384]{1,0:T(8,128)(2,1)S(1)}, u32[]{:S(2)}, u32[]{:S(2)}) %collective-permute-start.4) | collective-permute-done | bytes 245792 | tf_op jit(solution)/shard_map/ppermute | solution.py:359
  37.3 0.3 activate_b.1
  37.6 0.3 collective-permute-start.8
  37.9 1.9 %collective-permute-start.9 = (bf16[160,384]{1,0:T(8,128)(2,1)S(1)}, bf16[160,384]{1,0:T(8,128)(2,1)S(1)}, u32[]{:S(2)}, u32[]{:S(2)}) collective-permute-start(bf16[160,384]{1,0:T(8,128)(2,1)S(1)} %get-tuple-element.37), channel_id=1, source_target_pairs={{4,8},{8,4},{5,9},{9,5},{6,10},{10,6},{7,11},{11,7},{20,24},{24,20... | collective-permute-start | bytes 368648 | tf_op jit(solution)/shard_map/ppermute | solution.py:386
  39.8 0.0 copy-done.1
  39.8 2.6 %next_own.1.partial = f32[2,320,384]{2,1,0:T(8,128)S(1)} custom-call(s32[1]{0:T(128)} %bitcast.1.span_ref, s32[4]{0:T(128)S(1)} %copy-done.1, bf16[2,320,384]{2,1,0:T(8,128)(2,1)S(1)} %get-tuple-element.33.mid, bf16[3,1152,1152]{2,1,0:T(8,128)(2,1)S(1)} %load_conv.1._.w), custom_call_target="tpu_custom_call" | custom-call | flops 1698693120 | bytes 1048576 | tf_op jit(solution)/shard_map/next_own/pallas_call | solution.py:388
  42.4 0.0 collective-permute-done.6.pair_a
  42.4 0.0 collective-permute-done.7.mid_a
  42.5 0.0 collective-permute-done.8.pair_b
  42.5 1.9 %collective-permute-done.9.mid_b = bf16[160,384]{1,0:T(8,128)(2,1)S(1)} collective-permute-done((bf16[160,384]{1,0:T(8,128)(2,1)S(1)}, bf16[160,384]{1,0:T(8,128)(2,1)S(1)}, u32[]{:S(2)}, u32[]{:S(2)}) %collective-permute-start.9) | collective-permute-done | bytes 122912 | tf_op jit(solution)/shard_map/ppermute | solution.py:386
  44.3 2.0 %next_edge.1 = bf16[2,320,384]{2,1,0:T(8,128)(2,1)S(1)} custom-call(s32[1]{0:T(128)} %bitcast.tile_ref, s32[1]{0:T(128)} %bitcast.1.span_ref, s32[4]{0:T(128)S(1)} %copy-done.1, bf16[160,384]{1,0:T(8,128)(2,1)S(1)} %collective-permute-done.6.pair_a, bf16[160,384]{1,0:T(8,128)(2,1)S(1)} %collective-permute-done.7.mid_a, ...), custom_call_target="tpu_custom_call" | custom-call | flops 849346560 | bytes 1048576 | tf_op jit(solution)/shard_map/next_edge/pallas_call | solution.py:395
  46.3 4.2 %collective-permute-start.10 = (bf16[2,320,384]{2,1,0:T(8,128)(2,1)S(1)}, bf16[2,320,384]{2,1,0:T(8,128)(2,1)S(1)}, u32[]{:S(2)}, u32[]{:S(2)}) collective-permute-start(bf16[2,320,384]{2,1,0:T(8,128)(2,1)S(1)} %next_edge.1), channel_id=1, source_target_pairs={{1,2},{2,1},{5,6},{6,5},{9,10},{10,9},{13,14},{14,13},{17,18},{18,... | collective-permute-start | bytes 1474568 | tf_op jit(solution)/shard_map/ppermute | solution.py:403
  50.5 0.1 collective-permute-start.11
  50.6 4.6 %own.1 = (f32[2,320,384]{2,1,0:T(8,128)S(1)}, bf16[2,320,384]{2,1,0:T(8,128)(2,1)}) custom-call(s32[1]{0:T(128)} %bitcast.tile_ref, s32[1]{0:T(128)} %bitcast.1.span_ref, s32[4]{0:T(128)S(1)} %copy-done.1, bf16[2,320,384]{2,1,0:T(8,128)(2,1)S(1)} %get-tuple-element.33.mid, bf16[160,384]{1,0:T(8,128)(2,1)S(1)} %collective-permute-done.6.pair_a, ...), custom_call_target="tpu_custom_call" | custom-call | flops 2548039680 | bytes 1048576 | tf_op jit(solution)/shard_map/own/pallas_call | solution.py:405
  55.2 1.8 %collective-permute-done.10.link_got = bf16[2,320,384]{2,1,0:T(8,128)(2,1)S(1)} collective-permute-done((bf16[2,320,384]{2,1,0:T(8,128)(2,1)S(1)}, bf16[2,320,384]{2,1,0:T(8,128)(2,1)S(1)}, u32[]{:S(2)}, u32[]{:S(2)}) %collective-permute-start.10) | collective-permute-done | bytes 491552 | tf_op jit(solution)/shard_map/ppermute | solution.py:403
  57.0 0.0 collective-permute-done.11.core_got
  57.0 0.9 %finish.1 = bf16[2,320,384]{2,1,0:T(8,128)(2,1)} custom-call(s32[1]{0:T(128)} %bitcast.1.span_ref, f32[2,320,384]{2,1,0:T(8,128)S(1)} %get-tuple-element.39.own, bf16[2,320,384]{2,1,0:T(8,128)(2,1)S(1)} %collective-permute-done.10.link_got, bf16[2,320,384]{2,1,0:T(8,128)(2,1)S(1)} %collective-permute-done.11.core_got), custom_call_target="tpu_custom_call" | custom-call | bytes 1048576 | tf_op jit(solution)/shard_map/finish/pallas_call | solution.py:412
Async XLA Ops:
  1.7 13.1 %collective-permute-start.1 = (bf16[320,384]{1,0:T(8,128)(2,1)S(1)}, bf16[320,384]{1,0:T(8,128)(2,1)S(1)}, u32[]{:S(2)}, u32[]{:S(2)}) collective-permute-start(bf16[320,384]{1,0:T(8,128)(2,1)S(1)} %get-tuple-element.22), channel_id=1, source_target_pairs={{0,0},{1,8},{2,2},{3,10},{4,4},{5,12},{6,6},{7,14},{8,1},{9,9},{10... | collective-permute-start | bytes 737288 | tf_op jit(solution)/shard_map/ppermute | solution.py:326
  6.5 11.0 %collective-permute-start = (bf16[320,384]{1,0:T(8,128)(2,1)S(1)}, bf16[320,384]{1,0:T(8,128)(2,1)S(1)}, u32[]{:S(2)}, u32[]{:S(2)}) collective-permute-start(bf16[320,384]{1,0:T(8,128)(2,1)S(1)} %get-tuple-element.21), channel_id=1, source_target_pairs={{0,4},{1,12},{2,6},{3,14},{4,0},{5,8},{6,2},{7,10},{8,5},{9,13},{1... | collective-permute-start | bytes 737288 | tf_op jit(solution)/shard_map/ppermute | solution.py:327
  14.9 2.6 %collective-permute-start.2 = (bf16[320,384]{1,0:T(8,128)(2,1)S(1)}, bf16[320,384]{1,0:T(8,128)(2,1)S(1)}, u32[]{:S(2)}, u32[]{:S(2)}) collective-permute-start(bf16[320,384]{1,0:T(8,128)(2,1)S(1)} %collective-permute-done.1.own_a), channel_id=1, source_target_pairs={{0,1},{1,0},{2,3},{3,2},{4,5},{5,4},{6,7},{7,6},{8,9},{9,8},{10,11... | collective-permute-start | bytes 737288 | tf_op jit(solution)/shard_map/ppermute | solution.py:337
  17.5 1.5 %collective-permute-start.3 = (bf16[320,384]{1,0:T(8,128)(2,1)S(1)}, bf16[320,384]{1,0:T(8,128)(2,1)S(1)}, u32[]{:S(2)}, u32[]{:S(2)}) collective-permute-start(bf16[320,384]{1,0:T(8,128)(2,1)S(1)} %collective-permute-done.own_b), channel_id=1, source_target_pairs={{0,1},{1,0},{2,3},{3,2},{4,5},{5,4},{6,7},{7,6},{8,9},{9,8},{10,11... | collective-permute-start | bytes 737288 | tf_op jit(solution)/shard_map/ppermute | solution.py:338
  21.1 9.8 %collective-permute-start.5 = (bf16[320,384]{1,0:T(8,128)(2,1)S(1)}, bf16[320,384]{1,0:T(8,128)(2,1)S(1)}, u32[]{:S(2)}, u32[]{:S(2)}) collective-permute-start(bf16[320,384]{1,0:T(8,128)(2,1)S(1)} %get-tuple-element.31), channel_id=1, source_target_pairs={{0,0},{1,8},{2,2},{3,10},{4,4},{5,12},{6,6},{7,14},{8,1},{9,9},{10... | collective-permute-start | bytes 737288 | tf_op jit(solution)/shard_map/ppermute | solution.py:355
  26.9 10.3 %collective-permute-start.4 = (bf16[320,384]{1,0:T(8,128)(2,1)S(1)}, bf16[320,384]{1,0:T(8,128)(2,1)S(1)}, u32[]{:S(2)}, u32[]{:S(2)}) collective-permute-start(bf16[320,384]{1,0:T(8,128)(2,1)S(1)} %attend_rest.1._), channel_id=1, source_target_pairs={{0,4},{1,12},{2,6},{3,14},{4,0},{5,8},{6,2},{7,10},{8,5},{9,13},{1... | collective-permute-start | bytes 737288 | tf_op jit(solution)/shard_map/ppermute | solution.py:359
  27.4 3.5 %copy-start = (f32[384]{0:T(512)S(1)}, f32[384]{0:T(512)}, u32[]{:S(2)}) copy-start(f32[384]{0:T(512)} %gain.5) | copy-start | bytes 4612
  30.9 8.9 %copy-start.1 = (s32[4]{0:T(128)S(1)}, s32[4]{0:T(128)}, u32[]{:S(2)}) copy-start(s32[4]{0:T(128)} %clips.5) | copy-start | bytes 52
  31.3 11.2 %collective-permute-start.6 = (bf16[160,384]{1,0:T(8,128)(2,1)S(1)}, bf16[160,384]{1,0:T(8,128)(2,1)S(1)}, u32[]{:S(2)}, u32[]{:S(2)}) collective-permute-start(bf16[160,384]{1,0:T(8,128)(2,1)S(1)} %get-tuple-element.34), channel_id=1, source_target_pairs={{0,4},{4,0},{8,12},{12,8},{1,5},{5,1},{9,13},{13,9},{2,6},{6,2},{1... | collective-permute-start | bytes 368648 | tf_op jit(solution)/shard_map/ppermute | solution.py:377
  33.6 8.8 %collective-permute-start.7 = (bf16[160,384]{1,0:T(8,128)(2,1)S(1)}, bf16[160,384]{1,0:T(8,128)(2,1)S(1)}, u32[]{:S(2)}, u32[]{:S(2)}) collective-permute-start(bf16[160,384]{1,0:T(8,128)(2,1)S(1)} %get-tuple-element.35), channel_id=1, source_target_pairs={{4,8},{8,4},{5,9},{9,5},{6,10},{10,6},{7,11},{11,7},{20,24},{24,20... | collective-permute-start | bytes 368648 | tf_op jit(solution)/shard_map/ppermute | solution.py:378
  37.6 4.9 %collective-permute-start.8 = (bf16[160,384]{1,0:T(8,128)(2,1)S(1)}, bf16[160,384]{1,0:T(8,128)(2,1)S(1)}, u32[]{:S(2)}, u32[]{:S(2)}) collective-permute-start(bf16[160,384]{1,0:T(8,128)(2,1)S(1)} %get-tuple-element.36), channel_id=1, source_target_pairs={{0,4},{4,0},{8,12},{12,8},{1,5},{5,1},{9,13},{13,9},{2,6},{6,2},{1... | collective-permute-start | bytes 368648 | tf_op jit(solution)/shard_map/ppermute | solution.py:385
  37.9 6.5 %collective-permute-start.9 = (bf16[160,384]{1,0:T(8,128)(2,1)S(1)}, bf16[160,384]{1,0:T(8,128)(2,1)S(1)}, u32[]{:S(2)}, u32[]{:S(2)}) collective-permute-start(bf16[160,384]{1,0:T(8,128)(2,1)S(1)} %get-tuple-element.37), channel_id=1, source_target_pairs={{4,8},{8,4},{5,9},{9,5},{6,10},{10,6},{7,11},{11,7},{20,24},{24,20... | collective-permute-start | bytes 368648 | tf_op jit(solution)/shard_map/ppermute | solution.py:386
  46.3 10.7 %collective-permute-start.10 = (bf16[2,320,384]{2,1,0:T(8,128)(2,1)S(1)}, bf16[2,320,384]{2,1,0:T(8,128)(2,1)S(1)}, u32[]{:S(2)}, u32[]{:S(2)}) collective-permute-start(bf16[2,320,384]{2,1,0:T(8,128)(2,1)S(1)} %next_edge.1), channel_id=1, source_target_pairs={{1,2},{2,1},{5,6},{6,5},{9,10},{10,9},{13,14},{14,13},{17,18},{18,... | collective-permute-start | bytes 1474568 | tf_op jit(solution)/shard_map/ppermute | solution.py:403
  50.5 6.5 %collective-permute-start.11 = (bf16[2,320,384]{2,1,0:T(8,128)(2,1)S(1)}, bf16[2,320,384]{2,1,0:T(8,128)(2,1)S(1)}, u32[]{:S(2)}, u32[]{:S(2)}) collective-permute-start(bf16[2,320,384]{2,1,0:T(8,128)(2,1)S(1)} %next_edge.1), channel_id=1, source_target_pairs={{0,1},{1,0},{2,3},{3,2},{4,5},{5,4},{6,7},{7,6},{8,9},{9,8},{10,11... | collective-permute-start | bytes 1474568 | tf_op jit(solution)/shard_map/ppermute | solution.py:404
